TPU v7x, 512 devices: a whole 4x8x8 slice. The times are simulated.
512 devices in a mesh: seq: 64 (over z_hi, x, y), width: 8 (over z_lo, core).
Axes of the slice: x: 4, y: 8, z: 8 (z_hi: 2, z_lo: 4; z = z_hi * 4 + z_lo), core: 2. Of those that a mesh axis runs over, the one named last changes fastest.
Arguments:
- projected: bfloat16 [32768, 3, 4096], P('seq', None, 'width'), may hold values from -6 to 6
- short_filter: float32 [3, 3, 4096], P(None, None, 'width'), may hold values from -3.5 to 3.5
- long_filter: bfloat16 [256, 128], P('width'), may hold values from -0.5 to 0.5
- out_weight: bfloat16 [4096, 4096], P('seq', 'width'), may hold values from -0.09375 to 0.09375
Outputs:
- mixed: bfloat16 [32768, 4096], P('seq', 'width')
All inputs are finite; a program needn't handle non-finite values.
Results may differ from a plain program's by a relative error of at most 0.0057.
Values may be sent and summed in bfloat16 or wider, within the bound.
No kernel may reach another device: no remote copies, remote signals or barrier semaphores. Data moves between devices by JAX's collectives and lax.ppermute only.
A program may use at most 64 MiB of HBM per device.

v0:
```python
import jax
import jax.numpy as jnp
from jax import lax
from jax.sharding import PartitionSpec as P


def from_behind(array, axis, by):
    devices = lax.axis_size(axis)
    pairs = [(i, i + by) for i in range(devices) if 0 <= i + by < devices]
    return lax.ppermute(array, axis, pairs)


def featurize_joined(joined, short_filter):
    values = joined.astype(jnp.float32)
    return (
        short_filter[0] * values[2:]
        + short_filter[1] * values[1:-1]
        + short_filter[2] * values[:-2]
    )


def toeplitz_of(long_filter):
    span = long_filter.shape[1]
    row_ids = jnp.arange(span, dtype=jnp.int32)[:, None]
    col_ids = jnp.arange(2 * span - 1, dtype=jnp.int32)[None, :]
    tap_index = row_ids - col_ids + (span - 1)
    inside = (tap_index >= 0) & (tap_index < span)
    picked = jnp.take(long_filter, jnp.clip(tap_index, 0, span - 1), axis=1)
    return jnp.where(inside[None], picked, jnp.zeros_like(picked))


def long_conv(extended, toeplitz, out_rows):
    span = toeplitz.shape[1]
    groups = toeplitz.shape[0]
    channels = extended.shape[1]

    def one_block(block_index):
        window_rows = lax.dynamic_slice_in_dim(extended, block_index * span, 2 * span - 1, 0)
        window_rows = window_rows.reshape(2 * span - 1, groups, channels // groups)
        result = jnp.einsum(
            "gij,jgc->igc", toeplitz, window_rows, preferred_element_type=jnp.float32
        )
        return result.reshape(span, channels)

    blocks = lax.map(one_block, jnp.arange(out_rows // span, dtype=jnp.int32))
    return blocks.reshape(out_rows, channels)


def on_device(projected, short_filter, long_filter, out_weight):
    tok_rows = projected.shape[0]
    span = long_filter.shape[1]
    tail_rows = projected[tok_rows - span - 1 :]
    previous = from_behind(tail_rows, "seq", 1)
    joined = jnp.concatenate([previous, projected], axis=0)
    featured = featurize_joined(joined, short_filter)
    extended = (featured[:, 1] * featured[:, 2]).astype(jnp.bfloat16)
    query = featured[span - 1 :, 0]
    filtered = long_conv(extended, toeplitz_of(long_filter), tok_rows)
    gated = (query * filtered).astype(jnp.bfloat16)
    gathered = lax.all_gather(gated, "width", axis=1, tiled=True)
    mixed = jnp.dot(
        gathered,
        lax.all_gather(out_weight, "seq", axis=0, tiled=True),
        preferred_element_type=jnp.float32,
    )
    return mixed.astype(jnp.bfloat16)


def solution(mesh):
    in_specs = (
        P("seq", None, "width"),
        P(None, None, "width"),
        P("width", None),
        P("seq", "width"),
    )
    out_specs = P("seq", "width")
    return jax.shard_map(
        on_device, mesh=mesh, in_specs=in_specs, out_specs=out_specs, check_vma=False
    )
```

profile of v0, /device:TPU:4, one launch (start us, length us, event | category | flops | bytes accessed | tf_op | source)
XLA Modules:
  0.0 351.0 jit_solution(13737784177788745816)
XLA Ops:
  6.5 0.0 all-gather.3.cloned.1.call-start
  6.5 1.1 slice.31
  7.6 3.5 collective-permute-start
  11.2 0.7 slice_bitcast_fusion.3
  11.9 0.3 reshape.76
  12.3 0.8 copy.9
  13.1 65.9 %gather_fusion = bf16[32640,32]{1,0:T(8,128)(2,1)} fusion(bf16[32,128]{0,1:T(8,128)(2,1)S(1)} %copy.9, s32[32768]{0:T(1024)S(1)} %pad_clamp_fusion), kind=kCustom, calls=%fused_computation | custom fusion | bytes 4308480 | tf_op jit(solution)/shard_map/jit(_take)/gather | solution.py:28
  79.0 6.9 %copy.10 = bf16[32640,32]{0,1:T(8,128)(2,1)S(1)} copy(bf16[32640,32]{1,0:T(8,128)(2,1)} %gather_fusion) | data formatting | bytes 4177920 | tf_op jit(solution)/shard_map/jit(_take)/gather | solution.py:28
  85.8 7.8 %reshape.79 = bf16[128,255,32]{1,0,2:T(8,128)(2,1)} reshape(bf16[32640,32]{0,1:T(8,128)(2,1)S(1)} %copy.10) | data formatting | bytes 4177920 | tf_op jit(solution)/shard_map/jit(_take)/gather | solution.py:28
  93.6 0.1 fusion.10
  93.7 1.9 select_bitcast_fusion
  95.7 0.0 collective-permute-done
  95.7 0.6 maximum_convert_fusion
  96.3 1.2 fusion
  97.4 1.9 copy-done
  99.3 0.2 fusion.5
  99.5 12.1 %while.10 = (s32[]{:T(128)}, f32[4,128,512]{2,1,0:T(8,128)}, s32[4]{0:T(128)S(1)}, bf16[639,512]{1,0:T(8,128)(2,1)S(1)}, bf16[32,128,255]{2,1,0:T(8,128)(2,1)S(1...) while((s32[]{:T(128)}, f32[4,128,512]{2,1,0:T(8,128)}, s32[4]{0:T(128)S(1)}, ...), condition=%wide.region_1.2_spmd, body=%wide.region_0.1_spmd.sunk | while | flops 33423364 | bytes 4705947 | solution.py:45
  99.5 0.6 dynamic_slice.11
  100.8 0.1 constant_dynamic-slice_fusion.2
  100.9 0.1 copy.18
  101.0 0.6 fusion.22
  101.6 0.2 copy.19
  101.8 0.8 constant_dynamic-update-slice_fusion.2
  102.6 0.6 dynamic_slice.11
  103.8 0.1 constant_dynamic-slice_fusion.2
  103.9 0.1 copy.18
  104.0 0.6 fusion.22
  104.7 0.2 copy.19
  104.8 0.7 constant_dynamic-update-slice_fusion.2
  105.6 0.6 dynamic_slice.11
  106.9 0.1 constant_dynamic-slice_fusion.2
  106.9 0.1 copy.18
  107.1 0.6 fusion.22
  107.7 0.2 copy.19
  107.9 0.7 constant_dynamic-update-slice_fusion.2
  108.6 0.6 dynamic_slice.11
  109.9 0.1 constant_dynamic-slice_fusion.2
  110.0 0.1 copy.18
  110.1 0.6 fusion.22
  110.7 0.2 copy.19
  110.9 0.7 constant_dynamic-update-slice_fusion.2
  111.6 2.6 fusion.4
  114.2 0.0 all-gather.3.cloned.1.call-update
  114.2 0.0 all-gather.5.cloned.1.call-start
  114.3 0.7 all-gather.5.cloned.1.call-update
  115.0 60.9 %all-gather.3.cloned.1.call-done = bf16[512,4096]{1,0:T(8,128)(2,1)} async-done(((bf16[512,512]{1,0:T(8,128)(2,1)}), bf16[512,4096]{1,0:T(8,128)(2,1)}) %all-gather.3.cloned.1.call-update) | async-done | bytes 4194320 | tf_op jit(solution)/shard_map/all_gather | solution.py:60
  175.9 161.7 %all-gather.5.cloned.1.call-done = bf16[4096,512]{1,0:T(8,128)(2,1)} async-done(((bf16[64,512]{1,0:T(8,128)(2,1)}), bf16[4096,512]{1,0:T(8,128)(2,1)}) %all-gather.5.cloned.1.call-update) | async-done | bytes 4194320 | tf_op jit(solution)/shard_map/all_gather | solution.py:63
  337.5 6.6 %convolution_convert_fusion = bf16[512,512]{1,0:T(8,128)(2,1)} fusion(bf16[512,4096]{1,0:T(8,128)(2,1)} %all-gather.3.cloned.1.call-done, bf16[4096,512]{1,0:T(8,128)(2,1)} %all-gather.5.cloned.1.call-done), kind=kOutput, calls=%fused_computation.12 | convolution fusion | flops 2147745792 | bytes 8912896 | tf_op jit(solution)/shard_map/dot_general | solution.py:61
  (7 shorter events, 0.1 us)
Async XLA Ops:
  6.5 169.4 %all-gather.3.cloned.1.call-start = ((), (), s32[]{:S(2)}) async-start(), calls=%async_computation | async-start | bytes 4718592 | tf_op jit(solution)/shard_map/all_gather | solution.py:60
  7.6 88.0 %collective-permute-start = (bf16[129,3,512]{2,0,1:T(8,128)(2,1)S(1)}, bf16[129,3,512]{2,0,1:T(8,128)(2,1)S(1)}, u32[]{:S(2)}, u32[]{:S(2)}) collective-permute-start(bf16[129,3,512]{2,0,1:T(8,128)(2,1)S(1)} %slice.31), channel_id=1, source_target_pairs={{0,8},{8,16},{16,24},{24,32},{32,40},{40,48},{48,56},{56,64},{64,7... | collective-permute-start | bytes 1188872 | tf_op jit(solution)/shard_map/ppermute | solution.py:10
  93.6 2.0 copy-start.1
  97.4 1.9 copy-start
  114.2 223.3 %all-gather.5.cloned.1.call-start = ((), (), s32[]{:S(2)}) async-start(), calls=%async_computation.1 | async-start | bytes 4259840 | tf_op jit(solution)/shard_map/all_gather | solution.py:63
Sparse Core Ops, SparseCore 0:
  114.4 61.4 all-gather.2
  180.4 157.0 all-gather.4
where the time goes:
time: 351 us
  waiting for transfers between devices  223 us (64%)
  local copies, waits for them, and re-layouts  92.3 us (26%)
  between operations  13.5 us (4%)
  matrix products  9.11 us (3%)
  other arithmetic  6.61 us (2%)
  starting transfers between devices  3.53 us (1%)
    all_gather x1, waiting for transfers between devices, on_device(): lax.all_gather(out_weight, 'seq', axis=0, tiled=True)  162 us
    gather x3, local copies, waits for them, and re-layouts, toeplitz_of(): picked = jnp.take(long_filter, jnp.clip(tap_index, 0, span - 1), axis=1)  80.5 us
    all_gather x1, waiting for transfers between devices, on_device(): gathered = lax.all_gather(gated, 'width', axis=1, tiled=True)  60.9 us
  transfers between devices with their start and end apart: 3, of which 2 were waited for; matrix products, arithmetic and copies ran while one was open for 24% of the time, Pallas kernels for 0%

commit v1 on v0

v1 whole, which is shorter than its diff:
```python
import jax
import jax.numpy as jnp
from jax import lax
from jax.sharding import Mesh
from jax.sharding import PartitionSpec as P

SEQ_PARTS = (("zh", 2), ("x", 4), ("y", 8))
WIDTH_PARTS = (("zl", 4), ("c", 2))
SEQ = tuple(n for n, _ in SEQ_PARTS)
WIDTH = tuple(n for n, _ in WIDTH_PARTS)


def from_behind(array):
    total = 1
    for _, size in SEQ_PARTS:
        total *= size
    pairs = [(i, i + 1) for i in range(total - 1)]
    return lax.ppermute(array, SEQ, pairs)


def toeplitz_blocks(long_filter):
    groups, span = long_filter.shape
    period = 3 * span
    row = jnp.concatenate(
        [
            jnp.zeros((groups, 1), long_filter.dtype),
            long_filter[:, ::-1],
            jnp.zeros((groups, period - span - 1), long_filter.dtype),
        ],
        axis=1,
    )
    tiled = jnp.broadcast_to(row[:, None, :], (groups, span, period))
    flat = tiled.reshape(groups, span * period)[:, : span * (period - 1)]
    return flat.reshape(groups, span, period - 1)[:, :, : 2 * span]


def on_device(projected, short_filter, long_filter, out_weight):
    tok_rows = projected.shape[0]
    groups, span = long_filter.shape
    channels = projected.shape[2]

    partner = lax.ppermute(out_weight, "zh", [(0, 1), (1, 0)])
    zh = lax.axis_index("zh")
    pair = jnp.where(zh == 0, jnp.stack([out_weight, partner]), jnp.stack([partner, out_weight]))
    weight_xy = lax.all_gather(pair, ("x", "y"), axis=0, tiled=False)
    weight = jnp.transpose(weight_xy, (1, 0, 2, 3)).reshape(-1, weight_xy.shape[-1])

    tail = projected[tok_rows - span - 2 :]
    previous = from_behind(tail)
    joined = jnp.concatenate([previous, projected], axis=0).astype(jnp.float32)
    featured = (
        short_filter[0] * joined[2:]
        + short_filter[1] * joined[1:-1]
        + short_filter[2] * joined[:-2]
    )
    product = (featured[:, 1] * featured[:, 2]).astype(jnp.bfloat16)
    query = featured[span:, 0]

    blocks = product.reshape(tok_rows // span + 1, span, groups, channels // groups)
    window = jnp.concatenate([blocks[:-1], blocks[1:]], axis=1)
    toeplitz = toeplitz_blocks(long_filter)
    filtered = jnp.einsum(
        "gij,bjgc->bigc", toeplitz, window, preferred_element_type=jnp.float32
    ).reshape(tok_rows, channels)
    gated = (query * filtered).astype(jnp.bfloat16)

    g_zl = lax.all_gather(gated, "zl", axis=1, tiled=False)
    g_all = lax.all_gather(g_zl, "c", axis=2, tiled=False)
    gathered = g_all.reshape(tok_rows, -1)

    mixed = jnp.dot(gathered, weight, preferred_element_type=jnp.float32)
    return mixed.astype(jnp.bfloat16)


def solution(mesh):
    names = SEQ + WIDTH
    sizes = tuple(s for _, s in SEQ_PARTS + WIDTH_PARTS)
    fine = Mesh(mesh.devices.reshape(sizes), names)
    in_specs = (
        P(SEQ, None, WIDTH),
        P(None, None, WIDTH),
        P(WIDTH, None),
        P(SEQ, WIDTH),
    )
    out_specs = P(SEQ, WIDTH)
    return jax.shard_map(
        on_device, mesh=fine, in_specs=in_specs, out_specs=out_specs, check_vma=False
    )
```

time: 351 us -> 242 us (0.69)
  the two profiles are of different devices: /device:TPU:4 before, /device:TPU:8 now
where the time goes in v1:
time: 242 us; the launch traced here: 241 us
  waiting for transfers between devices  170 us (70%)
  local copies, waits for them, and re-layouts  32.3 us (13%)
  between operations  13.2 us (5%)
  starting transfers between devices  9.51 us (4%)
  matrix products  8.5 us (4%)
  other arithmetic  7.82 us (3%)
    all_gather x1, waiting for transfers between devices, on_device(): weight_xy = lax.all_gather(pair, ('x', 'y'), axis=0, tiled=False)  91.8 us
    all_gather x1, waiting for transfers between devices, on_device(): g_zl = lax.all_gather(gated, 'zl', axis=1, tiled=False)  63.5 us
    all_gather x1, waiting for transfers between devices, on_device(): g_all = lax.all_gather(g_zl, 'c', axis=2, tiled=False)  10.3 us
    slice x5, local copies, waits for them, and re-layouts, on_device(): window = jnp.concatenate([blocks[:-1], blocks[1:]], axis=1)  8.37 us
    reshape x1, local copies, waits for them, and re-layouts, toeplitz_blocks(): return flat.reshape(groups, span, period - 1)[:, :, :2 * span]  7.98 us
    dot_general x1, matrix products, on_device(): mixed = jnp.dot(gathered, weight, preferred_element_type=jnp.float32)  6.61 us
    unnamed x10, local copies, waits for them, and re-layouts  6.34 us
    ppermute x1, starting transfers between devices, on_device(): partner = lax.ppermute(out_weight, 'zh', [(0, 1), (1, 0)])  5.95 us
  transfers between devices with their start and end apart: 5, of which 4 were waited for; matrix products, arithmetic and copies ran while one was open for 6% of the time, Pallas kernels for 0%

profile of v1, /device:TPU:8, one launch (start us, length us, event | category | flops | bytes accessed | tf_op | source)
XLA Modules:
  0.0 241.2 jit_solution(16136537904694680190)
XLA Ops:
  6.5 0.0 copy-start.3
  6.5 0.0 all-gather.5.cloned.1.call-start
  6.5 1.9 slice.51
  8.4 3.5 %collective-permute-start = (bf16[130,3,512]{2,0,1:T(8,128)(2,1)}, bf16[130,3,512]{2,0,1:T(8,128)(2,1)S(1)}, u32[]{:S(2)}, u32[]{:S(2)}) collective-permute-start(bf16[130,3,512]{2,0,1:T(8,128)(2,1)} %slice.51), channel_id=1, source_target_pairs={{0,8},{8,16},{16,24},{24,32},{32,40},{40,48},{48,56},{56,64},{64,7... | collective-permute-start | bytes 1198088 | tf_op jit(solution)/shard_map/ppermute | solution.py:18
  11.9 2.6 %copy.11 = bf16[512,3,512]{0,2,1:T(8,128)(2,1)} copy(bf16[512,3,512]{2,0,1:T(8,128)(2,1)} %param.4) | data formatting | bytes 3145728 | tf_op args[0]
  14.5 0.0 copy-done.3
  14.5 0.1 rev.3
  14.6 0.1 pad.6.clone
  14.7 0.1 maximum_maximum_fusion
  14.7 0.3 broadcast_in_dim.14
  15.0 1.9 copy.18
  16.9 0.2 slice.74
  17.1 8.0 %reshape.86 = bf16[32,128,383]{2,1,0:T(8,128)(2,1)} reshape(bf16[32,49024]{1,0:T(8,128)(2,1)S(1)} %slice.74) | data formatting | bytes 6275072 | tf_op jit(solution)/shard_map/reshape | solution.py:34
  25.1 0.7 slice_bitcast_fusion.6
  25.8 0.0 collective-permute-done
  25.8 0.3 copy.10
  26.1 2.3 maximum_convert_fusion
  28.4 3.3 %fusion = f32[640,3,512]{0,2,1:T(8,128)S(1)} fusion(f32[642,3,512]{0,2,1:T(8,128)S(1)} %maximum_convert_fusion, f32[3,512]{1,0:T(4,128)S(1)} %get-tuple-element.8, f32[3,512]{1,0:T(4,128)S(1)} %get-tuple-element.9, f32[3,512]{1,0:T(4,128)S(1)} %get-tuple-element.7), kind=kLoop, calls=%fused_computation.1 | loop fusion | flops 4915200 | bytes 15747072 | tf_op jit(solution)/shard_map/add | solution.py:52
  31.7 0.0 copy-start
  31.7 1.9 copy-done
  33.6 0.1 fusion.4
  33.7 0.0 copy-start.1
  33.7 1.1 fusion.10
  34.8 2.3 slice.61
  37.0 2.0 copy.12
  39.0 2.0 slice.63
  40.9 1.1 copy.13
  42.1 0.0 copy-done.1
  42.1 1.9 fusion.3
  44.0 0.4 copy.14
  44.4 0.4 reshape.87
  44.8 1.4 fusion.5
  46.2 0.0 copy-start.2
  46.2 1.0 copy.15
  47.2 0.0 all-gather.5.cloned.1.call-update
  47.3 0.0 all-gather.9.cloned.1.call-start
  47.3 63.5 %all-gather.5.cloned.1.call-done = bf16[512,4,512]{2,0,1:T(8,128)(2,1)} async-done(((bf16[512,1,512]{2,0,1:T(8,128)(2,1)}), bf16[512,4,512]{2,0,1:T(8,128)(2,1)}) %all-gather.5.cloned.1.call-update) | async-done | bytes 2097168 | tf_op jit(solution)/shard_map/all_gather | solution.py:67
  110.8 4.2 %copy.16 = bf16[512,4,512]{0,2,1:T(8,128)(2,1)} copy(bf16[512,4,512]{2,0,1:T(8,128)(2,1)} %all-gather.5.cloned.1.call-done) | data formatting | bytes 4194304 | tf_op jit(solution)/shard_map/all_gather | solution.py:67
  115.0 0.0 all-gather.9.cloned.1.call-update
  115.0 0.0 all-gather.7.cloned.1.call-start
  115.0 0.0 copy-done.2
  115.1 6.0 %collective-permute-start.1 = (bf16[64,512]{1,0:T(8,128)(2,1)S(1)}, bf16[64,512]{1,0:T(8,128)(2,1)S(1)}, u32[]{:S(2)}, u32[]{:S(2)}) collective-permute-start(bf16[64,512]{1,0:T(8,128)(2,1)S(1)} %copy-done.2), channel_id=1, source_target_pairs={{0,256},{256,0},{1,257},{257,1},{2,258},{258,2},{3,259},{259,3},{4... | collective-permute-start | bytes 196616 | tf_op jit(solution)/shard_map/ppermute | solution.py:42
  121.0 4.2 %collective-permute-done.1 = bf16[64,512]{1,0:T(8,128)(2,1)S(1)} collective-permute-done((bf16[64,512]{1,0:T(8,128)(2,1)S(1)}, bf16[64,512]{1,0:T(8,128)(2,1)S(1)}, u32[]{:S(2)}, u32[]{:S(2)}) %collective-permute-start.1) | collective-permute-done | bytes 65568 | tf_op jit(solution)/shard_map/ppermute | solution.py:42
  125.2 0.7 maximum_select_fusion
  125.9 0.0 all-gather.7.cloned.1.call-update
  125.9 10.3 %all-gather.9.cloned.1.call-done = bf16[512,4,1024]{0,2,1:T(8,128)(2,1)} async-done(((bf16[512,4,512]{0,2,1:T(8,128)(2,1)}), bf16[512,4,1024]{0,2,1:T(8,128)(2,1)}) %all-gather.9.cloned.1.call-update) | async-done | bytes 4194320 | tf_op jit(solution)/shard_map/all_gather | solution.py:68
  136.2 91.8 %all-gather.7.cloned.1.call-done = bf16[32,2,64,512]{3,2,0,1:T(8,128)(2,1)} async-done(((bf16[1,2,64,512]{3,2,0,1:T(8,128)(2,1)}), bf16[32,2,64,512]{3,2,0,1:T(8,128)(2,1)}) %all-gather.7.cloned.1.call-update) | async-done | bytes 4194320 | tf_op jit(solution)/shard_map/all_gather | solution.py:45
  228.0 6.6 %convolution_convert_fusion = bf16[512,512]{1,0:T(8,128)(2,1)} fusion(bf16[512,4096]{0,1:T(8,128)(2,1)} %bitcast.36, bf16[4096,512]{1,0:T(8,128)(2,1)} %bitcast.37), kind=kOutput, calls=%fused_computation.11 | convolution fusion | flops 2147745792 | bytes 8912896 | tf_op jit(solution)/shard_map/dot_general | solution.py:71
  (2 shorter events, 0.0 us)
Async XLA Ops:
  6.5 8.0 %copy-start.3 = (bf16[32,128]{1,0:T(8,128)(2,1)S(1)}, bf16[32,128]{1,0:T(8,128)(2,1)}, u32[]{:S(2)}) copy-start(bf16[32,128]{1,0:T(8,128)(2,1)} %param.6) | copy-start | bytes 24580
  6.5 104.2 %all-gather.5.cloned.1.call-start = ((), (), s32[]{:S(2)}) async-start(), calls=%async_computation | async-start | bytes 2621440 | tf_op jit(solution)/shard_map/all_gather | solution.py:67
  8.4 17.4 %collective-permute-start = (bf16[130,3,512]{2,0,1:T(8,128)(2,1)}, bf16[130,3,512]{2,0,1:T(8,128)(2,1)S(1)}, u32[]{:S(2)}, u32[]{:S(2)}) collective-permute-start(bf16[130,3,512]{2,0,1:T(8,128)(2,1)} %slice.51), channel_id=1, source_target_pairs={{0,8},{8,16},{16,24},{24,32},{32,40},{40,48},{48,56},{56,64},{64,7... | collective-permute-start | bytes 1198088 | tf_op jit(solution)/shard_map/ppermute | solution.py:18
  31.7 1.9 copy-start
  33.7 8.4 %copy-start.1 = (bf16[32,128,383]{2,1,0:T(8,128)(2,1)S(1)}, bf16[32,128,383]{2,1,0:T(8,128)(2,1)}, u32[]{:S(2)}) copy-start(bf16[32,128,383]{2,1,0:T(8,128)(2,1)} %reshape.86) | copy-start | bytes 9412612
  46.2 68.8 %copy-start.2 = (bf16[64,512]{1,0:T(8,128)(2,1)S(1)}, bf16[64,512]{1,0:T(8,128)(2,1)}, u32[]{:S(2)}) copy-start(bf16[64,512]{1,0:T(8,128)(2,1)} %param.7) | copy-start | bytes 196612
  47.3 88.9 %all-gather.9.cloned.1.call-start = ((), (), s32[]{:S(2)}) async-start(), calls=%async_computation.2 | async-start | bytes 6291456 | tf_op jit(solution)/shard_map/all_gather | solution.py:68
  115.0 113.0 %all-gather.7.cloned.1.call-start = ((), (), s32[]{:S(2)}) async-start(), calls=%async_computation.1 | async-start | bytes 4325376 | tf_op jit(solution)/shard_map/all_gather | solution.py:45
  115.1 10.2 %collective-permute-start.1 = (bf16[64,512]{1,0:T(8,128)(2,1)S(1)}, bf16[64,512]{1,0:T(8,128)(2,1)S(1)}, u32[]{:S(2)}, u32[]{:S(2)}) collective-permute-start(bf16[64,512]{1,0:T(8,128)(2,1)S(1)} %copy-done.2), channel_id=1, source_target_pairs={{0,256},{256,0},{1,257},{257,1},{2,258},{258,2},{3,259},{259,3},{4... | collective-permute-start | bytes 196616 | tf_op jit(solution)/shard_map/ppermute | solution.py:42
Sparse Core Ops, SparseCore 0:
  47.4 63.3 all-gather.4
  115.1 21.0 all-gather.8
  139.4 88.5 all-gather.6

commit v2 on v1

--- a/solution.py
+++ b/solution.py
@@ -1,6 +1,8 @@
 import jax
 import jax.numpy as jnp
 from jax import lax
+from jax.experimental import pallas as pl
+from jax.experimental.pallas import tpu as pltpu
 from jax.sharding import Mesh
 from jax.sharding import PartitionSpec as P
 
@@ -18,20 +20,53 @@
     return lax.ppermute(array, SEQ, pairs)
 
 
+def toeplitz_kernel(row_ref, out_ref):
+    groups, span, width = out_ref.shape
+    period = row_ref.shape[1]
+
+    def one_group(g, carry):
+        row = row_ref[pl.ds(g, 1), :]
+        tiled = jnp.broadcast_to(row, (span, period))
+        rolled = pltpu.roll(tiled, shift=0, axis=1, stride=1, stride_axis=0)
+        out_ref[g] = rolled[:, :width].astype(out_ref.dtype)
+        return carry
+
+    lax.fori_loop(0, groups, one_group, 0)
+
+
 def toeplitz_blocks(long_filter):
     groups, span = long_filter.shape
     period = 3 * span
     row = jnp.concatenate(
         [
-            jnp.zeros((groups, 1), long_filter.dtype),
-            long_filter[:, ::-1],
-            jnp.zeros((groups, period - span - 1), long_filter.dtype),
+            jnp.zeros((groups, 1), jnp.float32),
+            long_filter[:, ::-1].astype(jnp.float32),
+            jnp.zeros((groups, period - span - 1), jnp.float32),
         ],
         axis=1,
     )
-    tiled = jnp.broadcast_to(row[:, None, :], (groups, span, period))
-    flat = tiled.reshape(groups, span * period)[:, : span * (period - 1)]
-    return flat.reshape(groups, span, period - 1)[:, :, : 2 * span]
+    return pl.pallas_call(
+        toeplitz_kernel,
+        out_shape=jax.ShapeDtypeStruct((groups, span, 2 * span), long_filter.dtype),
+    )(row)
+
+
+def line_gather(block, axis_name, size):
+    pieces = [None] * size
+    index = lax.axis_index(axis_name)
+    received = {}
+    for offset in range(1, size):
+        for sign in (1, -1):
+            d = sign * offset
+            pairs = [(i, i + d) for i in range(size) if 0 <= i + d < size]
+            received[d] = lax.ppermute(block, axis_name, pairs)
+    parts = []
+    for source in range(size):
+        choice = jnp.zeros_like(block)
+        for d, value in received.items():
+            choice = jnp.where(index - d == source, value, choice)
+        parts.append(jnp.where(index == source, block, choice))
+    return jnp.stack(parts, axis=1)
 
 
 def on_device(projected, short_filter, long_filter, out_weight):
@@ -64,8 +99,10 @@
     ).reshape(tok_rows, channels)
     gated = (query * filtered).astype(jnp.bfloat16)
 
-    g_zl = lax.all_gather(gated, "zl", axis=1, tiled=False)
-    g_all = lax.all_gather(g_zl, "c", axis=2, tiled=False)
+    g_zl = line_gather(gated, "zl", 4)
+    other = lax.ppermute(g_zl, "c", [(0, 1), (1, 0)])
+    core = lax.axis_index("c")
+    g_all = jnp.where(core == 0, jnp.stack([g_zl, other], axis=2), jnp.stack([other, g_zl], axis=2))
     gathered = g_all.reshape(tok_rows, -1)
 
     mixed = jnp.dot(gathered, weight, preferred_element_type=jnp.float32)

time: 242 us -> 144 us (0.60)
  the two profiles are of different devices: /device:TPU:8 before, /device:TPU:385 now
where the time goes in v2:
time: 144 us; the launch traced here: 143 us
  waiting for transfers between devices  64.3 us (45%)
  starting transfers between devices  25.7 us (18%)
  other arithmetic  14.3 us (10%)
  between operations  13.7 us (10%)
  local copies, waits for them, and re-layouts  11.2 us (8%)
  matrix products  8.49 us (6%)
  Pallas kernels  5.57 us (4%)
    ppermute x6, waiting for transfers between devices, line_gather(): received[d] = lax.ppermute(block, axis_name, pairs)  37.5 us
    ppermute x6, starting transfers between devices, line_gather(): received[d] = lax.ppermute(block, axis_name, pairs)  17.5 us
    ppermute x1, waiting for transfers between devices, from_behind(): return lax.ppermute(array, SEQ, pairs)  14.5 us
    ppermute x1, waiting for transfers between devices, on_device(): partner = lax.ppermute(out_weight, 'zh', [(0, 1), (1, 0)])  8.1 us
    dot_general x1, matrix products, on_device(): mixed = jnp.dot(gathered, weight, preferred_element_type=jnp.float32)  6.61 us
    pallas_call x1, Pallas kernels, toeplitz_blocks(): pl.pallas_call(toeplitz_kernel, out_shape=jax.ShapeDtypeStruct((groups, s...  5.57 us
    ppermute x1, waiting for transfers between devices, on_device(): other = lax.ppermute(g_zl, 'c', [(0, 1), (1, 0)])  4.1 us
    ppermute x1, starting transfers between devices, from_behind(): return lax.ppermute(array, SEQ, pairs)  3.78 us
  transfers between devices with their start and end apart: 10, of which 6 were waited for; matrix products, arithmetic and copies ran while one was open for 17% of the time, Pallas kernels for 4%

profile of v2, /device:TPU:385, one launch (start us, length us, event | category | flops | bytes accessed | tf_op | source)
XLA Modules:
  0.0 143.2 jit_solution(16886624309636257826)
XLA Ops:
  6.5 0.0 all-gather.2.cloned.1.call-start
  6.5 2.0 %collective-permute-start.8 = (bf16[64,512]{1,0:T(8,128)(2,1)}, bf16[64,512]{1,0:T(8,128)(2,1)S(1)}, u32[]{:S(2)}, u32[]{:S(2)}) collective-permute-start(bf16[64,512]{1,0:T(8,128)(2,1)} %param.7), channel_id=1, source_target_pairs={{0,256},{256,0},{1,257},{257,1},{2,258},{258,2},{3,259},{259,3},{4... | collective-permute-start | bytes 196616 | tf_op jit(solution)/shard_map/ppermute | solution.py:77
  8.6 8.1 %collective-permute-done.8 = bf16[64,512]{1,0:T(8,128)(2,1)S(1)} collective-permute-done((bf16[64,512]{1,0:T(8,128)(2,1)}, bf16[64,512]{1,0:T(8,128)(2,1)S(1)}, u32[]{:S(2)}, u32[]{:S(2)}) %collective-permute-start.8) | collective-permute-done | bytes 65568 | tf_op jit(solution)/shard_map/ppermute | solution.py:77
  16.7 1.6 %maximum_select_fusion.1 = bf16[1,2,64,512]{3,2,0,1:T(8,128)(2,1)} fusion(bf16[1,1,64,512]{3,2,0,1:T(8,128)(2,1)S(1)} %bitcast.54, bf16[1,1,64,512]{3,2,0,1:T(8,128)(2,1)} %bitcast.53, pred[]{:T(512)S(6)} %eq.119), kind=kLoop, calls=%fused_computation.24 | loop fusion | flops 196608 | bytes 262145 | tf_op jit(solution)/shard_map/jit(_where)/select_n | solution.py:79
  18.3 0.0 all-gather.2.cloned.1.call-update
  18.3 1.1 slice.45
  19.4 3.8 %collective-permute-start = (bf16[130,3,512]{2,0,1:T(8,128)(2,1)S(1)}, bf16[130,3,512]{2,0,1:T(8,128)(2,1)S(1)}, u32[]{:S(2)}, u32[]{:S(2)}) collective-permute-start(bf16[130,3,512]{2,0,1:T(8,128)(2,1)S(1)} %slice.45), channel_id=1, source_target_pairs={{0,8},{8,16},{16,24},{24,32},{32,40},{40,48},{48,56},{56,64},{64,7... | collective-permute-start | bytes 1198088 | tf_op jit(solution)/shard_map/ppermute | solution.py:20
  23.2 1.7 %copy.12 = bf16[512,3,512]{0,2,1:T(8,128)(2,1)S(1)} copy(bf16[512,3,512]{2,0,1:T(8,128)(2,1)} %param.4) | data formatting | bytes 3145728 | tf_op args[0]
  25.0 0.1 rev.3
  25.1 0.1 pad.14.clone
  25.1 0.7 maximum_maximum_fusion.row_ref
  25.8 5.6 %shard_map.46 = bf16[32,128,256]{2,1,0:T(8,128)(2,1)} custom-call(f32[32,384]{1,0:T(8,128)} %maximum_maximum_fusion.row_ref), custom_call_target="tpu_custom_call" | custom-call | tf_op jit(solution)/shard_map/pallas_call | solution.py:48
  31.4 14.5 %collective-permute-done = bf16[130,3,512]{2,0,1:T(8,128)(2,1)S(1)} collective-permute-done((bf16[130,3,512]{2,0,1:T(8,128)(2,1)S(1)}, bf16[130,3,512]{2,0,1:T(8,128)(2,1)S(1)}, u32[]{:S(2)}, u32[]{:S(2)}) %collective-permute-start) | collective-permute-done | bytes 399392 | tf_op jit(solution)/shard_map/ppermute | solution.py:20
  45.9 0.3 copy.11
  46.2 0.9 maximum_convert_fusion
  47.1 3.3 %fusion = f32[640,3,512]{0,2,1:T(8,128)S(1)} fusion(f32[642,3,512]{0,2,1:T(8,128)S(1)} %maximum_convert_fusion, f32[3,512]{1,0:T(4,128)S(1)} %get-tuple-element.10, f32[3,512]{1,0:T(4,128)S(1)} %get-tuple-element.11, f32[3,512]{1,0:T(4,128)S(1)} %get-tuple-element.9), kind=kLoop, calls=%fused_computation.2 | loop fusion | flops 4915200 | bytes 15747072 | tf_op jit(solution)/shard_map/add | solution.py:87
  50.4 1.9 %copy-done = f32[640,3,512]{0,2,1:T(8,128)} copy-done((f32[640,3,512]{0,2,1:T(8,128)}, f32[640,3,512]{0,2,1:T(8,128)S(1)}, u32[]{:S(2)}) %copy-start) | copy-done | bytes 3932184
  52.3 0.1 fusion.7
  52.4 0.9 fusion.14
  53.3 1.2 slice.55
  54.5 0.9 copy.13
  55.4 0.1 slice.57
  55.5 0.1 copy.14
  55.6 1.9 %fusion.4 = f32[4,128,32,16]{1,3,0,2:T(8,128)S(1)} fusion(bf16[32,128,256]{2,1,0:T(8,128)(2,1)S(1)} %copy-done.1, bf16[4,128,32,16]{1,3,0,2:T(8,128)(2,1)S(1)} %copy.14, bf16[4,128,32,16]{1,3,0,2:T(8,128)(2,1)} %copy.13), kind=kOutput, calls=%fused_computation.10 | convolution fusion | flops 136314880 | bytes 4194304 | tf_op jit(solution)/shard_map/gij,bjgc->bigc/dot_general | solution.py:97
  57.5 0.4 copy.15
  57.9 1.4 fusion.8
  59.3 0.7 collective-permute-start.1
  60.0 0.7 collective-permute-start.2
  60.7 9.5 %collective-permute-start.3 = (bf16[512,512]{0,1:T(8,128)(2,1)S(1)}, bf16[512,512]{0,1:T(8,128)(2,1)S(1)}, u32[]{:S(2)}, u32[]{:S(2)}) collective-permute-start(bf16[512,512]{0,1:T(8,128)(2,1)S(1)} %fusion.8), channel_id=1, source_target_pairs={{4,0},{6,2},{5,1},{7,3},{12,8},{14,10},{13,9},{15,11},{20,16},{22,... | collective-permute-start | bytes 1572872 | tf_op jit(solution)/shard_map/ppermute | solution.py:62
  70.2 1.3 collective-permute-start.4
  71.5 1.9 %collective-permute-start.5 = (bf16[512,512]{0,1:T(8,128)(2,1)S(1)}, bf16[512,512]{0,1:T(8,128)(2,1)S(1)}, u32[]{:S(2)}, u32[]{:S(2)}) collective-permute-start(bf16[512,512]{0,1:T(8,128)(2,1)S(1)} %fusion.8), channel_id=1, source_target_pairs={{2,0},{4,2},{6,4},{3,1},{5,3},{7,5},{10,8},{12,10},{14,12},{11,9},... | collective-permute-start | bytes 1572872 | tf_op jit(solution)/shard_map/ppermute | solution.py:62
  73.4 0.0 collective-permute-done.1
  73.4 3.4 %collective-permute-start.6 = (bf16[512,512]{0,1:T(8,128)(2,1)S(1)}, bf16[512,512]{0,1:T(8,128)(2,1)}, u32[]{:S(2)}, u32[]{:S(2)}) collective-permute-start(bf16[512,512]{0,1:T(8,128)(2,1)S(1)} %fusion.8), channel_id=1, source_target_pairs={{0,2},{2,4},{4,6},{1,3},{3,5},{5,7},{8,10},{10,12},{12,14},{9,11},... | collective-permute-start | bytes 1572872 | tf_op jit(solution)/shard_map/ppermute | solution.py:62
  76.9 0.0 collective-permute-done.2
  76.9 21.1 %collective-permute-done.3 = bf16[512,512]{0,1:T(8,128)(2,1)S(1)} collective-permute-done((bf16[512,512]{0,1:T(8,128)(2,1)S(1)}, bf16[512,512]{0,1:T(8,128)(2,1)S(1)}, u32[]{:S(2)}, u32[]{:S(2)}) %collective-permute-start.3) | collective-permute-done | bytes 524320 | tf_op jit(solution)/shard_map/ppermute | solution.py:62
  98.1 0.0 collective-permute-done.4
  98.1 11.2 %collective-permute-done.5 = bf16[512,512]{0,1:T(8,128)(2,1)S(1)} collective-permute-done((bf16[512,512]{0,1:T(8,128)(2,1)S(1)}, bf16[512,512]{0,1:T(8,128)(2,1)S(1)}, u32[]{:S(2)}, u32[]{:S(2)}) %collective-permute-start.5) | collective-permute-done | bytes 524320 | tf_op jit(solution)/shard_map/ppermute | solution.py:62
  109.3 5.1 %collective-permute-done.6 = bf16[512,512]{0,1:T(8,128)(2,1)} collective-permute-done((bf16[512,512]{0,1:T(8,128)(2,1)S(1)}, bf16[512,512]{0,1:T(8,128)(2,1)}, u32[]{:S(2)}, u32[]{:S(2)}) %collective-permute-start.6) | collective-permute-done | bytes 524320 | tf_op jit(solution)/shard_map/ppermute | solution.py:62
  114.4 0.2 select_bitcast_fusion.3
  114.6 1.2 select_bitcast_fusion.2
  115.8 0.2 select_bitcast_fusion.1
  116.0 0.2 select_bitcast_fusion
  116.2 1.7 %fusion.13 = (bf16[512,4,1,512]{0,3,1,2:T(8,128)(2,1)S(1)}, bf16[512,4,512]{0,2,1:T(8,128)(2,1)}) fusion(bf16[512,1,512]{0,2,1:T(8,128)(2,1)S(1)} %select_bitcast_fusion, bf16[512,1,512]{0,2,1:T(8,128)(2,1)S(1)} %select_bitcast_fusion.1, bf16[512,1,512]{0,2,1:T(8,128)(2,1)S(1)} %select_bitcast_fusion.2, bf16[512,1,512]{0,2,1:T(8,128)(2,1)S(1)} %select_bitcast_fusion.3), kind=kLoop, calls=%fused_computation.30 | loop fusion | flops 3145728 | bytes 6291456 | tf_op jit(solution)/shard_map/stack | solution.py:105
  117.9 2.4 %collective-permute-start.7 = (bf16[512,4,512]{0,2,1:T(8,128)(2,1)}, bf16[512,4,512]{0,2,1:T(8,128)(2,1)}, u32[]{:S(2)}, u32[]{:S(2)}) collective-permute-start(bf16[512,4,512]{0,2,1:T(8,128)(2,1)} %get-tuple-element.6), channel_id=1, source_target_pairs={{0,1},{1,0},{2,3},{3,2},{4,5},{5,4},{6,7},{7,6},{8,9},{9,8},{10,11... | collective-permute-start | bytes 6291464 | tf_op jit(solution)/shard_map/ppermute | solution.py:103
  120.3 4.1 %collective-permute-done.7 = bf16[512,4,512]{0,2,1:T(8,128)(2,1)} collective-permute-done((bf16[512,4,512]{0,2,1:T(8,128)(2,1)}, bf16[512,4,512]{0,2,1:T(8,128)(2,1)}, u32[]{:S(2)}, u32[]{:S(2)}) %collective-permute-start.7) | collective-permute-done | bytes 2097184 | tf_op jit(solution)/shard_map/ppermute | solution.py:103
  124.4 2.9 %maximum_select_fusion = bf16[512,4,2,512]{0,3,1,2:T(8,128)(2,1)S(1)} fusion(bf16[512,4,1,512]{0,3,1,2:T(8,128)(2,1)} %bitcast.12, bf16[512,4,1,512]{0,3,1,2:T(8,128)(2,1)S(1)} %get-tuple-element.5, pred[]{:T(512)S(6)} %eq.90), kind=kLoop, calls=%fused_computation | loop fusion | flops 6291456 | bytes 8388609 | tf_op jit(solution)/shard_map/jit(_where)/select_n | solution.py:105
  127.3 2.5 %copy.16 = bf16[512,4,2,512]{0,3,2,1:T(8,128)(2,1)} copy(bf16[512,4,2,512]{0,3,1,2:T(8,128)(2,1)S(1)} %maximum_select_fusion) | data formatting | bytes 8388608 | tf_op jit(solution)/shard_map/jit(_where)/select_n | solution.py:105
  129.7 6.6 %convolution_convert_fusion = bf16[512,512]{1,0:T(8,128)(2,1)} fusion(bf16[512,4096]{0,1:T(8,128)(2,1)} %bitcast.51, bf16[4096,512]{1,0:T(8,128)(2,1)} %bitcast.55), kind=kOutput, calls=%fused_computation.13 | convolution fusion | flops 2147745792 | bytes 8912896 | tf_op jit(solution)/shard_map/dot_general | solution.py:108
  (12 shorter events, 0.0 us)
Async XLA Ops:
  6.5 18.4 %copy-start.3 = (bf16[32,128]{1,0:T(8,128)(2,1)S(1)}, bf16[32,128]{1,0:T(8,128)(2,1)}, u32[]{:S(2)}) copy-start(bf16[32,128]{1,0:T(8,128)(2,1)} %param.6) | copy-start | bytes 24580
  6.5 24.9 %copy-start.2 = (f32[3,3,512]{2,1,0:T(4,128)S(1)}, f32[3,3,512]{2,1,0:T(4,128)}, u32[]{:S(2)}) copy-start(f32[3,3,512]{2,1,0:T(4,128)} %param.5) | copy-start | bytes 55300
  6.5 123.2 %all-gather.2.cloned.1.call-start = ((), (), s32[]{:S(2)}) async-start(), calls=%async_computation | async-start | bytes 4325376 | tf_op jit(solution)/shard_map/all_gather | solution.py:80
  6.5 10.2 %collective-permute-start.8 = (bf16[64,512]{1,0:T(8,128)(2,1)}, bf16[64,512]{1,0:T(8,128)(2,1)S(1)}, u32[]{:S(2)}, u32[]{:S(2)}) collective-permute-start(bf16[64,512]{1,0:T(8,128)(2,1)} %param.7), channel_id=1, source_target_pairs={{0,256},{256,0},{1,257},{257,1},{2,258},{258,2},{3,259},{259,3},{4... | collective-permute-start | bytes 196616 | tf_op jit(solution)/shard_map/ppermute | solution.py:77
  19.4 26.5 %collective-permute-start = (bf16[130,3,512]{2,0,1:T(8,128)(2,1)S(1)}, bf16[130,3,512]{2,0,1:T(8,128)(2,1)S(1)}, u32[]{:S(2)}, u32[]{:S(2)}) collective-permute-start(bf16[130,3,512]{2,0,1:T(8,128)(2,1)S(1)} %slice.45), channel_id=1, source_target_pairs={{0,8},{8,16},{16,24},{24,32},{32,40},{40,48},{48,56},{56,64},{64,7... | collective-permute-start | bytes 1198088 | tf_op jit(solution)/shard_map/ppermute | solution.py:20
  50.4 1.9 %copy-start = (f32[640,3,512]{0,2,1:T(8,128)}, f32[640,3,512]{0,2,1:T(8,128)S(1)}, u32[]{:S(2)}) copy-start(f32[640,3,512]{0,2,1:T(8,128)S(1)} %fusion) | copy-start | bytes 11796484
  52.4 3.2 %copy-start.1 = (bf16[32,128,256]{2,1,0:T(8,128)(2,1)S(1)}, bf16[32,128,256]{2,1,0:T(8,128)(2,1)}, u32[]{:S(2)}) copy-start(bf16[32,128,256]{2,1,0:T(8,128)(2,1)} %shard_map.46) | copy-start | bytes 6291460
  59.3 14.1 %collective-permute-start.1 = (bf16[512,512]{0,1:T(8,128)(2,1)S(1)}, bf16[512,512]{0,1:T(8,128)(2,1)S(1)}, u32[]{:S(2)}, u32[]{:S(2)}) collective-permute-start(bf16[512,512]{0,1:T(8,128)(2,1)S(1)} %fusion.8), channel_id=1, source_target_pairs={{6,0},{7,1},{14,8},{15,9},{22,16},{23,17},{30,24},{31,25},{38,32},... | collective-permute-start | bytes 1572872 | tf_op jit(solution)/shard_map/ppermute | solution.py:62
  60.0 16.9 %collective-permute-start.2 = (bf16[512,512]{0,1:T(8,128)(2,1)S(1)}, bf16[512,512]{0,1:T(8,128)(2,1)S(1)}, u32[]{:S(2)}, u32[]{:S(2)}) collective-permute-start(bf16[512,512]{0,1:T(8,128)(2,1)S(1)} %fusion.8), channel_id=1, source_target_pairs={{0,6},{1,7},{8,14},{9,15},{16,22},{17,23},{24,30},{25,31},{32,38},... | collective-permute-start | bytes 1572872 | tf_op jit(solution)/shard_map/ppermute | solution.py:62
  60.7 37.4 %collective-permute-start.3 = (bf16[512,512]{0,1:T(8,128)(2,1)S(1)}, bf16[512,512]{0,1:T(8,128)(2,1)S(1)}, u32[]{:S(2)}, u32[]{:S(2)}) collective-permute-start(bf16[512,512]{0,1:T(8,128)(2,1)S(1)} %fusion.8), channel_id=1, source_target_pairs={{4,0},{6,2},{5,1},{7,3},{12,8},{14,10},{13,9},{15,11},{20,16},{22,... | collective-permute-start | bytes 1572872 | tf_op jit(solution)/shard_map/ppermute | solution.py:62
  70.2 27.9 %collective-permute-start.4 = (bf16[512,512]{0,1:T(8,128)(2,1)S(1)}, bf16[512,512]{0,1:T(8,128)(2,1)S(1)}, u32[]{:S(2)}, u32[]{:S(2)}) collective-permute-start(bf16[512,512]{0,1:T(8,128)(2,1)S(1)} %fusion.8), channel_id=1, source_target_pairs={{0,4},{2,6},{1,5},{3,7},{8,12},{10,14},{9,13},{11,15},{16,20},{18,... | collective-permute-start | bytes 1572872 | tf_op jit(solution)/shard_map/ppermute | solution.py:62
  71.5 37.8 %collective-permute-start.5 = (bf16[512,512]{0,1:T(8,128)(2,1)S(1)}, bf16[512,512]{0,1:T(8,128)(2,1)S(1)}, u32[]{:S(2)}, u32[]{:S(2)}) collective-permute-start(bf16[512,512]{0,1:T(8,128)(2,1)S(1)} %fusion.8), channel_id=1, source_target_pairs={{2,0},{4,2},{6,4},{3,1},{5,3},{7,5},{10,8},{12,10},{14,12},{11,9},... | collective-permute-start | bytes 1572872 | tf_op jit(solution)/shard_map/ppermute | solution.py:62
  73.4 41.0 %collective-permute-start.6 = (bf16[512,512]{0,1:T(8,128)(2,1)S(1)}, bf16[512,512]{0,1:T(8,128)(2,1)}, u32[]{:S(2)}, u32[]{:S(2)}) collective-permute-start(bf16[512,512]{0,1:T(8,128)(2,1)S(1)} %fusion.8), channel_id=1, source_target_pairs={{0,2},{2,4},{4,6},{1,3},{3,5},{5,7},{8,10},{10,12},{12,14},{9,11},... | collective-permute-start | bytes 1572872 | tf_op jit(solution)/shard_map/ppermute | solution.py:62
  117.9 6.5 %collective-permute-start.7 = (bf16[512,4,512]{0,2,1:T(8,128)(2,1)}, bf16[512,4,512]{0,2,1:T(8,128)(2,1)}, u32[]{:S(2)}, u32[]{:S(2)}) collective-permute-start(bf16[512,4,512]{0,2,1:T(8,128)(2,1)} %get-tuple-element.6), channel_id=1, source_target_pairs={{0,1},{1,0},{2,3},{3,2},{4,5},{5,4},{6,7},{7,6},{8,9},{9,8},{10,11... | collective-permute-start | bytes 6291464 | tf_op jit(solution)/shard_map/ppermute | solution.py:103
Sparse Core Ops, SparseCore 0:
  18.4 86.1 all-gather.1

commit v3 on v2

--- a/solution.py
+++ b/solution.py
@@ -75,13 +75,14 @@
     channels = projected.shape[2]
 
     partner = lax.ppermute(out_weight, "zh", [(0, 1), (1, 0)])
+    tail = projected[tok_rows - span - 2 :]
+    previous = from_behind(tail)
+    partner, previous = lax.optimization_barrier((partner, previous))
+
     zh = lax.axis_index("zh")
     pair = jnp.where(zh == 0, jnp.stack([out_weight, partner]), jnp.stack([partner, out_weight]))
-    weight_xy = lax.all_gather(pair, ("x", "y"), axis=0, tiled=False)
-    weight = jnp.transpose(weight_xy, (1, 0, 2, 3)).reshape(-1, weight_xy.shape[-1])
+    weight_y = lax.all_gather(pair, "y", axis=0, tiled=False)
 
-    tail = projected[tok_rows - span - 2 :]
-    previous = from_behind(tail)
     joined = jnp.concatenate([previous, projected], axis=0).astype(jnp.float32)
     featured = (
         short_filter[0] * joined[2:]
@@ -99,13 +100,24 @@
     ).reshape(tok_rows, channels)
     gated = (query * filtered).astype(jnp.bfloat16)
 
+    weight_y, gated = lax.optimization_barrier((weight_y, gated))
+    weight_xy = lax.all_gather(weight_y, "x", axis=0, tiled=False)
+
     g_zl = line_gather(gated, "zl", 4)
     other = lax.ppermute(g_zl, "c", [(0, 1), (1, 0)])
     core = lax.axis_index("c")
-    g_all = jnp.where(core == 0, jnp.stack([g_zl, other], axis=2), jnp.stack([other, g_zl], axis=2))
-    gathered = g_all.reshape(tok_rows, -1)
+    out_cols = weight_xy.shape[-1]
 
-    mixed = jnp.dot(gathered, weight, preferred_element_type=jnp.float32)
+    def weight_rows(zl, c):
+        x = 2 * (zl % 2) + c
+        piece = lax.dynamic_index_in_dim(weight_xy, x, axis=0, keepdims=False)[:, zl // 2]
+        return piece.reshape(-1, out_cols)
+
+    mixed = jnp.zeros((tok_rows, out_cols), jnp.float32)
+    for zl in range(4):
+        mixed = mixed + jnp.dot(g_zl[:, zl], weight_rows(zl, core), preferred_element_type=jnp.float32)
+    for zl in range(4):
+        mixed = mixed + jnp.dot(other[:, zl], weight_rows(zl, 1 - core), preferred_element_type=jnp.float32)
     return mixed.astype(jnp.bfloat16)
 
 

time: 144 us -> 157 us (1.090)
  the two profiles are of different devices: /device:TPU:385 before, /device:TPU:1 now
where the time goes in v3:
time: 157 us; the launch traced here: 156 us
  waiting for transfers between devices  62.9 us (40%)
  starting transfers between devices  39.8 us (25%)
  local copies, waits for them, and re-layouts  14 us (9%)
  between operations  13.7 us (9%)
  matrix products  10.9 us (7%)
  other arithmetic  8.92 us (6%)
  Pallas kernels  5.54 us (4%)
    all_gather x1, waiting for transfers between devices, on_device(): weight_y = lax.all_gather(pair, 'y', axis=0, tiled=False)  29.9 us
    ppermute x6, waiting for transfers between devices, line_gather(): received[d] = lax.ppermute(block, axis_name, pairs)  20.6 us
    ppermute x6, starting transfers between devices, line_gather(): received[d] = lax.ppermute(block, axis_name, pairs)  19.9 us
    all_gather x1, waiting for transfers between devices, on_device(): weight_xy = lax.all_gather(weight_y, 'x', axis=0, tiled=False)  11.9 us
    ppermute x1, starting transfers between devices, on_device(): partner = lax.ppermute(out_weight, 'zh', [(0, 1), (1, 0)])  10.6 us
    dot_general x4, matrix products, on_device(): jnp.dot(other[:, zl], weight_rows(zl, 1 - core), preferred_element_type=j...  6.11 us
    pallas_call x1, Pallas kernels, toeplitz_blocks(): pl.pallas_call(toeplitz_kernel, out_shape=jax.ShapeDtypeStruct((groups, s...  5.54 us
    ppermute x1, starting transfers between devices, on_device(): other = lax.ppermute(g_zl, 'c', [(0, 1), (1, 0)])  5.11 us
  transfers between devices with their start and end apart: 11, of which 4 were waited for; matrix products, arithmetic and copies ran while one was open for 14% of the time, Pallas kernels for 4%

profile of v3, /device:TPU:1, one launch (start us, length us, event | category | flops | bytes accessed | tf_op | source)
XLA Modules:
  0.0 155.7 jit_solution(5598932959178874463)
XLA Ops:
  6.5 1.1 slice.80
  7.6 4.1 %collective-permute-start.1 = (bf16[130,3,512]{2,0,1:T(8,128)(2,1)S(1)}, bf16[130,3,512]{2,0,1:T(8,128)(2,1)S(1)}, u32[]{:S(2)}, u32[]{:S(2)}) collective-permute-start(bf16[130,3,512]{2,0,1:T(8,128)(2,1)S(1)} %slice.80), channel_id=1, source_target_pairs={{0,8},{8,16},{16,24},{24,32},{32,40},{40,48},{48,56},{56,64},{64,7... | collective-permute-start | bytes 1198088 | tf_op jit(solution)/shard_map/ppermute | solution.py:20
  11.7 10.6 %collective-permute-start = (bf16[64,512]{1,0:T(8,128)(2,1)}, bf16[64,512]{1,0:T(8,128)(2,1)S(1)}, u32[]{:S(2)}, u32[]{:S(2)}) collective-permute-start(bf16[64,512]{1,0:T(8,128)(2,1)} %param.7), channel_id=1, source_target_pairs={{0,256},{256,0},{1,257},{257,1},{2,258},{258,2},{3,259},{259,3},{4... | collective-permute-start | bytes 196616 | tf_op jit(solution)/shard_map/ppermute | solution.py:77
  22.3 0.8 rev.3
  23.2 0.7 maximum_maximum_fusion.row_ref
  23.9 0.3 collective-permute-done
  24.3 1.6 %maximum_select_fusion = bf16[1,2,64,512]{3,2,1,0:T(8,128)(2,1)} fusion(bf16[1,1,64,512]{3,2,1,0:T(8,128)(2,1)S(1)} %bitcast.94, bf16[1,1,64,512]{3,2,1,0:T(8,128)(2,1)} %bitcast.93, pred[]{:T(512)S(6)} %eq.88), kind=kLoop, calls=%fused_computation.42 | loop fusion | flops 196608 | bytes 262145 | tf_op jit(solution)/shard_map/jit(_where)/select_n | solution.py:83
  25.9 0.7 slice_bitcast_fusion.11
  26.6 1.7 %copy.11 = bf16[512,3,512]{0,2,1:T(8,128)(2,1)S(1)} copy(bf16[512,3,512]{2,0,1:T(8,128)(2,1)} %param.4) | data formatting | bytes 3145728 | tf_op args[0]
  28.4 5.5 %shard_map.46 = bf16[32,128,256]{2,1,0:T(8,128)(2,1)} custom-call(f32[32,384]{1,0:T(8,128)} %maximum_maximum_fusion.row_ref), custom_call_target="tpu_custom_call" | custom-call | tf_op jit(solution)/shard_map/pallas_call | solution.py:48
  33.9 0.3 copy.10
  34.2 0.9 maximum_convert_fusion
  35.1 3.3 %fusion = f32[640,3,512]{0,2,1:T(8,128)S(1)} fusion(f32[642,3,512]{0,2,1:T(8,128)S(1)} %maximum_convert_fusion, f32[3,512]{1,0:T(4,128)S(1)} %get-tuple-element.28, f32[3,512]{1,0:T(4,128)S(1)} %get-tuple-element.29, f32[3,512]{1,0:T(4,128)S(1)} %get-tuple-element.27), kind=kLoop, calls=%fused_computation.1 | loop fusion | flops 4915200 | bytes 15747072 | tf_op jit(solution)/shard_map/add | solution.py:88
  38.5 1.1 fusion.28
  39.6 0.8 copy-done
  40.4 1.3 slice.91
  41.7 0.9 copy.12
  42.9 1.9 %fusion.4 = f32[4,128,32,16]{1,3,0,2:T(8,128)S(1)} fusion(bf16[32,128,256]{2,1,0:T(8,128)(2,1)S(1)} %copy-done.1, bf16[4,128,32,16]{1,3,0,2:T(8,128)(2,1)S(1)} %copy.13, bf16[4,128,32,16]{1,3,0,2:T(8,128)(2,1)} %copy.12), kind=kOutput, calls=%fused_computation.9 | convolution fusion | flops 136314880 | bytes 4194304 | tf_op jit(solution)/shard_map/gij,bjgc->bigc/dot_general | solution.py:98
  44.7 0.4 copy.14
  45.2 1.4 fusion.15
  46.6 29.9 %all-gather.4.cloned.1.call-done = bf16[8,2,64,512]{3,2,1,0:T(8,128)(2,1)} async-done(((bf16[1,2,64,512]{3,2,1,0:T(8,128)(2,1)}), bf16[8,2,64,512]{3,2,1,0:T(8,128)(2,1)}) %all-gather.4.cloned.1.call-update) | async-done | bytes 1048592 | tf_op jit(solution)/shard_map/all_gather | solution.py:84
  76.5 1.3 collective-permute-start.2
  77.8 6.3 %collective-permute-start.3 = (bf16[512,512]{0,1:T(8,128)(2,1)S(1)}, bf16[512,512]{0,1:T(8,128)(2,1)S(1)}, u32[]{:S(2)}, u32[]{:S(2)}) collective-permute-start(bf16[512,512]{0,1:T(8,128)(2,1)S(1)} %fusion.15), channel_id=1, source_target_pairs={{0,6},{1,7},{8,14},{9,15},{16,22},{17,23},{24,30},{25,31},{32,38},... | collective-permute-start | bytes 1572872 | tf_op jit(solution)/shard_map/ppermute | solution.py:62
  84.1 1.3 collective-permute-start.4
  85.4 4.9 %collective-permute-start.5 = (bf16[512,512]{0,1:T(8,128)(2,1)S(1)}, bf16[512,512]{0,1:T(8,128)(2,1)S(1)}, u32[]{:S(2)}, u32[]{:S(2)}) collective-permute-start(bf16[512,512]{0,1:T(8,128)(2,1)S(1)} %fusion.15), channel_id=1, source_target_pairs={{0,4},{2,6},{1,5},{3,7},{8,12},{10,14},{9,13},{11,15},{16,20},{18,... | collective-permute-start | bytes 1572872 | tf_op jit(solution)/shard_map/ppermute | solution.py:62
  90.4 1.3 collective-permute-start.6
  91.7 4.8 %collective-permute-start.7 = (bf16[512,512]{0,1:T(8,128)(2,1)S(1)}, bf16[512,512]{0,1:T(8,128)(2,1)}, u32[]{:S(2)}, u32[]{:S(2)}) collective-permute-start(bf16[512,512]{0,1:T(8,128)(2,1)S(1)} %fusion.15), channel_id=1, source_target_pairs={{0,2},{2,4},{4,6},{1,3},{3,5},{5,7},{8,10},{10,12},{12,14},{9,11},... | collective-permute-start | bytes 1572872 | tf_op jit(solution)/shard_map/ppermute | solution.py:62
  96.5 20.6 %collective-permute-done.4 = bf16[512,512]{0,1:T(8,128)(2,1)S(1)} collective-permute-done((bf16[512,512]{0,1:T(8,128)(2,1)S(1)}, bf16[512,512]{0,1:T(8,128)(2,1)S(1)}, u32[]{:S(2)}, u32[]{:S(2)}) %collective-permute-start.4) | collective-permute-done | bytes 524320 | tf_op jit(solution)/shard_map/ppermute | solution.py:62
  117.1 0.2 select_select_fusion.2
  117.3 0.2 select_select_fusion.1
  117.5 0.2 select_select_fusion
  117.7 0.2 select_select_fusion.3
  117.9 0.3 copy-done.4
  118.2 0.2 copy-done.6
  118.5 0.3 pad_maximum_fusion
  118.8 5.1 %collective-permute-start.8 = (bf16[512,4,512]{0,2,1:T(8,128)(2,1)S(1)}, bf16[512,4,512]{0,2,1:T(8,128)(2,1)}, u32[]{:S(2)}, u32[]{:S(2)}) collective-permute-start(bf16[512,4,512]{0,2,1:T(8,128)(2,1)S(1)} %pad_maximum_fusion), channel_id=1, source_target_pairs={{0,1},{1,0},{2,3},{3,2},{4,5},{5,4},{6,7},{7,6},{8,9},{9,8},{10,11... | collective-permute-start | bytes 6291464 | tf_op jit(solution)/shard_map/ppermute | solution.py:107
  123.9 11.9 %all-gather.6.cloned.1.call-done = bf16[32,2,64,512]{3,2,1,0:T(8,128)(2,1)} async-done(((bf16[8,2,64,512]{3,2,1,0:T(8,128)(2,1)}), bf16[32,2,64,512]{3,2,1,0:T(8,128)(2,1)}) %all-gather.6.cloned.1.call-update) | async-done | bytes 4194320 | tf_op jit(solution)/shard_map/all_gather | solution.py:104
  135.8 2.7 %dynamic-slice_bitcast_fusion.3 = (bf16[8,2,64,512]{3,2,1,0:T(8,128)(2,1)S(1)}, bf16[8,2,64,512]{3,2,1,0:T(8,128)(2,1)S(1)}, bf16[8,2,64,512]{3,2,1,0:T(8,128)(2,1)S(1)}, bf16[8,2,64,512]{3,2,1,0:T(8,128)(2,1)S(1)}) fusion(bf16[4,8,2,64,512]{4,3,2,1,0:T(8,128)(2,1)} %bitcast.83, s32[]{:T(128)S(6)} %select_n.218, s32[]{:T(128)S(6)} %select_n.263, ...), kind=kLoop, calls=%fused_computation.29 | loop fusion | bytes 8388624 | tf_op jit(solution)/shard_map/jit(dynamic_index_in_dim)/squeeze | solution.py:113
  138.7 0.9 copy-done.5
  139.5 0.5 fusion.29
  140.0 0.5 fusion.30
  140.6 0.5 fusion.31
  141.1 0.2 fusion.26
  141.3 1.5 fusion.22
  142.8 1.5 fusion.21
  144.3 1.6 %fusion.20 = f32[512,512]{1,0:T(8,128)S(1)} fusion(bf16[512,512]{1,0:T(8,128)(2,1)S(1)} %bitcast.87, bf16[512,4,512]{0,2,1:T(8,128)(2,1)} %collective-permute-done.8), kind=kOutput, calls=%fused_computation.33 | convolution fusion | flops 268435456 | bytes 2097152 | tf_op jit(solution)/shard_map/dot_general | solution.py:120
  145.9 1.5 fusion.19
  147.4 1.5 fusion.14
  (35 shorter events, 0.9 us)
Async XLA Ops:
  6.5 69.9 %all-gather.4.cloned.1.call-start = ((), (), s32[]{:S(2)}) async-start(), calls=%async_computation | async-start | bytes 1179648 | tf_op jit(solution)/shard_map/all_gather | solution.py:84
  7.6 16.6 %collective-permute-start.1 = (bf16[130,3,512]{2,0,1:T(8,128)(2,1)S(1)}, bf16[130,3,512]{2,0,1:T(8,128)(2,1)S(1)}, u32[]{:S(2)}, u32[]{:S(2)}) collective-permute-start(bf16[130,3,512]{2,0,1:T(8,128)(2,1)S(1)} %slice.80), channel_id=1, source_target_pairs={{0,8},{8,16},{16,24},{24,32},{32,40},{40,48},{48,56},{56,64},{64,7... | collective-permute-start | bytes 1198088 | tf_op jit(solution)/shard_map/ppermute | solution.py:20
  11.7 12.5 %collective-permute-start = (bf16[64,512]{1,0:T(8,128)(2,1)}, bf16[64,512]{1,0:T(8,128)(2,1)S(1)}, u32[]{:S(2)}, u32[]{:S(2)}) collective-permute-start(bf16[64,512]{1,0:T(8,128)(2,1)} %param.7), channel_id=1, source_target_pairs={{0,256},{256,0},{1,257},{257,1},{2,258},{258,2},{3,259},{259,3},{4... | collective-permute-start | bytes 196616 | tf_op jit(solution)/shard_map/ppermute | solution.py:77
  25.9 110.0 %all-gather.6.cloned.1.call-start = ((), (), s32[]{:S(2)}) async-start(), calls=%async_computation.1 | async-start | bytes 5242880 | tf_op jit(solution)/shard_map/all_gather | solution.py:104
  38.4 2.1 %copy-start = (f32[640,3,512]{0,2,1:T(8,128)}, f32[640,3,512]{0,2,1:T(8,128)S(1)}, u32[]{:S(2)}) copy-start(f32[640,3,512]{0,2,1:T(8,128)S(1)} %fusion) | copy-start | bytes 11796484
  40.4 2.4 %copy-start.1 = (bf16[32,128,256]{2,1,0:T(8,128)(2,1)S(1)}, bf16[32,128,256]{2,1,0:T(8,128)(2,1)}, u32[]{:S(2)}) copy-start(bf16[32,128,256]{2,1,0:T(8,128)(2,1)} %shard_map.46) | copy-start | bytes 6291460
  76.5 15.2 %collective-permute-start.2 = (bf16[512,512]{0,1:T(8,128)(2,1)S(1)}, bf16[512,512]{0,1:T(8,128)(2,1)S(1)}, u32[]{:S(2)}, u32[]{:S(2)}) collective-permute-start(bf16[512,512]{0,1:T(8,128)(2,1)S(1)} %fusion.15), channel_id=1, source_target_pairs={{6,0},{7,1},{14,8},{15,9},{22,16},{23,17},{30,24},{31,25},{38,32},... | collective-permute-start | bytes 1572872 | tf_op jit(solution)/shard_map/ppermute | solution.py:62
  77.8 18.7 %collective-permute-start.3 = (bf16[512,512]{0,1:T(8,128)(2,1)S(1)}, bf16[512,512]{0,1:T(8,128)(2,1)S(1)}, u32[]{:S(2)}, u32[]{:S(2)}) collective-permute-start(bf16[512,512]{0,1:T(8,128)(2,1)S(1)} %fusion.15), channel_id=1, source_target_pairs={{0,6},{1,7},{8,14},{9,15},{16,22},{17,23},{24,30},{25,31},{32,38},... | collective-permute-start | bytes 1572872 | tf_op jit(solution)/shard_map/ppermute | solution.py:62
  84.1 33.0 %collective-permute-start.4 = (bf16[512,512]{0,1:T(8,128)(2,1)S(1)}, bf16[512,512]{0,1:T(8,128)(2,1)S(1)}, u32[]{:S(2)}, u32[]{:S(2)}) collective-permute-start(bf16[512,512]{0,1:T(8,128)(2,1)S(1)} %fusion.15), channel_id=1, source_target_pairs={{4,0},{6,2},{5,1},{7,3},{12,8},{14,10},{13,9},{15,11},{20,16},{22,... | collective-permute-start | bytes 1572872 | tf_op jit(solution)/shard_map/ppermute | solution.py:62
  85.4 31.7 %collective-permute-start.5 = (bf16[512,512]{0,1:T(8,128)(2,1)S(1)}, bf16[512,512]{0,1:T(8,128)(2,1)S(1)}, u32[]{:S(2)}, u32[]{:S(2)}) collective-permute-start(bf16[512,512]{0,1:T(8,128)(2,1)S(1)} %fusion.15), channel_id=1, source_target_pairs={{0,4},{2,6},{1,5},{3,7},{8,12},{10,14},{9,13},{11,15},{16,20},{18,... | collective-permute-start | bytes 1572872 | tf_op jit(solution)/shard_map/ppermute | solution.py:62
  90.4 26.8 %collective-permute-start.6 = (bf16[512,512]{0,1:T(8,128)(2,1)S(1)}, bf16[512,512]{0,1:T(8,128)(2,1)S(1)}, u32[]{:S(2)}, u32[]{:S(2)}) collective-permute-start(bf16[512,512]{0,1:T(8,128)(2,1)S(1)} %fusion.15), channel_id=1, source_target_pairs={{2,0},{4,2},{6,4},{3,1},{5,3},{7,5},{10,8},{12,10},{14,12},{11,9},... | collective-permute-start | bytes 1572872 | tf_op jit(solution)/shard_map/ppermute | solution.py:62
  91.7 25.4 %collective-permute-start.7 = (bf16[512,512]{0,1:T(8,128)(2,1)S(1)}, bf16[512,512]{0,1:T(8,128)(2,1)}, u32[]{:S(2)}, u32[]{:S(2)}) collective-permute-start(bf16[512,512]{0,1:T(8,128)(2,1)S(1)} %fusion.15), channel_id=1, source_target_pairs={{0,2},{2,4},{4,6},{1,3},{3,5},{5,7},{8,10},{10,12},{12,14},{9,11},... | collective-permute-start | bytes 1572872 | tf_op jit(solution)/shard_map/ppermute | solution.py:62
  117.3 0.9 copy-start.4
  117.5 0.9 copy-start.6
  117.7 0.8 copy-start.8
  117.9 0.9 copy-start.2
  118.8 22.5 %collective-permute-start.8 = (bf16[512,4,512]{0,2,1:T(8,128)(2,1)S(1)}, bf16[512,4,512]{0,2,1:T(8,128)(2,1)}, u32[]{:S(2)}, u32[]{:S(2)}) collective-permute-start(bf16[512,4,512]{0,2,1:T(8,128)(2,1)S(1)} %pad_maximum_fusion), channel_id=1, source_target_pairs={{0,1},{1,0},{2,3},{3,2},{4,5},{5,4},{6,7},{7,6},{8,9},{9,8},{10,11... | collective-permute-start | bytes 6291464 | tf_op jit(solution)/shard_map/ppermute | solution.py:107
  138.5 1.0 copy-start.5
  138.7 1.4 copy-start.7
  139.5 1.1 copy-start.9
  144.3 3.1 %copy-start.3 = (bf16[512,512]{0,1:T(8,128)(2,1)S(1)}, bf16[512,512]{0,1:T(8,128)(2,1)}, u32[]{:S(2)}) copy-start(bf16[512,512]{0,1:T(8,128)(2,1)} %copy-done.2) | copy-start | bytes 1572868
Sparse Core Ops, SparseCore 0:
  26.0 50.4 all-gather.3
  78.6 57.2 all-gather.5

commit v4 on v3

--- a/solution.py
+++ b/solution.py
@@ -81,7 +81,8 @@
 
     zh = lax.axis_index("zh")
     pair = jnp.where(zh == 0, jnp.stack([out_weight, partner]), jnp.stack([partner, out_weight]))
-    weight_y = lax.all_gather(pair, "y", axis=0, tiled=False)
+    weight_xy = lax.all_gather(pair, ("x", "y"), axis=0, tiled=False)
+    weight_xy = weight_xy.reshape(4, 8, *weight_xy.shape[1:])
 
     joined = jnp.concatenate([previous, projected], axis=0).astype(jnp.float32)
     featured = (
@@ -99,9 +100,6 @@
         "gij,bjgc->bigc", toeplitz, window, preferred_element_type=jnp.float32
     ).reshape(tok_rows, channels)
     gated = (query * filtered).astype(jnp.bfloat16)
-
-    weight_y, gated = lax.optimization_barrier((weight_y, gated))
-    weight_xy = lax.all_gather(weight_y, "x", axis=0, tiled=False)
 
     g_zl = line_gather(gated, "zl", 4)
     other = lax.ppermute(g_zl, "c", [(0, 1), (1, 0)])

time: 157 us -> 147 us (0.936)
  the two profiles are of different devices: /device:TPU:1 before, /device:TPU:8 now
where the time goes in v4:
time: 147 us
  waiting for transfers between devices  60.1 us (41%)
  starting transfers between devices  34.7 us (24%)
  between operations  13.8 us (9%)
  local copies, waits for them, and re-layouts  12.7 us (9%)
  matrix products  10.9 us (7%)
  other arithmetic  8.92 us (6%)
  Pallas kernels  5.57 us (4%)
    all_gather x1, waiting for transfers between devices, on_device(): weight_xy = lax.all_gather(pair, ('x', 'y'), axis=0, tiled=False)  35.7 us
    ppermute x6, waiting for transfers between devices, line_gather(): received[d] = lax.ppermute(block, axis_name, pairs)  21.3 us
    ppermute x6, starting transfers between devices, line_gather(): received[d] = lax.ppermute(block, axis_name, pairs)  18.3 us
    ppermute x1, starting transfers between devices, on_device(): partner = lax.ppermute(out_weight, 'zh', [(0, 1), (1, 0)])  10.9 us
    dot_general x4, matrix products, on_device(): jnp.dot(other[:, zl], weight_rows(zl, 1 - core), preferred_element_type=j...  6.1 us
    pallas_call x1, Pallas kernels, toeplitz_blocks(): pl.pallas_call(toeplitz_kernel, out_shape=jax.ShapeDtypeStruct((groups, s...  5.57 us
    unnamed x25, local copies, waits for them, and re-layouts  4.2 us
    slice x5, local copies, waits for them, and re-layouts, on_device(): window = jnp.concatenate([blocks[:-1], blocks[1:]], axis=1)  3.54 us
  transfers between devices with their start and end apart: 10, of which 5 were waited for; matrix products, arithmetic and copies ran while one was open for 13% of the time, Pallas kernels for 4%

profile of v4, /device:TPU:8, one launch (start us, length us, event | category | flops | bytes accessed | tf_op | source)
XLA Modules:
  0.0 146.6 jit_solution(16415689509696154881)
XLA Ops:
  6.5 1.1 slice.81
  7.7 3.5 %collective-permute-start.1 = (bf16[130,3,512]{2,0,1:T(8,128)(2,1)S(1)}, bf16[130,3,512]{2,0,1:T(8,128)(2,1)S(1)}, u32[]{:S(2)}, u32[]{:S(2)}) collective-permute-start(bf16[130,3,512]{2,0,1:T(8,128)(2,1)S(1)} %slice.81), channel_id=1, source_target_pairs={{0,8},{8,16},{16,24},{24,32},{32,40},{40,48},{48,56},{56,64},{64,7... | collective-permute-start | bytes 1198088 | tf_op jit(solution)/shard_map/ppermute | solution.py:20
  11.1 10.9 %collective-permute-start = (bf16[64,512]{1,0:T(8,128)(2,1)}, bf16[64,512]{1,0:T(8,128)(2,1)S(1)}, u32[]{:S(2)}, u32[]{:S(2)}) collective-permute-start(bf16[64,512]{1,0:T(8,128)(2,1)} %param.7), channel_id=1, source_target_pairs={{0,256},{256,0},{1,257},{257,1},{2,258},{258,2},{3,259},{259,3},{4... | collective-permute-start | bytes 196616 | tf_op jit(solution)/shard_map/ppermute | solution.py:77
  22.1 3.1 %collective-permute-done = bf16[64,512]{1,0:T(8,128)(2,1)S(1)} collective-permute-done((bf16[64,512]{1,0:T(8,128)(2,1)}, bf16[64,512]{1,0:T(8,128)(2,1)S(1)}, u32[]{:S(2)}, u32[]{:S(2)}) %collective-permute-start) | collective-permute-done | bytes 65568 | tf_op jit(solution)/shard_map/ppermute | solution.py:77
  25.2 1.6 %maximum_select_fusion = bf16[1,2,64,512]{3,2,1,0:T(8,128)(2,1)} fusion(bf16[1,1,64,512]{3,2,1,0:T(8,128)(2,1)S(1)} %bitcast.94, bf16[1,1,64,512]{3,2,1,0:T(8,128)(2,1)} %bitcast.93, pred[]{:T(512)S(6)} %eq.94), kind=kLoop, calls=%fused_computation.42 | loop fusion | flops 196608 | bytes 262145 | tf_op jit(solution)/shard_map/jit(_where)/select_n | solution.py:83
  26.8 1.7 %copy.11 = bf16[512,3,512]{0,2,1:T(8,128)(2,1)S(1)} copy(bf16[512,3,512]{2,0,1:T(8,128)(2,1)} %param.4) | data formatting | bytes 3145728 | tf_op args[0]
  28.7 0.7 maximum_maximum_fusion.row_ref
  29.4 5.6 %shard_map.46 = bf16[32,128,256]{2,1,0:T(8,128)(2,1)} custom-call(f32[32,384]{1,0:T(8,128)} %maximum_maximum_fusion.row_ref), custom_call_target="tpu_custom_call" | custom-call | tf_op jit(solution)/shard_map/pallas_call | solution.py:48
  35.0 0.3 copy.10
  35.3 0.9 maximum_convert_fusion
  36.1 3.3 %fusion = f32[640,3,512]{0,2,1:T(8,128)S(1)} fusion(f32[642,3,512]{0,2,1:T(8,128)S(1)} %maximum_convert_fusion, f32[3,512]{1,0:T(4,128)S(1)} %get-tuple-element.24, f32[3,512]{1,0:T(4,128)S(1)} %get-tuple-element.25, f32[3,512]{1,0:T(4,128)S(1)} %get-tuple-element.23), kind=kLoop, calls=%fused_computation.1 | loop fusion | flops 4915200 | bytes 15747072 | tf_op jit(solution)/shard_map/add | solution.py:89
  39.6 1.1 fusion.28
  40.7 0.9 copy-done
  41.6 1.3 slice.91
  42.9 0.9 copy.12
  44.0 1.9 %fusion.4 = f32[4,128,32,16]{1,3,0,2:T(8,128)S(1)} fusion(bf16[32,128,256]{2,1,0:T(8,128)(2,1)S(1)} %copy-done.1, bf16[4,128,32,16]{1,3,0,2:T(8,128)(2,1)S(1)} %copy.13, bf16[4,128,32,16]{1,3,0,2:T(8,128)(2,1)} %copy.12), kind=kOutput, calls=%fused_computation.9 | convolution fusion | flops 136314880 | bytes 4194304 | tf_op jit(solution)/shard_map/gij,bjgc->bigc/dot_general | solution.py:99
  45.9 0.4 copy.14
  46.3 1.4 fusion.15
  47.7 1.3 collective-permute-start.2
  49.0 6.4 %collective-permute-start.3 = (bf16[512,512]{0,1:T(8,128)(2,1)S(1)}, bf16[512,512]{0,1:T(8,128)(2,1)S(1)}, u32[]{:S(2)}, u32[]{:S(2)}) collective-permute-start(bf16[512,512]{0,1:T(8,128)(2,1)S(1)} %fusion.15), channel_id=1, source_target_pairs={{0,6},{1,7},{8,14},{9,15},{16,22},{17,23},{24,30},{25,31},{32,38},... | collective-permute-start | bytes 1572872 | tf_op jit(solution)/shard_map/ppermute | solution.py:62
  55.4 1.3 collective-permute-start.4
  56.7 5.5 %collective-permute-start.5 = (bf16[512,512]{0,1:T(8,128)(2,1)S(1)}, bf16[512,512]{0,1:T(8,128)(2,1)S(1)}, u32[]{:S(2)}, u32[]{:S(2)}) collective-permute-start(bf16[512,512]{0,1:T(8,128)(2,1)S(1)} %fusion.15), channel_id=1, source_target_pairs={{0,4},{2,6},{1,5},{3,7},{8,12},{10,14},{9,13},{11,15},{16,20},{18,... | collective-permute-start | bytes 1572872 | tf_op jit(solution)/shard_map/ppermute | solution.py:62
  62.2 1.3 collective-permute-start.6
  63.5 2.8 %collective-permute-done.2 = bf16[512,512]{0,1:T(8,128)(2,1)S(1)} collective-permute-done((bf16[512,512]{0,1:T(8,128)(2,1)S(1)}, bf16[512,512]{0,1:T(8,128)(2,1)S(1)}, u32[]{:S(2)}, u32[]{:S(2)}) %collective-permute-start.2) | collective-permute-done | bytes 524320 | tf_op jit(solution)/shard_map/ppermute | solution.py:62
  66.4 2.6 %collective-permute-start.7 = (bf16[512,512]{0,1:T(8,128)(2,1)S(1)}, bf16[512,512]{0,1:T(8,128)(2,1)}, u32[]{:S(2)}, u32[]{:S(2)}) collective-permute-start(bf16[512,512]{0,1:T(8,128)(2,1)S(1)} %fusion.15), channel_id=1, source_target_pairs={{0,2},{2,4},{4,6},{1,3},{3,5},{5,7},{8,10},{10,12},{12,14},{9,11},... | collective-permute-start | bytes 1572872 | tf_op jit(solution)/shard_map/ppermute | solution.py:62
  68.9 17.0 %collective-permute-done.4 = bf16[512,512]{0,1:T(8,128)(2,1)S(1)} collective-permute-done((bf16[512,512]{0,1:T(8,128)(2,1)S(1)}, bf16[512,512]{0,1:T(8,128)(2,1)S(1)}, u32[]{:S(2)}, u32[]{:S(2)}) %collective-permute-start.4) | collective-permute-done | bytes 524320 | tf_op jit(solution)/shard_map/ppermute | solution.py:62
  86.0 1.5 collective-permute-done.6
  87.4 0.2 select_select_fusion.2
  87.6 0.2 select_select_fusion.1
  87.8 0.2 select_select_fusion
  88.0 0.2 select_select_fusion.3
  88.2 0.2 copy-done.4
  88.4 0.2 copy-done.6
  88.6 0.2 copy-done.8
  88.8 0.3 pad_maximum_fusion
  89.1 1.9 %collective-permute-start.8 = (bf16[512,4,512]{0,2,1:T(8,128)(2,1)S(1)}, bf16[512,4,512]{0,2,1:T(8,128)(2,1)}, u32[]{:S(2)}, u32[]{:S(2)}) collective-permute-start(bf16[512,4,512]{0,2,1:T(8,128)(2,1)S(1)} %pad_maximum_fusion), channel_id=1, source_target_pairs={{0,1},{1,0},{2,3},{3,2},{4,5},{5,4},{6,7},{7,6},{8,9},{9,8},{10,11... | collective-permute-start | bytes 6291464 | tf_op jit(solution)/shard_map/ppermute | solution.py:105
  91.0 35.7 %all-gather.2.cloned.1.call-done = bf16[32,2,64,512]{3,2,1,0:T(8,128)(2,1)} async-done(((bf16[1,2,64,512]{3,2,1,0:T(8,128)(2,1)}), bf16[32,2,64,512]{3,2,1,0:T(8,128)(2,1)}) %all-gather.2.cloned.1.call-update) | async-done | bytes 4194320 | tf_op jit(solution)/shard_map/all_gather | solution.py:84
  126.7 2.7 %dynamic-slice_bitcast_fusion.3 = (bf16[8,2,64,512]{3,2,1,0:T(8,128)(2,1)S(1)}, bf16[8,2,64,512]{3,2,1,0:T(8,128)(2,1)S(1)}, bf16[8,2,64,512]{3,2,1,0:T(8,128)(2,1)S(1)}, bf16[8,2,64,512]{3,2,1,0:T(8,128)(2,1)S(1)}) fusion(bf16[4,8,2,64,512]{4,3,2,1,0:T(8,128)(2,1)} %bitcast.83, s32[]{:T(128)S(6)} %select_n.218, s32[]{:T(128)S(6)} %select_n.263, ...), kind=kLoop, calls=%fused_computation.29 | loop fusion | bytes 8388624 | tf_op jit(solution)/shard_map/jit(dynamic_index_in_dim)/squeeze | solution.py:111
  129.5 0.9 copy-done.5
  130.4 0.5 fusion.29
  130.9 0.5 fusion.30
  131.5 0.5 fusion.31
  132.0 0.2 fusion.26
  132.1 1.5 %fusion.22 = f32[512,512]{1,0:T(8,128)S(1)} fusion(bf16[512,512]{1,0:T(8,128)(2,1)S(1)} %bitcast.90, bf16[512,4,512]{0,2,1:T(8,128)(2,1)} %collective-permute-done.8), kind=kOutput, calls=%fused_computation.37 | convolution fusion | flops 268435456 | bytes 2097152 | tf_op jit(solution)/shard_map/dot_general | solution.py:118
  133.6 1.5 %fusion.21 = f32[512,512]{1,0:T(8,128)S(1)} fusion(bf16[512,512]{1,0:T(8,128)(2,1)S(1)} %bitcast.89, bf16[512,4,512]{0,2,1:T(8,128)(2,1)} %collective-permute-done.8), kind=kOutput, calls=%fused_computation.35 | convolution fusion | flops 268435456 | bytes 2097152 | tf_op jit(solution)/shard_map/dot_general | solution.py:118
  135.2 1.6 %fusion.20 = f32[512,512]{1,0:T(8,128)S(1)} fusion(bf16[512,512]{1,0:T(8,128)(2,1)S(1)} %bitcast.87, bf16[512,4,512]{0,2,1:T(8,128)(2,1)} %collective-permute-done.8), kind=kOutput, calls=%fused_computation.33 | convolution fusion | flops 268435456 | bytes 2097152 | tf_op jit(solution)/shard_map/dot_general | solution.py:118
  136.7 1.5 %fusion.19 = f32[512,512]{1,0:T(8,128)S(1)} fusion(bf16[512,512]{1,0:T(8,128)(2,1)S(1)} %bitcast.86, bf16[512,4,512]{0,2,1:T(8,128)(2,1)} %collective-permute-done.8), kind=kOutput, calls=%fused_computation.31 | convolution fusion | flops 268435456 | bytes 2097152 | tf_op jit(solution)/shard_map/dot_general | solution.py:118
  138.3 1.5 %fusion.14 = bf16[512,512]{1,0:T(8,128)(2,1)} fusion(f32[512,512]{1,0:T(8,128)S(1)} %fusion.19, f32[512,512]{1,0:T(8,128)S(1)} %fusion.20, f32[512,512]{1,0:T(8,128)S(1)} %fusion.21, f32[512,512]{1,0:T(8,128)S(1)} %fusion.22, f32[512,512]{1,0:T(8,128)S(1)} %fusion.31, f32[512,512]{1,0:T(8,128)S(1)} %fusion.30, f32[512,512]{1,0:T(8,128)S(1)} %fusion.29, ...), kind=kOutput, calls=%fused_computation.19 | convolution fusion | flops 270532608 | bytes 8912896 | tf_op jit(solution)/shard_map/dot_general | solution.py:116
  (36 shorter events, 0.9 us)
Async XLA Ops:
  6.5 22.0 %copy-start.11 = (bf16[32,128]{1,0:T(8,128)(2,1)S(1)}, bf16[32,128]{1,0:T(8,128)(2,1)}, u32[]{:S(2)}) copy-start(bf16[32,128]{1,0:T(8,128)(2,1)} %param.6) | copy-start | bytes 24580
  6.5 120.1 %all-gather.2.cloned.1.call-start = ((), (), s32[]{:S(2)}) async-start(), calls=%async_computation | async-start | bytes 4325376 | tf_op jit(solution)/shard_map/all_gather | solution.py:84
  7.7 17.5 %collective-permute-start.1 = (bf16[130,3,512]{2,0,1:T(8,128)(2,1)S(1)}, bf16[130,3,512]{2,0,1:T(8,128)(2,1)S(1)}, u32[]{:S(2)}, u32[]{:S(2)}) collective-permute-start(bf16[130,3,512]{2,0,1:T(8,128)(2,1)S(1)} %slice.81), channel_id=1, source_target_pairs={{0,8},{8,16},{16,24},{24,32},{32,40},{40,48},{48,56},{56,64},{64,7... | collective-permute-start | bytes 1198088 | tf_op jit(solution)/shard_map/ppermute | solution.py:20
  11.1 14.0 %collective-permute-start = (bf16[64,512]{1,0:T(8,128)(2,1)}, bf16[64,512]{1,0:T(8,128)(2,1)S(1)}, u32[]{:S(2)}, u32[]{:S(2)}) collective-permute-start(bf16[64,512]{1,0:T(8,128)(2,1)} %param.7), channel_id=1, source_target_pairs={{0,256},{256,0},{1,257},{257,1},{2,258},{258,2},{3,259},{259,3},{4... | collective-permute-start | bytes 196616 | tf_op jit(solution)/shard_map/ppermute | solution.py:77
  26.8 8.2 %copy-start.10 = (f32[3,3,512]{2,1,0:T(4,128)S(1)}, f32[3,3,512]{2,1,0:T(4,128)}, u32[]{:S(2)}) copy-start(f32[3,3,512]{2,1,0:T(4,128)} %param.5) | copy-start | bytes 55300
  39.4 2.1 %copy-start = (f32[640,3,512]{0,2,1:T(8,128)}, f32[640,3,512]{0,2,1:T(8,128)S(1)}, u32[]{:S(2)}) copy-start(f32[640,3,512]{0,2,1:T(8,128)S(1)} %fusion) | copy-start | bytes 11796484
  41.6 2.4 %copy-start.1 = (bf16[32,128,256]{2,1,0:T(8,128)(2,1)S(1)}, bf16[32,128,256]{2,1,0:T(8,128)(2,1)}, u32[]{:S(2)}) copy-start(bf16[32,128,256]{2,1,0:T(8,128)(2,1)} %shard_map.46) | copy-start | bytes 6291460
  47.7 18.7 %collective-permute-start.2 = (bf16[512,512]{0,1:T(8,128)(2,1)S(1)}, bf16[512,512]{0,1:T(8,128)(2,1)S(1)}, u32[]{:S(2)}, u32[]{:S(2)}) collective-permute-start(bf16[512,512]{0,1:T(8,128)(2,1)S(1)} %fusion.15), channel_id=1, source_target_pairs={{6,0},{7,1},{14,8},{15,9},{22,16},{23,17},{30,24},{31,25},{38,32},... | collective-permute-start | bytes 1572872 | tf_op jit(solution)/shard_map/ppermute | solution.py:62
  49.0 19.9 %collective-permute-start.3 = (bf16[512,512]{0,1:T(8,128)(2,1)S(1)}, bf16[512,512]{0,1:T(8,128)(2,1)S(1)}, u32[]{:S(2)}, u32[]{:S(2)}) collective-permute-start(bf16[512,512]{0,1:T(8,128)(2,1)S(1)} %fusion.15), channel_id=1, source_target_pairs={{0,6},{1,7},{8,14},{9,15},{16,22},{17,23},{24,30},{25,31},{32,38},... | collective-permute-start | bytes 1572872 | tf_op jit(solution)/shard_map/ppermute | solution.py:62
  55.4 30.5 %collective-permute-start.4 = (bf16[512,512]{0,1:T(8,128)(2,1)S(1)}, bf16[512,512]{0,1:T(8,128)(2,1)S(1)}, u32[]{:S(2)}, u32[]{:S(2)}) collective-permute-start(bf16[512,512]{0,1:T(8,128)(2,1)S(1)} %fusion.15), channel_id=1, source_target_pairs={{4,0},{6,2},{5,1},{7,3},{12,8},{14,10},{13,9},{15,11},{20,16},{22,... | collective-permute-start | bytes 1572872 | tf_op jit(solution)/shard_map/ppermute | solution.py:62
  56.7 29.2 %collective-permute-start.5 = (bf16[512,512]{0,1:T(8,128)(2,1)S(1)}, bf16[512,512]{0,1:T(8,128)(2,1)S(1)}, u32[]{:S(2)}, u32[]{:S(2)}) collective-permute-start(bf16[512,512]{0,1:T(8,128)(2,1)S(1)} %fusion.15), channel_id=1, source_target_pairs={{0,4},{2,6},{1,5},{3,7},{8,12},{10,14},{9,13},{11,15},{16,20},{18,... | collective-permute-start | bytes 1572872 | tf_op jit(solution)/shard_map/ppermute | solution.py:62
  62.2 25.2 %collective-permute-start.6 = (bf16[512,512]{0,1:T(8,128)(2,1)S(1)}, bf16[512,512]{0,1:T(8,128)(2,1)S(1)}, u32[]{:S(2)}, u32[]{:S(2)}) collective-permute-start(bf16[512,512]{0,1:T(8,128)(2,1)S(1)} %fusion.15), channel_id=1, source_target_pairs={{2,0},{4,2},{6,4},{3,1},{5,3},{7,5},{10,8},{12,10},{14,12},{11,9},... | collective-permute-start | bytes 1572872 | tf_op jit(solution)/shard_map/ppermute | solution.py:62
  66.4 21.1 %collective-permute-start.7 = (bf16[512,512]{0,1:T(8,128)(2,1)S(1)}, bf16[512,512]{0,1:T(8,128)(2,1)}, u32[]{:S(2)}, u32[]{:S(2)}) collective-permute-start(bf16[512,512]{0,1:T(8,128)(2,1)S(1)} %fusion.15), channel_id=1, source_target_pairs={{0,2},{2,4},{4,6},{1,3},{3,5},{5,7},{8,10},{10,12},{12,14},{9,11},... | collective-permute-start | bytes 1572872 | tf_op jit(solution)/shard_map/ppermute | solution.py:62
  87.6 0.8 copy-start.4
  87.8 0.8 copy-start.6
  88.0 0.8 copy-start.8
  88.2 0.9 copy-start.2
  89.1 43.1 %collective-permute-start.8 = (bf16[512,4,512]{0,2,1:T(8,128)(2,1)S(1)}, bf16[512,4,512]{0,2,1:T(8,128)(2,1)}, u32[]{:S(2)}, u32[]{:S(2)}) collective-permute-start(bf16[512,4,512]{0,2,1:T(8,128)(2,1)S(1)} %pad_maximum_fusion), channel_id=1, source_target_pairs={{0,1},{1,0},{2,3},{3,2},{4,5},{5,4},{6,7},{7,6},{8,9},{9,8},{10,11... | collective-permute-start | bytes 6291464 | tf_op jit(solution)/shard_map/ppermute | solution.py:105
  129.4 1.0 copy-start.5
  129.5 1.4 copy-start.7
  130.4 1.1 copy-start.9
  135.2 3.1 %copy-start.3 = (bf16[512,512]{0,1:T(8,128)(2,1)S(1)}, bf16[512,512]{0,1:T(8,128)(2,1)}, u32[]{:S(2)}) copy-start(bf16[512,512]{0,1:T(8,128)(2,1)} %copy-done.2) | copy-start | bytes 1572868
Sparse Core Ops, SparseCore 0:
  26.9 99.7 all-gather.1

commit v5 on v4

--- a/solution.py
+++ b/solution.py
@@ -81,7 +81,8 @@
 
     zh = lax.axis_index("zh")
     pair = jnp.where(zh == 0, jnp.stack([out_weight, partner]), jnp.stack([partner, out_weight]))
-    weight_xy = lax.all_gather(pair, ("x", "y"), axis=0, tiled=False)
+    spread = jnp.broadcast_to(pair[None], (32, *pair.shape))
+    weight_xy = lax.all_to_all(spread, ("x", "y"), 0, 0, tiled=True)
     weight_xy = weight_xy.reshape(4, 8, *weight_xy.shape[1:])
 
     joined = jnp.concatenate([previous, projected], axis=0).astype(jnp.float32)

time: 147 us -> 152 us (1.034)
  the two profiles are of different devices: /device:TPU:8 before, /device:TPU:64 now
where the time goes in v5:
time: 152 us; the launch traced here: 151 us
  waiting for transfers between devices  63.4 us (42%)
  starting transfers between devices  48.8 us (32%)
  local copies, waits for them, and re-layouts  14.1 us (9%)
  matrix products  10.9 us (7%)
  other arithmetic  8.34 us (5%)
  Pallas kernels  5.52 us (4%)
    ppermute x6, waiting for transfers between devices, line_gather(): received[d] = lax.ppermute(block, axis_name, pairs)  35.9 us
    all_to_all x1, waiting for transfers between devices, on_device(): weight_xy = lax.all_to_all(spread, ('x', 'y'), 0, 0, tiled=True)  24.7 us
    all_to_all x1, starting transfers between devices, on_device(): weight_xy = lax.all_to_all(spread, ('x', 'y'), 0, 0, tiled=True)  21.1 us
    ppermute x6, starting transfers between devices, line_gather(): received[d] = lax.ppermute(block, axis_name, pairs)  12.2 us
    ppermute x1, starting transfers between devices, on_device(): partner = lax.ppermute(out_weight, 'zh', [(0, 1), (1, 0)])  10 us
    dot_general x4, matrix products, on_device(): jnp.dot(other[:, zl], weight_rows(zl, 1 - core), preferred_element_type=j...  6.11 us
    pallas_call x1, Pallas kernels, toeplitz_blocks(): pl.pallas_call(toeplitz_kernel, out_shape=jax.ShapeDtypeStruct((groups, s...  5.52 us
    slice x5, local copies, waits for them, and re-layouts, on_device(): window = jnp.concatenate([blocks[:-1], blocks[1:]], axis=1)  3.53 us
  transfers between devices with their start and end apart: 10, of which 5 were waited for; matrix products, arithmetic and copies ran while one was open for 12% of the time, Pallas kernels for 4%

profile of v5, /device:TPU:64, one launch (start us, length us, event | category | flops | bytes accessed | tf_op | source)
XLA Modules:
  0.0 151.5 jit_solution(6998223647319351683)
XLA Ops:
  0.0 1.1 slice.81
  1.1 3.5 %collective-permute-start.1 = (bf16[130,3,512]{2,0,1:T(8,128)(2,1)S(1)}, bf16[130,3,512]{2,0,1:T(8,128)(2,1)S(1)}, u32[]{:S(2)}, u32[]{:S(2)}) collective-permute-start(bf16[130,3,512]{2,0,1:T(8,128)(2,1)S(1)} %slice.81), channel_id=1, source_target_pairs={{0,8},{8,16},{16,24},{24,32},{32,40},{40,48},{48,56},{56,64},{64,7... | collective-permute-start | bytes 1198088 | tf_op jit(solution)/shard_map/ppermute | solution.py:20
  4.6 10.0 %collective-permute-start = (bf16[64,512]{1,0:T(8,128)(2,1)}, bf16[64,512]{1,0:T(8,128)(2,1)S(1)}, u32[]{:S(2)}, u32[]{:S(2)}) collective-permute-start(bf16[64,512]{1,0:T(8,128)(2,1)} %param.7), channel_id=1, source_target_pairs={{0,256},{256,0},{1,257},{257,1},{2,258},{258,2},{3,259},{259,3},{4... | collective-permute-start | bytes 196616 | tf_op jit(solution)/shard_map/ppermute | solution.py:77
  14.6 2.8 %collective-permute-done = bf16[64,512]{1,0:T(8,128)(2,1)S(1)} collective-permute-done((bf16[64,512]{1,0:T(8,128)(2,1)}, bf16[64,512]{1,0:T(8,128)(2,1)S(1)}, u32[]{:S(2)}, u32[]{:S(2)}) %collective-permute-start) | collective-permute-done | bytes 65568 | tf_op jit(solution)/shard_map/ppermute | solution.py:77
  17.4 1.0 maximum_select_fusion
  18.5 2.5 %broadcast_in_dim.14 = bf16[32,2,64,512]{3,2,1,0:T(8,128)(2,1)} broadcast(bf16[2,64,512]{2,1,0:T(8,128)(2,1)S(1)} %maximum_select_fusion), dimensions={1,2,3} | broadcast | bytes 4325376 | tf_op jit(solution)/shard_map/broadcast_in_dim | solution.py:84
  21.0 21.1 %all-to-all-start = ((bf16[32,2,64,512]{3,2,1,0:T(8,128)(2,1)}), bf16[32,2,64,512]{3,2,1,0:T(8,128)(2,1)}, u32[]{:S(2)}, u32[]{:S(2)}) async-start(bf16[32,2,64,512]{3,2,1,0:T(8,128)(2,1)} %broadcast_in_dim.14), calls=%async_computation | async-start | bytes 8388608 | tf_op jit(solution)/shard_map/all_to_all | solution.py:85
  42.2 0.7 copy.11
  43.1 0.7 maximum_maximum_fusion.row_ref
  43.8 5.5 %shard_map.46 = bf16[32,128,256]{2,1,0:T(8,128)(2,1)} custom-call(f32[32,384]{1,0:T(8,128)} %maximum_maximum_fusion.row_ref), custom_call_target="tpu_custom_call" | custom-call | tf_op jit(solution)/shard_map/pallas_call | solution.py:48
  49.3 0.3 copy.10
  49.6 0.9 maximum_convert_fusion
  50.5 3.3 %fusion = f32[640,3,512]{0,2,1:T(8,128)S(1)} fusion(f32[642,3,512]{0,2,1:T(8,128)S(1)} %maximum_convert_fusion, f32[3,512]{1,0:T(4,128)S(1)} %get-tuple-element.24, f32[3,512]{1,0:T(4,128)S(1)} %get-tuple-element.25, f32[3,512]{1,0:T(4,128)S(1)} %get-tuple-element.23), kind=kLoop, calls=%fused_computation.1 | loop fusion | flops 4915200 | bytes 15747072 | tf_op jit(solution)/shard_map/add | solution.py:90
  53.9 1.1 fusion.28
  55.0 0.8 copy-done
  55.8 1.3 slice.91
  57.2 0.9 copy.12
  58.3 1.9 %fusion.4 = f32[4,128,32,16]{1,3,0,2:T(8,128)S(1)} fusion(bf16[32,128,256]{2,1,0:T(8,128)(2,1)S(1)} %copy-done.1, bf16[4,128,32,16]{1,3,0,2:T(8,128)(2,1)S(1)} %copy.13, bf16[4,128,32,16]{1,3,0,2:T(8,128)(2,1)} %copy.12), kind=kOutput, calls=%fused_computation.9 | convolution fusion | flops 136314880 | bytes 4194304 | tf_op jit(solution)/shard_map/gij,bjgc->bigc/dot_general | solution.py:100
  60.2 0.4 copy.14
  60.6 1.4 fusion.15
  62.0 3.4 %collective-permute-start.7 = (bf16[512,512]{0,1:T(8,128)(2,1)S(1)}, bf16[512,512]{0,1:T(8,128)(2,1)S(1)}, u32[]{:S(2)}, u32[]{:S(2)}) collective-permute-start(bf16[512,512]{0,1:T(8,128)(2,1)S(1)} %fusion.15), channel_id=1, source_target_pairs={{0,2},{2,4},{4,6},{1,3},{3,5},{5,7},{8,10},{10,12},{12,14},{9,11},... | collective-permute-start | bytes 1572872 | tf_op jit(solution)/shard_map/ppermute | solution.py:62
  65.4 2.5 %collective-permute-start.6 = (bf16[512,512]{0,1:T(8,128)(2,1)S(1)}, bf16[512,512]{0,1:T(8,128)(2,1)S(1)}, u32[]{:S(2)}, u32[]{:S(2)}) collective-permute-start(bf16[512,512]{0,1:T(8,128)(2,1)S(1)} %fusion.15), channel_id=1, source_target_pairs={{2,0},{4,2},{6,4},{3,1},{5,3},{7,5},{10,8},{12,10},{14,12},{11,9},... | collective-permute-start | bytes 1572872 | tf_op jit(solution)/shard_map/ppermute | solution.py:62
  67.9 2.8 %collective-permute-start.5 = (bf16[512,512]{0,1:T(8,128)(2,1)S(1)}, bf16[512,512]{0,1:T(8,128)(2,1)S(1)}, u32[]{:S(2)}, u32[]{:S(2)}) collective-permute-start(bf16[512,512]{0,1:T(8,128)(2,1)S(1)} %fusion.15), channel_id=1, source_target_pairs={{0,4},{2,6},{1,5},{3,7},{8,12},{10,14},{9,13},{11,15},{16,20},{18,... | collective-permute-start | bytes 1572872 | tf_op jit(solution)/shard_map/ppermute | solution.py:62
  70.7 1.3 collective-permute-start.4
  72.0 0.7 collective-permute-start.3
  72.7 27.4 %collective-permute-done.7 = bf16[512,512]{0,1:T(8,128)(2,1)S(1)} collective-permute-done((bf16[512,512]{0,1:T(8,128)(2,1)S(1)}, bf16[512,512]{0,1:T(8,128)(2,1)S(1)}, u32[]{:S(2)}, u32[]{:S(2)}) %collective-permute-start.7) | collective-permute-done | bytes 524320 | tf_op jit(solution)/shard_map/ppermute | solution.py:62
  100.2 1.5 %collective-permute-start.2 = (bf16[512,512]{0,1:T(8,128)(2,1)S(1)}, bf16[512,512]{0,1:T(8,128)(2,1)}, u32[]{:S(2)}, u32[]{:S(2)}) collective-permute-start(bf16[512,512]{0,1:T(8,128)(2,1)S(1)} %fusion.15), channel_id=1, source_target_pairs={{6,0},{7,1},{14,8},{15,9},{22,16},{23,17},{30,24},{31,25},{38,32},... | collective-permute-start | bytes 1572872 | tf_op jit(solution)/shard_map/ppermute | solution.py:62
  101.7 2.9 %collective-permute-done.6 = bf16[512,512]{0,1:T(8,128)(2,1)S(1)} collective-permute-done((bf16[512,512]{0,1:T(8,128)(2,1)S(1)}, bf16[512,512]{0,1:T(8,128)(2,1)S(1)}, u32[]{:S(2)}, u32[]{:S(2)}) %collective-permute-start.6) | collective-permute-done | bytes 524320 | tf_op jit(solution)/shard_map/ppermute | solution.py:62
  104.6 5.5 %collective-permute-done.5 = bf16[512,512]{0,1:T(8,128)(2,1)S(1)} collective-permute-done((bf16[512,512]{0,1:T(8,128)(2,1)S(1)}, bf16[512,512]{0,1:T(8,128)(2,1)S(1)}, u32[]{:S(2)}, u32[]{:S(2)}) %collective-permute-start.5) | collective-permute-done | bytes 524320 | tf_op jit(solution)/shard_map/ppermute | solution.py:62
  110.1 0.2 select_select_fusion
  110.3 0.2 select_select_fusion.1
  110.5 0.2 select_select_fusion.2
  110.7 0.2 select_select_fusion.3
  110.9 0.2 copy-done.4
  111.1 0.2 copy-done.6
  111.5 0.3 pad_maximum_fusion
  111.8 1.9 %collective-permute-start.8 = (bf16[512,4,512]{0,2,1:T(8,128)(2,1)S(1)}, bf16[512,4,512]{0,2,1:T(8,128)(2,1)}, u32[]{:S(2)}, u32[]{:S(2)}) collective-permute-start(bf16[512,4,512]{0,2,1:T(8,128)(2,1)S(1)} %pad_maximum_fusion), channel_id=1, source_target_pairs={{0,1},{1,0},{2,3},{3,2},{4,5},{5,4},{6,7},{7,6},{8,9},{9,8},{10,11... | collective-permute-start | bytes 6291464 | tf_op jit(solution)/shard_map/ppermute | solution.py:106
  113.7 24.7 %all-to-all-done = bf16[32,2,64,512]{3,2,1,0:T(8,128)(2,1)} async-done(((bf16[32,2,64,512]{3,2,1,0:T(8,128)(2,1)}), bf16[32,2,64,512]{3,2,1,0:T(8,128)(2,1)}, u32[]{:S(2)}, u32[]{:S(2)}) %all-to-all-start) | async-done | bytes 4194336 | tf_op jit(solution)/shard_map/all_to_all | solution.py:85
  138.4 2.7 %dynamic-slice_bitcast_fusion.3 = (bf16[8,2,64,512]{3,2,1,0:T(8,128)(2,1)S(1)}, bf16[8,2,64,512]{3,2,1,0:T(8,128)(2,1)S(1)}, bf16[8,2,64,512]{3,2,1,0:T(8,128)(2,1)S(1)}, bf16[8,2,64,512]{3,2,1,0:T(8,128)(2,1)S(1)}) fusion(bf16[4,8,2,64,512]{4,3,2,1,0:T(8,128)(2,1)} %bitcast.9, s32[]{:T(128)S(6)} %select_n.215, s32[]{:T(128)S(6)} %select_n.260, ...), kind=kLoop, calls=%fused_computation.29 | loop fusion | bytes 8388624 | tf_op jit(solution)/shard_map/jit(dynamic_index_in_dim)/squeeze | solution.py:112
  141.3 0.9 copy-done.7
  142.1 0.5 fusion.30
  142.6 0.5 fusion.31
  143.2 0.5 fusion.29
  143.9 1.5 fusion.20
  145.4 1.5 %fusion.22 = f32[512,512]{1,0:T(8,128)S(1)} fusion(bf16[512,512]{1,0:T(8,128)(2,1)S(1)} %bitcast.88, bf16[512,4,512]{0,2,1:T(8,128)(2,1)} %collective-permute-done.8), kind=kOutput, calls=%fused_computation.37 | convolution fusion | flops 268435456 | bytes 2097152 | tf_op jit(solution)/shard_map/dot_general | solution.py:119
  146.9 1.6 %fusion.19 = f32[512,512]{1,0:T(8,128)S(1)} fusion(bf16[512,512]{1,0:T(8,128)(2,1)S(1)} %bitcast.86, bf16[512,4,512]{0,2,1:T(8,128)(2,1)} %collective-permute-done.8), kind=kOutput, calls=%fused_computation.31 | convolution fusion | flops 268435456 | bytes 2097152 | tf_op jit(solution)/shard_map/dot_general | solution.py:119
  148.5 1.5 %fusion.21 = f32[512,512]{1,0:T(8,128)S(1)} fusion(bf16[512,512]{1,0:T(8,128)(2,1)S(1)} %bitcast.85, bf16[512,4,512]{0,2,1:T(8,128)(2,1)} %collective-permute-done.8), kind=kOutput, calls=%fused_computation.35 | convolution fusion | flops 268435456 | bytes 2097152 | tf_op jit(solution)/shard_map/dot_general | solution.py:119
  150.0 1.5 fusion.14
  (42 shorter events, 1.2 us)
Async XLA Ops:
  1.1 16.3 %collective-permute-start.1 = (bf16[130,3,512]{2,0,1:T(8,128)(2,1)S(1)}, bf16[130,3,512]{2,0,1:T(8,128)(2,1)S(1)}, u32[]{:S(2)}, u32[]{:S(2)}) collective-permute-start(bf16[130,3,512]{2,0,1:T(8,128)(2,1)S(1)} %slice.81), channel_id=1, source_target_pairs={{0,8},{8,16},{16,24},{24,32},{32,40},{40,48},{48,56},{56,64},{64,7... | collective-permute-start | bytes 1198088 | tf_op jit(solution)/shard_map/ppermute | solution.py:20
  4.6 12.8 %collective-permute-start = (bf16[64,512]{1,0:T(8,128)(2,1)}, bf16[64,512]{1,0:T(8,128)(2,1)S(1)}, u32[]{:S(2)}, u32[]{:S(2)}) collective-permute-start(bf16[64,512]{1,0:T(8,128)(2,1)} %param.7), channel_id=1, source_target_pairs={{0,256},{256,0},{1,257},{257,1},{2,258},{258,2},{3,259},{259,3},{4... | collective-permute-start | bytes 196616 | tf_op jit(solution)/shard_map/ppermute | solution.py:77
  17.4 3.5 %copy-start.11 = (bf16[130,3,512]{2,0,1:T(8,128)(2,1)}, bf16[130,3,512]{2,0,1:T(8,128)(2,1)S(1)}, u32[]{:S(2)}) copy-start(bf16[130,3,512]{2,0,1:T(8,128)(2,1)S(1)} %collective-permute-done.1) | copy-start | bytes 1198084
  21.0 21.2 %copy-start.10 = (bf16[512,3,512]{2,0,1:T(8,128)(2,1)S(1)}, bf16[512,3,512]{2,0,1:T(8,128)(2,1)}, u32[]{:S(2)}) copy-start(bf16[512,3,512]{2,0,1:T(8,128)(2,1)} %param.4) | copy-start | bytes 4718596
  21.0 117.4 %all-to-all-start = ((bf16[32,2,64,512]{3,2,1,0:T(8,128)(2,1)}), bf16[32,2,64,512]{3,2,1,0:T(8,128)(2,1)}, u32[]{:S(2)}, u32[]{:S(2)}) async-start(bf16[32,2,64,512]{3,2,1,0:T(8,128)(2,1)} %broadcast_in_dim.14), calls=%async_computation | async-start | bytes 8388608 | tf_op jit(solution)/shard_map/all_to_all | solution.py:85
  42.2 0.8 copy-start.14
  42.2 7.2 %copy-start.13 = (f32[3,3,512]{2,1,0:T(4,128)S(1)}, f32[3,3,512]{2,1,0:T(4,128)}, u32[]{:S(2)}) copy-start(f32[3,3,512]{2,1,0:T(4,128)} %param.5) | copy-start | bytes 55300
  42.9 6.4 %copy-start.12 = (bf16[130,3,512]{2,0,1:T(8,128)(2,1)S(1)}, bf16[130,3,512]{2,0,1:T(8,128)(2,1)}, u32[]{:S(2)}) copy-start(bf16[130,3,512]{2,0,1:T(8,128)(2,1)} %copy-done.11) | copy-start | bytes 1198084
  53.8 2.1 %copy-start = (f32[640,3,512]{0,2,1:T(8,128)}, f32[640,3,512]{0,2,1:T(8,128)S(1)}, u32[]{:S(2)}) copy-start(f32[640,3,512]{0,2,1:T(8,128)S(1)} %fusion) | copy-start | bytes 11796484
  55.8 2.4 %copy-start.1 = (bf16[32,128,256]{2,1,0:T(8,128)(2,1)S(1)}, bf16[32,128,256]{2,1,0:T(8,128)(2,1)}, u32[]{:S(2)}) copy-start(bf16[32,128,256]{2,1,0:T(8,128)(2,1)} %shard_map.46) | copy-start | bytes 6291460
  62.0 38.2 %collective-permute-start.7 = (bf16[512,512]{0,1:T(8,128)(2,1)S(1)}, bf16[512,512]{0,1:T(8,128)(2,1)S(1)}, u32[]{:S(2)}, u32[]{:S(2)}) collective-permute-start(bf16[512,512]{0,1:T(8,128)(2,1)S(1)} %fusion.15), channel_id=1, source_target_pairs={{0,2},{2,4},{4,6},{1,3},{3,5},{5,7},{8,10},{10,12},{12,14},{9,11},... | collective-permute-start | bytes 1572872 | tf_op jit(solution)/shard_map/ppermute | solution.py:62
  65.4 39.2 %collective-permute-start.6 = (bf16[512,512]{0,1:T(8,128)(2,1)S(1)}, bf16[512,512]{0,1:T(8,128)(2,1)S(1)}, u32[]{:S(2)}, u32[]{:S(2)}) collective-permute-start(bf16[512,512]{0,1:T(8,128)(2,1)S(1)} %fusion.15), channel_id=1, source_target_pairs={{2,0},{4,2},{6,4},{3,1},{5,3},{7,5},{10,8},{12,10},{14,12},{11,9},... | collective-permute-start | bytes 1572872 | tf_op jit(solution)/shard_map/ppermute | solution.py:62
  67.9 42.2 %collective-permute-start.5 = (bf16[512,512]{0,1:T(8,128)(2,1)S(1)}, bf16[512,512]{0,1:T(8,128)(2,1)S(1)}, u32[]{:S(2)}, u32[]{:S(2)}) collective-permute-start(bf16[512,512]{0,1:T(8,128)(2,1)S(1)} %fusion.15), channel_id=1, source_target_pairs={{0,4},{2,6},{1,5},{3,7},{8,12},{10,14},{9,13},{11,15},{16,20},{18,... | collective-permute-start | bytes 1572872 | tf_op jit(solution)/shard_map/ppermute | solution.py:62
  70.7 39.4 %collective-permute-start.4 = (bf16[512,512]{0,1:T(8,128)(2,1)S(1)}, bf16[512,512]{0,1:T(8,128)(2,1)S(1)}, u32[]{:S(2)}, u32[]{:S(2)}) collective-permute-start(bf16[512,512]{0,1:T(8,128)(2,1)S(1)} %fusion.15), channel_id=1, source_target_pairs={{4,0},{6,2},{5,1},{7,3},{12,8},{14,10},{13,9},{15,11},{20,16},{22,... | collective-permute-start | bytes 1572872 | tf_op jit(solution)/shard_map/ppermute | solution.py:62
  72.0 38.1 %collective-permute-start.3 = (bf16[512,512]{0,1:T(8,128)(2,1)S(1)}, bf16[512,512]{0,1:T(8,128)(2,1)S(1)}, u32[]{:S(2)}, u32[]{:S(2)}) collective-permute-start(bf16[512,512]{0,1:T(8,128)(2,1)S(1)} %fusion.15), channel_id=1, source_target_pairs={{0,6},{1,7},{8,14},{9,15},{16,22},{17,23},{24,30},{25,31},{32,38},... | collective-permute-start | bytes 1572872 | tf_op jit(solution)/shard_map/ppermute | solution.py:62
  100.2 10.0 %collective-permute-start.2 = (bf16[512,512]{0,1:T(8,128)(2,1)S(1)}, bf16[512,512]{0,1:T(8,128)(2,1)}, u32[]{:S(2)}, u32[]{:S(2)}) collective-permute-start(bf16[512,512]{0,1:T(8,128)(2,1)S(1)} %fusion.15), channel_id=1, source_target_pairs={{6,0},{7,1},{14,8},{15,9},{22,16},{23,17},{30,24},{31,25},{38,32},... | collective-permute-start | bytes 1572872 | tf_op jit(solution)/shard_map/ppermute | solution.py:62
  110.3 0.8 copy-start.4
  110.5 0.8 copy-start.6
  110.7 0.8 copy-start.8
  110.9 0.9 copy-start.2
  111.8 32.1 %collective-permute-start.8 = (bf16[512,4,512]{0,2,1:T(8,128)(2,1)S(1)}, bf16[512,4,512]{0,2,1:T(8,128)(2,1)}, u32[]{:S(2)}, u32[]{:S(2)}) collective-permute-start(bf16[512,4,512]{0,2,1:T(8,128)(2,1)S(1)} %pad_maximum_fusion), channel_id=1, source_target_pairs={{0,1},{1,0},{2,3},{3,2},{4,5},{5,4},{6,7},{7,6},{8,9},{9,8},{10,11... | collective-permute-start | bytes 6291464 | tf_op jit(solution)/shard_map/ppermute | solution.py:106
  141.1 1.0 copy-start.7
  141.2 1.4 copy-start.5
  142.1 1.1 copy-start.9
  146.9 3.1 %copy-start.3 = (bf16[512,512]{0,1:T(8,128)(2,1)S(1)}, bf16[512,512]{0,1:T(8,128)(2,1)}, u32[]{:S(2)}) copy-start(bf16[512,512]{0,1:T(8,128)(2,1)} %copy-done.2) | copy-start | bytes 1572868

commit v6 on v4

--- a/solution.py
+++ b/solution.py
@@ -79,10 +79,11 @@
     previous = from_behind(tail)
     partner, previous = lax.optimization_barrier((partner, previous))
 
+    own_xy = lax.all_gather(out_weight, ("x", "y"), axis=0, tiled=False)
+    other_xy = lax.all_gather(partner, ("x", "y"), axis=0, tiled=False)
     zh = lax.axis_index("zh")
-    pair = jnp.where(zh == 0, jnp.stack([out_weight, partner]), jnp.stack([partner, out_weight]))
-    weight_xy = lax.all_gather(pair, ("x", "y"), axis=0, tiled=False)
-    weight_xy = weight_xy.reshape(4, 8, *weight_xy.shape[1:])
+    own_xy = own_xy.reshape(4, 8, *out_weight.shape)
+    other_xy = other_xy.reshape(4, 8, *out_weight.shape)
 
     joined = jnp.concatenate([previous, projected], axis=0).astype(jnp.float32)
     featured = (
@@ -104,11 +105,13 @@
     g_zl = line_gather(gated, "zl", 4)
     other = lax.ppermute(g_zl, "c", [(0, 1), (1, 0)])
     core = lax.axis_index("c")
-    out_cols = weight_xy.shape[-1]
+    out_cols = out_weight.shape[-1]
 
     def weight_rows(zl, c):
         x = 2 * (zl % 2) + c
-        piece = lax.dynamic_index_in_dim(weight_xy, x, axis=0, keepdims=False)[:, zl // 2]
+        own = lax.dynamic_index_in_dim(own_xy, x, axis=0, keepdims=False)
+        other = lax.dynamic_index_in_dim(other_xy, x, axis=0, keepdims=False)
+        piece = jnp.where(zh == zl // 2, own, other)
         return piece.reshape(-1, out_cols)
 
     mixed = jnp.zeros((tok_rows, out_cols), jnp.float32)

time: 147 us -> 201 us (1.37)
  the two profiles are of different devices: /device:TPU:8 before, /device:TPU:16 now
where the time goes in v6:
time: 201 us
  waiting for transfers between devices  115 us (57%)
  starting transfers between devices  34.7 us (17%)
  between operations  13.7 us (7%)
  matrix products  10.8 us (5%)
  local copies, waits for them, and re-layouts  10.6 us (5%)
  other arithmetic  9.81 us (5%)
  Pallas kernels  5.57 us (3%)
    all_gather x1, waiting for transfers between devices, on_device(): other_xy = lax.all_gather(partner, ('x', 'y'), axis=0, tiled=False)  83.9 us
    ppermute x6, waiting for transfers between devices, line_gather(): received[d] = lax.ppermute(block, axis_name, pairs)  22.1 us
    ppermute x6, starting transfers between devices, line_gather(): received[d] = lax.ppermute(block, axis_name, pairs)  18.3 us
    ppermute x1, starting transfers between devices, on_device(): partner = lax.ppermute(out_weight, 'zh', [(0, 1), (1, 0)])  10.9 us
    all_gather x1, waiting for transfers between devices, on_device(): own_xy = lax.all_gather(out_weight, ('x', 'y'), axis=0, tiled=False)  8.62 us
    dot_general x4, matrix products, on_device(): jnp.dot(other[:, zl], weight_rows(zl, 1 - core), preferred_element_type=j...  6.07 us
    pallas_call x1, Pallas kernels, toeplitz_blocks(): pl.pallas_call(toeplitz_kernel, out_shape=jax.ShapeDtypeStruct((groups, s...  5.57 us
  transfers between devices with their start and end apart: 11, of which 7 were waited for; matrix products, arithmetic and copies ran while one was open for 11% of the time, Pallas kernels for 3%

profile of v6, /device:TPU:16, one launch (start us, length us, event | category | flops | bytes accessed | tf_op | source)
XLA Modules:
  0.0 200.7 jit_solution(10853212382698997244)
XLA Ops:
  6.5 0.7 all-gather.5.cloned.1.call-update
  7.3 10.9 %collective-permute-start = (bf16[64,512]{1,0:T(8,128)(2,1)}, bf16[64,512]{1,0:T(8,128)(2,1)S(1)}, u32[]{:S(2)}, u32[]{:S(2)}) collective-permute-start(bf16[64,512]{1,0:T(8,128)(2,1)} %param.7), channel_id=1, source_target_pairs={{0,256},{256,0},{1,257},{257,1},{2,258},{258,2},{3,259},{259,3},{4... | collective-permute-start | bytes 196616 | tf_op jit(solution)/shard_map/ppermute | solution.py:77
  18.2 1.1 slice.57
  19.3 3.5 %collective-permute-start.1 = (bf16[130,3,512]{2,0,1:T(8,128)(2,1)S(1)}, bf16[130,3,512]{2,0,1:T(8,128)(2,1)S(1)}, u32[]{:S(2)}, u32[]{:S(2)}) collective-permute-start(bf16[130,3,512]{2,0,1:T(8,128)(2,1)S(1)} %slice.57), channel_id=1, source_target_pairs={{0,8},{8,16},{16,24},{24,32},{32,40},{40,48},{48,56},{56,64},{64,7... | collective-permute-start | bytes 1198088 | tf_op jit(solution)/shard_map/ppermute | solution.py:20
  22.8 0.8 rev.3
  23.7 0.7 maximum_maximum_fusion.row_ref
  24.4 0.7 slice_bitcast_fusion.11
  25.1 1.7 copy.11
  26.9 5.6 %shard_map.46 = bf16[32,128,256]{2,1,0:T(8,128)(2,1)} custom-call(f32[32,384]{1,0:T(8,128)} %maximum_maximum_fusion.row_ref), custom_call_target="tpu_custom_call" | custom-call | tf_op jit(solution)/shard_map/pallas_call | solution.py:48
  32.5 0.3 copy.10
  32.8 0.9 maximum_convert_fusion
  33.7 3.3 %fusion = f32[640,3,512]{0,2,1:T(8,128)S(1)} fusion(f32[642,3,512]{0,2,1:T(8,128)S(1)} %maximum_convert_fusion, f32[3,512]{1,0:T(4,128)S(1)} %get-tuple-element.20, f32[3,512]{1,0:T(4,128)S(1)} %get-tuple-element.21, f32[3,512]{1,0:T(4,128)S(1)} %get-tuple-element.19), kind=kLoop, calls=%fused_computation.1 | loop fusion | flops 4915200 | bytes 15747072 | tf_op jit(solution)/shard_map/add | solution.py:90
  37.1 1.1 fusion.24
  38.2 0.8 copy-done
  39.0 1.3 slice.67
  40.3 0.9 copy.12
  41.5 1.9 fusion.4
  43.4 0.4 copy.14
  43.8 1.4 fusion.15
  45.2 1.3 collective-permute-start.2
  46.5 6.4 %collective-permute-start.3 = (bf16[512,512]{0,1:T(8,128)(2,1)S(1)}, bf16[512,512]{0,1:T(8,128)(2,1)S(1)}, u32[]{:S(2)}, u32[]{:S(2)}) collective-permute-start(bf16[512,512]{0,1:T(8,128)(2,1)S(1)} %fusion.15), channel_id=1, source_target_pairs={{0,6},{1,7},{8,14},{9,15},{16,22},{17,23},{24,30},{25,31},{32,38},... | collective-permute-start | bytes 1572872 | tf_op jit(solution)/shard_map/ppermute | solution.py:62
  52.9 1.3 collective-permute-start.4
  54.2 5.5 %collective-permute-start.5 = (bf16[512,512]{0,1:T(8,128)(2,1)S(1)}, bf16[512,512]{0,1:T(8,128)(2,1)S(1)}, u32[]{:S(2)}, u32[]{:S(2)}) collective-permute-start(bf16[512,512]{0,1:T(8,128)(2,1)S(1)} %fusion.15), channel_id=1, source_target_pairs={{0,4},{2,6},{1,5},{3,7},{8,12},{10,14},{9,13},{11,15},{16,20},{18,... | collective-permute-start | bytes 1572872 | tf_op jit(solution)/shard_map/ppermute | solution.py:62
  59.7 1.3 collective-permute-start.6
  61.0 2.8 %collective-permute-done.2 = bf16[512,512]{0,1:T(8,128)(2,1)S(1)} collective-permute-done((bf16[512,512]{0,1:T(8,128)(2,1)S(1)}, bf16[512,512]{0,1:T(8,128)(2,1)S(1)}, u32[]{:S(2)}, u32[]{:S(2)}) %collective-permute-start.2) | collective-permute-done | bytes 524320 | tf_op jit(solution)/shard_map/ppermute | solution.py:62
  63.8 2.6 %collective-permute-start.7 = (bf16[512,512]{0,1:T(8,128)(2,1)S(1)}, bf16[512,512]{0,1:T(8,128)(2,1)}, u32[]{:S(2)}, u32[]{:S(2)}) collective-permute-start(bf16[512,512]{0,1:T(8,128)(2,1)S(1)} %fusion.15), channel_id=1, source_target_pairs={{0,2},{2,4},{4,6},{1,3},{3,5},{5,7},{8,10},{10,12},{12,14},{9,11},... | collective-permute-start | bytes 1572872 | tf_op jit(solution)/shard_map/ppermute | solution.py:62
  66.4 18.1 %collective-permute-done.4 = bf16[512,512]{0,1:T(8,128)(2,1)S(1)} collective-permute-done((bf16[512,512]{0,1:T(8,128)(2,1)S(1)}, bf16[512,512]{0,1:T(8,128)(2,1)S(1)}, u32[]{:S(2)}, u32[]{:S(2)}) %collective-permute-start.4) | collective-permute-done | bytes 524320 | tf_op jit(solution)/shard_map/ppermute | solution.py:62
  84.5 0.9 collective-permute-done.6
  85.4 0.2 collective-permute-done.7
  85.8 0.2 select_select_fusion.2
  86.0 0.2 select_select_fusion.1
  86.4 0.2 copy-done.2
  86.6 0.2 copy-done.4
  86.8 0.2 copy-done.6
  87.0 0.3 pad_maximum_fusion
  87.3 1.9 collective-permute-start.8
  89.2 8.6 %all-gather.5.cloned.1.call-done = bf16[2048,512]{1,0:T(8,128)(2,1)} async-done(((bf16[64,512]{1,0:T(8,128)(2,1)}), bf16[2048,512]{1,0:T(8,128)(2,1)}) %all-gather.5.cloned.1.call-update) | async-done | bytes 2097168 | tf_op jit(solution)/shard_map/all_gather | solution.py:82
  97.8 83.9 %all-gather.7.cloned.1.call-done = bf16[2048,512]{1,0:T(8,128)(2,1)} async-done(((bf16[64,512]{1,0:T(8,128)(2,1)}), bf16[2048,512]{1,0:T(8,128)(2,1)}) %all-gather.7.cloned.1.call-update) | async-done | bytes 2097168 | tf_op jit(solution)/shard_map/all_gather | solution.py:83
  181.8 2.5 %broadcast_select_fusion.7 = (bf16[1,8,64,512]{3,2,1,0:T(8,128)(2,1)S(1)}, bf16[1,8,64,512]{3,2,1,0:T(8,128)(2,1)S(1)}, bf16[1,8,64,512]{3,2,1,0:T(8,128)(2,1)S(...) fusion(pred[]{:T(512)S(6)} %eq.103, ...), kind=kLoop, calls=%fused_computation.45 | loop fusion | flops 2097152 | bytes 8388626 | tf_op jit(solution)/shard_map/jit(_where)/select_n | solution.py:114
  184.3 0.5 fusion.25
  184.8 0.5 copy-done.7
  185.3 0.5 fusion.26
  185.8 0.5 fusion.27
  186.3 1.5 fusion.22
  187.8 1.5 fusion.21
  189.3 1.6 fusion.20
  190.8 1.5 fusion.19
  192.4 1.5 fusion.14
  (34 shorter events, 0.9 us)
Async XLA Ops:
  6.5 91.3 %all-gather.5.cloned.1.call-start = ((), (), s32[]{:S(2)}) async-start(), calls=%async_computation | async-start | bytes 2162688 | tf_op jit(solution)/shard_map/all_gather | solution.py:82
  7.3 174.5 %all-gather.7.cloned.1.call-start = ((), (), s32[]{:S(2)}) async-start(), calls=%async_computation.1 | async-start | bytes 2162688 | tf_op jit(solution)/shard_map/all_gather | solution.py:83
  7.3 25.1 %collective-permute-start = (bf16[64,512]{1,0:T(8,128)(2,1)}, bf16[64,512]{1,0:T(8,128)(2,1)S(1)}, u32[]{:S(2)}, u32[]{:S(2)}) collective-permute-start(bf16[64,512]{1,0:T(8,128)(2,1)} %param.7), channel_id=1, source_target_pairs={{0,256},{256,0},{1,257},{257,1},{2,258},{258,2},{3,259},{259,3},{4... | collective-permute-start | bytes 196616 | tf_op jit(solution)/shard_map/ppermute | solution.py:77
  19.3 13.2 %collective-permute-start.1 = (bf16[130,3,512]{2,0,1:T(8,128)(2,1)S(1)}, bf16[130,3,512]{2,0,1:T(8,128)(2,1)S(1)}, u32[]{:S(2)}, u32[]{:S(2)}) collective-permute-start(bf16[130,3,512]{2,0,1:T(8,128)(2,1)S(1)} %slice.57), channel_id=1, source_target_pairs={{0,8},{8,16},{16,24},{24,32},{32,40},{40,48},{48,56},{56,64},{64,7... | collective-permute-start | bytes 1198088 | tf_op jit(solution)/shard_map/ppermute | solution.py:20
  32.4 1.2 copy-start.10
  37.0 2.0 %copy-start = (f32[640,3,512]{0,2,1:T(8,128)}, f32[640,3,512]{0,2,1:T(8,128)S(1)}, u32[]{:S(2)}) copy-start(f32[640,3,512]{0,2,1:T(8,128)S(1)} %fusion) | copy-start | bytes 11796484
  39.0 2.5 %copy-start.1 = (bf16[32,128,256]{2,1,0:T(8,128)(2,1)S(1)}, bf16[32,128,256]{2,1,0:T(8,128)(2,1)}, u32[]{:S(2)}) copy-start(bf16[32,128,256]{2,1,0:T(8,128)(2,1)} %shard_map.46) | copy-start | bytes 6291460
  45.2 18.7 %collective-permute-start.2 = (bf16[512,512]{0,1:T(8,128)(2,1)S(1)}, bf16[512,512]{0,1:T(8,128)(2,1)S(1)}, u32[]{:S(2)}, u32[]{:S(2)}) collective-permute-start(bf16[512,512]{0,1:T(8,128)(2,1)S(1)} %fusion.15), channel_id=1, source_target_pairs={{6,0},{7,1},{14,8},{15,9},{22,16},{23,17},{30,24},{31,25},{38,32},... | collective-permute-start | bytes 1572872 | tf_op jit(solution)/shard_map/ppermute | solution.py:62
  46.5 19.9 %collective-permute-start.3 = (bf16[512,512]{0,1:T(8,128)(2,1)S(1)}, bf16[512,512]{0,1:T(8,128)(2,1)S(1)}, u32[]{:S(2)}, u32[]{:S(2)}) collective-permute-start(bf16[512,512]{0,1:T(8,128)(2,1)S(1)} %fusion.15), channel_id=1, source_target_pairs={{0,6},{1,7},{8,14},{9,15},{16,22},{17,23},{24,30},{25,31},{32,38},... | collective-permute-start | bytes 1572872 | tf_op jit(solution)/shard_map/ppermute | solution.py:62
  52.9 31.6 %collective-permute-start.4 = (bf16[512,512]{0,1:T(8,128)(2,1)S(1)}, bf16[512,512]{0,1:T(8,128)(2,1)S(1)}, u32[]{:S(2)}, u32[]{:S(2)}) collective-permute-start(bf16[512,512]{0,1:T(8,128)(2,1)S(1)} %fusion.15), channel_id=1, source_target_pairs={{4,0},{6,2},{5,1},{7,3},{12,8},{14,10},{13,9},{15,11},{20,16},{22,... | collective-permute-start | bytes 1572872 | tf_op jit(solution)/shard_map/ppermute | solution.py:62
  54.2 30.3 %collective-permute-start.5 = (bf16[512,512]{0,1:T(8,128)(2,1)S(1)}, bf16[512,512]{0,1:T(8,128)(2,1)S(1)}, u32[]{:S(2)}, u32[]{:S(2)}) collective-permute-start(bf16[512,512]{0,1:T(8,128)(2,1)S(1)} %fusion.15), channel_id=1, source_target_pairs={{0,4},{2,6},{1,5},{3,7},{8,12},{10,14},{9,13},{11,15},{16,20},{18,... | collective-permute-start | bytes 1572872 | tf_op jit(solution)/shard_map/ppermute | solution.py:62
  59.7 25.7 %collective-permute-start.6 = (bf16[512,512]{0,1:T(8,128)(2,1)S(1)}, bf16[512,512]{0,1:T(8,128)(2,1)S(1)}, u32[]{:S(2)}, u32[]{:S(2)}) collective-permute-start(bf16[512,512]{0,1:T(8,128)(2,1)S(1)} %fusion.15), channel_id=1, source_target_pairs={{2,0},{4,2},{6,4},{3,1},{5,3},{7,5},{10,8},{12,10},{14,12},{11,9},... | collective-permute-start | bytes 1572872 | tf_op jit(solution)/shard_map/ppermute | solution.py:62
  63.8 21.8 %collective-permute-start.7 = (bf16[512,512]{0,1:T(8,128)(2,1)S(1)}, bf16[512,512]{0,1:T(8,128)(2,1)}, u32[]{:S(2)}, u32[]{:S(2)}) collective-permute-start(bf16[512,512]{0,1:T(8,128)(2,1)S(1)} %fusion.15), channel_id=1, source_target_pairs={{0,2},{2,4},{4,6},{1,3},{3,5},{5,7},{8,10},{10,12},{12,14},{9,11},... | collective-permute-start | bytes 1572872 | tf_op jit(solution)/shard_map/ppermute | solution.py:62
  85.8 0.8 copy-start.2
  86.0 0.8 copy-start.4
  86.2 0.8 copy-start.6
  86.4 0.9 copy-start.8
  87.3 99.0 %collective-permute-start.8 = (bf16[512,4,512]{0,2,1:T(8,128)(2,1)S(1)}, bf16[512,4,512]{0,2,1:T(8,128)(2,1)}, u32[]{:S(2)}, u32[]{:S(2)}) collective-permute-start(bf16[512,4,512]{0,2,1:T(8,128)(2,1)S(1)} %pad_maximum_fusion), channel_id=1, source_target_pairs={{0,1},{1,0},{2,3},{3,2},{4,5},{5,4},{6,7},{7,6},{8,9},{9,8},{10,11... | collective-permute-start | bytes 6291464 | tf_op jit(solution)/shard_map/ppermute | solution.py:106
  181.8 2.5 %copy-start.5 = (bf16[512,512]{0,1:T(8,128)(2,1)S(1)}, bf16[512,512]{0,1:T(8,128)(2,1)}, u32[]{:S(2)}) copy-start(bf16[512,512]{0,1:T(8,128)(2,1)} %copy-done.4) | copy-start | bytes 1572868
  184.3 1.0 copy-start.7
  184.3 1.5 copy-start.9
  189.3 3.1 %copy-start.3 = (bf16[512,512]{0,1:T(8,128)(2,1)S(1)}, bf16[512,512]{0,1:T(8,128)(2,1)}, u32[]{:S(2)}) copy-start(bf16[512,512]{0,1:T(8,128)(2,1)} %copy-done.2) | copy-start | bytes 1572868
Sparse Core Ops, SparseCore 0:
  10.5 87.2 all-gather.4
  101.0 80.7 all-gather.6

commit v7 on v2

--- a/solution.py
+++ b/solution.py
@@ -80,16 +80,14 @@
     weight_xy = lax.all_gather(pair, ("x", "y"), axis=0, tiled=False)
     weight = jnp.transpose(weight_xy, (1, 0, 2, 3)).reshape(-1, weight_xy.shape[-1])
 
-    tail = projected[tok_rows - span - 2 :]
-    previous = from_behind(tail)
-    joined = jnp.concatenate([previous, projected], axis=0).astype(jnp.float32)
-    featured = (
-        short_filter[0] * joined[2:]
-        + short_filter[1] * joined[1:-1]
-        + short_filter[2] * joined[:-2]
-    )
-    product = (featured[:, 1] * featured[:, 2]).astype(jnp.bfloat16)
-    query = featured[span:, 0]
+    kv_tail = projected[tok_rows - span - 2 :, 1:]
+    q_tail = projected[tok_rows - 2 :, 0][None]
+    received = from_behind(jnp.concatenate([kv_tail, q_tail], axis=0))
+    kv = jnp.concatenate([received[: span + 2], projected[:, 1:]], axis=0).astype(jnp.float32)
+    f_kv = short_filter[0, 1:] * kv[2:] + short_filter[1, 1:] * kv[1:-1] + short_filter[2, 1:] * kv[:-2]
+    product = (f_kv[:, 0] * f_kv[:, 1]).astype(jnp.bfloat16)
+    q = jnp.concatenate([received[span + 2], projected[:, 0]], axis=0).astype(jnp.float32)
+    query = short_filter[0, 0] * q[2:] + short_filter[1, 0] * q[1:-1] + short_filter[2, 0] * q[:-2]
 
     blocks = product.reshape(tok_rows // span + 1, span, groups, channels // groups)
     window = jnp.concatenate([blocks[:-1], blocks[1:]], axis=1)

time: 144 us -> 134 us (0.931)
  waiting for transfers between devices: 64.3 us -> 57.2 us
  other arithmetic: 14.3 us -> 11.3 us
    ppermute x1, waiting for transfers between devices: 14.5 us -> 7.44 us  [from_behind(): return lax.ppermute(array, SEQ, pairs)]
    unnamed x9 -> x7, local copies, waits for them, and re-layouts: 3.62 us -> 1.02 us
    add x1, other arithmetic: 3.29 us -> 0.77 us  [on_device(): short_filter[0, 1:] * kv[2:] + short_filter[1, 1:] * kv[1:-1]]
    slice x5 -> x7, local copies, waits for them, and re-layouts: 3.16 us -> 3.58 us  [on_device(): window = jnp.concatenate([blocks[:-1], blocks[1:]], axis=1)]
where the time goes in v7:
time: 134 us
  waiting for transfers between devices  57.2 us (43%)
  starting transfers between devices  26 us (19%)
  between operations  13.7 us (10%)
  other arithmetic  11.3 us (8%)
  local copies, waits for them, and re-layouts  11 us (8%)
  matrix products  8.56 us (6%)
  Pallas kernels  5.66 us (4%)
    ppermute x6, waiting for transfers between devices, line_gather(): received[d] = lax.ppermute(block, axis_name, pairs)  37.5 us
    ppermute x6, starting transfers between devices, line_gather(): received[d] = lax.ppermute(block, axis_name, pairs)  18 us
    ppermute x1, waiting for transfers between devices, on_device(): partner = lax.ppermute(out_weight, 'zh', [(0, 1), (1, 0)])  8.1 us
    ppermute x1, waiting for transfers between devices, from_behind(): return lax.ppermute(array, SEQ, pairs)  7.44 us
    dot_general x1, matrix products, on_device(): mixed = jnp.dot(gathered, weight, preferred_element_type=jnp.float32)  6.61 us
    pallas_call x1, Pallas kernels, toeplitz_blocks(): pl.pallas_call(toeplitz_kernel, out_shape=jax.ShapeDtypeStruct((groups, s...  5.66 us
    ppermute x1, waiting for transfers between devices, on_device(): other = lax.ppermute(g_zl, 'c', [(0, 1), (1, 0)])  4.1 us
    ppermute x1, starting transfers between devices, from_behind(): return lax.ppermute(array, SEQ, pairs)  3.78 us
  transfers between devices with their start and end apart: 10, of which 6 were waited for; matrix products, arithmetic and copies ran while one was open for 17% of the time, Pallas kernels for 4%

profile of v7, /device:TPU:385, one launch (start us, length us, event | category | flops | bytes accessed | tf_op | source)
XLA Modules:
  0.0 133.5 jit_solution(7167346116999280747)
XLA Ops:
  6.5 1.9 %collective-permute-start.8 = (bf16[64,512]{1,0:T(8,128)(2,1)}, bf16[64,512]{1,0:T(8,128)(2,1)S(1)}, u32[]{:S(2)}, u32[]{:S(2)}) collective-permute-start(bf16[64,512]{1,0:T(8,128)(2,1)} %param.7), channel_id=1, source_target_pairs={{0,256},{256,0},{1,257},{257,1},{2,258},{258,2},{3,259},{259,3},{4... | collective-permute-start | bytes 196616 | tf_op jit(solution)/shard_map/ppermute | solution.py:77
  8.5 8.1 %collective-permute-done.8 = bf16[64,512]{1,0:T(8,128)(2,1)S(1)} collective-permute-done((bf16[64,512]{1,0:T(8,128)(2,1)}, bf16[64,512]{1,0:T(8,128)(2,1)S(1)}, u32[]{:S(2)}, u32[]{:S(2)}) %collective-permute-start.8) | collective-permute-done | bytes 65568 | tf_op jit(solution)/shard_map/ppermute | solution.py:77
  16.6 1.6 %maximum_select_fusion.1 = bf16[1,2,64,512]{3,2,0,1:T(8,128)(2,1)} fusion(bf16[1,1,64,512]{3,2,0,1:T(8,128)(2,1)S(1)} %bitcast.61, bf16[1,1,64,512]{3,2,0,1:T(8,128)(2,1)} %bitcast.60, pred[]{:T(512)S(6)} %eq.119), kind=kLoop, calls=%fused_computation.30 | loop fusion | flops 196608 | bytes 262145 | tf_op jit(solution)/shard_map/jit(_where)/select_n | solution.py:79
  18.1 0.0 all-gather.2.cloned.1.call-update
  18.2 1.0 slice.75
  19.2 0.7 slice_bitcast_fusion.3
  19.9 3.8 %collective-permute-start = (bf16[131,2,512]{2,0,1:T(8,128)(2,1)S(1)}, bf16[131,2,512]{2,0,1:T(8,128)(2,1)S(1)}, u32[]{:S(2)}, u32[]{:S(2)}) collective-permute-start(bf16[131,2,512]{2,0,1:T(8,128)(2,1)S(1)} %pad_maximum_fusion.1), channel_id=1, source_target_pairs={{0,8},{8,16},{16,24},{24,32},{32,40},{40,48},{48,56},{56,64},{64,7... | collective-permute-start | bytes 804872 | tf_op jit(solution)/shard_map/ppermute | solution.py:20
  23.7 0.8 rev.3
  24.5 0.1 pad.14.clone
  24.6 0.7 maximum_maximum_fusion.row_ref
  25.3 0.7 fusion.17
  26.1 5.7 %shard_map.46 = bf16[32,128,256]{2,1,0:T(8,128)(2,1)} custom-call(f32[32,384]{1,0:T(8,128)} %maximum_maximum_fusion.row_ref), custom_call_target="tpu_custom_call" | custom-call | tf_op jit(solution)/shard_map/pallas_call | solution.py:48
  31.7 1.0 copy.17
  32.7 7.4 %collective-permute-done = bf16[131,2,512]{2,0,1:T(8,128)(2,1)S(1)} collective-permute-done((bf16[131,2,512]{2,0,1:T(8,128)(2,1)S(1)}, bf16[131,2,512]{2,0,1:T(8,128)(2,1)S(1)}, u32[]{:S(2)}, u32[]{:S(2)}) %collective-permute-start) | collective-permute-done | bytes 268320 | tf_op jit(solution)/shard_map/ppermute | solution.py:20
  40.2 0.4 maximum_convert_fusion
  40.6 0.8 fusion
  41.3 0.2 fusion.7
  41.6 0.9 fusion.16
  42.4 0.2 copy.9
  42.7 0.1 slice.95
  42.8 0.9 copy.11
  43.7 1.3 copy.10
  44.9 0.1 slice.97
  45.1 0.1 copy.12
  45.2 2.0 %fusion.4 = f32[4,128,32,16]{1,3,0,2:T(8,128)S(1)} fusion(bf16[32,128,256]{2,1,0:T(8,128)(2,1)S(1)} %copy-done, bf16[4,128,32,16]{1,3,0,2:T(8,128)(2,1)S(1)} %copy.12, bf16[4,128,32,16]{1,3,0,2:T(8,128)(2,1)} %copy.11), kind=kOutput, calls=%fused_computation.9 | convolution fusion | flops 136314880 | bytes 4194304 | tf_op jit(solution)/shard_map/gij,bjgc->bigc/dot_general | solution.py:95
  47.1 0.4 copy.13
  47.6 0.2 copy.16
  47.8 0.3 maximum_convert_fusion.1
  48.1 0.9 fusion.8
  49.0 0.7 collective-permute-start.1
  49.7 0.7 collective-permute-start.2
  50.4 10.0 %collective-permute-start.3 = (bf16[512,512]{0,1:T(8,128)(2,1)S(1)}, bf16[512,512]{0,1:T(8,128)(2,1)S(1)}, u32[]{:S(2)}, u32[]{:S(2)}) collective-permute-start(bf16[512,512]{0,1:T(8,128)(2,1)S(1)} %fusion.8), channel_id=1, source_target_pairs={{4,0},{6,2},{5,1},{7,3},{12,8},{14,10},{13,9},{15,11},{20,16},{22,... | collective-permute-start | bytes 1572872 | tf_op jit(solution)/shard_map/ppermute | solution.py:62
  60.4 1.3 collective-permute-start.4
  61.7 1.9 %collective-permute-start.5 = (bf16[512,512]{0,1:T(8,128)(2,1)S(1)}, bf16[512,512]{0,1:T(8,128)(2,1)S(1)}, u32[]{:S(2)}, u32[]{:S(2)}) collective-permute-start(bf16[512,512]{0,1:T(8,128)(2,1)S(1)} %fusion.8), channel_id=1, source_target_pairs={{2,0},{4,2},{6,4},{3,1},{5,3},{7,5},{10,8},{12,10},{14,12},{11,9},... | collective-permute-start | bytes 1572872 | tf_op jit(solution)/shard_map/ppermute | solution.py:62
  63.6 3.4 %collective-permute-start.6 = (bf16[512,512]{0,1:T(8,128)(2,1)S(1)}, bf16[512,512]{0,1:T(8,128)(2,1)}, u32[]{:S(2)}, u32[]{:S(2)}) collective-permute-start(bf16[512,512]{0,1:T(8,128)(2,1)S(1)} %fusion.8), channel_id=1, source_target_pairs={{0,2},{2,4},{4,6},{1,3},{3,5},{5,7},{8,10},{10,12},{12,14},{9,11},... | collective-permute-start | bytes 1572872 | tf_op jit(solution)/shard_map/ppermute | solution.py:62
  67.1 21.1 %collective-permute-done.3 = bf16[512,512]{0,1:T(8,128)(2,1)S(1)} collective-permute-done((bf16[512,512]{0,1:T(8,128)(2,1)S(1)}, bf16[512,512]{0,1:T(8,128)(2,1)S(1)}, u32[]{:S(2)}, u32[]{:S(2)}) %collective-permute-start.3) | collective-permute-done | bytes 524320 | tf_op jit(solution)/shard_map/ppermute | solution.py:62
  88.3 11.2 %collective-permute-done.5 = bf16[512,512]{0,1:T(8,128)(2,1)S(1)} collective-permute-done((bf16[512,512]{0,1:T(8,128)(2,1)S(1)}, bf16[512,512]{0,1:T(8,128)(2,1)S(1)}, u32[]{:S(2)}, u32[]{:S(2)}) %collective-permute-start.5) | collective-permute-done | bytes 524320 | tf_op jit(solution)/shard_map/ppermute | solution.py:62
  99.5 5.2 %collective-permute-done.6 = bf16[512,512]{0,1:T(8,128)(2,1)} collective-permute-done((bf16[512,512]{0,1:T(8,128)(2,1)S(1)}, bf16[512,512]{0,1:T(8,128)(2,1)}, u32[]{:S(2)}, u32[]{:S(2)}) %collective-permute-start.6) | collective-permute-done | bytes 524320 | tf_op jit(solution)/shard_map/ppermute | solution.py:62
  104.6 0.2 select_bitcast_fusion.3
  104.8 1.2 select_bitcast_fusion.2
  106.0 0.2 select_bitcast_fusion.1
  106.2 0.2 select_bitcast_fusion
  106.4 1.7 %fusion.15 = (bf16[512,4,1,512]{0,3,1,2:T(8,128)(2,1)S(1)}, bf16[512,4,512]{0,2,1:T(8,128)(2,1)}) fusion(bf16[512,1,512]{0,2,1:T(8,128)(2,1)S(1)} %select_bitcast_fusion, bf16[512,1,512]{0,2,1:T(8,128)(2,1)S(1)} %select_bitcast_fusion.1, bf16[512,1,512]{0,2,1:T(8,128)(2,1)S(1)} %select_bitcast_fusion.2, bf16[512,1,512]{0,2,1:T(8,128)(2,1)S(1)} %select_bitcast_fusion.3), kind=kLoop, calls=%fused_computation.37 | loop fusion | flops 3145728 | bytes 6291456 | tf_op jit(solution)/shard_map/stack | solution.py:103
  108.1 2.4 %collective-permute-start.7 = (bf16[512,4,512]{0,2,1:T(8,128)(2,1)}, bf16[512,4,512]{0,2,1:T(8,128)(2,1)}, u32[]{:S(2)}, u32[]{:S(2)}) collective-permute-start(bf16[512,4,512]{0,2,1:T(8,128)(2,1)} %get-tuple-element.6), channel_id=1, source_target_pairs={{0,1},{1,0},{2,3},{3,2},{4,5},{5,4},{6,7},{7,6},{8,9},{9,8},{10,11... | collective-permute-start | bytes 6291464 | tf_op jit(solution)/shard_map/ppermute | solution.py:101
  110.5 4.1 %collective-permute-done.7 = bf16[512,4,512]{0,2,1:T(8,128)(2,1)} collective-permute-done((bf16[512,4,512]{0,2,1:T(8,128)(2,1)}, bf16[512,4,512]{0,2,1:T(8,128)(2,1)}, u32[]{:S(2)}, u32[]{:S(2)}) %collective-permute-start.7) | collective-permute-done | bytes 2097184 | tf_op jit(solution)/shard_map/ppermute | solution.py:101
  114.6 3.0 %maximum_select_fusion = bf16[512,4,2,512]{0,3,1,2:T(8,128)(2,1)S(1)} fusion(bf16[512,4,1,512]{0,3,1,2:T(8,128)(2,1)} %bitcast.17, bf16[512,4,1,512]{0,3,1,2:T(8,128)(2,1)S(1)} %get-tuple-element.5, pred[]{:T(512)S(6)} %eq.90), kind=kLoop, calls=%fused_computation | loop fusion | flops 6291456 | bytes 8388609 | tf_op jit(solution)/shard_map/jit(_where)/select_n | solution.py:103
  117.6 2.5 %copy.14 = bf16[512,4,2,512]{0,3,2,1:T(8,128)(2,1)} copy(bf16[512,4,2,512]{0,3,1,2:T(8,128)(2,1)S(1)} %maximum_select_fusion) | data formatting | bytes 8388608 | tf_op jit(solution)/shard_map/jit(_where)/select_n | solution.py:103
  120.1 6.6 %convolution_convert_fusion = bf16[512,512]{1,0:T(8,128)(2,1)} fusion(bf16[512,4096]{0,1:T(8,128)(2,1)} %bitcast.56, bf16[4096,512]{1,0:T(8,128)(2,1)} %bitcast.65), kind=kOutput, calls=%fused_computation.13 | convolution fusion | flops 2147745792 | bytes 8912896 | tf_op jit(solution)/shard_map/dot_general | solution.py:106
  (22 shorter events, 0.1 us)
Async XLA Ops:
  6.5 113.5 %all-gather.2.cloned.1.call-start = ((), (), s32[]{:S(2)}) async-start(), calls=%async_computation | async-start | bytes 4325376 | tf_op jit(solution)/shard_map/all_gather | solution.py:80
  6.5 10.0 %collective-permute-start.8 = (bf16[64,512]{1,0:T(8,128)(2,1)}, bf16[64,512]{1,0:T(8,128)(2,1)S(1)}, u32[]{:S(2)}, u32[]{:S(2)}) collective-permute-start(bf16[64,512]{1,0:T(8,128)(2,1)} %param.7), channel_id=1, source_target_pairs={{0,256},{256,0},{1,257},{257,1},{2,258},{258,2},{3,259},{259,3},{4... | collective-permute-start | bytes 196616 | tf_op jit(solution)/shard_map/ppermute | solution.py:77
  19.9 20.2 %collective-permute-start = (bf16[131,2,512]{2,0,1:T(8,128)(2,1)S(1)}, bf16[131,2,512]{2,0,1:T(8,128)(2,1)S(1)}, u32[]{:S(2)}, u32[]{:S(2)}) collective-permute-start(bf16[131,2,512]{2,0,1:T(8,128)(2,1)S(1)} %pad_maximum_fusion.1), channel_id=1, source_target_pairs={{0,8},{8,16},{16,24},{24,32},{32,40},{40,48},{48,56},{56,64},{64,7... | collective-permute-start | bytes 804872 | tf_op jit(solution)/shard_map/ppermute | solution.py:20
  26.0 5.7 %slice-start.1 = ((bf16[512,3,512]{2,0,1:T(8,128)(2,1)}), bf16[512,1,512]{2,0,1:T(8,128)(2,1)S(1)}, s32[]{:S(2)}) async-start(bf16[512,3,512]{2,0,1:T(8,128)(2,1)} %param.4), calls=%async_computation.2 | async-start | bytes 1048576 | tf_op jit(solution)/shard_map/slice | solution.py:89
  26.0 6.7 %copy-start.2 = (f32[3,3,512]{2,1,0:T(4,128)S(1)}, f32[3,3,512]{2,1,0:T(4,128)}, u32[]{:S(2)}) copy-start(f32[3,3,512]{2,1,0:T(4,128)} %param.5) | copy-start | bytes 55300
  26.0 14.1 %slice-start = ((bf16[512,3,512]{2,0,1:T(8,128)(2,1)}), bf16[512,2,512]{2,0,1:T(8,128)(2,1)S(1)}, s32[]{:S(2)}) async-start(bf16[512,3,512]{2,0,1:T(8,128)(2,1)} %param.4), calls=%async_computation.1 | async-start | bytes 2097152 | tf_op jit(solution)/shard_map/slice | solution.py:86
  42.6 2.5 %copy-start = (bf16[32,128,256]{2,1,0:T(8,128)(2,1)S(1)}, bf16[32,128,256]{2,1,0:T(8,128)(2,1)}, u32[]{:S(2)}) copy-start(bf16[32,128,256]{2,1,0:T(8,128)(2,1)} %shard_map.46) | copy-start | bytes 6291460
  45.2 2.6 %copy-start.1 = (bf16[512,1,512]{0,2,1:T(8,128)(2,1)S(1)}, bf16[512,1,512]{0,2,1:T(8,128)(2,1)}, u32[]{:S(2)}) copy-start(bf16[512,1,512]{0,2,1:T(8,128)(2,1)} %copy.17) | copy-start | bytes 1572868
  49.0 14.6 %collective-permute-start.1 = (bf16[512,512]{0,1:T(8,128)(2,1)S(1)}, bf16[512,512]{0,1:T(8,128)(2,1)S(1)}, u32[]{:S(2)}, u32[]{:S(2)}) collective-permute-start(bf16[512,512]{0,1:T(8,128)(2,1)S(1)} %fusion.8), channel_id=1, source_target_pairs={{6,0},{7,1},{14,8},{15,9},{22,16},{23,17},{30,24},{31,25},{38,32},... | collective-permute-start | bytes 1572872 | tf_op jit(solution)/shard_map/ppermute | solution.py:62
  49.7 17.4 %collective-permute-start.2 = (bf16[512,512]{0,1:T(8,128)(2,1)S(1)}, bf16[512,512]{0,1:T(8,128)(2,1)S(1)}, u32[]{:S(2)}, u32[]{:S(2)}) collective-permute-start(bf16[512,512]{0,1:T(8,128)(2,1)S(1)} %fusion.8), channel_id=1, source_target_pairs={{0,6},{1,7},{8,14},{9,15},{16,22},{17,23},{24,30},{25,31},{32,38},... | collective-permute-start | bytes 1572872 | tf_op jit(solution)/shard_map/ppermute | solution.py:62
  50.4 37.8 %collective-permute-start.3 = (bf16[512,512]{0,1:T(8,128)(2,1)S(1)}, bf16[512,512]{0,1:T(8,128)(2,1)S(1)}, u32[]{:S(2)}, u32[]{:S(2)}) collective-permute-start(bf16[512,512]{0,1:T(8,128)(2,1)S(1)} %fusion.8), channel_id=1, source_target_pairs={{4,0},{6,2},{5,1},{7,3},{12,8},{14,10},{13,9},{15,11},{20,16},{22,... | collective-permute-start | bytes 1572872 | tf_op jit(solution)/shard_map/ppermute | solution.py:62
  60.4 27.9 %collective-permute-start.4 = (bf16[512,512]{0,1:T(8,128)(2,1)S(1)}, bf16[512,512]{0,1:T(8,128)(2,1)S(1)}, u32[]{:S(2)}, u32[]{:S(2)}) collective-permute-start(bf16[512,512]{0,1:T(8,128)(2,1)S(1)} %fusion.8), channel_id=1, source_target_pairs={{0,4},{2,6},{1,5},{3,7},{8,12},{10,14},{9,13},{11,15},{16,20},{18,... | collective-permute-start | bytes 1572872 | tf_op jit(solution)/shard_map/ppermute | solution.py:62
  61.7 37.8 %collective-permute-start.5 = (bf16[512,512]{0,1:T(8,128)(2,1)S(1)}, bf16[512,512]{0,1:T(8,128)(2,1)S(1)}, u32[]{:S(2)}, u32[]{:S(2)}) collective-permute-start(bf16[512,512]{0,1:T(8,128)(2,1)S(1)} %fusion.8), channel_id=1, source_target_pairs={{2,0},{4,2},{6,4},{3,1},{5,3},{7,5},{10,8},{12,10},{14,12},{11,9},... | collective-permute-start | bytes 1572872 | tf_op jit(solution)/shard_map/ppermute | solution.py:62
  63.6 41.0 %collective-permute-start.6 = (bf16[512,512]{0,1:T(8,128)(2,1)S(1)}, bf16[512,512]{0,1:T(8,128)(2,1)}, u32[]{:S(2)}, u32[]{:S(2)}) collective-permute-start(bf16[512,512]{0,1:T(8,128)(2,1)S(1)} %fusion.8), channel_id=1, source_target_pairs={{0,2},{2,4},{4,6},{1,3},{3,5},{5,7},{8,10},{10,12},{12,14},{9,11},... | collective-permute-start | bytes 1572872 | tf_op jit(solution)/shard_map/ppermute | solution.py:62
  108.1 6.5 %collective-permute-start.7 = (bf16[512,4,512]{0,2,1:T(8,128)(2,1)}, bf16[512,4,512]{0,2,1:T(8,128)(2,1)}, u32[]{:S(2)}, u32[]{:S(2)}) collective-permute-start(bf16[512,4,512]{0,2,1:T(8,128)(2,1)} %get-tuple-element.6), channel_id=1, source_target_pairs={{0,1},{1,0},{2,3},{3,2},{4,5},{5,4},{6,7},{7,6},{8,9},{9,8},{10,11... | collective-permute-start | bytes 6291464 | tf_op jit(solution)/shard_map/ppermute | solution.py:101
Sparse Core Ops, SparseCore 0:
  18.3 86.1 all-gather.1

commit v8 on v7

--- a/solution.py
+++ b/solution.py
@@ -51,22 +51,77 @@
     )(row)
 
 
-def line_gather(block, axis_name, size):
-    pieces = [None] * size
+def line_slots(block, axis_name, size):
     index = lax.axis_index(axis_name)
     received = {}
     for offset in range(1, size):
-        for sign in (1, -1):
-            d = sign * offset
+        for d in (offset, -offset):
             pairs = [(i, i + d) for i in range(size) if 0 <= i + d < size]
             received[d] = lax.ppermute(block, axis_name, pairs)
-    parts = []
-    for source in range(size):
-        choice = jnp.zeros_like(block)
-        for d, value in received.items():
-            choice = jnp.where(index - d == source, value, choice)
-        parts.append(jnp.where(index == source, block, choice))
-    return jnp.stack(parts, axis=1)
+    slots = [block]
+    for k in range(1, size):
+        slots.append(jnp.where(index + k < size, received[-k], received[size - k]))
+    return jnp.stack(slots)
+
+
+def partial_kernel(table_ref, piece_ref, weight_ref, out_ref, acc_ref):
+    k = pl.program_id(0)
+
+    @pl.when(k == 0)
+    def _():
+        acc_ref[...] = jnp.zeros_like(acc_ref)
+
+    rows = weight_ref[0, :, 0]
+    rows = rows.reshape(-1, rows.shape[-1])
+    acc_ref[...] += jnp.dot(piece_ref[0], rows, preferred_element_type=jnp.float32)
+
+    @pl.when(k == pl.num_programs(0) - 1)
+    def _():
+        out_ref[...] = acc_ref[...]
+
+
+def final_kernel(table_ref, piece_ref, weight_ref, carry_ref, out_ref, acc_ref):
+    k = pl.program_id(0)
+
+    @pl.when(k == 0)
+    def _():
+        acc_ref[...] = carry_ref[...]
+
+    rows = weight_ref[0, :, 0]
+    rows = rows.reshape(-1, rows.shape[-1])
+    acc_ref[...] += jnp.dot(piece_ref[0], rows, preferred_element_type=jnp.float32)
+
+    @pl.when(k == pl.num_programs(0) - 1)
+    def _():
+        out_ref[...] = acc_ref[...].astype(out_ref.dtype)
+
+
+def block_matmul(table, pieces, weight, carry=None):
+    n, tok, width = pieces.shape
+    _, ys, _, rows, cols = weight.shape
+    in_specs = [
+        pl.BlockSpec((1, tok, width), lambda k, t: (k, 0, 0)),
+        pl.BlockSpec((1, ys, 1, rows, cols), lambda k, t: (t[0, k], 0, t[1, k], 0, 0)),
+    ]
+    args = [table, pieces, weight]
+    if carry is None:
+        kernel, out_dtype = partial_kernel, jnp.float32
+    else:
+        kernel, out_dtype = final_kernel, jnp.bfloat16
+        in_specs.append(pl.BlockSpec((tok, cols), lambda k, t: (0, 0)))
+        args.append(carry)
+    grid_spec = pltpu.PrefetchScalarGridSpec(
+        num_scalar_prefetch=1,
+        grid=(n,),
+        in_specs=in_specs,
+        out_specs=pl.BlockSpec((tok, cols), lambda k, t: (0, 0)),
+        scratch_shapes=[pltpu.VMEM((tok, cols), jnp.float32)],
+    )
+    return pl.pallas_call(
+        kernel,
+        grid_spec=grid_spec,
+        out_shape=jax.ShapeDtypeStruct((tok, cols), out_dtype),
+    )(*args)
 
 
 def on_device(projected, short_filter, long_filter, out_weight):
@@ -78,7 +133,6 @@
     zh = lax.axis_index("zh")
     pair = jnp.where(zh == 0, jnp.stack([out_weight, partner]), jnp.stack([partner, out_weight]))
     weight_xy = lax.all_gather(pair, ("x", "y"), axis=0, tiled=False)
-    weight = jnp.transpose(weight_xy, (1, 0, 2, 3)).reshape(-1, weight_xy.shape[-1])
 
     kv_tail = projected[tok_rows - span - 2 :, 1:]
     q_tail = projected[tok_rows - 2 :, 0][None]
@@ -97,14 +151,19 @@
     ).reshape(tok_rows, channels)
     gated = (query * filtered).astype(jnp.bfloat16)
 
-    g_zl = line_gather(gated, "zl", 4)
-    other = lax.ppermute(g_zl, "c", [(0, 1), (1, 0)])
+    own = line_slots(gated, "zl", 4)
+    other = lax.ppermute(own, "c", [(0, 1), (1, 0)])
+    zl = lax.axis_index("zl")
     core = lax.axis_index("c")
-    g_all = jnp.where(core == 0, jnp.stack([g_zl, other], axis=2), jnp.stack([other, g_zl], axis=2))
-    gathered = g_all.reshape(tok_rows, -1)
+    sources = (zl + jnp.arange(4, dtype=jnp.int32)) % 4
 
-    mixed = jnp.dot(gathered, weight, preferred_element_type=jnp.float32)
-    return mixed.astype(jnp.bfloat16)
+    def table_for(c):
+        w = 2 * sources + c
+        return jnp.stack([w % 4, w // 4]).astype(jnp.int32)
+
+    weight = weight_xy.reshape(4, 8, *weight_xy.shape[1:])
+    carry = block_matmul(table_for(core), own, weight)
+    return block_matmul(table_for(1 - core), other, weight, carry)
 
 
 def solution(mesh):

time: 134 us -> 131 us (0.978)
  the two profiles are of different devices: /device:TPU:385 before, /device:TPU:8 now
where the time goes in v8:
time: 131 us; the launch traced here: 130 us
  waiting for transfers between devices  43.3 us (33%)
  starting transfers between devices  37.7 us (29%)
  Pallas kernels  17.3 us (13%)
  between operations  13.7 us (10%)
  local copies, waits for them, and re-layouts  9.34 us (7%)
  other arithmetic  6.84 us (5%)
  matrix products  1.88 us (1%)
    ppermute x6, waiting for transfers between devices, line_slots(): received[d] = lax.ppermute(block, axis_name, pairs)  28.6 us
    ppermute x6, starting transfers between devices, line_slots(): received[d] = lax.ppermute(block, axis_name, pairs)  21.3 us
    pallas_call x2, Pallas kernels, block_matmul(): pl.pallas_call(kernel, grid_spec=grid_spec, out_shape=jax.ShapeDtypeStruc...  11.6 us
    all_gather x1, waiting for transfers between devices, on_device(): weight_xy = lax.all_gather(pair, ('x', 'y'), axis=0, tiled=False)  11.3 us
    ppermute x1, starting transfers between devices, on_device(): partner = lax.ppermute(out_weight, 'zh', [(0, 1), (1, 0)])  11 us
    pallas_call x1, Pallas kernels, toeplitz_blocks(): pl.pallas_call(toeplitz_kernel, out_shape=jax.ShapeDtypeStruct((groups, s...  5.7 us
    slice x7, local copies, waits for them, and re-layouts, on_device(): window = jnp.concatenate([blocks[:-1], blocks[1:]], axis=1)  5.42 us
    ppermute x1, starting transfers between devices, from_behind(): return lax.ppermute(array, SEQ, pairs)  3.47 us
  transfers between devices with their start and end apart: 10, of which 3 were waited for; matrix products, arithmetic and copies ran while one was open for 13% of the time, Pallas kernels for 9%

profile of v8, /device:TPU:8, one launch (start us, length us, event | category | flops | bytes accessed | tf_op | source)
XLA Modules:
  0.0 130.1 jit_solution(15608290003196365411)
XLA Ops:
  6.5 11.0 %collective-permute-start.8 = (bf16[64,512]{1,0:T(8,128)(2,1)}, bf16[64,512]{1,0:T(8,128)(2,1)S(1)}, u32[]{:S(2)}, u32[]{:S(2)}) collective-permute-start(bf16[64,512]{1,0:T(8,128)(2,1)} %param.7), channel_id=1, source_target_pairs={{0,256},{256,0},{1,257},{257,1},{2,258},{258,2},{3,259},{259,3},{4... | collective-permute-start | bytes 196616 | tf_op jit(solution)/shard_map/ppermute | solution.py:132
  17.6 3.4 %collective-permute-done.8 = bf16[64,512]{1,0:T(8,128)(2,1)S(1)} collective-permute-done((bf16[64,512]{1,0:T(8,128)(2,1)}, bf16[64,512]{1,0:T(8,128)(2,1)S(1)}, u32[]{:S(2)}, u32[]{:S(2)}) %collective-permute-start.8) | collective-permute-done | bytes 65568 | tf_op jit(solution)/shard_map/ppermute | solution.py:132
  20.9 1.6 %maximum_select_fusion = bf16[1,2,64,512]{3,2,1,0:T(8,128)(2,1)} fusion(bf16[1,1,64,512]{3,2,1,0:T(8,128)(2,1)S(1)} %bitcast.52, bf16[1,1,64,512]{3,2,1,0:T(8,128)(2,1)} %bitcast.51, pred[]{:T(512)S(6)} %eq.7), kind=kLoop, calls=%fused_computation.29 | loop fusion | flops 196608 | bytes 262145 | tf_op jit(solution)/shard_map/jit(_where)/select_n | solution.py:134
  22.5 0.0 all-gather.2.cloned.1.call-update
  22.5 1.0 slice.75
  23.6 0.2 copy.25
  23.8 0.7 slice_bitcast_fusion.5
  24.5 1.1 pad_maximum_fusion.1
  25.6 3.5 %collective-permute-start = (bf16[131,2,512]{2,1,0:T(2,128)(2,1)}, bf16[131,2,512]{2,1,0:T(2,128)(2,1)S(1)}, u32[]{:S(2)}, u32[]{:S(2)}) collective-permute-start(bf16[131,2,512]{2,1,0:T(2,128)(2,1)} %pad_maximum_fusion.1), channel_id=1, source_target_pairs={{0,8},{8,16},{16,24},{24,32},{32,40},{40,48},{48,56},{56,64},{64,7... | collective-permute-start | bytes 804872 | tf_op jit(solution)/shard_map/ppermute | solution.py:20
  29.0 0.8 rev.3
  29.8 0.1 pad.12.clone
  29.9 0.7 maximum_maximum_fusion.row_ref
  30.6 5.7 %shard_map.46 = bf16[32,128,256]{2,1,0:T(8,128)(2,1)} custom-call(f32[32,384]{1,0:T(8,128)} %maximum_maximum_fusion.row_ref), custom_call_target="tpu_custom_call" | custom-call | tf_op jit(solution)/shard_map/pallas_call | solution.py:48
  36.4 0.0 collective-permute-done
  36.4 0.2 slice.102
  36.6 0.4 maximum_convert_fusion
  37.0 0.8 fusion
  37.8 0.2 fusion.7
  38.0 0.9 fusion.18
  38.9 0.2 copy.18
  39.1 0.1 slice.95
  39.2 0.9 copy.20
  40.1 1.3 copy.19
  41.4 0.9 slice.97
  42.3 1.1 copy.21
  43.5 1.9 %fusion.4 = f32[4,128,32,16]{1,3,0,2:T(8,128)S(1)} fusion(bf16[32,128,256]{2,1,0:T(8,128)(2,1)S(1)} %copy-done, bf16[4,128,32,16]{1,3,0,2:T(8,128)(2,1)S(1)} %copy.21, bf16[4,128,32,16]{1,3,0,2:T(8,128)(2,1)} %copy.20), kind=kOutput, calls=%fused_computation.8 | convolution fusion | flops 136314880 | bytes 4194304 | tf_op jit(solution)/shard_map/gij,bjgc->bigc/dot_general | solution.py:149
  45.3 0.4 copy.22
  45.8 0.1 copy.28
  45.9 0.3 copy.23
  46.2 0.2 maximum_convert_fusion.1
  46.4 0.4 fusion.10
  46.7 1.3 collective-permute-start.1
  48.0 6.8 %collective-permute-start.2 = (bf16[512,512]{1,0:T(8,128)(2,1)S(1)}, bf16[512,512]{1,0:T(8,128)(2,1)S(1)}, u32[]{:S(2)}, u32[]{:S(2)}) collective-permute-start(bf16[512,512]{1,0:T(8,128)(2,1)S(1)} %fusion.10), channel_id=1, source_target_pairs={{0,6},{1,7},{8,14},{9,15},{16,22},{17,23},{24,30},{25,31},{32,38},... | collective-permute-start | bytes 1572872 | tf_op jit(solution)/shard_map/ppermute | solution.py:60
  54.9 1.3 collective-permute-start.3
  56.2 5.5 %collective-permute-start.4 = (bf16[512,512]{1,0:T(8,128)(2,1)S(1)}, bf16[512,512]{1,0:T(8,128)(2,1)S(1)}, u32[]{:S(2)}, u32[]{:S(2)}) collective-permute-start(bf16[512,512]{1,0:T(8,128)(2,1)S(1)} %fusion.10), channel_id=1, source_target_pairs={{0,4},{2,6},{1,5},{3,7},{8,12},{10,14},{9,13},{11,15},{16,20},{18,... | collective-permute-start | bytes 1572872 | tf_op jit(solution)/shard_map/ppermute | solution.py:60
  61.7 1.3 collective-permute-start.5
  63.0 5.1 %collective-permute-start.6 = (bf16[512,512]{1,0:T(8,128)(2,1)S(1)}, bf16[512,512]{1,0:T(8,128)(2,1)S(1)}, u32[]{:S(2)}, u32[]{:S(2)}) collective-permute-start(bf16[512,512]{1,0:T(8,128)(2,1)S(1)} %fusion.10), channel_id=1, source_target_pairs={{0,2},{2,4},{4,6},{1,3},{3,5},{5,7},{8,10},{10,12},{12,14},{9,11},... | collective-permute-start | bytes 1572872 | tf_op jit(solution)/shard_map/ppermute | solution.py:60
  68.1 0.1 select_bitcast_fusion.2
  68.2 28.6 %collective-permute-done.3 = bf16[512,512]{1,0:T(8,128)(2,1)S(1)} collective-permute-done((bf16[512,512]{1,0:T(8,128)(2,1)S(1)}, bf16[512,512]{1,0:T(8,128)(2,1)S(1)}, u32[]{:S(2)}, u32[]{:S(2)}) %collective-permute-start.3) | collective-permute-done | bytes 524320 | tf_op jit(solution)/shard_map/ppermute | solution.py:60
  96.8 0.1 select_bitcast_fusion.1
  96.9 0.1 select_bitcast_fusion
  96.9 0.3 pad_maximum_fusion.piece_ref
  97.2 1.9 %collective-permute-start.7 = (bf16[4,512,512]{2,1,0:T(8,128)(2,1)S(1)}, bf16[4,512,512]{2,1,0:T(8,128)(2,1)}, u32[]{:S(2)}, u32[]{:S(2)}) collective-permute-start(bf16[4,512,512]{2,1,0:T(8,128)(2,1)S(1)} %pad_maximum_fusion.piece_ref), channel_id=1, source_target_pairs={{0,1},{1,0},{2,3},{3,2},{4,5},{5,4},{6,7},{7,6},{8,9},{9,8},{10,11... | collective-permute-start | bytes 6291464 | tf_op jit(solution)/shard_map/ppermute | solution.py:155
  99.2 0.6 pad_add_fusion.1.table_ref
  99.8 0.6 pad_add_fusion.table_ref
  100.4 11.3 %all-gather.2.cloned.1.call-done = bf16[32,2,64,512]{3,2,1,0:T(8,128)(2,1)} async-done(((bf16[1,2,64,512]{3,2,1,0:T(8,128)(2,1)}), bf16[32,2,64,512]{3,2,1,0:T(8,128)(2,1)}) %all-gather.2.cloned.1.call-update) | async-done | bytes 4194320 | tf_op jit(solution)/shard_map/all_gather | solution.py:135
  111.7 5.7 %shard_map.47.carry_ref = f32[512,512]{1,0:T(8,128)} custom-call(s32[2,4]{1,0:T(2,128)} %pad_add_fusion.1.table_ref, bf16[4,512,512]{2,1,0:T(8,128)(2,1)} %copy-done.1, bf16[4,8,2,64,512]{4,3,2,1,0:T(8,128)(2,1)} %bitcast.46), custom_call_target="tpu_custom_call" | custom-call | tf_op jit(solution)/shard_map/pallas_call | solution.py:120
  117.5 5.8 %shard_map.48 = bf16[512,512]{1,0:T(8,128)(2,1)} custom-call(s32[2,4]{1,0:T(2,128)} %pad_add_fusion.table_ref, bf16[4,512,512]{2,1,0:T(8,128)(2,1)} %collective-permute-done.7.piece_ref, bf16[4,8,2,64,512]{4,3,2,1,0:T(8,128)(2,1)} %bitcast.47, f32[512,512]{1,0:T(8,128)} %shard_map.47.carry_ref), custom_call_target="tpu_custom_call" | custom-call | tf_op jit(solution)/shard_map/pallas_call | solution.py:120
  (27 shorter events, 0.2 us)
Async XLA Ops:
  6.5 23.4 %copy-start.3 = (f32[3,3,512]{2,1,0:T(4,128)S(1)}, f32[3,3,512]{2,1,0:T(4,128)}, u32[]{:S(2)}) copy-start(f32[3,3,512]{2,1,0:T(4,128)} %param.5) | copy-start | bytes 55300
  6.5 105.2 %all-gather.2.cloned.1.call-start = ((), (), s32[]{:S(2)}) async-start(), calls=%async_computation | async-start | bytes 4325376 | tf_op jit(solution)/shard_map/all_gather | solution.py:135
  6.5 14.4 %collective-permute-start.8 = (bf16[64,512]{1,0:T(8,128)(2,1)}, bf16[64,512]{1,0:T(8,128)(2,1)S(1)}, u32[]{:S(2)}, u32[]{:S(2)}) collective-permute-start(bf16[64,512]{1,0:T(8,128)(2,1)} %param.7), channel_id=1, source_target_pairs={{0,256},{256,0},{1,257},{257,1},{2,258},{258,2},{3,259},{259,3},{4... | collective-permute-start | bytes 196616 | tf_op jit(solution)/shard_map/ppermute | solution.py:132
  25.6 10.8 %collective-permute-start = (bf16[131,2,512]{2,1,0:T(2,128)(2,1)}, bf16[131,2,512]{2,1,0:T(2,128)(2,1)S(1)}, u32[]{:S(2)}, u32[]{:S(2)}) collective-permute-start(bf16[131,2,512]{2,1,0:T(2,128)(2,1)} %pad_maximum_fusion.1), channel_id=1, source_target_pairs={{0,8},{8,16},{16,24},{24,32},{32,40},{40,48},{48,56},{56,64},{64,7... | collective-permute-start | bytes 804872 | tf_op jit(solution)/shard_map/ppermute | solution.py:20
  30.6 5.7 %copy-start.2 = (bf16[512,3,512]{2,0,1:T(8,128)(2,1)S(1)}, bf16[512,3,512]{2,0,1:T(8,128)(2,1)}, u32[]{:S(2)}) copy-start(bf16[512,3,512]{2,0,1:T(8,128)(2,1)} %param.4) | copy-start | bytes 4718596
  30.6 6.0 %slice-start = ((bf16[512,3,512]{2,0,1:T(8,128)(2,1)}), bf16[512,2,512]{2,0,1:T(8,128)(2,1)S(1)}, s32[]{:S(2)}) async-start(bf16[512,3,512]{2,0,1:T(8,128)(2,1)} %param.4), calls=%async_computation.1 | async-start | bytes 2097152 | tf_op jit(solution)/shard_map/slice | solution.py:140
  39.2 4.2 %copy-start = (bf16[32,128,256]{2,1,0:T(8,128)(2,1)S(1)}, bf16[32,128,256]{2,1,0:T(8,128)(2,1)}, u32[]{:S(2)}) copy-start(bf16[32,128,256]{2,1,0:T(8,128)(2,1)} %shard_map.46) | copy-start | bytes 6291460
  46.7 16.3 %collective-permute-start.1 = (bf16[512,512]{1,0:T(8,128)(2,1)S(1)}, bf16[512,512]{1,0:T(8,128)(2,1)S(1)}, u32[]{:S(2)}, u32[]{:S(2)}) collective-permute-start(bf16[512,512]{1,0:T(8,128)(2,1)S(1)} %fusion.10), channel_id=1, source_target_pairs={{2,0},{4,2},{6,4},{3,1},{5,3},{7,5},{10,8},{12,10},{14,12},{11,9},... | collective-permute-start | bytes 1572872 | tf_op jit(solution)/shard_map/ppermute | solution.py:60
  48.0 20.1 %collective-permute-start.2 = (bf16[512,512]{1,0:T(8,128)(2,1)S(1)}, bf16[512,512]{1,0:T(8,128)(2,1)S(1)}, u32[]{:S(2)}, u32[]{:S(2)}) collective-permute-start(bf16[512,512]{1,0:T(8,128)(2,1)S(1)} %fusion.10), channel_id=1, source_target_pairs={{0,6},{1,7},{8,14},{9,15},{16,22},{17,23},{24,30},{25,31},{32,38},... | collective-permute-start | bytes 1572872 | tf_op jit(solution)/shard_map/ppermute | solution.py:60
  54.9 41.9 %collective-permute-start.3 = (bf16[512,512]{1,0:T(8,128)(2,1)S(1)}, bf16[512,512]{1,0:T(8,128)(2,1)S(1)}, u32[]{:S(2)}, u32[]{:S(2)}) collective-permute-start(bf16[512,512]{1,0:T(8,128)(2,1)S(1)} %fusion.10), channel_id=1, source_target_pairs={{4,0},{6,2},{5,1},{7,3},{12,8},{14,10},{13,9},{15,11},{20,16},{22,... | collective-permute-start | bytes 1572872 | tf_op jit(solution)/shard_map/ppermute | solution.py:60
  56.2 40.6 %collective-permute-start.4 = (bf16[512,512]{1,0:T(8,128)(2,1)S(1)}, bf16[512,512]{1,0:T(8,128)(2,1)S(1)}, u32[]{:S(2)}, u32[]{:S(2)}) collective-permute-start(bf16[512,512]{1,0:T(8,128)(2,1)S(1)} %fusion.10), channel_id=1, source_target_pairs={{0,4},{2,6},{1,5},{3,7},{8,12},{10,14},{9,13},{11,15},{16,20},{18,... | collective-permute-start | bytes 1572872 | tf_op jit(solution)/shard_map/ppermute | solution.py:60
  61.7 35.2 %collective-permute-start.5 = (bf16[512,512]{1,0:T(8,128)(2,1)S(1)}, bf16[512,512]{1,0:T(8,128)(2,1)S(1)}, u32[]{:S(2)}, u32[]{:S(2)}) collective-permute-start(bf16[512,512]{1,0:T(8,128)(2,1)S(1)} %fusion.10), channel_id=1, source_target_pairs={{6,0},{7,1},{14,8},{15,9},{22,16},{23,17},{30,24},{31,25},{38,32},... | collective-permute-start | bytes 1572872 | tf_op jit(solution)/shard_map/ppermute | solution.py:60
  63.0 33.9 %collective-permute-start.6 = (bf16[512,512]{1,0:T(8,128)(2,1)S(1)}, bf16[512,512]{1,0:T(8,128)(2,1)S(1)}, u32[]{:S(2)}, u32[]{:S(2)}) collective-permute-start(bf16[512,512]{1,0:T(8,128)(2,1)S(1)} %fusion.10), channel_id=1, source_target_pairs={{0,2},{2,4},{4,6},{1,3},{3,5},{5,7},{8,10},{10,12},{12,14},{9,11},... | collective-permute-start | bytes 1572872 | tf_op jit(solution)/shard_map/ppermute | solution.py:60
  97.2 14.5 %copy-start.1 = (bf16[4,512,512]{2,1,0:T(8,128)(2,1)}, bf16[4,512,512]{2,1,0:T(8,128)(2,1)S(1)}, u32[]{:S(2)}) copy-start(bf16[4,512,512]{2,1,0:T(8,128)(2,1)S(1)} %pad_maximum_fusion.piece_ref) | copy-start | bytes 6291460
  97.2 20.2 %collective-permute-start.7 = (bf16[4,512,512]{2,1,0:T(8,128)(2,1)S(1)}, bf16[4,512,512]{2,1,0:T(8,128)(2,1)}, u32[]{:S(2)}, u32[]{:S(2)}) collective-permute-start(bf16[4,512,512]{2,1,0:T(8,128)(2,1)S(1)} %pad_maximum_fusion.piece_ref), channel_id=1, source_target_pairs={{0,1},{1,0},{2,3},{3,2},{4,5},{5,4},{6,7},{7,6},{8,9},{9,8},{10,11... | collective-permute-start | bytes 6291464 | tf_op jit(solution)/shard_map/ppermute | solution.py:155
Sparse Core Ops, SparseCore 0:
  22.7 88.9 all-gather.1

commit v9 on v8

--- a/solution.py
+++ b/solution.py
@@ -155,15 +155,16 @@
     other = lax.ppermute(own, "c", [(0, 1), (1, 0)])
     zl = lax.axis_index("zl")
     core = lax.axis_index("c")
-    sources = (zl + jnp.arange(4, dtype=jnp.int32)) % 4
-
-    def table_for(c):
-        w = 2 * sources + c
-        return jnp.stack([w % 4, w // 4]).astype(jnp.int32)
-
-    weight = weight_xy.reshape(4, 8, *weight_xy.shape[1:])
-    carry = block_matmul(table_for(core), own, weight)
-    return block_matmul(table_for(1 - core), other, weight, carry)
+    blocks = jnp.concatenate([own, other])
+    order = []
+    for w in range(8):
+        slot = (w // 2 - zl) % 4
+        order.append(jnp.where(w % 2 == core, slot, 4 + slot))
+    by_w = jnp.take(blocks, jnp.stack(order), axis=0, mode="clip")
+    g5 = by_w.reshape(2, 4, tok_rows, 8, -1)
+    w5 = weight_xy.reshape(4, 8, 2, g5.shape[-1], -1)
+    mixed = jnp.einsum("zxtyr,xyzro->to", g5, w5, preferred_element_type=jnp.float32)
+    return mixed.astype(jnp.bfloat16)
 
 
 def solution(mesh):

time: 131 us -> 133 us (1.015)
  the two profiles are of different devices: /device:TPU:8 before, /device:TPU:385 now
where the time goes in v9:
time: 133 us; the launch traced here: 132 us
  waiting for transfers between devices  48.8 us (37%)
  starting transfers between devices  30.1 us (23%)
  local copies, waits for them, and re-layouts  16.7 us (13%)
  between operations  13.7 us (10%)
  other arithmetic  8.85 us (7%)
  matrix products  8.55 us (6%)
  Pallas kernels  5.67 us (4%)
    ppermute x6, waiting for transfers between devices, line_slots(): received[d] = lax.ppermute(block, axis_name, pairs)  29.5 us
    ppermute x6, starting transfers between devices, line_slots(): received[d] = lax.ppermute(block, axis_name, pairs)  18.7 us
    ppermute x1, waiting for transfers between devices, on_device(): partner = lax.ppermute(out_weight, 'zh', [(0, 1), (1, 0)])  8.1 us
    ppermute x1, waiting for transfers between devices, from_behind(): return lax.ppermute(array, SEQ, pairs)  7.43 us
    dot_general x1, matrix products, on_device(): jnp.einsum('zxtyr,xyzro->to', g5, w5, preferred_element_type=jnp.float32)  6.61 us
    ppermute x1, starting transfers between devices, on_device(): other = lax.ppermute(own, 'c', [(0, 1), (1, 0)])  5.75 us
    pallas_call x1, Pallas kernels, toeplitz_blocks(): pl.pallas_call(toeplitz_kernel, out_shape=jax.ShapeDtypeStruct((groups, s...  5.67 us
    gather x1, local copies, waits for them, and re-layouts, on_device(): by_w = jnp.take(blocks, jnp.stack(order), axis=0, mode='clip')  5.01 us
  transfers between devices with their start and end apart: 10, of which 5 were waited for; matrix products, arithmetic and copies ran while one was open for 20% of the time, Pallas kernels for 4%

profile of v9, /device:TPU:385, one launch (start us, length us, event | category | flops | bytes accessed | tf_op | source)
XLA Modules:
  0.0 132.4 jit_solution(5321475935048185762)
XLA Ops:
  6.5 1.9 %collective-permute-start.8 = (bf16[64,512]{1,0:T(8,128)(2,1)}, bf16[64,512]{1,0:T(8,128)(2,1)S(1)}, u32[]{:S(2)}, u32[]{:S(2)}) collective-permute-start(bf16[64,512]{1,0:T(8,128)(2,1)} %param.7), channel_id=1, source_target_pairs={{0,256},{256,0},{1,257},{257,1},{2,258},{258,2},{3,259},{259,3},{4... | collective-permute-start | bytes 196616 | tf_op jit(solution)/shard_map/ppermute | solution.py:132
  8.5 8.1 %collective-permute-done.8 = bf16[64,512]{1,0:T(8,128)(2,1)S(1)} collective-permute-done((bf16[64,512]{1,0:T(8,128)(2,1)}, bf16[64,512]{1,0:T(8,128)(2,1)S(1)}, u32[]{:S(2)}, u32[]{:S(2)}) %collective-permute-start.8) | collective-permute-done | bytes 65568 | tf_op jit(solution)/shard_map/ppermute | solution.py:132
  16.6 1.6 %maximum_select_fusion = bf16[1,2,64,512]{3,2,1,0:T(8,128)(2,1)} fusion(bf16[1,1,64,512]{3,2,1,0:T(8,128)(2,1)S(1)} %bitcast.74, bf16[1,1,64,512]{3,2,1,0:T(8,128)(2,1)} %bitcast.73, pred[]{:T(512)S(6)} %eq.26), kind=kLoop, calls=%fused_computation.32 | loop fusion | flops 196608 | bytes 262145 | tf_op jit(solution)/shard_map/jit(_where)/select_n | solution.py:134
  18.2 0.0 all-gather.2.cloned.1.call-update
  18.2 1.0 slice.75
  19.2 0.7 slice_bitcast_fusion.3
  20.0 3.8 %collective-permute-start = (bf16[131,2,512]{2,0,1:T(8,128)(2,1)S(1)}, bf16[131,2,512]{2,0,1:T(8,128)(2,1)S(1)}, u32[]{:S(2)}, u32[]{:S(2)}) collective-permute-start(bf16[131,2,512]{2,0,1:T(8,128)(2,1)S(1)} %pad_maximum_fusion.1), channel_id=1, source_target_pairs={{0,8},{8,16},{16,24},{24,32},{32,40},{40,48},{48,56},{56,64},{64,7... | collective-permute-start | bytes 804872 | tf_op jit(solution)/shard_map/ppermute | solution.py:20
  23.7 0.8 rev.3
  24.5 0.1 pad.10.clone
  24.6 0.7 maximum_maximum_fusion.row_ref
  25.3 0.7 fusion.25
  26.1 5.7 %shard_map.46 = bf16[32,128,256]{2,1,0:T(8,128)(2,1)} custom-call(f32[32,384]{1,0:T(8,128)} %maximum_maximum_fusion.row_ref), custom_call_target="tpu_custom_call" | custom-call | tf_op jit(solution)/shard_map/pallas_call | solution.py:48
  31.7 1.0 copy.28
  32.8 7.4 %collective-permute-done = bf16[131,2,512]{2,0,1:T(8,128)(2,1)S(1)} collective-permute-done((bf16[131,2,512]{2,0,1:T(8,128)(2,1)S(1)}, bf16[131,2,512]{2,0,1:T(8,128)(2,1)S(1)}, u32[]{:S(2)}, u32[]{:S(2)}) %collective-permute-start) | collective-permute-done | bytes 268320 | tf_op jit(solution)/shard_map/ppermute | solution.py:20
  40.2 0.4 maximum_convert_fusion
  40.6 0.8 fusion.2
  41.4 0.2 fusion.12
  41.6 0.9 fusion.24
  42.4 0.2 copy.19
  42.7 0.1 slice.95
  42.8 0.9 copy.21
  43.7 1.3 copy.20
  45.0 0.1 slice.97
  45.1 0.1 copy.22
  45.2 1.9 %fusion.6 = f32[4,128,32,16]{1,3,0,2:T(8,128)S(1)} fusion(bf16[32,128,256]{2,1,0:T(8,128)(2,1)S(1)} %copy-done, bf16[4,128,32,16]{1,3,0,2:T(8,128)(2,1)S(1)} %copy.22, bf16[4,128,32,16]{1,3,0,2:T(8,128)(2,1)} %copy.21), kind=kOutput, calls=%fused_computation.11 | convolution fusion | flops 136314880 | bytes 4194304 | tf_op jit(solution)/shard_map/gij,bjgc->bigc/dot_general | solution.py:149
  47.2 0.4 copy.23
  47.6 0.2 copy.27
  47.8 0.3 maximum_convert_fusion.1
  48.1 1.8 %constant_dynamic-update-slice_fusion.4 = (bf16[8,512,512]{1,2,0:T(8,128)(2,1)}, bf16[512,512]{0,1:T(8,128)(2,1)S(1)}) fusion(f32[64,8,4,128]{3,2,1,0:T(4,128)S(1)} %bitcast.68, f32[514,512]{0,1:T(8,128)S(1)} %maximum_convert_fusion.1, f32[512]{0:T(512)S(1)} %bitcast.76, f32[512]{0:T(512)S(1)} %bitcast.77, f32[512]{0:T(512)S(1)} %bitcast.75), kind=kLoop, calls=%fused_computation.38 | loop fusion | flops 1835007 | bytes 5249024
  49.9 1.9 %collective-permute-start.1 = (bf16[512,512]{0,1:T(8,128)(2,1)S(1)}, bf16[512,512]{0,1:T(8,128)(2,1)S(1)}, u32[]{:S(2)}, u32[]{:S(2)}) collective-permute-start(bf16[512,512]{0,1:T(8,128)(2,1)S(1)} %get-tuple-element.12), channel_id=1, source_target_pairs={{2,0},{4,2},{6,4},{3,1},{5,3},{7,5},{10,8},{12,10},{14,12},{11,9},... | collective-permute-start | bytes 1572872 | tf_op jit(solution)/shard_map/ppermute | solution.py:60
  51.8 0.7 collective-permute-start.2
  52.5 6.7 %collective-permute-start.3 = (bf16[512,512]{0,1:T(8,128)(2,1)S(1)}, bf16[512,512]{0,1:T(8,128)(2,1)S(1)}, u32[]{:S(2)}, u32[]{:S(2)}) collective-permute-start(bf16[512,512]{0,1:T(8,128)(2,1)S(1)} %get-tuple-element.12), channel_id=1, source_target_pairs={{4,0},{6,2},{5,1},{7,3},{12,8},{14,10},{13,9},{15,11},{20,16},{22,... | collective-permute-start | bytes 1572872 | tf_op jit(solution)/shard_map/ppermute | solution.py:60
  59.2 1.3 collective-permute-start.4
  60.6 0.7 collective-permute-start.5
  61.3 7.3 %collective-permute-start.6 = (bf16[512,512]{0,1:T(8,128)(2,1)S(1)}, bf16[512,512]{0,1:T(8,128)(2,1)S(1)}, u32[]{:S(2)}, u32[]{:S(2)}) collective-permute-start(bf16[512,512]{0,1:T(8,128)(2,1)S(1)} %get-tuple-element.12), channel_id=1, source_target_pairs={{0,2},{2,4},{4,6},{1,3},{3,5},{5,7},{8,10},{10,12},{12,14},{9,11},... | collective-permute-start | bytes 1572872 | tf_op jit(solution)/shard_map/ppermute | solution.py:60
  68.6 0.0 collective-permute-done.2
  68.6 0.9 constant_dynamic-update-slice_fusion.3
  69.6 23.9 %collective-permute-done.3 = bf16[512,512]{0,1:T(8,128)(2,1)S(1)} collective-permute-done((bf16[512,512]{0,1:T(8,128)(2,1)S(1)}, bf16[512,512]{0,1:T(8,128)(2,1)S(1)}, u32[]{:S(2)}, u32[]{:S(2)}) %collective-permute-start.3) | collective-permute-done | bytes 524320 | tf_op jit(solution)/shard_map/ppermute | solution.py:60
  93.5 0.9 constant_dynamic-update-slice_fusion.2
  94.4 5.6 %collective-permute-done.6 = bf16[512,512]{0,1:T(8,128)(2,1)S(1)} collective-permute-done((bf16[512,512]{0,1:T(8,128)(2,1)S(1)}, bf16[512,512]{0,1:T(8,128)(2,1)S(1)}, u32[]{:S(2)}, u32[]{:S(2)}) %collective-permute-start.6) | collective-permute-done | bytes 524320 | tf_op jit(solution)/shard_map/ppermute | solution.py:60
  100.0 1.0 constant_dynamic-update-slice_fusion.1
  100.9 0.3 pad_maximum_fusion
  101.2 5.7 %collective-permute-start.7 = (bf16[4,512,512]{1,2,0:T(8,128)(2,1)S(1)}, bf16[4,512,512]{1,2,0:T(8,128)(2,1)}, u32[]{:S(2)}, u32[]{:S(2)}) collective-permute-start(bf16[4,512,512]{1,2,0:T(8,128)(2,1)S(1)} %pad_maximum_fusion), channel_id=1, source_target_pairs={{0,1},{1,0},{2,3},{3,2},{4,5},{5,4},{6,7},{7,6},{8,9},{9,8},{10,11... | collective-permute-start | bytes 6291464 | tf_op jit(solution)/shard_map/ppermute | solution.py:155
  107.0 0.1 stack.69
  107.1 3.7 %collective-permute-done.7 = bf16[4,512,512]{1,2,0:T(8,128)(2,1)} collective-permute-done((bf16[4,512,512]{1,2,0:T(8,128)(2,1)S(1)}, bf16[4,512,512]{1,2,0:T(8,128)(2,1)}, u32[]{:S(2)}, u32[]{:S(2)}) %collective-permute-start.7) | collective-permute-done | bytes 2097184 | tf_op jit(solution)/shard_map/ppermute | solution.py:155
  110.9 3.1 %constant_dynamic-update-slice_fusion = bf16[8,512,512]{1,2,0:T(8,128)(2,1)} fusion(bf16[8,512,512]{1,2,0:T(8,128)(2,1)} %get-tuple-element.5, bf16[4,512,512]{1,2,0:T(8,128)(2,1)} %collective-permute-done.7), kind=kLoop, calls=%fused_computation.34 | loop fusion | bytes 4194304 | tf_op jit(solution)/shard_map/concatenate | solution.py:158
  113.9 5.0 %gather_fusion = bf16[8,512,512]{1,2,0:T(8,128)(2,1)} fusion(bf16[8,512,512]{1,2,0:T(8,128)(2,1)} %constant_dynamic-update-slice_fusion, s32[1024]{0:T(1024)S(1)} %pad_clamp_fusion), kind=kCustom, calls=%fused_computation | custom fusion | bytes 8388640 | tf_op jit(solution)/shard_map/jit(_take)/gather | solution.py:163
  118.9 6.6 %fusion.13 = bf16[512,512]{1,0:T(8,128)(2,1)} fusion(bf16[4,8,2,64,512]{4,3,2,1,0:T(8,128)(2,1)} %bitcast.78, bf16[2,4,512,8,64]{2,4,3,1,0:T(8,128)(2,1)} %bitcast.67), kind=kOutput, calls=%fused_computation.16 | convolution fusion | flops 2147745792 | bytes 8912896 | tf_op jit(solution)/shard_map/zxtyr,xyzro->to/dot_general | solution.py:166
  (23 shorter events, 0.1 us)
Async XLA Ops:
  6.5 112.4 %all-gather.2.cloned.1.call-start = ((), (), s32[]{:S(2)}) async-start(), calls=%async_computation | async-start | bytes 4325376 | tf_op jit(solution)/shard_map/all_gather | solution.py:135
  6.5 10.0 %collective-permute-start.8 = (bf16[64,512]{1,0:T(8,128)(2,1)}, bf16[64,512]{1,0:T(8,128)(2,1)S(1)}, u32[]{:S(2)}, u32[]{:S(2)}) collective-permute-start(bf16[64,512]{1,0:T(8,128)(2,1)} %param.7), channel_id=1, source_target_pairs={{0,256},{256,0},{1,257},{257,1},{2,258},{258,2},{3,259},{259,3},{4... | collective-permute-start | bytes 196616 | tf_op jit(solution)/shard_map/ppermute | solution.py:132
  20.0 20.2 %collective-permute-start = (bf16[131,2,512]{2,0,1:T(8,128)(2,1)S(1)}, bf16[131,2,512]{2,0,1:T(8,128)(2,1)S(1)}, u32[]{:S(2)}, u32[]{:S(2)}) collective-permute-start(bf16[131,2,512]{2,0,1:T(8,128)(2,1)S(1)} %pad_maximum_fusion.1), channel_id=1, source_target_pairs={{0,8},{8,16},{16,24},{24,32},{32,40},{40,48},{48,56},{56,64},{64,7... | collective-permute-start | bytes 804872 | tf_op jit(solution)/shard_map/ppermute | solution.py:20
  26.0 5.7 %slice-start.1 = ((bf16[512,3,512]{2,0,1:T(8,128)(2,1)}), bf16[512,1,512]{2,0,1:T(8,128)(2,1)S(1)}, s32[]{:S(2)}) async-start(bf16[512,3,512]{2,0,1:T(8,128)(2,1)} %param.4), calls=%async_computation.2 | async-start | bytes 1048576 | tf_op jit(solution)/shard_map/slice | solution.py:143
  26.0 6.7 %copy-start.2 = (f32[3,3,512]{2,1,0:T(4,128)S(1)}, f32[3,3,512]{2,1,0:T(4,128)}, u32[]{:S(2)}) copy-start(f32[3,3,512]{2,1,0:T(4,128)} %param.5) | copy-start | bytes 55300
  26.1 14.1 %slice-start = ((bf16[512,3,512]{2,0,1:T(8,128)(2,1)}), bf16[512,2,512]{2,0,1:T(8,128)(2,1)S(1)}, s32[]{:S(2)}) async-start(bf16[512,3,512]{2,0,1:T(8,128)(2,1)} %param.4), calls=%async_computation.1 | async-start | bytes 2097152 | tf_op jit(solution)/shard_map/slice | solution.py:140
  42.7 2.5 %copy-start = (bf16[32,128,256]{2,1,0:T(8,128)(2,1)S(1)}, bf16[32,128,256]{2,1,0:T(8,128)(2,1)}, u32[]{:S(2)}) copy-start(bf16[32,128,256]{2,1,0:T(8,128)(2,1)} %shard_map.46) | copy-start | bytes 6291460
  45.2 2.6 %copy-start.1 = (bf16[512,1,512]{0,2,1:T(8,128)(2,1)S(1)}, bf16[512,1,512]{0,2,1:T(8,128)(2,1)}, u32[]{:S(2)}) copy-start(bf16[512,1,512]{0,2,1:T(8,128)(2,1)} %copy.28) | copy-start | bytes 1572868
  49.9 11.4 %collective-permute-start.1 = (bf16[512,512]{0,1:T(8,128)(2,1)S(1)}, bf16[512,512]{0,1:T(8,128)(2,1)S(1)}, u32[]{:S(2)}, u32[]{:S(2)}) collective-permute-start(bf16[512,512]{0,1:T(8,128)(2,1)S(1)} %get-tuple-element.12), channel_id=1, source_target_pairs={{2,0},{4,2},{6,4},{3,1},{5,3},{7,5},{10,8},{12,10},{14,12},{11,9},... | collective-permute-start | bytes 1572872 | tf_op jit(solution)/shard_map/ppermute | solution.py:60
  51.8 16.8 %collective-permute-start.2 = (bf16[512,512]{0,1:T(8,128)(2,1)S(1)}, bf16[512,512]{0,1:T(8,128)(2,1)S(1)}, u32[]{:S(2)}, u32[]{:S(2)}) collective-permute-start(bf16[512,512]{0,1:T(8,128)(2,1)S(1)} %get-tuple-element.12), channel_id=1, source_target_pairs={{0,6},{1,7},{8,14},{9,15},{16,22},{17,23},{24,30},{25,31},{32,38},... | collective-permute-start | bytes 1572872 | tf_op jit(solution)/shard_map/ppermute | solution.py:60
  52.5 41.0 %collective-permute-start.3 = (bf16[512,512]{0,1:T(8,128)(2,1)S(1)}, bf16[512,512]{0,1:T(8,128)(2,1)S(1)}, u32[]{:S(2)}, u32[]{:S(2)}) collective-permute-start(bf16[512,512]{0,1:T(8,128)(2,1)S(1)} %get-tuple-element.12), channel_id=1, source_target_pairs={{4,0},{6,2},{5,1},{7,3},{12,8},{14,10},{13,9},{15,11},{20,16},{22,... | collective-permute-start | bytes 1572872 | tf_op jit(solution)/shard_map/ppermute | solution.py:60
  59.2 34.2 %collective-permute-start.4 = (bf16[512,512]{0,1:T(8,128)(2,1)S(1)}, bf16[512,512]{0,1:T(8,128)(2,1)S(1)}, u32[]{:S(2)}, u32[]{:S(2)}) collective-permute-start(bf16[512,512]{0,1:T(8,128)(2,1)S(1)} %get-tuple-element.12), channel_id=1, source_target_pairs={{0,4},{2,6},{1,5},{3,7},{8,12},{10,14},{9,13},{11,15},{16,20},{18,... | collective-permute-start | bytes 1572872 | tf_op jit(solution)/shard_map/ppermute | solution.py:60
  60.6 33.9 %collective-permute-start.5 = (bf16[512,512]{0,1:T(8,128)(2,1)S(1)}, bf16[512,512]{0,1:T(8,128)(2,1)S(1)}, u32[]{:S(2)}, u32[]{:S(2)}) collective-permute-start(bf16[512,512]{0,1:T(8,128)(2,1)S(1)} %get-tuple-element.12), channel_id=1, source_target_pairs={{6,0},{7,1},{14,8},{15,9},{22,16},{23,17},{30,24},{31,25},{38,32},... | collective-permute-start | bytes 1572872 | tf_op jit(solution)/shard_map/ppermute | solution.py:60
  61.3 38.7 %collective-permute-start.6 = (bf16[512,512]{0,1:T(8,128)(2,1)S(1)}, bf16[512,512]{0,1:T(8,128)(2,1)S(1)}, u32[]{:S(2)}, u32[]{:S(2)}) collective-permute-start(bf16[512,512]{0,1:T(8,128)(2,1)S(1)} %get-tuple-element.12), channel_id=1, source_target_pairs={{0,2},{2,4},{4,6},{1,3},{3,5},{5,7},{8,10},{10,12},{12,14},{9,11},... | collective-permute-start | bytes 1572872 | tf_op jit(solution)/shard_map/ppermute | solution.py:60
  101.2 9.6 %collective-permute-start.7 = (bf16[4,512,512]{1,2,0:T(8,128)(2,1)S(1)}, bf16[4,512,512]{1,2,0:T(8,128)(2,1)}, u32[]{:S(2)}, u32[]{:S(2)}) collective-permute-start(bf16[4,512,512]{1,2,0:T(8,128)(2,1)S(1)} %pad_maximum_fusion), channel_id=1, source_target_pairs={{0,1},{1,0},{2,3},{3,2},{4,5},{5,4},{6,7},{7,6},{8,9},{9,8},{10,11... | collective-permute-start | bytes 6291464 | tf_op jit(solution)/shard_map/ppermute | solution.py:155
Sparse Core Ops, SparseCore 0:
  18.3 86.1 all-gather.1

commit v10 on v8

--- a/solution.py
+++ b/solution.py
@@ -62,6 +62,26 @@
     for k in range(1, size):
         slots.append(jnp.where(index + k < size, received[-k], received[size - k]))
     return jnp.stack(slots)
+
+
+def ring_gather(piece, axis_name, size, absolute=True):
+    index = lax.axis_index(axis_name)
+    right = [(i, (i + 1) % size) for i in range(size)]
+    left = [(i, (i - 1) % size) for i in range(size)]
+    relative = [None] * size
+    relative[0] = piece
+    from_left = piece
+    from_right = piece
+    for step in range(1, size // 2 + 1):
+        from_left = lax.ppermute(from_left, axis_name, right)
+        relative[(size - step) % size] = from_left
+        if step < size - step:
+            from_right = lax.ppermute(from_right, axis_name, left)
+            relative[step] = from_right
+    if not absolute:
+        return jnp.stack(relative)
+    stacked = jnp.stack(relative + relative)
+    return lax.dynamic_slice_in_dim(stacked, (size - index) % size, size, axis=0)
 
 
 def partial_kernel(table_ref, piece_ref, weight_ref, out_ref, acc_ref):
@@ -132,7 +152,8 @@
     partner = lax.ppermute(out_weight, "zh", [(0, 1), (1, 0)])
     zh = lax.axis_index("zh")
     pair = jnp.where(zh == 0, jnp.stack([out_weight, partner]), jnp.stack([partner, out_weight]))
-    weight_xy = lax.all_gather(pair, ("x", "y"), axis=0, tiled=False)
+    weight_y = ring_gather(pair, "y", 8)
+    weight_xy = ring_gather(weight_y, "x", 4, absolute=False)
 
     kv_tail = projected[tok_rows - span - 2 :, 1:]
     q_tail = projected[tok_rows - 2 :, 0][None]
@@ -159,11 +180,10 @@
 
     def table_for(c):
         w = 2 * sources + c
-        return jnp.stack([w % 4, w // 4]).astype(jnp.int32)
-
-    weight = weight_xy.reshape(4, 8, *weight_xy.shape[1:])
-    carry = block_matmul(table_for(core), own, weight)
-    return block_matmul(table_for(1 - core), other, weight, carry)
+        return jnp.stack([(w - lax.axis_index("x")) % 4, w // 4]).astype(jnp.int32)
+
+    carry = block_matmul(table_for(core), own, weight_xy)
+    return block_matmul(table_for(1 - core), other, weight_xy, carry)
 
 
 def solution(mesh):

time: 131 us -> 161 us (1.23)
  the two profiles are of different devices: /device:TPU:8 before, /device:TPU:152 now
where the time goes in v10:
time: 161 us; the launch traced here: 160 us
  starting transfers between devices  73.2 us (45%)
  waiting for transfers between devices  30.9 us (19%)
  local copies, waits for them, and re-layouts  26.5 us (16%)
  Pallas kernels  17.2 us (11%)
  other arithmetic  9.54 us (6%)
  matrix products  1.9 us (1%)
    ppermute x6, starting transfers between devices, ring_gather(): from_left = lax.ppermute(from_left, axis_name, right)  27.6 us
    ppermute x6, waiting for transfers between devices, ring_gather(): from_left = lax.ppermute(from_left, axis_name, right)  20.2 us
    ppermute x6, starting transfers between devices, line_slots(): received[d] = lax.ppermute(block, axis_name, pairs)  19.3 us
    unnamed x27, local copies, waits for them, and re-layouts  13.2 us
    pallas_call x2, Pallas kernels, block_matmul(): pl.pallas_call(kernel, grid_spec=grid_spec, out_shape=jax.ShapeDtypeStruc...  11.6 us
    ppermute x4, starting transfers between devices, ring_gather(): from_right = lax.ppermute(from_right, axis_name, left)  10.4 us
    ppermute x1, starting transfers between devices, on_device(): partner = lax.ppermute(out_weight, 'zh', [(0, 1), (1, 0)])  9.25 us
    ppermute x4, waiting for transfers between devices, ring_gather(): from_right = lax.ppermute(from_right, axis_name, left)  7.63 us
  transfers between devices with their start and end apart: 19, of which 5 were waited for; matrix products, arithmetic and copies ran while one was open for 23% of the time, Pallas kernels for 7%

profile of v10, /device:TPU:152, one launch (start us, length us, event | category | flops | bytes accessed | tf_op | source)
XLA Modules:
  0.0 159.8 jit_solution(11742655794460793689)
XLA Ops:
  0.0 9.2 %collective-permute-start.8 = (bf16[64,512]{1,0:T(8,128)(2,1)}, bf16[64,512]{1,0:T(8,128)(2,1)S(1)}, u32[]{:S(2)}, u32[]{:S(2)}) collective-permute-start(bf16[64,512]{1,0:T(8,128)(2,1)} %param.7), channel_id=1, source_target_pairs={{0,256},{256,0},{1,257},{257,1},{2,258},{258,2},{3,259},{259,3},{4... | collective-permute-start | bytes 196616 | tf_op jit(solution)/shard_map/ppermute | solution.py:152
  9.3 1.0 slice.75
  10.3 0.7 slice_bitcast_fusion.5
  11.6 4.7 %collective-permute-start = (bf16[131,2,512]{2,1,0:T(2,128)(2,1)S(1)}, bf16[131,2,512]{2,1,0:T(2,128)(2,1)S(1)}, u32[]{:S(2)}, u32[]{:S(2)}) collective-permute-start(bf16[131,2,512]{2,1,0:T(2,128)(2,1)S(1)} %pad_maximum_fusion.2), channel_id=1, source_target_pairs={{0,8},{8,16},{16,24},{24,32},{32,40},{40,48},{48,56},{56,64},{64,7... | collective-permute-start | bytes 804872 | tf_op jit(solution)/shard_map/ppermute | solution.py:20
  16.3 1.1 slice_bitcast_fusion
  17.5 0.7 maximum_maximum_fusion.row_ref
  18.3 1.9 %collective-permute-start.9 = (bf16[2,64,512]{2,1,0:T(8,128)(2,1)S(1)}, bf16[2,64,512]{2,1,0:T(8,128)(2,1)S(1)}, u32[]{:S(2)}, u32[]{:S(2)}) collective-permute-start(bf16[2,64,512]{2,1,0:T(8,128)(2,1)S(1)} %maximum_select_fusion.1), channel_id=1, source_target_pairs={{0,56},{8,0},{16,8},{24,16},{32,24},{40,32},{48,40},{56,48},{1,57}... | collective-permute-start | bytes 393224 | tf_op jit(solution)/shard_map/ppermute | solution.py:79
  20.2 5.1 %collective-permute-start.12 = (bf16[2,64,512]{2,1,0:T(8,128)(2,1)S(1)}, bf16[2,64,512]{2,1,0:T(8,128)(2,1)S(1)}, u32[]{:S(2)}, u32[]{:S(2)}) collective-permute-start(bf16[2,64,512]{2,1,0:T(8,128)(2,1)S(1)} %maximum_select_fusion.1), channel_id=1, source_target_pairs={{0,8},{8,16},{16,24},{24,32},{32,40},{40,48},{48,56},{56,0},{1,9},... | collective-permute-start | bytes 393224 | tf_op jit(solution)/shard_map/ppermute | solution.py:76
  25.4 5.6 %shard_map.46 = bf16[32,128,256]{2,1,0:T(8,128)(2,1)} custom-call(f32[32,384]{1,0:T(8,128)} %maximum_maximum_fusion.row_ref), custom_call_target="tpu_custom_call" | custom-call | tf_op jit(solution)/shard_map/pallas_call | solution.py:48
  31.7 1.9 %collective-permute-start.10 = (bf16[2,64,512]{2,1,0:T(8,128)(2,1)S(1)}, bf16[2,64,512]{2,1,0:T(8,128)(2,1)}, u32[]{:S(2)}, u32[]{:S(2)}) collective-permute-start(bf16[2,64,512]{2,1,0:T(8,128)(2,1)S(1)} %collective-permute-done.9), channel_id=1, source_target_pairs={{0,56},{8,0},{16,8},{24,16},{32,24},{40,32},{48,40},{56,48},{1,57}... | collective-permute-start | bytes 393224 | tf_op jit(solution)/shard_map/ppermute | solution.py:79
  33.7 5.1 %collective-permute-start.13 = (bf16[2,64,512]{2,1,0:T(8,128)(2,1)S(1)}, bf16[2,64,512]{2,1,0:T(8,128)(2,1)}, u32[]{:S(2)}, u32[]{:S(2)}) collective-permute-start(bf16[2,64,512]{2,1,0:T(8,128)(2,1)S(1)} %collective-permute-done.12), channel_id=1, source_target_pairs={{0,8},{8,16},{16,24},{24,32},{32,40},{40,48},{48,56},{56,0},{1,9},... | collective-permute-start | bytes 393224 | tf_op jit(solution)/shard_map/ppermute | solution.py:76
  38.8 0.7 bitcast_dynamic-update-slice_fusion.12
  39.5 0.7 copy-done.3
  40.8 0.8 fusion
  41.8 0.9 fusion.20
  43.0 0.9 copy.12
  44.0 1.3 copy.11
  45.2 0.9 slice.97
  46.1 1.1 copy.13
  47.3 1.9 %fusion.4 = f32[4,128,32,16]{1,3,0,2:T(8,128)S(1)} fusion(bf16[32,128,256]{2,1,0:T(8,128)(2,1)S(1)} %copy-done, bf16[4,128,32,16]{1,3,0,2:T(8,128)(2,1)S(1)} %copy.13, bf16[4,128,32,16]{1,3,0,2:T(8,128)(2,1)} %copy.12), kind=kOutput, calls=%fused_computation.9 | convolution fusion | flops 136314880 | bytes 4194304 | tf_op jit(solution)/shard_map/gij,bjgc->bigc/dot_general | solution.py:170
  50.0 0.7 slice_bitcast_fusion.4
  51.2 2.5 %collective-permute-start.1 = (bf16[512,512]{1,0:T(8,128)(2,1)S(1)}, bf16[512,512]{1,0:T(8,128)(2,1)S(1)}, u32[]{:S(2)}, u32[]{:S(2)}) collective-permute-start(bf16[512,512]{1,0:T(8,128)(2,1)S(1)} %fusion.10), channel_id=1, source_target_pairs={{2,0},{4,2},{6,4},{3,1},{5,3},{7,5},{10,8},{12,10},{14,12},{11,9},... | collective-permute-start | bytes 1572872 | tf_op jit(solution)/shard_map/ppermute | solution.py:60
  53.7 0.7 collective-permute-start.2
  54.4 7.0 %collective-permute-start.3 = (bf16[512,512]{1,0:T(8,128)(2,1)S(1)}, bf16[512,512]{1,0:T(8,128)(2,1)S(1)}, u32[]{:S(2)}, u32[]{:S(2)}) collective-permute-start(bf16[512,512]{1,0:T(8,128)(2,1)S(1)} %fusion.10), channel_id=1, source_target_pairs={{4,0},{6,2},{5,1},{7,3},{12,8},{14,10},{13,9},{15,11},{20,16},{22,... | collective-permute-start | bytes 1572872 | tf_op jit(solution)/shard_map/ppermute | solution.py:60
  61.5 1.9 %collective-permute-start.11 = (bf16[2,64,512]{2,1,0:T(8,128)(2,1)}, bf16[2,64,512]{2,1,0:T(8,128)(2,1)S(1)}, u32[]{:S(2)}, u32[]{:S(2)}) collective-permute-start(bf16[2,64,512]{2,1,0:T(8,128)(2,1)} %collective-permute-done.10), channel_id=1, source_target_pairs={{0,56},{8,0},{16,8},{24,16},{32,24},{40,32},{48,40},{56,48},{1,57}... | collective-permute-start | bytes 393224 | tf_op jit(solution)/shard_map/ppermute | solution.py:79
  63.4 5.1 %collective-permute-start.14 = (bf16[2,64,512]{2,1,0:T(8,128)(2,1)}, bf16[2,64,512]{2,1,0:T(8,128)(2,1)S(1)}, u32[]{:S(2)}, u32[]{:S(2)}) collective-permute-start(bf16[2,64,512]{2,1,0:T(8,128)(2,1)} %collective-permute-done.13), channel_id=1, source_target_pairs={{0,8},{8,16},{16,24},{24,32},{32,40},{40,48},{48,56},{56,0},{1,9},... | collective-permute-start | bytes 393224 | tf_op jit(solution)/shard_map/ppermute | solution.py:76
  68.5 1.6 bitcast_dynamic-update-slice_fusion.10
  70.1 1.3 collective-permute-start.4
  71.4 5.4 %collective-permute-start.15 = (bf16[2,64,512]{2,1,0:T(8,128)(2,1)S(1)}, bf16[2,64,512]{2,1,0:T(8,128)(2,1)S(1)}, u32[]{:S(2)}, u32[]{:S(2)}) collective-permute-start(bf16[2,64,512]{2,1,0:T(8,128)(2,1)S(1)} %collective-permute-done.14), channel_id=1, source_target_pairs={{0,8},{8,16},{16,24},{24,32},{32,40},{40,48},{48,56},{56,0},{1,9},... | collective-permute-start | bytes 393224 | tf_op jit(solution)/shard_map/ppermute | solution.py:76
  77.5 1.8 %collective-permute-done.15 = bf16[2,64,512]{2,1,0:T(8,128)(2,1)S(1)} collective-permute-done((bf16[2,64,512]{2,1,0:T(8,128)(2,1)S(1)}, bf16[2,64,512]{2,1,0:T(8,128)(2,1)S(1)}, u32[]{:S(2)}, u32[]{:S(2)}) %collective-permute-start.15) | collective-permute-done | bytes 131104 | tf_op jit(solution)/shard_map/ppermute | solution.py:76
  79.3 0.7 collective-permute-start.5
  81.3 1.6 bitcast_dynamic-update-slice_fusion.2
  84.9 1.5 bitcast_dynamic-update-slice_fusion.11
  88.4 1.6 bitcast_dynamic-update-slice_fusion.3
  90.6 1.3 constant_dynamic-slice_fusion
  91.9 7.1 %collective-permute-start.6 = (bf16[512,512]{1,0:T(8,128)(2,1)S(1)}, bf16[512,512]{1,0:T(8,128)(2,1)S(1)}, u32[]{:S(2)}, u32[]{:S(2)}) collective-permute-start(bf16[512,512]{1,0:T(8,128)(2,1)S(1)} %fusion.10), channel_id=1, source_target_pairs={{0,2},{2,4},{4,6},{1,3},{3,5},{5,7},{8,10},{10,12},{12,14},{9,11},... | collective-permute-start | bytes 1572872 | tf_op jit(solution)/shard_map/ppermute | solution.py:60
  99.1 3.4 %collective-permute-start.17 = (bf16[8,2,64,512]{3,2,1,0:T(8,128)(2,1)S(1)}, bf16[8,2,64,512]{3,2,1,0:T(8,128)(2,1)}, u32[]{:S(2)}, u32[]{:S(2)}) collective-permute-start(bf16[8,2,64,512]{3,2,1,0:T(8,128)(2,1)S(1)} %constant_dynamic-slice_fusion), channel_id=1, source_target_pairs={{0,64},{64,128},{128,192},{192,0},{1,65},{65,129},{129,193},{193,1... | collective-permute-start | bytes 3145736 | tf_op jit(solution)/shard_map/ppermute | solution.py:76
  102.7 3.1 %collective-permute-done.6 = bf16[512,512]{1,0:T(8,128)(2,1)S(1)} collective-permute-done((bf16[512,512]{1,0:T(8,128)(2,1)S(1)}, bf16[512,512]{1,0:T(8,128)(2,1)S(1)}, u32[]{:S(2)}, u32[]{:S(2)}) %collective-permute-start.6) | collective-permute-done | bytes 524320 | tf_op jit(solution)/shard_map/ppermute | solution.py:60
  106.1 1.9 %collective-permute-start.7 = (bf16[4,512,512]{2,1,0:T(8,128)(2,1)S(1)}, bf16[4,512,512]{2,1,0:T(8,128)(2,1)}, u32[]{:S(2)}, u32[]{:S(2)}) collective-permute-start(bf16[4,512,512]{2,1,0:T(8,128)(2,1)S(1)} %pad_maximum_fusion.1.piece_ref), channel_id=1, source_target_pairs={{0,1},{1,0},{2,3},{3,2},{4,5},{5,4},{6,7},{7,6},{8,9},{9,8},{10,11... | collective-permute-start | bytes 6291464 | tf_op jit(solution)/shard_map/ppermute | solution.py:176
  108.0 4.7 %collective-permute-start.16 = (bf16[8,2,64,512]{3,2,1,0:T(8,128)(2,1)S(1)}, bf16[8,2,64,512]{3,2,1,0:T(8,128)(2,1)}, u32[]{:S(2)}, u32[]{:S(2)}) collective-permute-start(bf16[8,2,64,512]{3,2,1,0:T(8,128)(2,1)S(1)} %constant_dynamic-slice_fusion), channel_id=1, source_target_pairs={{0,192},{64,0},{128,64},{192,128},{1,193},{65,1},{129,65},{193,129... | collective-permute-start | bytes 3145736 | tf_op jit(solution)/shard_map/ppermute | solution.py:79
  112.7 9.5 %collective-permute-done.17 = bf16[8,2,64,512]{3,2,1,0:T(8,128)(2,1)} collective-permute-done((bf16[8,2,64,512]{3,2,1,0:T(8,128)(2,1)S(1)}, bf16[8,2,64,512]{3,2,1,0:T(8,128)(2,1)}, u32[]{:S(2)}, u32[]{:S(2)}) %collective-permute-start.17) | collective-permute-done | bytes 1048608 | tf_op jit(solution)/shard_map/ppermute | solution.py:76
  122.2 3.4 %collective-permute-start.18 = (bf16[8,2,64,512]{3,2,1,0:T(8,128)(2,1)}, bf16[8,2,64,512]{3,2,1,0:T(8,128)(2,1)}, u32[]{:S(2)}, u32[]{:S(2)}) collective-permute-start(bf16[8,2,64,512]{3,2,1,0:T(8,128)(2,1)} %collective-permute-done.17), channel_id=1, source_target_pairs={{0,64},{64,128},{128,192},{192,0},{1,65},{65,129},{129,193},{193,1... | collective-permute-start | bytes 3145736 | tf_op jit(solution)/shard_map/ppermute | solution.py:76
  126.8 1.3 fusion.22
  128.1 7.6 %collective-permute-done.16 = bf16[8,2,64,512]{3,2,1,0:T(8,128)(2,1)} collective-permute-done((bf16[8,2,64,512]{3,2,1,0:T(8,128)(2,1)S(1)}, bf16[8,2,64,512]{3,2,1,0:T(8,128)(2,1)}, u32[]{:S(2)}, u32[]{:S(2)}) %collective-permute-start.16) | collective-permute-done | bytes 1048608 | tf_op jit(solution)/shard_map/ppermute | solution.py:79
  135.8 8.8 %collective-permute-done.18 = bf16[8,2,64,512]{3,2,1,0:T(8,128)(2,1)} collective-permute-done((bf16[8,2,64,512]{3,2,1,0:T(8,128)(2,1)}, bf16[8,2,64,512]{3,2,1,0:T(8,128)(2,1)}, u32[]{:S(2)}, u32[]{:S(2)}) %collective-permute-start.18) | collective-permute-done | bytes 1048608 | tf_op jit(solution)/shard_map/ppermute | solution.py:76
  144.6 3.6 %pad_maximum_fusion.weight_ref = bf16[4,8,2,64,512]{4,3,2,1,0:T(8,128)(2,1)} fusion(bf16[1,8,2,64,512]{4,3,2,1,0:T(8,128)(2,1)} %bitcast.30, bf16[1,8,2,64,512]{4,3,2,1,0:T(8,128)(2,1)} %bitcast.29, bf16[1,8,2,64,512]{4,3,2,1,0:T(8,128)(2,1)} %bitcast.28, bf16[1,8,2,64,512]{4,3,2,1,0:T(8,128)(2,1)S(1)} %fusion.22), kind=kLoop, calls=%fused_computation | loop fusion | flops 6291456 | bytes 8388608 | tf_op jit(solution)/shard_map/stack | solution.py:82
  148.2 5.7 %shard_map.47.carry_ref = f32[512,512]{1,0:T(8,128)} custom-call(s32[2,4]{1,0:T(2,128)} %pad_add_fusion.1.table_ref, bf16[4,512,512]{2,1,0:T(8,128)(2,1)} %copy-done.1, bf16[4,8,2,64,512]{4,3,2,1,0:T(8,128)(2,1)} %pad_maximum_fusion.weight_ref), custom_call_target="tpu_custom_call" | custom-call | tf_op jit(solution)/shard_map/pallas_call | solution.py:140
  153.9 5.8 %shard_map.48 = bf16[512,512]{1,0:T(8,128)(2,1)} custom-call(s32[2,4]{1,0:T(2,128)} %pad_add_fusion.table_ref, bf16[4,512,512]{2,1,0:T(8,128)(2,1)} %collective-permute-done.7.piece_ref, bf16[4,8,2,64,512]{4,3,2,1,0:T(8,128)(2,1)} %pad_maximum_fusion.weight_ref, f32[512,512]{1,0:T(8,128)} %shard_map.47.carry_ref), custom_call_target="tpu_custom_call" | custom-call | tf_op jit(solution)/shard_map/pallas_call | solution.py:140
  (67 shorter events, 12.2 us)
Async XLA Ops:
  0.0 18.3 %copy-start.2 = (bf16[64,512]{1,0:T(8,128)(2,1)S(1)}, bf16[64,512]{1,0:T(8,128)(2,1)}, u32[]{:S(2)}) copy-start(bf16[64,512]{1,0:T(8,128)(2,1)} %param.7) | copy-start | bytes 196612
  0.0 17.4 %copy-start.5 = (bf16[32,128]{1,0:T(8,128)(2,1)S(1)}, bf16[32,128]{1,0:T(8,128)(2,1)}, u32[]{:S(2)}) copy-start(bf16[32,128]{1,0:T(8,128)(2,1)} %param.6) | copy-start | bytes 24580
  0.0 18.2 %copy-start.4 = (f32[3,3,512]{2,1,0:T(4,128)S(1)}, f32[3,3,512]{2,1,0:T(4,128)}, u32[]{:S(2)}) copy-start(f32[3,3,512]{2,1,0:T(4,128)} %param.5) | copy-start | bytes 55300
  0.0 18.3 %collective-permute-start.8 = (bf16[64,512]{1,0:T(8,128)(2,1)}, bf16[64,512]{1,0:T(8,128)(2,1)S(1)}, u32[]{:S(2)}, u32[]{:S(2)}) collective-permute-start(bf16[64,512]{1,0:T(8,128)(2,1)} %param.7), channel_id=1, source_target_pairs={{0,256},{256,0},{1,257},{257,1},{2,258},{258,2},{3,259},{259,3},{4... | collective-permute-start | bytes 196616 | tf_op jit(solution)/shard_map/ppermute | solution.py:152
  11.6 27.9 %collective-permute-start = (bf16[131,2,512]{2,1,0:T(2,128)(2,1)S(1)}, bf16[131,2,512]{2,1,0:T(2,128)(2,1)S(1)}, u32[]{:S(2)}, u32[]{:S(2)}) collective-permute-start(bf16[131,2,512]{2,1,0:T(2,128)(2,1)S(1)} %pad_maximum_fusion.2), channel_id=1, source_target_pairs={{0,8},{8,16},{16,24},{24,32},{32,40},{40,48},{48,56},{56,64},{64,7... | collective-permute-start | bytes 804872 | tf_op jit(solution)/shard_map/ppermute | solution.py:20
  18.3 13.4 %collective-permute-start.9 = (bf16[2,64,512]{2,1,0:T(8,128)(2,1)S(1)}, bf16[2,64,512]{2,1,0:T(8,128)(2,1)S(1)}, u32[]{:S(2)}, u32[]{:S(2)}) collective-permute-start(bf16[2,64,512]{2,1,0:T(8,128)(2,1)S(1)} %maximum_select_fusion.1), channel_id=1, source_target_pairs={{0,56},{8,0},{16,8},{24,16},{32,24},{40,32},{48,40},{56,48},{1,57}... | collective-permute-start | bytes 393224 | tf_op jit(solution)/shard_map/ppermute | solution.py:79
  20.2 13.4 %collective-permute-start.12 = (bf16[2,64,512]{2,1,0:T(8,128)(2,1)S(1)}, bf16[2,64,512]{2,1,0:T(8,128)(2,1)S(1)}, u32[]{:S(2)}, u32[]{:S(2)}) collective-permute-start(bf16[2,64,512]{2,1,0:T(8,128)(2,1)S(1)} %maximum_select_fusion.1), channel_id=1, source_target_pairs={{0,8},{8,16},{16,24},{24,32},{32,40},{40,48},{48,56},{56,0},{1,9},... | collective-permute-start | bytes 393224 | tf_op jit(solution)/shard_map/ppermute | solution.py:76
  25.4 15.0 %slice-start = ((bf16[512,3,512]{2,0,1:T(8,128)(2,1)}), bf16[512,2,512]{2,0,1:T(8,128)(2,1)S(1)}, s32[]{:S(2)}) async-start(bf16[512,3,512]{2,0,1:T(8,128)(2,1)} %param.4), calls=%async_computation | async-start | bytes 2097152 | tf_op jit(solution)/shard_map/slice | solution.py:161
  31.7 29.7 %collective-permute-start.10 = (bf16[2,64,512]{2,1,0:T(8,128)(2,1)S(1)}, bf16[2,64,512]{2,1,0:T(8,128)(2,1)}, u32[]{:S(2)}, u32[]{:S(2)}) collective-permute-start(bf16[2,64,512]{2,1,0:T(8,128)(2,1)S(1)} %collective-permute-done.9), channel_id=1, source_target_pairs={{0,56},{8,0},{16,8},{24,16},{32,24},{40,32},{48,40},{56,48},{1,57}... | collective-permute-start | bytes 393224 | tf_op jit(solution)/shard_map/ppermute | solution.py:79
  33.7 29.7 %collective-permute-start.13 = (bf16[2,64,512]{2,1,0:T(8,128)(2,1)S(1)}, bf16[2,64,512]{2,1,0:T(8,128)(2,1)}, u32[]{:S(2)}, u32[]{:S(2)}) collective-permute-start(bf16[2,64,512]{2,1,0:T(8,128)(2,1)S(1)} %collective-permute-done.12), channel_id=1, source_target_pairs={{0,8},{8,16},{16,24},{24,32},{32,40},{40,48},{48,56},{56,0},{1,9},... | collective-permute-start | bytes 393224 | tf_op jit(solution)/shard_map/ppermute | solution.py:76
  39.5 0.7 copy-start.3
  43.0 4.2 %copy-start = (bf16[32,128,256]{2,1,0:T(8,128)(2,1)S(1)}, bf16[32,128,256]{2,1,0:T(8,128)(2,1)}, u32[]{:S(2)}) copy-start(bf16[32,128,256]{2,1,0:T(8,128)(2,1)} %shard_map.46) | copy-start | bytes 6291460
  51.2 40.7 %collective-permute-start.1 = (bf16[512,512]{1,0:T(8,128)(2,1)S(1)}, bf16[512,512]{1,0:T(8,128)(2,1)S(1)}, u32[]{:S(2)}, u32[]{:S(2)}) collective-permute-start(bf16[512,512]{1,0:T(8,128)(2,1)S(1)} %fusion.10), channel_id=1, source_target_pairs={{2,0},{4,2},{6,4},{3,1},{5,3},{7,5},{10,8},{12,10},{14,12},{11,9},... | collective-permute-start | bytes 1572872 | tf_op jit(solution)/shard_map/ppermute | solution.py:60
  53.7 45.4 %collective-permute-start.2 = (bf16[512,512]{1,0:T(8,128)(2,1)S(1)}, bf16[512,512]{1,0:T(8,128)(2,1)S(1)}, u32[]{:S(2)}, u32[]{:S(2)}) collective-permute-start(bf16[512,512]{1,0:T(8,128)(2,1)S(1)} %fusion.10), channel_id=1, source_target_pairs={{0,6},{1,7},{8,14},{9,15},{16,22},{17,23},{24,30},{25,31},{32,38},... | collective-permute-start | bytes 1572872 | tf_op jit(solution)/shard_map/ppermute | solution.py:60
  54.4 48.2 %collective-permute-start.3 = (bf16[512,512]{1,0:T(8,128)(2,1)S(1)}, bf16[512,512]{1,0:T(8,128)(2,1)S(1)}, u32[]{:S(2)}, u32[]{:S(2)}) collective-permute-start(bf16[512,512]{1,0:T(8,128)(2,1)S(1)} %fusion.10), channel_id=1, source_target_pairs={{4,0},{6,2},{5,1},{7,3},{12,8},{14,10},{13,9},{15,11},{20,16},{22,... | collective-permute-start | bytes 1572872 | tf_op jit(solution)/shard_map/ppermute | solution.py:60
  61.5 8.6 %collective-permute-start.11 = (bf16[2,64,512]{2,1,0:T(8,128)(2,1)}, bf16[2,64,512]{2,1,0:T(8,128)(2,1)S(1)}, u32[]{:S(2)}, u32[]{:S(2)}) collective-permute-start(bf16[2,64,512]{2,1,0:T(8,128)(2,1)} %collective-permute-done.10), channel_id=1, source_target_pairs={{0,56},{8,0},{16,8},{24,16},{32,24},{40,32},{48,40},{56,48},{1,57}... | collective-permute-start | bytes 393224 | tf_op jit(solution)/shard_map/ppermute | solution.py:79
  63.4 8.0 %collective-permute-start.14 = (bf16[2,64,512]{2,1,0:T(8,128)(2,1)}, bf16[2,64,512]{2,1,0:T(8,128)(2,1)S(1)}, u32[]{:S(2)}, u32[]{:S(2)}) collective-permute-start(bf16[2,64,512]{2,1,0:T(8,128)(2,1)} %collective-permute-done.13), channel_id=1, source_target_pairs={{0,8},{8,16},{16,24},{24,32},{32,40},{40,48},{48,56},{56,0},{1,9},... | collective-permute-start | bytes 393224 | tf_op jit(solution)/shard_map/ppermute | solution.py:76
  70.1 32.5 %collective-permute-start.4 = (bf16[512,512]{1,0:T(8,128)(2,1)S(1)}, bf16[512,512]{1,0:T(8,128)(2,1)S(1)}, u32[]{:S(2)}, u32[]{:S(2)}) collective-permute-start(bf16[512,512]{1,0:T(8,128)(2,1)S(1)} %fusion.10), channel_id=1, source_target_pairs={{0,4},{2,6},{1,5},{3,7},{8,12},{10,14},{9,13},{11,15},{16,20},{18,... | collective-permute-start | bytes 1572872 | tf_op jit(solution)/shard_map/ppermute | solution.py:60
  71.4 7.9 %collective-permute-start.15 = (bf16[2,64,512]{2,1,0:T(8,128)(2,1)S(1)}, bf16[2,64,512]{2,1,0:T(8,128)(2,1)S(1)}, u32[]{:S(2)}, u32[]{:S(2)}) collective-permute-start(bf16[2,64,512]{2,1,0:T(8,128)(2,1)S(1)} %collective-permute-done.14), channel_id=1, source_target_pairs={{0,8},{8,16},{16,24},{24,32},{32,40},{40,48},{48,56},{56,0},{1,9},... | collective-permute-start | bytes 393224 | tf_op jit(solution)/shard_map/ppermute | solution.py:76
  79.3 23.3 %collective-permute-start.5 = (bf16[512,512]{1,0:T(8,128)(2,1)S(1)}, bf16[512,512]{1,0:T(8,128)(2,1)S(1)}, u32[]{:S(2)}, u32[]{:S(2)}) collective-permute-start(bf16[512,512]{1,0:T(8,128)(2,1)S(1)} %fusion.10), channel_id=1, source_target_pairs={{6,0},{7,1},{14,8},{15,9},{22,16},{23,17},{30,24},{31,25},{38,32},... | collective-permute-start | bytes 1572872 | tf_op jit(solution)/shard_map/ppermute | solution.py:60
  91.9 13.8 %collective-permute-start.6 = (bf16[512,512]{1,0:T(8,128)(2,1)S(1)}, bf16[512,512]{1,0:T(8,128)(2,1)S(1)}, u32[]{:S(2)}, u32[]{:S(2)}) collective-permute-start(bf16[512,512]{1,0:T(8,128)(2,1)S(1)} %fusion.10), channel_id=1, source_target_pairs={{0,2},{2,4},{4,6},{1,3},{3,5},{5,7},{8,10},{10,12},{12,14},{9,11},... | collective-permute-start | bytes 1572872 | tf_op jit(solution)/shard_map/ppermute | solution.py:60
  99.1 23.1 %collective-permute-start.17 = (bf16[8,2,64,512]{3,2,1,0:T(8,128)(2,1)S(1)}, bf16[8,2,64,512]{3,2,1,0:T(8,128)(2,1)}, u32[]{:S(2)}, u32[]{:S(2)}) collective-permute-start(bf16[8,2,64,512]{3,2,1,0:T(8,128)(2,1)S(1)} %constant_dynamic-slice_fusion), channel_id=1, source_target_pairs={{0,64},{64,128},{128,192},{192,0},{1,65},{65,129},{129,193},{193,1... | collective-permute-start | bytes 3145736 | tf_op jit(solution)/shard_map/ppermute | solution.py:76
  106.1 42.1 %copy-start.1 = (bf16[4,512,512]{2,1,0:T(8,128)(2,1)}, bf16[4,512,512]{2,1,0:T(8,128)(2,1)S(1)}, u32[]{:S(2)}) copy-start(bf16[4,512,512]{2,1,0:T(8,128)(2,1)S(1)} %pad_maximum_fusion.1.piece_ref) | copy-start | bytes 6291460
  106.1 47.8 %collective-permute-start.7 = (bf16[4,512,512]{2,1,0:T(8,128)(2,1)S(1)}, bf16[4,512,512]{2,1,0:T(8,128)(2,1)}, u32[]{:S(2)}, u32[]{:S(2)}) collective-permute-start(bf16[4,512,512]{2,1,0:T(8,128)(2,1)S(1)} %pad_maximum_fusion.1.piece_ref), channel_id=1, source_target_pairs={{0,1},{1,0},{2,3},{3,2},{4,5},{5,4},{6,7},{7,6},{8,9},{9,8},{10,11... | collective-permute-start | bytes 6291464 | tf_op jit(solution)/shard_map/ppermute | solution.py:176
  108.0 27.7 %collective-permute-start.16 = (bf16[8,2,64,512]{3,2,1,0:T(8,128)(2,1)S(1)}, bf16[8,2,64,512]{3,2,1,0:T(8,128)(2,1)}, u32[]{:S(2)}, u32[]{:S(2)}) collective-permute-start(bf16[8,2,64,512]{3,2,1,0:T(8,128)(2,1)S(1)} %constant_dynamic-slice_fusion), channel_id=1, source_target_pairs={{0,192},{64,0},{128,64},{192,128},{1,193},{65,1},{129,65},{193,129... | collective-permute-start | bytes 3145736 | tf_op jit(solution)/shard_map/ppermute | solution.py:79
  122.2 22.4 %collective-permute-start.18 = (bf16[8,2,64,512]{3,2,1,0:T(8,128)(2,1)}, bf16[8,2,64,512]{3,2,1,0:T(8,128)(2,1)}, u32[]{:S(2)}, u32[]{:S(2)}) collective-permute-start(bf16[8,2,64,512]{3,2,1,0:T(8,128)(2,1)} %collective-permute-done.17), channel_id=1, source_target_pairs={{0,64},{64,128},{128,192},{192,0},{1,65},{65,129},{129,193},{193,1... | collective-permute-start | bytes 3145736 | tf_op jit(solution)/shard_map/ppermute | solution.py:76

commit v11 on v8

--- a/solution.py
+++ b/solution.py
@@ -131,7 +131,7 @@
 
     partner = lax.ppermute(out_weight, "zh", [(0, 1), (1, 0)])
     zh = lax.axis_index("zh")
-    pair = jnp.where(zh == 0, jnp.stack([out_weight, partner]), jnp.stack([partner, out_weight]))
+    pair = jnp.stack([out_weight, partner])
     weight_xy = lax.all_gather(pair, ("x", "y"), axis=0, tiled=False)
 
     kv_tail = projected[tok_rows - span - 2 :, 1:]
@@ -159,7 +159,7 @@
 
     def table_for(c):
         w = 2 * sources + c
-        return jnp.stack([w % 4, w // 4]).astype(jnp.int32)
+        return jnp.stack([w % 4, (w // 4 + zh) % 2]).astype(jnp.int32)
 
     weight = weight_xy.reshape(4, 8, *weight_xy.shape[1:])
     carry = block_matmul(table_for(core), own, weight)

time: 131 us -> 131 us (level)
  waiting for transfers between devices: 43.3 us -> 50.5 us
  starting transfers between devices: 37.7 us -> 30.6 us
    all_gather x1, waiting for transfers between devices: 11.3 us -> 22.6 us  [on_device(): weight_xy = lax.all_gather(pair, ('x', 'y'), axis=0, tiled=False)]
    ppermute x6, starting transfers between devices: 21.3 us -> 14.2 us  [line_slots(): received[d] = lax.ppermute(block, axis_name, pairs)]
    ppermute x6, waiting for transfers between devices: 28.6 us -> 24.4 us  [line_slots(): received[d] = lax.ppermute(block, axis_name, pairs)]
    select_n x3 -> x2, other arithmetic: 1.62 us -> 0.06 us  [table_for(): return jnp.stack([w % 4, (w // 4 + zh) % 2]).astype(jnp.int32)]
    another operation x2 -> x3, other arithmetic: 1.14 us -> 2.65 us  [the longest x1 1.5 us: on_device(): pair = jnp.stack([out_weight, partner])]
  transfers between devices with their start and end apart: 10 -> 10, of which waited for: 3 -> 5; matrix products, arithmetic and copies ran while one was open for 13% -> 13% of each run, Pallas kernels for 9% -> 9%
where the time goes in v11:
time: 131 us; the launch traced here: 130 us
  waiting for transfers between devices  50.5 us (39%)
  starting transfers between devices  30.6 us (23%)
  Pallas kernels  17.3 us (13%)
  between operations  13.7 us (10%)
  local copies, waits for them, and re-layouts  9.34 us (7%)
  other arithmetic  6.77 us (5%)
  matrix products  1.87 us (1%)
    ppermute x6, waiting for transfers between devices, line_slots(): received[d] = lax.ppermute(block, axis_name, pairs)  24.4 us
    all_gather x1, waiting for transfers between devices, on_device(): weight_xy = lax.all_gather(pair, ('x', 'y'), axis=0, tiled=False)  22.6 us
    ppermute x6, starting transfers between devices, line_slots(): received[d] = lax.ppermute(block, axis_name, pairs)  14.2 us
    pallas_call x2, Pallas kernels, block_matmul(): pl.pallas_call(kernel, grid_spec=grid_spec, out_shape=jax.ShapeDtypeStruc...  11.6 us
    ppermute x1, starting transfers between devices, on_device(): partner = lax.ppermute(out_weight, 'zh', [(0, 1), (1, 0)])  11 us
    pallas_call x1, Pallas kernels, toeplitz_blocks(): pl.pallas_call(toeplitz_kernel, out_shape=jax.ShapeDtypeStruct((groups, s...  5.7 us
    slice x7, local copies, waits for them, and re-layouts, on_device(): window = jnp.concatenate([blocks[:-1], blocks[1:]], axis=1)  5.42 us
    ppermute x1, starting transfers between devices, from_behind(): return lax.ppermute(array, SEQ, pairs)  3.47 us
  transfers between devices with their start and end apart: 10, of which 5 were waited for; matrix products, arithmetic and copies ran while one was open for 13% of the time, Pallas kernels for 9%

profile of v11, /device:TPU:8, one launch (start us, length us, event | category | flops | bytes accessed | tf_op | source)
XLA Modules:
  0.0 130.0 jit_solution(6749078888194786038)
XLA Ops:
  6.5 11.0 %collective-permute-start.8 = (bf16[64,512]{1,0:T(8,128)(2,1)}, bf16[64,512]{1,0:T(8,128)(2,1)S(1)}, u32[]{:S(2)}, u32[]{:S(2)}) collective-permute-start(bf16[64,512]{1,0:T(8,128)(2,1)} %param.7), channel_id=1, source_target_pairs={{0,256},{256,0},{1,257},{257,1},{2,258},{258,2},{3,259},{259,3},{4... | collective-permute-start | bytes 196616 | tf_op jit(solution)/shard_map/ppermute | solution.py:132
  17.6 3.4 %collective-permute-done.8 = bf16[64,512]{1,0:T(8,128)(2,1)S(1)} collective-permute-done((bf16[64,512]{1,0:T(8,128)(2,1)}, bf16[64,512]{1,0:T(8,128)(2,1)S(1)}, u32[]{:S(2)}, u32[]{:S(2)}) %collective-permute-start.8) | collective-permute-done | bytes 65568 | tf_op jit(solution)/shard_map/ppermute | solution.py:132
  20.9 1.5 %pad_maximum_fusion.2 = bf16[2,64,512]{2,1,0:T(8,128)(2,1)} fusion(bf16[1,64,512]{2,1,0:T(8,128)(2,1)S(1)} %bitcast.52, bf16[1,64,512]{2,1,0:T(8,128)(2,1)} %bitcast.51), kind=kLoop, calls=%fused_computation.29 | loop fusion | flops 65536 | bytes 262144 | tf_op jit(solution)/shard_map/stack | solution.py:134
  22.5 1.0 slice.75
  23.5 0.2 copy.25
  23.7 0.7 slice_bitcast_fusion.5
  24.4 1.1 pad_maximum_fusion.1
  25.5 3.5 %collective-permute-start = (bf16[131,2,512]{2,1,0:T(2,128)(2,1)}, bf16[131,2,512]{2,1,0:T(2,128)(2,1)S(1)}, u32[]{:S(2)}, u32[]{:S(2)}) collective-permute-start(bf16[131,2,512]{2,1,0:T(2,128)(2,1)} %pad_maximum_fusion.1), channel_id=1, source_target_pairs={{0,8},{8,16},{16,24},{24,32},{32,40},{40,48},{48,56},{56,64},{64,7... | collective-permute-start | bytes 804872 | tf_op jit(solution)/shard_map/ppermute | solution.py:20
  29.0 0.8 rev.3
  29.7 0.1 pad.10.clone
  29.8 0.7 maximum_maximum_fusion.row_ref
  30.6 5.7 %shard_map.46 = bf16[32,128,256]{2,1,0:T(8,128)(2,1)} custom-call(f32[32,384]{1,0:T(8,128)} %maximum_maximum_fusion.row_ref), custom_call_target="tpu_custom_call" | custom-call | tf_op jit(solution)/shard_map/pallas_call | solution.py:48
  36.3 0.2 slice.102
  36.5 0.4 maximum_convert_fusion
  36.9 0.8 fusion
  37.7 0.2 fusion.7
  37.9 0.9 fusion.20
  38.8 0.2 copy.19
  39.0 0.1 slice.97
  39.2 0.9 copy.21
  40.0 1.3 copy.18
  41.3 0.9 slice.95
  42.2 1.1 copy.20
  43.4 1.9 %fusion.4 = f32[4,128,32,16]{1,3,0,2:T(8,128)S(1)} fusion(bf16[32,128,256]{2,1,0:T(8,128)(2,1)S(1)} %copy-done, bf16[4,128,32,16]{1,3,0,2:T(8,128)(2,1)} %copy.21, bf16[4,128,32,16]{1,3,0,2:T(8,128)(2,1)S(1)} %copy.20), kind=kOutput, calls=%fused_computation.8 | convolution fusion | flops 136314880 | bytes 4194304 | tf_op jit(solution)/shard_map/gij,bjgc->bigc/dot_general | solution.py:149
  45.3 0.4 copy.22
  45.7 0.1 copy.28
  45.8 0.3 copy.23
  46.1 0.2 maximum_convert_fusion.1
  46.3 0.4 fusion.10
  46.7 1.3 collective-permute-start.5
  48.0 1.9 %collective-permute-start.6 = (bf16[512,512]{1,0:T(8,128)(2,1)S(1)}, bf16[512,512]{1,0:T(8,128)(2,1)S(1)}, u32[]{:S(2)}, u32[]{:S(2)}) collective-permute-start(bf16[512,512]{1,0:T(8,128)(2,1)S(1)} %fusion.10), channel_id=1, source_target_pairs={{0,2},{2,4},{4,6},{1,3},{3,5},{5,7},{8,10},{10,12},{12,14},{9,11},... | collective-permute-start | bytes 1572872 | tf_op jit(solution)/shard_map/ppermute | solution.py:60
  49.9 1.3 collective-permute-start.3
  51.2 7.0 %collective-permute-start.4 = (bf16[512,512]{1,0:T(8,128)(2,1)S(1)}, bf16[512,512]{1,0:T(8,128)(2,1)S(1)}, u32[]{:S(2)}, u32[]{:S(2)}) collective-permute-start(bf16[512,512]{1,0:T(8,128)(2,1)S(1)} %fusion.10), channel_id=1, source_target_pairs={{0,4},{2,6},{1,5},{3,7},{8,12},{10,14},{9,13},{11,15},{16,20},{18,... | collective-permute-start | bytes 1572872 | tf_op jit(solution)/shard_map/ppermute | solution.py:60
  58.2 1.3 collective-permute-start.1
  59.5 5.8 %collective-permute-done.5 = bf16[512,512]{1,0:T(8,128)(2,1)S(1)} collective-permute-done((bf16[512,512]{1,0:T(8,128)(2,1)S(1)}, bf16[512,512]{1,0:T(8,128)(2,1)S(1)}, u32[]{:S(2)}, u32[]{:S(2)}) %collective-permute-start.5) | collective-permute-done | bytes 524320 | tf_op jit(solution)/shard_map/ppermute | solution.py:60
  65.3 1.4 %collective-permute-start.2 = (bf16[512,512]{1,0:T(8,128)(2,1)S(1)}, bf16[512,512]{1,0:T(8,128)(2,1)S(1)}, u32[]{:S(2)}, u32[]{:S(2)}) collective-permute-start(bf16[512,512]{1,0:T(8,128)(2,1)S(1)} %fusion.10), channel_id=1, source_target_pairs={{0,6},{1,7},{8,14},{9,15},{16,22},{17,23},{24,30},{25,31},{32,38},... | collective-permute-start | bytes 1572872 | tf_op jit(solution)/shard_map/ppermute | solution.py:60
  66.7 0.1 select_bitcast_fusion
  66.8 17.8 %collective-permute-done.3 = bf16[512,512]{1,0:T(8,128)(2,1)S(1)} collective-permute-done((bf16[512,512]{1,0:T(8,128)(2,1)S(1)}, bf16[512,512]{1,0:T(8,128)(2,1)S(1)}, u32[]{:S(2)}, u32[]{:S(2)}) %collective-permute-start.3) | collective-permute-done | bytes 524320 | tf_op jit(solution)/shard_map/ppermute | solution.py:60
  84.6 0.1 select_bitcast_fusion.1
  84.7 0.8 collective-permute-done.1
  85.5 0.1 select_bitcast_fusion.2
  85.6 0.3 pad_maximum_fusion.piece_ref
  85.8 1.9 %collective-permute-start.7 = (bf16[4,512,512]{2,1,0:T(8,128)(2,1)S(1)}, bf16[4,512,512]{2,1,0:T(8,128)(2,1)}, u32[]{:S(2)}, u32[]{:S(2)}) collective-permute-start(bf16[4,512,512]{2,1,0:T(8,128)(2,1)S(1)} %pad_maximum_fusion.piece_ref), channel_id=1, source_target_pairs={{0,1},{1,0},{2,3},{3,2},{4,5},{5,4},{6,7},{7,6},{8,9},{9,8},{10,11... | collective-permute-start | bytes 6291464 | tf_op jit(solution)/shard_map/ppermute | solution.py:155
  87.8 0.6 pad_add_fusion.table_ref
  88.4 0.6 pad_add_fusion.1.table_ref
  89.0 22.6 %all-gather.3.cloned.1.call-done = bf16[64,64,512]{2,1,0:T(8,128)(2,1)} async-done(((bf16[2,64,512]{2,1,0:T(8,128)(2,1)}), bf16[64,64,512]{2,1,0:T(8,128)(2,1)}) %all-gather.3.cloned.1.call-update) | async-done | bytes 4194320 | tf_op jit(solution)/shard_map/all_gather | solution.py:135
  111.6 5.7 %shard_map.47.carry_ref = f32[512,512]{1,0:T(8,128)} custom-call(s32[2,4]{1,0:T(2,128)} %pad_add_fusion.1.table_ref, bf16[4,512,512]{2,1,0:T(8,128)(2,1)} %copy-done.1, bf16[4,8,2,64,512]{4,3,2,1,0:T(8,128)(2,1)} %bitcast.46), custom_call_target="tpu_custom_call" | custom-call | tf_op jit(solution)/shard_map/pallas_call | solution.py:120
  117.4 5.8 %shard_map.48 = bf16[512,512]{1,0:T(8,128)(2,1)} custom-call(s32[2,4]{1,0:T(2,128)} %pad_add_fusion.table_ref, bf16[4,512,512]{2,1,0:T(8,128)(2,1)} %collective-permute-done.7.piece_ref, bf16[4,8,2,64,512]{4,3,2,1,0:T(8,128)(2,1)} %bitcast.47, f32[512,512]{1,0:T(8,128)} %shard_map.47.carry_ref), custom_call_target="tpu_custom_call" | custom-call | tf_op jit(solution)/shard_map/pallas_call | solution.py:120
  (27 shorter events, 0.2 us)
Async XLA Ops:
  6.5 23.3 %copy-start.3 = (f32[3,3,512]{2,1,0:T(4,128)S(1)}, f32[3,3,512]{2,1,0:T(4,128)}, u32[]{:S(2)}) copy-start(f32[3,3,512]{2,1,0:T(4,128)} %param.5) | copy-start | bytes 55300
  6.5 105.1 %all-gather.3.cloned.1.call-start = ((), (), s32[]{:S(2)}) async-start(), calls=%async_computation | async-start | bytes 4325376 | tf_op jit(solution)/shard_map/all_gather | solution.py:135
  6.5 14.4 %collective-permute-start.8 = (bf16[64,512]{1,0:T(8,128)(2,1)}, bf16[64,512]{1,0:T(8,128)(2,1)S(1)}, u32[]{:S(2)}, u32[]{:S(2)}) collective-permute-start(bf16[64,512]{1,0:T(8,128)(2,1)} %param.7), channel_id=1, source_target_pairs={{0,256},{256,0},{1,257},{257,1},{2,258},{258,2},{3,259},{259,3},{4... | collective-permute-start | bytes 196616 | tf_op jit(solution)/shard_map/ppermute | solution.py:132
  25.5 10.8 %collective-permute-start = (bf16[131,2,512]{2,1,0:T(2,128)(2,1)}, bf16[131,2,512]{2,1,0:T(2,128)(2,1)S(1)}, u32[]{:S(2)}, u32[]{:S(2)}) collective-permute-start(bf16[131,2,512]{2,1,0:T(2,128)(2,1)} %pad_maximum_fusion.1), channel_id=1, source_target_pairs={{0,8},{8,16},{16,24},{24,32},{32,40},{40,48},{48,56},{56,64},{64,7... | collective-permute-start | bytes 804872 | tf_op jit(solution)/shard_map/ppermute | solution.py:20
  30.5 5.7 %copy-start.2 = (bf16[512,3,512]{2,0,1:T(8,128)(2,1)S(1)}, bf16[512,3,512]{2,0,1:T(8,128)(2,1)}, u32[]{:S(2)}) copy-start(bf16[512,3,512]{2,0,1:T(8,128)(2,1)} %param.4) | copy-start | bytes 4718596
  30.5 6.0 %slice-start = ((bf16[512,3,512]{2,0,1:T(8,128)(2,1)}), bf16[512,2,512]{2,0,1:T(8,128)(2,1)S(1)}, s32[]{:S(2)}) async-start(bf16[512,3,512]{2,0,1:T(8,128)(2,1)} %param.4), calls=%async_computation.1 | async-start | bytes 2097152 | tf_op jit(solution)/shard_map/slice | solution.py:140
  39.1 4.2 %copy-start = (bf16[32,128,256]{2,1,0:T(8,128)(2,1)S(1)}, bf16[32,128,256]{2,1,0:T(8,128)(2,1)}, u32[]{:S(2)}) copy-start(bf16[32,128,256]{2,1,0:T(8,128)(2,1)} %shard_map.46) | copy-start | bytes 6291460
  46.7 18.7 %collective-permute-start.5 = (bf16[512,512]{1,0:T(8,128)(2,1)S(1)}, bf16[512,512]{1,0:T(8,128)(2,1)S(1)}, u32[]{:S(2)}, u32[]{:S(2)}) collective-permute-start(bf16[512,512]{1,0:T(8,128)(2,1)S(1)} %fusion.10), channel_id=1, source_target_pairs={{6,0},{7,1},{14,8},{15,9},{22,16},{23,17},{30,24},{31,25},{38,32},... | collective-permute-start | bytes 1572872 | tf_op jit(solution)/shard_map/ppermute | solution.py:60
  48.0 18.8 %collective-permute-start.6 = (bf16[512,512]{1,0:T(8,128)(2,1)S(1)}, bf16[512,512]{1,0:T(8,128)(2,1)S(1)}, u32[]{:S(2)}, u32[]{:S(2)}) collective-permute-start(bf16[512,512]{1,0:T(8,128)(2,1)S(1)} %fusion.10), channel_id=1, source_target_pairs={{0,2},{2,4},{4,6},{1,3},{3,5},{5,7},{8,10},{10,12},{12,14},{9,11},... | collective-permute-start | bytes 1572872 | tf_op jit(solution)/shard_map/ppermute | solution.py:60
  49.9 34.8 %collective-permute-start.3 = (bf16[512,512]{1,0:T(8,128)(2,1)S(1)}, bf16[512,512]{1,0:T(8,128)(2,1)S(1)}, u32[]{:S(2)}, u32[]{:S(2)}) collective-permute-start(bf16[512,512]{1,0:T(8,128)(2,1)S(1)} %fusion.10), channel_id=1, source_target_pairs={{4,0},{6,2},{5,1},{7,3},{12,8},{14,10},{13,9},{15,11},{20,16},{22,... | collective-permute-start | bytes 1572872 | tf_op jit(solution)/shard_map/ppermute | solution.py:60
  51.2 33.5 %collective-permute-start.4 = (bf16[512,512]{1,0:T(8,128)(2,1)S(1)}, bf16[512,512]{1,0:T(8,128)(2,1)S(1)}, u32[]{:S(2)}, u32[]{:S(2)}) collective-permute-start(bf16[512,512]{1,0:T(8,128)(2,1)S(1)} %fusion.10), channel_id=1, source_target_pairs={{0,4},{2,6},{1,5},{3,7},{8,12},{10,14},{9,13},{11,15},{16,20},{18,... | collective-permute-start | bytes 1572872 | tf_op jit(solution)/shard_map/ppermute | solution.py:60
  58.2 27.3 %collective-permute-start.1 = (bf16[512,512]{1,0:T(8,128)(2,1)S(1)}, bf16[512,512]{1,0:T(8,128)(2,1)S(1)}, u32[]{:S(2)}, u32[]{:S(2)}) collective-permute-start(bf16[512,512]{1,0:T(8,128)(2,1)S(1)} %fusion.10), channel_id=1, source_target_pairs={{2,0},{4,2},{6,4},{3,1},{5,3},{7,5},{10,8},{12,10},{14,12},{11,9},... | collective-permute-start | bytes 1572872 | tf_op jit(solution)/shard_map/ppermute | solution.py:60
  65.3 20.2 %collective-permute-start.2 = (bf16[512,512]{1,0:T(8,128)(2,1)S(1)}, bf16[512,512]{1,0:T(8,128)(2,1)S(1)}, u32[]{:S(2)}, u32[]{:S(2)}) collective-permute-start(bf16[512,512]{1,0:T(8,128)(2,1)S(1)} %fusion.10), channel_id=1, source_target_pairs={{0,6},{1,7},{8,14},{9,15},{16,22},{17,23},{24,30},{25,31},{32,38},... | collective-permute-start | bytes 1572872 | tf_op jit(solution)/shard_map/ppermute | solution.py:60
  85.8 25.8 %copy-start.1 = (bf16[4,512,512]{2,1,0:T(8,128)(2,1)}, bf16[4,512,512]{2,1,0:T(8,128)(2,1)S(1)}, u32[]{:S(2)}) copy-start(bf16[4,512,512]{2,1,0:T(8,128)(2,1)S(1)} %pad_maximum_fusion.piece_ref) | copy-start | bytes 6291460
  85.8 31.5 %collective-permute-start.7 = (bf16[4,512,512]{2,1,0:T(8,128)(2,1)S(1)}, bf16[4,512,512]{2,1,0:T(8,128)(2,1)}, u32[]{:S(2)}, u32[]{:S(2)}) collective-permute-start(bf16[4,512,512]{2,1,0:T(8,128)(2,1)S(1)} %pad_maximum_fusion.piece_ref), channel_id=1, source_target_pairs={{0,1},{1,0},{2,3},{3,2},{4,5},{5,4},{6,7},{7,6},{8,9},{9,8},{10,11... | collective-permute-start | bytes 6291464 | tf_op jit(solution)/shard_map/ppermute | solution.py:155
Sparse Core Ops, SparseCore 0:
  22.6 88.9 all-gather.2

commit v12 on v11

--- a/solution.py
+++ b/solution.py
@@ -64,46 +64,52 @@
     return jnp.stack(slots)
 
 
-def partial_kernel(table_ref, piece_ref, weight_ref, out_ref, acc_ref):
+def partial_kernel(table_ref, piece_ref, weight_a_ref, weight_b_ref, out_ref, acc_ref):
     k = pl.program_id(0)
 
     @pl.when(k == 0)
     def _():
         acc_ref[...] = jnp.zeros_like(acc_ref)
 
-    rows = weight_ref[0, :, 0]
-    rows = rows.reshape(-1, rows.shape[-1])
-    acc_ref[...] += jnp.dot(piece_ref[0], rows, preferred_element_type=jnp.float32)
+    acc_ref[...] += two_blocks(piece_ref, weight_a_ref, weight_b_ref)
 
     @pl.when(k == pl.num_programs(0) - 1)
     def _():
         out_ref[...] = acc_ref[...]
 
 
-def final_kernel(table_ref, piece_ref, weight_ref, carry_ref, out_ref, acc_ref):
+def final_kernel(table_ref, piece_ref, weight_a_ref, weight_b_ref, carry_ref, out_ref, acc_ref):
     k = pl.program_id(0)
 
     @pl.when(k == 0)
     def _():
         acc_ref[...] = carry_ref[...]
 
-    rows = weight_ref[0, :, 0]
-    rows = rows.reshape(-1, rows.shape[-1])
-    acc_ref[...] += jnp.dot(piece_ref[0], rows, preferred_element_type=jnp.float32)
+    acc_ref[...] += two_blocks(piece_ref, weight_a_ref, weight_b_ref)
 
     @pl.when(k == pl.num_programs(0) - 1)
     def _():
         out_ref[...] = acc_ref[...].astype(out_ref.dtype)
 
 
+def two_blocks(piece_ref, weight_a_ref, weight_b_ref):
+    rows_a = weight_a_ref[0, :, 0]
+    rows_b = weight_b_ref[0, :, 0]
+    rows_a = rows_a.reshape(-1, rows_a.shape[-1])
+    rows_b = rows_b.reshape(-1, rows_b.shape[-1])
+    total = jnp.dot(piece_ref[0], rows_a, preferred_element_type=jnp.float32)
+    return total + jnp.dot(piece_ref[1], rows_b, preferred_element_type=jnp.float32)
+
+
 def block_matmul(table, pieces, weight, carry=None):
     n, tok, width = pieces.shape
     _, ys, _, rows, cols = weight.shape
     in_specs = [
-        pl.BlockSpec((1, tok, width), lambda k, t: (k, 0, 0)),
-        pl.BlockSpec((1, ys, 1, rows, cols), lambda k, t: (t[0, k], 0, t[1, k], 0, 0)),
+        pl.BlockSpec((2, tok, width), lambda k, t: (k, 0, 0)),
+        pl.BlockSpec((1, ys, 1, rows, cols), lambda k, t: (t[0, 2 * k], 0, t[1, 2 * k], 0, 0)),
+        pl.BlockSpec((1, ys, 1, rows, cols), lambda k, t: (t[0, 2 * k + 1], 0, t[1, 2 * k + 1], 0, 0)),
     ]
-    args = [table, pieces, weight]
+    args = [table, pieces, weight, weight]
     if carry is None:
         kernel, out_dtype = partial_kernel, jnp.float32
     else:
@@ -112,7 +118,7 @@
         args.append(carry)
     grid_spec = pltpu.PrefetchScalarGridSpec(
         num_scalar_prefetch=1,
-        grid=(n,),
+        grid=(n // 2,),
         in_specs=in_specs,
         out_specs=pl.BlockSpec((tok, cols), lambda k, t: (0, 0)),
         scratch_shapes=[pltpu.VMEM((tok, cols), jnp.float32)],

time: 131 us -> 129 us (0.985)
  Pallas kernels: 17.3 us -> 15.5 us
    pallas_call x2, Pallas kernels: 11.6 us -> 9.85 us  [block_matmul(): pl.pallas_call(kernel, grid_spec=grid_spec, out_shape=jax.ShapeDtypeStruc...]
  transfers between devices with their start and end apart: 10 -> 10, of which waited for: 5 -> 5; matrix products, arithmetic and copies ran while one was open for 13% -> 13% of each run, Pallas kernels for 9% -> 8%
where the time goes in v12:
time: 129 us; the launch traced here: 128 us
  waiting for transfers between devices  50.5 us (39%)
  starting transfers between devices  30.6 us (24%)
  Pallas kernels  15.5 us (12%)
  between operations  13.7 us (11%)
  local copies, waits for them, and re-layouts  9.34 us (7%)
  other arithmetic  6.77 us (5%)
  matrix products  1.87 us (1%)
    ppermute x6, waiting for transfers between devices, line_slots(): received[d] = lax.ppermute(block, axis_name, pairs)  24.4 us
    all_gather x1, waiting for transfers between devices, on_device(): weight_xy = lax.all_gather(pair, ('x', 'y'), axis=0, tiled=False)  22.6 us
    ppermute x6, starting transfers between devices, line_slots(): received[d] = lax.ppermute(block, axis_name, pairs)  14.2 us
    ppermute x1, starting transfers between devices, on_device(): partner = lax.ppermute(out_weight, 'zh', [(0, 1), (1, 0)])  11 us
    pallas_call x2, Pallas kernels, block_matmul(): pl.pallas_call(kernel, grid_spec=grid_spec, out_shape=jax.ShapeDtypeStruc...  9.85 us
    pallas_call x1, Pallas kernels, toeplitz_blocks(): pl.pallas_call(toeplitz_kernel, out_shape=jax.ShapeDtypeStruct((groups, s...  5.7 us
    slice x7, local copies, waits for them, and re-layouts, on_device(): window = jnp.concatenate([blocks[:-1], blocks[1:]], axis=1)  5.42 us
    ppermute x1, starting transfers between devices, from_behind(): return lax.ppermute(array, SEQ, pairs)  3.47 us
  transfers between devices with their start and end apart: 10, of which 5 were waited for; matrix products, arithmetic and copies ran while one was open for 13% of the time, Pallas kernels for 8%

profile of v12, /device:TPU:8, one launch (start us, length us, event | category | flops | bytes accessed | tf_op | source)
XLA Modules:
  0.0 128.3 jit_solution(3048494057048901910)
XLA Ops:
  6.5 11.0 %collective-permute-start.8 = (bf16[64,512]{1,0:T(8,128)(2,1)}, bf16[64,512]{1,0:T(8,128)(2,1)S(1)}, u32[]{:S(2)}, u32[]{:S(2)}) collective-permute-start(bf16[64,512]{1,0:T(8,128)(2,1)} %param.7), channel_id=1, source_target_pairs={{0,256},{256,0},{1,257},{257,1},{2,258},{258,2},{3,259},{259,3},{4... | collective-permute-start | bytes 196616 | tf_op jit(solution)/shard_map/ppermute | solution.py:138
  17.6 3.4 %collective-permute-done.8 = bf16[64,512]{1,0:T(8,128)(2,1)S(1)} collective-permute-done((bf16[64,512]{1,0:T(8,128)(2,1)}, bf16[64,512]{1,0:T(8,128)(2,1)S(1)}, u32[]{:S(2)}, u32[]{:S(2)}) %collective-permute-start.8) | collective-permute-done | bytes 65568 | tf_op jit(solution)/shard_map/ppermute | solution.py:138
  20.9 1.5 %pad_maximum_fusion.2 = bf16[2,64,512]{2,1,0:T(8,128)(2,1)} fusion(bf16[1,64,512]{2,1,0:T(8,128)(2,1)S(1)} %bitcast.54, bf16[1,64,512]{2,1,0:T(8,128)(2,1)} %bitcast.53), kind=kLoop, calls=%fused_computation.29 | loop fusion | flops 65536 | bytes 262144 | tf_op jit(solution)/shard_map/stack | solution.py:140
  22.5 1.0 slice.75
  23.5 0.2 copy.25
  23.7 0.7 slice_bitcast_fusion.5
  24.4 1.1 pad_maximum_fusion.1
  25.5 3.5 %collective-permute-start = (bf16[131,2,512]{2,1,0:T(2,128)(2,1)}, bf16[131,2,512]{2,1,0:T(2,128)(2,1)S(1)}, u32[]{:S(2)}, u32[]{:S(2)}) collective-permute-start(bf16[131,2,512]{2,1,0:T(2,128)(2,1)} %pad_maximum_fusion.1), channel_id=1, source_target_pairs={{0,8},{8,16},{16,24},{24,32},{32,40},{40,48},{48,56},{56,64},{64,7... | collective-permute-start | bytes 804872 | tf_op jit(solution)/shard_map/ppermute | solution.py:20
  29.0 0.8 rev.3
  29.7 0.1 pad.10.clone
  29.8 0.7 maximum_maximum_fusion.row_ref
  30.6 5.7 %shard_map.46 = bf16[32,128,256]{2,1,0:T(8,128)(2,1)} custom-call(f32[32,384]{1,0:T(8,128)} %maximum_maximum_fusion.row_ref), custom_call_target="tpu_custom_call" | custom-call | tf_op jit(solution)/shard_map/pallas_call | solution.py:48
  36.3 0.2 slice.102
  36.5 0.4 maximum_convert_fusion
  36.9 0.8 fusion
  37.7 0.2 fusion.7
  37.9 0.9 fusion.20
  38.8 0.2 copy.19
  39.0 0.1 slice.97
  39.2 0.9 copy.21
  40.0 1.3 copy.18
  41.3 0.9 slice.95
  42.2 1.1 copy.20
  43.4 1.9 %fusion.4 = f32[4,128,32,16]{1,3,0,2:T(8,128)S(1)} fusion(bf16[32,128,256]{2,1,0:T(8,128)(2,1)S(1)} %copy-done, bf16[4,128,32,16]{1,3,0,2:T(8,128)(2,1)} %copy.21, bf16[4,128,32,16]{1,3,0,2:T(8,128)(2,1)S(1)} %copy.20), kind=kOutput, calls=%fused_computation.8 | convolution fusion | flops 136314880 | bytes 4194304 | tf_op jit(solution)/shard_map/gij,bjgc->bigc/dot_general | solution.py:155
  45.3 0.4 copy.22
  45.7 0.1 copy.28
  45.8 0.3 copy.23
  46.1 0.2 maximum_convert_fusion.1
  46.3 0.4 fusion.10
  46.7 1.3 %collective-permute-start.5 = (bf16[512,512]{1,0:T(8,128)(2,1)S(1)}, bf16[512,512]{1,0:T(8,128)(2,1)S(1)}, u32[]{:S(2)}, u32[]{:S(2)}) collective-permute-start(bf16[512,512]{1,0:T(8,128)(2,1)S(1)} %fusion.10), channel_id=1, source_target_pairs={{6,0},{7,1},{14,8},{15,9},{22,16},{23,17},{30,24},{31,25},{38,32},... | collective-permute-start | bytes 1572872 | tf_op jit(solution)/shard_map/ppermute | solution.py:60
  48.0 1.9 %collective-permute-start.6 = (bf16[512,512]{1,0:T(8,128)(2,1)S(1)}, bf16[512,512]{1,0:T(8,128)(2,1)S(1)}, u32[]{:S(2)}, u32[]{:S(2)}) collective-permute-start(bf16[512,512]{1,0:T(8,128)(2,1)S(1)} %fusion.10), channel_id=1, source_target_pairs={{0,2},{2,4},{4,6},{1,3},{3,5},{5,7},{8,10},{10,12},{12,14},{9,11},... | collective-permute-start | bytes 1572872 | tf_op jit(solution)/shard_map/ppermute | solution.py:60
  49.9 1.3 %collective-permute-start.3 = (bf16[512,512]{1,0:T(8,128)(2,1)S(1)}, bf16[512,512]{1,0:T(8,128)(2,1)S(1)}, u32[]{:S(2)}, u32[]{:S(2)}) collective-permute-start(bf16[512,512]{1,0:T(8,128)(2,1)S(1)} %fusion.10), channel_id=1, source_target_pairs={{4,0},{6,2},{5,1},{7,3},{12,8},{14,10},{13,9},{15,11},{20,16},{22,... | collective-permute-start | bytes 1572872 | tf_op jit(solution)/shard_map/ppermute | solution.py:60
  51.2 7.0 %collective-permute-start.4 = (bf16[512,512]{1,0:T(8,128)(2,1)S(1)}, bf16[512,512]{1,0:T(8,128)(2,1)S(1)}, u32[]{:S(2)}, u32[]{:S(2)}) collective-permute-start(bf16[512,512]{1,0:T(8,128)(2,1)S(1)} %fusion.10), channel_id=1, source_target_pairs={{0,4},{2,6},{1,5},{3,7},{8,12},{10,14},{9,13},{11,15},{16,20},{18,... | collective-permute-start | bytes 1572872 | tf_op jit(solution)/shard_map/ppermute | solution.py:60
  58.2 1.3 %collective-permute-start.1 = (bf16[512,512]{1,0:T(8,128)(2,1)S(1)}, bf16[512,512]{1,0:T(8,128)(2,1)S(1)}, u32[]{:S(2)}, u32[]{:S(2)}) collective-permute-start(bf16[512,512]{1,0:T(8,128)(2,1)S(1)} %fusion.10), channel_id=1, source_target_pairs={{2,0},{4,2},{6,4},{3,1},{5,3},{7,5},{10,8},{12,10},{14,12},{11,9},... | collective-permute-start | bytes 1572872 | tf_op jit(solution)/shard_map/ppermute | solution.py:60
  59.5 5.8 %collective-permute-done.5 = bf16[512,512]{1,0:T(8,128)(2,1)S(1)} collective-permute-done((bf16[512,512]{1,0:T(8,128)(2,1)S(1)}, bf16[512,512]{1,0:T(8,128)(2,1)S(1)}, u32[]{:S(2)}, u32[]{:S(2)}) %collective-permute-start.5) | collective-permute-done | bytes 524320 | tf_op jit(solution)/shard_map/ppermute | solution.py:60
  65.3 1.4 %collective-permute-start.2 = (bf16[512,512]{1,0:T(8,128)(2,1)S(1)}, bf16[512,512]{1,0:T(8,128)(2,1)S(1)}, u32[]{:S(2)}, u32[]{:S(2)}) collective-permute-start(bf16[512,512]{1,0:T(8,128)(2,1)S(1)} %fusion.10), channel_id=1, source_target_pairs={{0,6},{1,7},{8,14},{9,15},{16,22},{17,23},{24,30},{25,31},{32,38},... | collective-permute-start | bytes 1572872 | tf_op jit(solution)/shard_map/ppermute | solution.py:60
  66.7 0.1 select_bitcast_fusion
  66.8 17.8 %collective-permute-done.3 = bf16[512,512]{1,0:T(8,128)(2,1)S(1)} collective-permute-done((bf16[512,512]{1,0:T(8,128)(2,1)S(1)}, bf16[512,512]{1,0:T(8,128)(2,1)S(1)}, u32[]{:S(2)}, u32[]{:S(2)}) %collective-permute-start.3) | collective-permute-done | bytes 524320 | tf_op jit(solution)/shard_map/ppermute | solution.py:60
  84.6 0.1 select_bitcast_fusion.1
  84.7 0.8 collective-permute-done.1
  85.5 0.1 select_bitcast_fusion.2
  85.6 0.3 pad_maximum_fusion.piece_ref
  85.8 1.9 %collective-permute-start.7 = (bf16[4,512,512]{2,1,0:T(8,128)(2,1)S(1)}, bf16[4,512,512]{2,1,0:T(8,128)(2,1)}, u32[]{:S(2)}, u32[]{:S(2)}) collective-permute-start(bf16[4,512,512]{2,1,0:T(8,128)(2,1)S(1)} %pad_maximum_fusion.piece_ref), channel_id=1, source_target_pairs={{0,1},{1,0},{2,3},{3,2},{4,5},{5,4},{6,7},{7,6},{8,9},{9,8},{10,11... | collective-permute-start | bytes 6291464 | tf_op jit(solution)/shard_map/ppermute | solution.py:161
  87.8 0.6 pad_add_fusion.table_ref
  88.4 0.6 pad_add_fusion.1.table_ref
  89.0 22.6 %all-gather.3.cloned.1.call-done = bf16[64,64,512]{2,1,0:T(8,128)(2,1)} async-done(((bf16[2,64,512]{2,1,0:T(8,128)(2,1)}), bf16[64,64,512]{2,1,0:T(8,128)(2,1)}) %all-gather.3.cloned.1.call-update) | async-done | bytes 4194320 | tf_op jit(solution)/shard_map/all_gather | solution.py:141
  111.6 4.9 %shard_map.47.carry_ref = f32[512,512]{1,0:T(8,128)} custom-call(s32[2,4]{1,0:T(2,128)} %pad_add_fusion.1.table_ref, bf16[4,512,512]{2,1,0:T(8,128)(2,1)} %copy-done.1, bf16[4,8,2,64,512]{4,3,2,1,0:T(8,128)(2,1)} %bitcast.46, bf16[4,8,2,64,512]{4,3,2,1,0:T(8,128)(2,1)} %bitcast.47), custom_call_target="tpu_custom_call" | custom-call | tf_op jit(solution)/shard_map/pallas_call | solution.py:126
  116.5 5.0 %shard_map.48 = bf16[512,512]{1,0:T(8,128)(2,1)} custom-call(s32[2,4]{1,0:T(2,128)} %pad_add_fusion.table_ref, bf16[4,512,512]{2,1,0:T(8,128)(2,1)} %collective-permute-done.7.piece_ref, bf16[4,8,2,64,512]{4,3,2,1,0:T(8,128)(2,1)} %bitcast.48, bf16[4,8,2,64,512]{4,3,2,1,0:T(8,128)(2,1)} %bitcast.49, f32[512,512]{1,0:T(8,128)} %shard_map.47.carry_ref), custom_call_target="tpu_custom_call" | custom-call | tf_op jit(solution)/shard_map/pallas_call | solution.py:126
  (27 shorter events, 0.2 us)
Async XLA Ops:
  6.5 23.3 %copy-start.3 = (f32[3,3,512]{2,1,0:T(4,128)S(1)}, f32[3,3,512]{2,1,0:T(4,128)}, u32[]{:S(2)}) copy-start(f32[3,3,512]{2,1,0:T(4,128)} %param.5) | copy-start | bytes 55300
  6.5 105.1 %all-gather.3.cloned.1.call-start = ((), (), s32[]{:S(2)}) async-start(), calls=%async_computation | async-start | bytes 4325376 | tf_op jit(solution)/shard_map/all_gather | solution.py:141
  6.5 14.4 %collective-permute-start.8 = (bf16[64,512]{1,0:T(8,128)(2,1)}, bf16[64,512]{1,0:T(8,128)(2,1)S(1)}, u32[]{:S(2)}, u32[]{:S(2)}) collective-permute-start(bf16[64,512]{1,0:T(8,128)(2,1)} %param.7), channel_id=1, source_target_pairs={{0,256},{256,0},{1,257},{257,1},{2,258},{258,2},{3,259},{259,3},{4... | collective-permute-start | bytes 196616 | tf_op jit(solution)/shard_map/ppermute | solution.py:138
  25.5 10.8 %collective-permute-start = (bf16[131,2,512]{2,1,0:T(2,128)(2,1)}, bf16[131,2,512]{2,1,0:T(2,128)(2,1)S(1)}, u32[]{:S(2)}, u32[]{:S(2)}) collective-permute-start(bf16[131,2,512]{2,1,0:T(2,128)(2,1)} %pad_maximum_fusion.1), channel_id=1, source_target_pairs={{0,8},{8,16},{16,24},{24,32},{32,40},{40,48},{48,56},{56,64},{64,7... | collective-permute-start | bytes 804872 | tf_op jit(solution)/shard_map/ppermute | solution.py:20
  30.5 5.7 %copy-start.2 = (bf16[512,3,512]{2,0,1:T(8,128)(2,1)S(1)}, bf16[512,3,512]{2,0,1:T(8,128)(2,1)}, u32[]{:S(2)}) copy-start(bf16[512,3,512]{2,0,1:T(8,128)(2,1)} %param.4) | copy-start | bytes 4718596
  30.5 6.0 %slice-start = ((bf16[512,3,512]{2,0,1:T(8,128)(2,1)}), bf16[512,2,512]{2,0,1:T(8,128)(2,1)S(1)}, s32[]{:S(2)}) async-start(bf16[512,3,512]{2,0,1:T(8,128)(2,1)} %param.4), calls=%async_computation.1 | async-start | bytes 2097152 | tf_op jit(solution)/shard_map/slice | solution.py:146
  39.1 4.2 %copy-start = (bf16[32,128,256]{2,1,0:T(8,128)(2,1)S(1)}, bf16[32,128,256]{2,1,0:T(8,128)(2,1)}, u32[]{:S(2)}) copy-start(bf16[32,128,256]{2,1,0:T(8,128)(2,1)} %shard_map.46) | copy-start | bytes 6291460
  46.7 18.7 %collective-permute-start.5 = (bf16[512,512]{1,0:T(8,128)(2,1)S(1)}, bf16[512,512]{1,0:T(8,128)(2,1)S(1)}, u32[]{:S(2)}, u32[]{:S(2)}) collective-permute-start(bf16[512,512]{1,0:T(8,128)(2,1)S(1)} %fusion.10), channel_id=1, source_target_pairs={{6,0},{7,1},{14,8},{15,9},{22,16},{23,17},{30,24},{31,25},{38,32},... | collective-permute-start | bytes 1572872 | tf_op jit(solution)/shard_map/ppermute | solution.py:60
  48.0 18.8 %collective-permute-start.6 = (bf16[512,512]{1,0:T(8,128)(2,1)S(1)}, bf16[512,512]{1,0:T(8,128)(2,1)S(1)}, u32[]{:S(2)}, u32[]{:S(2)}) collective-permute-start(bf16[512,512]{1,0:T(8,128)(2,1)S(1)} %fusion.10), channel_id=1, source_target_pairs={{0,2},{2,4},{4,6},{1,3},{3,5},{5,7},{8,10},{10,12},{12,14},{9,11},... | collective-permute-start | bytes 1572872 | tf_op jit(solution)/shard_map/ppermute | solution.py:60
  49.9 34.8 %collective-permute-start.3 = (bf16[512,512]{1,0:T(8,128)(2,1)S(1)}, bf16[512,512]{1,0:T(8,128)(2,1)S(1)}, u32[]{:S(2)}, u32[]{:S(2)}) collective-permute-start(bf16[512,512]{1,0:T(8,128)(2,1)S(1)} %fusion.10), channel_id=1, source_target_pairs={{4,0},{6,2},{5,1},{7,3},{12,8},{14,10},{13,9},{15,11},{20,16},{22,... | collective-permute-start | bytes 1572872 | tf_op jit(solution)/shard_map/ppermute | solution.py:60
  51.2 33.5 %collective-permute-start.4 = (bf16[512,512]{1,0:T(8,128)(2,1)S(1)}, bf16[512,512]{1,0:T(8,128)(2,1)S(1)}, u32[]{:S(2)}, u32[]{:S(2)}) collective-permute-start(bf16[512,512]{1,0:T(8,128)(2,1)S(1)} %fusion.10), channel_id=1, source_target_pairs={{0,4},{2,6},{1,5},{3,7},{8,12},{10,14},{9,13},{11,15},{16,20},{18,... | collective-permute-start | bytes 1572872 | tf_op jit(solution)/shard_map/ppermute | solution.py:60
  58.2 27.3 %collective-permute-start.1 = (bf16[512,512]{1,0:T(8,128)(2,1)S(1)}, bf16[512,512]{1,0:T(8,128)(2,1)S(1)}, u32[]{:S(2)}, u32[]{:S(2)}) collective-permute-start(bf16[512,512]{1,0:T(8,128)(2,1)S(1)} %fusion.10), channel_id=1, source_target_pairs={{2,0},{4,2},{6,4},{3,1},{5,3},{7,5},{10,8},{12,10},{14,12},{11,9},... | collective-permute-start | bytes 1572872 | tf_op jit(solution)/shard_map/ppermute | solution.py:60
  65.3 20.2 %collective-permute-start.2 = (bf16[512,512]{1,0:T(8,128)(2,1)S(1)}, bf16[512,512]{1,0:T(8,128)(2,1)S(1)}, u32[]{:S(2)}, u32[]{:S(2)}) collective-permute-start(bf16[512,512]{1,0:T(8,128)(2,1)S(1)} %fusion.10), channel_id=1, source_target_pairs={{0,6},{1,7},{8,14},{9,15},{16,22},{17,23},{24,30},{25,31},{32,38},... | collective-permute-start | bytes 1572872 | tf_op jit(solution)/shard_map/ppermute | solution.py:60
  85.8 25.8 %copy-start.1 = (bf16[4,512,512]{2,1,0:T(8,128)(2,1)}, bf16[4,512,512]{2,1,0:T(8,128)(2,1)S(1)}, u32[]{:S(2)}) copy-start(bf16[4,512,512]{2,1,0:T(8,128)(2,1)S(1)} %pad_maximum_fusion.piece_ref) | copy-start | bytes 6291460
  85.8 30.7 %collective-permute-start.7 = (bf16[4,512,512]{2,1,0:T(8,128)(2,1)S(1)}, bf16[4,512,512]{2,1,0:T(8,128)(2,1)}, u32[]{:S(2)}, u32[]{:S(2)}) collective-permute-start(bf16[4,512,512]{2,1,0:T(8,128)(2,1)S(1)} %pad_maximum_fusion.piece_ref), channel_id=1, source_target_pairs={{0,1},{1,0},{2,3},{3,2},{4,5},{5,4},{6,7},{7,6},{8,9},{9,8},{10,11... | collective-permute-start | bytes 6291464 | tf_op jit(solution)/shard_map/ppermute | solution.py:161
Sparse Core Ops, SparseCore 0:
  22.6 88.9 all-gather.2

commit v13 on v12

--- a/solution.py
+++ b/solution.py
@@ -64,28 +64,21 @@
     return jnp.stack(slots)
 
 
-def partial_kernel(table_ref, piece_ref, weight_a_ref, weight_b_ref, out_ref, acc_ref):
+def matmul_kernel(table_ref, own_ref, other_ref, weight_a_ref, weight_b_ref, out_ref, acc_ref):
     k = pl.program_id(0)
+    half = pl.num_programs(0) // 2
 
     @pl.when(k == 0)
     def _():
         acc_ref[...] = jnp.zeros_like(acc_ref)
 
-    acc_ref[...] += two_blocks(piece_ref, weight_a_ref, weight_b_ref)
+    @pl.when(k < half)
+    def _():
+        acc_ref[...] += two_blocks(own_ref, weight_a_ref, weight_b_ref)
 
-    @pl.when(k == pl.num_programs(0) - 1)
+    @pl.when(k >= half)
     def _():
-        out_ref[...] = acc_ref[...]
-
-
-def final_kernel(table_ref, piece_ref, weight_a_ref, weight_b_ref, carry_ref, out_ref, acc_ref):
-    k = pl.program_id(0)
-
-    @pl.when(k == 0)
-    def _():
-        acc_ref[...] = carry_ref[...]
-
-    acc_ref[...] += two_blocks(piece_ref, weight_a_ref, weight_b_ref)
+        acc_ref[...] += two_blocks(other_ref, weight_a_ref, weight_b_ref)
 
     @pl.when(k == pl.num_programs(0) - 1)
     def _():
@@ -101,33 +94,28 @@
     return total + jnp.dot(piece_ref[1], rows_b, preferred_element_type=jnp.float32)
 
 
-def block_matmul(table, pieces, weight, carry=None):
-    n, tok, width = pieces.shape
+def block_matmul(table, own, other, weight):
+    n, tok, width = own.shape
     _, ys, _, rows, cols = weight.shape
+    steps = n // 2
     in_specs = [
-        pl.BlockSpec((2, tok, width), lambda k, t: (k, 0, 0)),
+        pl.BlockSpec((2, tok, width), lambda k, t: (jnp.minimum(k, steps - 1), 0, 0)),
+        pl.BlockSpec((2, tok, width), lambda k, t: (jnp.maximum(k - steps, 0), 0, 0)),
         pl.BlockSpec((1, ys, 1, rows, cols), lambda k, t: (t[0, 2 * k], 0, t[1, 2 * k], 0, 0)),
         pl.BlockSpec((1, ys, 1, rows, cols), lambda k, t: (t[0, 2 * k + 1], 0, t[1, 2 * k + 1], 0, 0)),
     ]
-    args = [table, pieces, weight, weight]
-    if carry is None:
-        kernel, out_dtype = partial_kernel, jnp.float32
-    else:
-        kernel, out_dtype = final_kernel, jnp.bfloat16
-        in_specs.append(pl.BlockSpec((tok, cols), lambda k, t: (0, 0)))
-        args.append(carry)
     grid_spec = pltpu.PrefetchScalarGridSpec(
         num_scalar_prefetch=1,
-        grid=(n // 2,),
+        grid=(2 * steps,),
         in_specs=in_specs,
         out_specs=pl.BlockSpec((tok, cols), lambda k, t: (0, 0)),
         scratch_shapes=[pltpu.VMEM((tok, cols), jnp.float32)],
     )
     return pl.pallas_call(
-        kernel,
+        matmul_kernel,
         grid_spec=grid_spec,
-        out_shape=jax.ShapeDtypeStruct((tok, cols), out_dtype),
-    )(*args)
+        out_shape=jax.ShapeDtypeStruct((tok, cols), jnp.bfloat16),
+    )(table, own, other, weight, weight)
 
 
 def on_device(projected, short_filter, long_filter, out_weight):
@@ -168,8 +156,8 @@
         return jnp.stack([w % 4, (w // 4 + zh) % 2]).astype(jnp.int32)
 
     weight = weight_xy.reshape(4, 8, *weight_xy.shape[1:])
-    carry = block_matmul(table_for(core), own, weight)
-    return block_matmul(table_for(1 - core), other, weight, carry)
+    table = jnp.concatenate([table_for(core), table_for(1 - core)], axis=1)
+    return block_matmul(table, own, other, weight)
 
 
 def solution(mesh):

time: 129 us -> 127 us (0.984)
  starting transfers between devices: 30.6 us -> 37.7 us
  waiting for transfers between devices: 50.5 us -> 43.8 us
  Pallas kernels: 15.5 us -> 13.1 us
    all_gather x1, waiting for transfers between devices: 22.6 us -> 8.29 us  [on_device(): weight_xy = lax.all_gather(pair, ('x', 'y'), axis=0, tiled=False)]
    ppermute x6, starting transfers between devices: 14.2 us -> 21.3 us  [line_slots(): received[d] = lax.ppermute(block, axis_name, pairs)]
    ppermute x6, waiting for transfers between devices: 24.4 us -> 28.6 us  [line_slots(): received[d] = lax.ppermute(block, axis_name, pairs)]
    ppermute x1, waiting for transfers between devices: 0.01 us -> 3.54 us  [on_device(): other = lax.ppermute(own, 'c', [(0, 1), (1, 0)])]
    pallas_call x2 -> x1, Pallas kernels: 9.85 us -> 7.36 us  [block_matmul(): pl.pallas_call(matmul_kernel, grid_spec=grid_spec, out_shape=jax.ShapeDty...]
  transfers between devices with their start and end apart: 10 -> 10, of which waited for: 5 -> 4; matrix products, arithmetic and copies ran while one was open for 13% -> 13% of each run, Pallas kernels for 8% -> 5%
where the time goes in v13:
time: 127 us; the launch traced here: 126 us
  waiting for transfers between devices  43.8 us (34%)
  starting transfers between devices  37.7 us (30%)
  between operations  13.7 us (11%)
  Pallas kernels  13.1 us (10%)
  local copies, waits for them, and re-layouts  9.34 us (7%)
  other arithmetic  6.29 us (5%)
  matrix products  1.88 us (1%)
    ppermute x6, waiting for transfers between devices, line_slots(): received[d] = lax.ppermute(block, axis_name, pairs)  28.6 us
    ppermute x6, starting transfers between devices, line_slots(): received[d] = lax.ppermute(block, axis_name, pairs)  21.3 us
    ppermute x1, starting transfers between devices, on_device(): partner = lax.ppermute(out_weight, 'zh', [(0, 1), (1, 0)])  11 us
    all_gather x1, waiting for transfers between devices, on_device(): weight_xy = lax.all_gather(pair, ('x', 'y'), axis=0, tiled=False)  8.29 us
    pallas_call x1, Pallas kernels, block_matmul(): pl.pallas_call(matmul_kernel, grid_spec=grid_spec, out_shape=jax.ShapeDty...  7.36 us
    pallas_call x1, Pallas kernels, toeplitz_blocks(): pl.pallas_call(toeplitz_kernel, out_shape=jax.ShapeDtypeStruct((groups, s...  5.7 us
    slice x7, local copies, waits for them, and re-layouts, on_device(): window = jnp.concatenate([blocks[:-1], blocks[1:]], axis=1)  5.42 us
    ppermute x1, waiting for transfers between devices, on_device(): other = lax.ppermute(own, 'c', [(0, 1), (1, 0)])  3.54 us
  transfers between devices with their start and end apart: 10, of which 4 were waited for; matrix products, arithmetic and copies ran while one was open for 13% of the time, Pallas kernels for 5%

profile of v13, /device:TPU:8, one launch (start us, length us, event | category | flops | bytes accessed | tf_op | source)
XLA Modules:
  0.0 125.8 jit_solution(10825559139233530899)
XLA Ops:
  6.5 11.0 %collective-permute-start.8 = (bf16[64,512]{1,0:T(8,128)(2,1)}, bf16[64,512]{1,0:T(8,128)(2,1)S(1)}, u32[]{:S(2)}, u32[]{:S(2)}) collective-permute-start(bf16[64,512]{1,0:T(8,128)(2,1)} %param.7), channel_id=1, source_target_pairs={{0,256},{256,0},{1,257},{257,1},{2,258},{258,2},{3,259},{259,3},{4... | collective-permute-start | bytes 196616 | tf_op jit(solution)/shard_map/ppermute | solution.py:126
  17.6 3.4 %collective-permute-done.8 = bf16[64,512]{1,0:T(8,128)(2,1)S(1)} collective-permute-done((bf16[64,512]{1,0:T(8,128)(2,1)}, bf16[64,512]{1,0:T(8,128)(2,1)S(1)}, u32[]{:S(2)}, u32[]{:S(2)}) %collective-permute-start.8) | collective-permute-done | bytes 65568 | tf_op jit(solution)/shard_map/ppermute | solution.py:126
  20.9 1.5 %pad_maximum_fusion.2 = bf16[2,64,512]{2,1,0:T(8,128)(2,1)} fusion(bf16[1,64,512]{2,1,0:T(8,128)(2,1)S(1)} %bitcast.52, bf16[1,64,512]{2,1,0:T(8,128)(2,1)} %bitcast.51), kind=kLoop, calls=%fused_computation.29 | loop fusion | flops 65536 | bytes 262144 | tf_op jit(solution)/shard_map/stack | solution.py:128
  22.4 0.0 all-gather.3.cloned.1.call-update
  22.5 1.0 slice.75
  23.5 0.2 copy.25
  23.7 0.7 slice_bitcast_fusion.5
  24.4 1.1 pad_maximum_fusion.1
  25.5 3.5 %collective-permute-start = (bf16[131,2,512]{2,1,0:T(2,128)(2,1)}, bf16[131,2,512]{2,1,0:T(2,128)(2,1)S(1)}, u32[]{:S(2)}, u32[]{:S(2)}) collective-permute-start(bf16[131,2,512]{2,1,0:T(2,128)(2,1)} %pad_maximum_fusion.1), channel_id=1, source_target_pairs={{0,8},{8,16},{16,24},{24,32},{32,40},{40,48},{48,56},{56,64},{64,7... | collective-permute-start | bytes 804872 | tf_op jit(solution)/shard_map/ppermute | solution.py:20
  29.0 0.8 rev.3
  29.7 0.1 pad.8.clone
  29.8 0.7 maximum_maximum_fusion.row_ref
  30.6 5.7 %shard_map.46 = bf16[32,128,256]{2,1,0:T(8,128)(2,1)} custom-call(f32[32,384]{1,0:T(8,128)} %maximum_maximum_fusion.row_ref), custom_call_target="tpu_custom_call" | custom-call | tf_op jit(solution)/shard_map/pallas_call | solution.py:48
  36.3 0.0 collective-permute-done
  36.3 0.2 slice.102
  36.5 0.4 maximum_convert_fusion
  36.9 0.8 fusion
  37.7 0.2 fusion.7
  37.9 0.9 fusion.20
  38.8 0.2 copy.18
  39.0 0.1 slice.95
  39.1 0.9 copy.20
  40.0 1.3 %copy.19 = bf16[512,1,512]{0,2,1:T(8,128)(2,1)S(1)} copy(bf16[512,1,512]{2,0,1:T(8,128)(2,1)} %get-tuple-element.6) | data formatting | bytes 1048576 | tf_op jit(solution)/shard_map/slice | solution.py:141
  41.3 0.9 slice.97
  42.2 1.1 copy.21
  43.4 1.9 %fusion.4 = f32[4,128,32,16]{1,3,0,2:T(8,128)S(1)} fusion(bf16[32,128,256]{2,1,0:T(8,128)(2,1)S(1)} %copy-done, bf16[4,128,32,16]{1,3,0,2:T(8,128)(2,1)S(1)} %copy.21, bf16[4,128,32,16]{1,3,0,2:T(8,128)(2,1)} %copy.20), kind=kOutput, calls=%fused_computation.8 | convolution fusion | flops 136314880 | bytes 4194304 | tf_op jit(solution)/shard_map/gij,bjgc->bigc/dot_general | solution.py:143
  45.3 0.4 copy.22
  45.7 0.1 copy.28
  45.8 0.3 copy.23
  46.1 0.2 maximum_convert_fusion.1
  46.3 0.4 fusion.10
  46.7 1.3 %collective-permute-start.1 = (bf16[512,512]{1,0:T(8,128)(2,1)S(1)}, bf16[512,512]{1,0:T(8,128)(2,1)S(1)}, u32[]{:S(2)}, u32[]{:S(2)}) collective-permute-start(bf16[512,512]{1,0:T(8,128)(2,1)S(1)} %fusion.10), channel_id=1, source_target_pairs={{2,0},{4,2},{6,4},{3,1},{5,3},{7,5},{10,8},{12,10},{14,12},{11,9},... | collective-permute-start | bytes 1572872 | tf_op jit(solution)/shard_map/ppermute | solution.py:60
  48.0 6.8 %collective-permute-start.2 = (bf16[512,512]{1,0:T(8,128)(2,1)S(1)}, bf16[512,512]{1,0:T(8,128)(2,1)S(1)}, u32[]{:S(2)}, u32[]{:S(2)}) collective-permute-start(bf16[512,512]{1,0:T(8,128)(2,1)S(1)} %fusion.10), channel_id=1, source_target_pairs={{0,6},{1,7},{8,14},{9,15},{16,22},{17,23},{24,30},{25,31},{32,38},... | collective-permute-start | bytes 1572872 | tf_op jit(solution)/shard_map/ppermute | solution.py:60
  54.8 1.3 %collective-permute-start.3 = (bf16[512,512]{1,0:T(8,128)(2,1)S(1)}, bf16[512,512]{1,0:T(8,128)(2,1)S(1)}, u32[]{:S(2)}, u32[]{:S(2)}) collective-permute-start(bf16[512,512]{1,0:T(8,128)(2,1)S(1)} %fusion.10), channel_id=1, source_target_pairs={{4,0},{6,2},{5,1},{7,3},{12,8},{14,10},{13,9},{15,11},{20,16},{22,... | collective-permute-start | bytes 1572872 | tf_op jit(solution)/shard_map/ppermute | solution.py:60
  56.1 5.5 %collective-permute-start.4 = (bf16[512,512]{1,0:T(8,128)(2,1)S(1)}, bf16[512,512]{1,0:T(8,128)(2,1)S(1)}, u32[]{:S(2)}, u32[]{:S(2)}) collective-permute-start(bf16[512,512]{1,0:T(8,128)(2,1)S(1)} %fusion.10), channel_id=1, source_target_pairs={{0,4},{2,6},{1,5},{3,7},{8,12},{10,14},{9,13},{11,15},{16,20},{18,... | collective-permute-start | bytes 1572872 | tf_op jit(solution)/shard_map/ppermute | solution.py:60
  61.6 1.3 %collective-permute-start.5 = (bf16[512,512]{1,0:T(8,128)(2,1)S(1)}, bf16[512,512]{1,0:T(8,128)(2,1)S(1)}, u32[]{:S(2)}, u32[]{:S(2)}) collective-permute-start(bf16[512,512]{1,0:T(8,128)(2,1)S(1)} %fusion.10), channel_id=1, source_target_pairs={{6,0},{7,1},{14,8},{15,9},{22,16},{23,17},{30,24},{31,25},{38,32},... | collective-permute-start | bytes 1572872 | tf_op jit(solution)/shard_map/ppermute | solution.py:60
  62.9 0.0 collective-permute-done.1
  62.9 5.1 %collective-permute-start.6 = (bf16[512,512]{1,0:T(8,128)(2,1)S(1)}, bf16[512,512]{1,0:T(8,128)(2,1)S(1)}, u32[]{:S(2)}, u32[]{:S(2)}) collective-permute-start(bf16[512,512]{1,0:T(8,128)(2,1)S(1)} %fusion.10), channel_id=1, source_target_pairs={{0,2},{2,4},{4,6},{1,3},{3,5},{5,7},{8,10},{10,12},{12,14},{9,11},... | collective-permute-start | bytes 1572872 | tf_op jit(solution)/shard_map/ppermute | solution.py:60
  68.0 0.1 select_bitcast_fusion.2
  68.1 28.6 %collective-permute-done.3 = bf16[512,512]{1,0:T(8,128)(2,1)S(1)} collective-permute-done((bf16[512,512]{1,0:T(8,128)(2,1)S(1)}, bf16[512,512]{1,0:T(8,128)(2,1)S(1)}, u32[]{:S(2)}, u32[]{:S(2)}) %collective-permute-start.3) | collective-permute-done | bytes 524320 | tf_op jit(solution)/shard_map/ppermute | solution.py:60
  96.7 0.1 select_bitcast_fusion.1
  96.8 0.1 select_bitcast_fusion
  96.9 0.3 pad_maximum_fusion.own_ref
  97.1 1.9 %collective-permute-start.7 = (bf16[4,512,512]{2,1,0:T(8,128)(2,1)S(1)}, bf16[4,512,512]{2,1,0:T(8,128)(2,1)}, u32[]{:S(2)}, u32[]{:S(2)}) collective-permute-start(bf16[4,512,512]{2,1,0:T(8,128)(2,1)S(1)} %pad_maximum_fusion.own_ref), channel_id=1, source_target_pairs={{0,1},{1,0},{2,3},{3,2},{4,5},{5,4},{6,7},{7,6},{8,9},{9,8},{10,11... | collective-permute-start | bytes 6291464 | tf_op jit(solution)/shard_map/ppermute | solution.py:149
  99.1 0.7 add_add_fusion.table_ref
  99.8 3.5 %collective-permute-done.7.other_ref = bf16[4,512,512]{2,1,0:T(8,128)(2,1)} collective-permute-done((bf16[4,512,512]{2,1,0:T(8,128)(2,1)S(1)}, bf16[4,512,512]{2,1,0:T(8,128)(2,1)}, u32[]{:S(2)}, u32[]{:S(2)}) %collective-permute-start.7) | collective-permute-done | bytes 2097184 | tf_op jit(solution)/shard_map/ppermute | solution.py:149
  103.3 8.3 %all-gather.3.cloned.1.call-done = bf16[64,64,512]{2,1,0:T(8,128)(2,1)} async-done(((bf16[2,64,512]{2,1,0:T(8,128)(2,1)}), bf16[64,64,512]{2,1,0:T(8,128)(2,1)}) %all-gather.3.cloned.1.call-update) | async-done | bytes 4194320 | tf_op jit(solution)/shard_map/all_gather | solution.py:129
  111.6 7.4 %shard_map.47 = bf16[512,512]{1,0:T(8,128)(2,1)} custom-call(s32[2,8]{1,0:T(2,128)} %add_add_fusion.table_ref, bf16[4,512,512]{2,1,0:T(8,128)(2,1)} %copy-done.1, bf16[4,512,512]{2,1,0:T(8,128)(2,1)} %collective-permute-done.7.other_ref, bf16[4,8,2,64,512]{4,3,2,1,0:T(8,128)(2,1)} %bitcast.46, bf16[4,8,2,64,512]{4,3,2,1,0:T(8,128)(2,1)} %bitcast.47), custom_call_target="tpu_custom_call" | custom-call | tf_op jit(solution)/shard_map/pallas_call | solution.py:114
  (25 shorter events, 0.2 us)
Async XLA Ops:
  6.5 23.3 %copy-start.3 = (f32[3,3,512]{2,1,0:T(4,128)S(1)}, f32[3,3,512]{2,1,0:T(4,128)}, u32[]{:S(2)}) copy-start(f32[3,3,512]{2,1,0:T(4,128)} %param.5) | copy-start | bytes 55300
  6.5 105.1 %all-gather.3.cloned.1.call-start = ((), (), s32[]{:S(2)}) async-start(), calls=%async_computation | async-start | bytes 4325376 | tf_op jit(solution)/shard_map/all_gather | solution.py:129
  6.5 14.4 %collective-permute-start.8 = (bf16[64,512]{1,0:T(8,128)(2,1)}, bf16[64,512]{1,0:T(8,128)(2,1)S(1)}, u32[]{:S(2)}, u32[]{:S(2)}) collective-permute-start(bf16[64,512]{1,0:T(8,128)(2,1)} %param.7), channel_id=1, source_target_pairs={{0,256},{256,0},{1,257},{257,1},{2,258},{258,2},{3,259},{259,3},{4... | collective-permute-start | bytes 196616 | tf_op jit(solution)/shard_map/ppermute | solution.py:126
  25.5 10.8 %collective-permute-start = (bf16[131,2,512]{2,1,0:T(2,128)(2,1)}, bf16[131,2,512]{2,1,0:T(2,128)(2,1)S(1)}, u32[]{:S(2)}, u32[]{:S(2)}) collective-permute-start(bf16[131,2,512]{2,1,0:T(2,128)(2,1)} %pad_maximum_fusion.1), channel_id=1, source_target_pairs={{0,8},{8,16},{16,24},{24,32},{32,40},{40,48},{48,56},{56,64},{64,7... | collective-permute-start | bytes 804872 | tf_op jit(solution)/shard_map/ppermute | solution.py:20
  30.5 5.7 %copy-start.2 = (bf16[512,3,512]{2,0,1:T(8,128)(2,1)S(1)}, bf16[512,3,512]{2,0,1:T(8,128)(2,1)}, u32[]{:S(2)}) copy-start(bf16[512,3,512]{2,0,1:T(8,128)(2,1)} %param.4) | copy-start | bytes 4718596
  30.5 6.0 %slice-start = ((bf16[512,3,512]{2,0,1:T(8,128)(2,1)}), bf16[512,2,512]{2,0,1:T(8,128)(2,1)S(1)}, s32[]{:S(2)}) async-start(bf16[512,3,512]{2,0,1:T(8,128)(2,1)} %param.4), calls=%async_computation.1 | async-start | bytes 2097152 | tf_op jit(solution)/shard_map/slice | solution.py:134
  39.1 4.2 %copy-start = (bf16[32,128,256]{2,1,0:T(8,128)(2,1)S(1)}, bf16[32,128,256]{2,1,0:T(8,128)(2,1)}, u32[]{:S(2)}) copy-start(bf16[32,128,256]{2,1,0:T(8,128)(2,1)} %shard_map.46) | copy-start | bytes 6291460
  46.7 16.3 %collective-permute-start.1 = (bf16[512,512]{1,0:T(8,128)(2,1)S(1)}, bf16[512,512]{1,0:T(8,128)(2,1)S(1)}, u32[]{:S(2)}, u32[]{:S(2)}) collective-permute-start(bf16[512,512]{1,0:T(8,128)(2,1)S(1)} %fusion.10), channel_id=1, source_target_pairs={{2,0},{4,2},{6,4},{3,1},{5,3},{7,5},{10,8},{12,10},{14,12},{11,9},... | collective-permute-start | bytes 1572872 | tf_op jit(solution)/shard_map/ppermute | solution.py:60
  48.0 20.1 %collective-permute-start.2 = (bf16[512,512]{1,0:T(8,128)(2,1)S(1)}, bf16[512,512]{1,0:T(8,128)(2,1)S(1)}, u32[]{:S(2)}, u32[]{:S(2)}) collective-permute-start(bf16[512,512]{1,0:T(8,128)(2,1)S(1)} %fusion.10), channel_id=1, source_target_pairs={{0,6},{1,7},{8,14},{9,15},{16,22},{17,23},{24,30},{25,31},{32,38},... | collective-permute-start | bytes 1572872 | tf_op jit(solution)/shard_map/ppermute | solution.py:60
  54.8 41.9 %collective-permute-start.3 = (bf16[512,512]{1,0:T(8,128)(2,1)S(1)}, bf16[512,512]{1,0:T(8,128)(2,1)S(1)}, u32[]{:S(2)}, u32[]{:S(2)}) collective-permute-start(bf16[512,512]{1,0:T(8,128)(2,1)S(1)} %fusion.10), channel_id=1, source_target_pairs={{4,0},{6,2},{5,1},{7,3},{12,8},{14,10},{13,9},{15,11},{20,16},{22,... | collective-permute-start | bytes 1572872 | tf_op jit(solution)/shard_map/ppermute | solution.py:60
  56.1 40.6 %collective-permute-start.4 = (bf16[512,512]{1,0:T(8,128)(2,1)S(1)}, bf16[512,512]{1,0:T(8,128)(2,1)S(1)}, u32[]{:S(2)}, u32[]{:S(2)}) collective-permute-start(bf16[512,512]{1,0:T(8,128)(2,1)S(1)} %fusion.10), channel_id=1, source_target_pairs={{0,4},{2,6},{1,5},{3,7},{8,12},{10,14},{9,13},{11,15},{16,20},{18,... | collective-permute-start | bytes 1572872 | tf_op jit(solution)/shard_map/ppermute | solution.py:60
  61.6 35.2 %collective-permute-start.5 = (bf16[512,512]{1,0:T(8,128)(2,1)S(1)}, bf16[512,512]{1,0:T(8,128)(2,1)S(1)}, u32[]{:S(2)}, u32[]{:S(2)}) collective-permute-start(bf16[512,512]{1,0:T(8,128)(2,1)S(1)} %fusion.10), channel_id=1, source_target_pairs={{6,0},{7,1},{14,8},{15,9},{22,16},{23,17},{30,24},{31,25},{38,32},... | collective-permute-start | bytes 1572872 | tf_op jit(solution)/shard_map/ppermute | solution.py:60
  62.9 33.9 %collective-permute-start.6 = (bf16[512,512]{1,0:T(8,128)(2,1)S(1)}, bf16[512,512]{1,0:T(8,128)(2,1)S(1)}, u32[]{:S(2)}, u32[]{:S(2)}) collective-permute-start(bf16[512,512]{1,0:T(8,128)(2,1)S(1)} %fusion.10), channel_id=1, source_target_pairs={{0,2},{2,4},{4,6},{1,3},{3,5},{5,7},{8,10},{10,12},{12,14},{9,11},... | collective-permute-start | bytes 1572872 | tf_op jit(solution)/shard_map/ppermute | solution.py:60
  97.1 14.5 %copy-start.1 = (bf16[4,512,512]{2,1,0:T(8,128)(2,1)}, bf16[4,512,512]{2,1,0:T(8,128)(2,1)S(1)}, u32[]{:S(2)}) copy-start(bf16[4,512,512]{2,1,0:T(8,128)(2,1)S(1)} %pad_maximum_fusion.own_ref) | copy-start | bytes 6291460
  97.1 6.2 %collective-permute-start.7 = (bf16[4,512,512]{2,1,0:T(8,128)(2,1)S(1)}, bf16[4,512,512]{2,1,0:T(8,128)(2,1)}, u32[]{:S(2)}, u32[]{:S(2)}) collective-permute-start(bf16[4,512,512]{2,1,0:T(8,128)(2,1)S(1)} %pad_maximum_fusion.own_ref), channel_id=1, source_target_pairs={{0,1},{1,0},{2,3},{3,2},{4,5},{5,4},{6,7},{7,6},{8,9},{9,8},{10,11... | collective-permute-start | bytes 6291464 | tf_op jit(solution)/shard_map/ppermute | solution.py:149
Sparse Core Ops, SparseCore 0:
  22.6 88.9 all-gather.2

commit v14 on v13

--- a/solution.py
+++ b/solution.py
@@ -61,7 +61,7 @@
     slots = [block]
     for k in range(1, size):
         slots.append(jnp.where(index + k < size, received[-k], received[size - k]))
-    return jnp.stack(slots)
+    return jnp.stack(slots, axis=1).reshape(block.shape[0], -1)
 
 
 def matmul_kernel(table_ref, own_ref, other_ref, weight_a_ref, weight_b_ref, out_ref, acc_ref):
@@ -88,19 +88,20 @@
 def two_blocks(piece_ref, weight_a_ref, weight_b_ref):
     rows_a = weight_a_ref[0, :, 0]
     rows_b = weight_b_ref[0, :, 0]
-    rows_a = rows_a.reshape(-1, rows_a.shape[-1])
-    rows_b = rows_b.reshape(-1, rows_b.shape[-1])
-    total = jnp.dot(piece_ref[0], rows_a, preferred_element_type=jnp.float32)
-    return total + jnp.dot(piece_ref[1], rows_b, preferred_element_type=jnp.float32)
+    rows = jnp.concatenate(
+        [rows_a.reshape(-1, rows_a.shape[-1]), rows_b.reshape(-1, rows_b.shape[-1])], axis=0
+    )
+    return jnp.dot(piece_ref[...], rows, preferred_element_type=jnp.float32)
 
 
 def block_matmul(table, own, other, weight):
-    n, tok, width = own.shape
+    tok, total = own.shape
     _, ys, _, rows, cols = weight.shape
-    steps = n // 2
+    width = ys * rows
+    steps = total // (2 * width)
     in_specs = [
-        pl.BlockSpec((2, tok, width), lambda k, t: (jnp.minimum(k, steps - 1), 0, 0)),
-        pl.BlockSpec((2, tok, width), lambda k, t: (jnp.maximum(k - steps, 0), 0, 0)),
+        pl.BlockSpec((tok, 2 * width), lambda k, t: (0, jnp.minimum(k, steps - 1))),
+        pl.BlockSpec((tok, 2 * width), lambda k, t: (0, jnp.maximum(k - steps, 0))),
         pl.BlockSpec((1, ys, 1, rows, cols), lambda k, t: (t[0, 2 * k], 0, t[1, 2 * k], 0, 0)),
         pl.BlockSpec((1, ys, 1, rows, cols), lambda k, t: (t[0, 2 * k + 1], 0, t[1, 2 * k + 1], 0, 0)),
     ]

time: 127 us -> 127 us (level)
  the two profiles are of different devices: /device:TPU:8 before, /device:TPU:385 now
where the time goes in v14:
time: 127 us; the launch traced here: 126 us
  waiting for transfers between devices  50.1 us (39%)
  starting transfers between devices  30.1 us (24%)
  between operations  13.7 us (11%)
  Pallas kernels  13 us (10%)
  local copies, waits for them, and re-layouts  11.4 us (9%)
  other arithmetic  5.95 us (5%)
  matrix products  1.88 us (1%)
    ppermute x6, waiting for transfers between devices, line_slots(): received[d] = lax.ppermute(block, axis_name, pairs)  31.3 us
    ppermute x6, starting transfers between devices, line_slots(): received[d] = lax.ppermute(block, axis_name, pairs)  18.7 us
    ppermute x1, waiting for transfers between devices, on_device(): partner = lax.ppermute(out_weight, 'zh', [(0, 1), (1, 0)])  8.11 us
    ppermute x1, waiting for transfers between devices, from_behind(): return lax.ppermute(array, SEQ, pairs)  7.44 us
    pallas_call x1, Pallas kernels, block_matmul(): pl.pallas_call(matmul_kernel, grid_spec=grid_spec, out_shape=jax.ShapeDty...  7.36 us
    ppermute x1, starting transfers between devices, on_device(): other = lax.ppermute(own, 'c', [(0, 1), (1, 0)])  5.7 us
    pallas_call x1, Pallas kernels, toeplitz_blocks(): pl.pallas_call(toeplitz_kernel, out_shape=jax.ShapeDtypeStruct((groups, s...  5.65 us
    ppermute x1, starting transfers between devices, from_behind(): return lax.ppermute(array, SEQ, pairs)  3.78 us
  transfers between devices with their start and end apart: 10, of which 5 were waited for; matrix products, arithmetic and copies ran while one was open for 12% of the time, Pallas kernels for 4%

profile of v14, /device:TPU:385, one launch (start us, length us, event | category | flops | bytes accessed | tf_op | source)
XLA Modules:
  0.0 126.1 jit_solution(8065361176340892739)
XLA Ops:
  6.5 1.9 %collective-permute-start.8 = (bf16[64,512]{1,0:T(8,128)(2,1)}, bf16[64,512]{1,0:T(8,128)(2,1)S(1)}, u32[]{:S(2)}, u32[]{:S(2)}) collective-permute-start(bf16[64,512]{1,0:T(8,128)(2,1)} %param.7), channel_id=1, source_target_pairs={{0,256},{256,0},{1,257},{257,1},{2,258},{258,2},{3,259},{259,3},{4... | collective-permute-start | bytes 196616 | tf_op jit(solution)/shard_map/ppermute | solution.py:127
  8.5 8.1 %collective-permute-done.8 = bf16[64,512]{1,0:T(8,128)(2,1)S(1)} collective-permute-done((bf16[64,512]{1,0:T(8,128)(2,1)}, bf16[64,512]{1,0:T(8,128)(2,1)S(1)}, u32[]{:S(2)}, u32[]{:S(2)}) %collective-permute-start.8) | collective-permute-done | bytes 65568 | tf_op jit(solution)/shard_map/ppermute | solution.py:127
  16.6 1.5 %pad_maximum_fusion.2 = bf16[2,64,512]{2,1,0:T(8,128)(2,1)} fusion(bf16[1,64,512]{2,1,0:T(8,128)(2,1)S(1)} %bitcast.56, bf16[1,64,512]{2,1,0:T(8,128)(2,1)} %bitcast.55), kind=kLoop, calls=%fused_computation.27 | loop fusion | flops 65536 | bytes 262144 | tf_op jit(solution)/shard_map/stack | solution.py:129
  18.1 1.0 slice.75
  19.1 0.7 slice_bitcast_fusion.3
  19.9 3.8 %collective-permute-start = (bf16[131,2,512]{2,0,1:T(8,128)(2,1)S(1)}, bf16[131,2,512]{2,0,1:T(8,128)(2,1)S(1)}, u32[]{:S(2)}, u32[]{:S(2)}) collective-permute-start(bf16[131,2,512]{2,0,1:T(8,128)(2,1)S(1)} %pad_maximum_fusion.1), channel_id=1, source_target_pairs={{0,8},{8,16},{16,24},{24,32},{32,40},{40,48},{48,56},{56,64},{64,7... | collective-permute-start | bytes 804872 | tf_op jit(solution)/shard_map/ppermute | solution.py:20
  23.7 0.8 rev.3
  24.4 0.1 pad.8.clone
  24.5 0.7 maximum_maximum_fusion.row_ref
  25.2 0.7 fusion.20
  26.0 5.7 %shard_map.46 = bf16[32,128,256]{2,1,0:T(8,128)(2,1)} custom-call(f32[32,384]{1,0:T(8,128)} %maximum_maximum_fusion.row_ref), custom_call_target="tpu_custom_call" | custom-call | tf_op jit(solution)/shard_map/pallas_call | solution.py:48
  31.6 1.0 copy.28
  32.7 7.4 %collective-permute-done = bf16[131,2,512]{2,0,1:T(8,128)(2,1)S(1)} collective-permute-done((bf16[131,2,512]{2,0,1:T(8,128)(2,1)S(1)}, bf16[131,2,512]{2,0,1:T(8,128)(2,1)S(1)}, u32[]{:S(2)}, u32[]{:S(2)}) %collective-permute-start) | collective-permute-done | bytes 268320 | tf_op jit(solution)/shard_map/ppermute | solution.py:20
  40.1 0.4 maximum_convert_fusion
  40.5 0.8 fusion
  41.3 0.2 fusion.7
  41.5 0.1 fusion.19
  41.6 0.2 copy.19
  41.8 0.1 slice.95
  41.9 0.9 copy.21
  42.8 0.2 copy.20
  43.0 0.1 slice.97
  43.2 0.1 copy.22
  43.3 0.4 copy-done
  43.7 1.9 %fusion.4 = f32[4,128,32,16]{1,3,0,2:T(8,128)S(1)} fusion(bf16[32,128,256]{2,1,0:T(8,128)(2,1)S(1)} %copy-done, bf16[4,128,32,16]{1,3,0,2:T(8,128)(2,1)S(1)} %copy.22, bf16[4,128,32,16]{1,3,0,2:T(8,128)(2,1)} %copy.21), kind=kOutput, calls=%fused_computation.8 | convolution fusion | flops 136314880 | bytes 4194304 | tf_op jit(solution)/shard_map/gij,bjgc->bigc/dot_general | solution.py:144
  45.6 0.4 copy.23
  46.0 0.2 copy.26
  46.2 0.4 copy-done.1
  46.6 0.3 maximum_convert_fusion.1
  46.9 0.9 fusion.8
  47.9 1.9 %collective-permute-start.1 = (bf16[512,512]{0,1:T(8,128)(2,1)S(1)}, bf16[512,512]{0,1:T(8,128)(2,1)S(1)}, u32[]{:S(2)}, u32[]{:S(2)}) collective-permute-start(bf16[512,512]{0,1:T(8,128)(2,1)S(1)} %fusion.8), channel_id=1, source_target_pairs={{2,0},{4,2},{6,4},{3,1},{5,3},{7,5},{10,8},{12,10},{14,12},{11,9},... | collective-permute-start | bytes 1572872 | tf_op jit(solution)/shard_map/ppermute | solution.py:60
  49.8 0.7 collective-permute-start.2
  50.5 6.7 %collective-permute-start.3 = (bf16[512,512]{0,1:T(8,128)(2,1)S(1)}, bf16[512,512]{0,1:T(8,128)(2,1)S(1)}, u32[]{:S(2)}, u32[]{:S(2)}) collective-permute-start(bf16[512,512]{0,1:T(8,128)(2,1)S(1)} %fusion.8), channel_id=1, source_target_pairs={{4,0},{6,2},{5,1},{7,3},{12,8},{14,10},{13,9},{15,11},{20,16},{22,... | collective-permute-start | bytes 1572872 | tf_op jit(solution)/shard_map/ppermute | solution.py:60
  57.2 1.3 %collective-permute-start.4 = (bf16[512,512]{0,1:T(8,128)(2,1)S(1)}, bf16[512,512]{0,1:T(8,128)(2,1)S(1)}, u32[]{:S(2)}, u32[]{:S(2)}) collective-permute-start(bf16[512,512]{0,1:T(8,128)(2,1)S(1)} %fusion.8), channel_id=1, source_target_pairs={{0,4},{2,6},{1,5},{3,7},{8,12},{10,14},{9,13},{11,15},{16,20},{18,... | collective-permute-start | bytes 1572872 | tf_op jit(solution)/shard_map/ppermute | solution.py:60
  58.5 0.7 collective-permute-start.5
  59.3 7.3 %collective-permute-start.6 = (bf16[512,512]{0,1:T(8,128)(2,1)S(1)}, bf16[512,512]{0,1:T(8,128)(2,1)S(1)}, u32[]{:S(2)}, u32[]{:S(2)}) collective-permute-start(bf16[512,512]{0,1:T(8,128)(2,1)S(1)} %fusion.8), channel_id=1, source_target_pairs={{0,2},{2,4},{4,6},{1,3},{3,5},{5,7},{8,10},{10,12},{12,14},{9,11},... | collective-permute-start | bytes 1572872 | tf_op jit(solution)/shard_map/ppermute | solution.py:60
  66.6 0.1 select_bitcast_fusion.2
  66.7 24.8 %collective-permute-done.3 = bf16[512,512]{0,1:T(8,128)(2,1)S(1)} collective-permute-done((bf16[512,512]{0,1:T(8,128)(2,1)S(1)}, bf16[512,512]{0,1:T(8,128)(2,1)S(1)}, u32[]{:S(2)}, u32[]{:S(2)}) %collective-permute-start.3) | collective-permute-done | bytes 524320 | tf_op jit(solution)/shard_map/ppermute | solution.py:60
  91.5 0.1 select_bitcast_fusion.1
  91.5 6.5 %collective-permute-done.6 = bf16[512,512]{0,1:T(8,128)(2,1)S(1)} collective-permute-done((bf16[512,512]{0,1:T(8,128)(2,1)S(1)}, bf16[512,512]{0,1:T(8,128)(2,1)S(1)}, u32[]{:S(2)}, u32[]{:S(2)}) %collective-permute-start.6) | collective-permute-done | bytes 524320 | tf_op jit(solution)/shard_map/ppermute | solution.py:60
  98.0 0.1 select_bitcast_fusion
  98.1 0.3 pad_maximum_fusion
  98.3 2.5 %copy.27.own_ref = bf16[512,2048]{1,0:T(8,128)(2,1)} copy(bf16[512,2048]{0,1:T(8,128)(2,1)S(1)} %bitcast.49) | data formatting | bytes 4194304 | tf_op jit(solution)/shard_map/reshape | solution.py:64
  100.8 5.7 %collective-permute-start.7 = (bf16[512,2048]{1,0:T(8,128)(2,1)}, bf16[512,2048]{1,0:T(8,128)(2,1)S(1)}, u32[]{:S(2)}, u32[]{:S(2)}) collective-permute-start(bf16[512,2048]{1,0:T(8,128)(2,1)} %copy.27.own_ref), channel_id=1, source_target_pairs={{0,1},{1,0},{2,3},{3,2},{4,5},{5,4},{6,7},{7,6},{8,9},{9,8},{10,11... | collective-permute-start | bytes 6291464 | tf_op jit(solution)/shard_map/ppermute | solution.py:150
  106.6 0.6 add_add_fusion.table_ref
  107.2 3.3 %collective-permute-done.7.other_ref = bf16[512,2048]{1,0:T(8,128)(2,1)S(1)} collective-permute-done((bf16[512,2048]{1,0:T(8,128)(2,1)}, bf16[512,2048]{1,0:T(8,128)(2,1)S(1)}, u32[]{:S(2)}, u32[]{:S(2)}) %collective-permute-start.7) | collective-permute-done | bytes 2097184 | tf_op jit(solution)/shard_map/ppermute | solution.py:150
  110.5 1.4 %copy-done.2 = bf16[512,2048]{1,0:T(8,128)(2,1)} copy-done((bf16[512,2048]{1,0:T(8,128)(2,1)}, bf16[512,2048]{1,0:T(8,128)(2,1)S(1)}, u32[]{:S(2)}) %copy-start.2) | copy-done | bytes 2097176
  111.9 7.4 %shard_map.47 = bf16[512,512]{1,0:T(8,128)(2,1)} custom-call(s32[2,8]{1,0:T(2,128)} %add_add_fusion.table_ref, bf16[512,2048]{1,0:T(8,128)(2,1)} %copy.27.own_ref, bf16[512,2048]{1,0:T(8,128)(2,1)} %copy-done.2, bf16[4,8,2,64,512]{4,3,2,1,0:T(8,128)(2,1)} %bitcast.47, bf16[4,8,2,64,512]{4,3,2,1,0:T(8,128)(2,1)} %bitcast.48), custom_call_target="tpu_custom_call" | custom-call | tf_op jit(solution)/shard_map/pallas_call | solution.py:115
  (25 shorter events, 0.2 us)
Async XLA Ops:
  6.5 104.0 %all-gather.3.cloned.1.call-start = ((), (), s32[]{:S(2)}) async-start(), calls=%async_computation | async-start | bytes 4325376 | tf_op jit(solution)/shard_map/all_gather | solution.py:130
  6.5 10.0 %collective-permute-start.8 = (bf16[64,512]{1,0:T(8,128)(2,1)}, bf16[64,512]{1,0:T(8,128)(2,1)S(1)}, u32[]{:S(2)}, u32[]{:S(2)}) collective-permute-start(bf16[64,512]{1,0:T(8,128)(2,1)} %param.7), channel_id=1, source_target_pairs={{0,256},{256,0},{1,257},{257,1},{2,258},{258,2},{3,259},{259,3},{4... | collective-permute-start | bytes 196616 | tf_op jit(solution)/shard_map/ppermute | solution.py:127
  19.9 20.2 %collective-permute-start = (bf16[131,2,512]{2,0,1:T(8,128)(2,1)S(1)}, bf16[131,2,512]{2,0,1:T(8,128)(2,1)S(1)}, u32[]{:S(2)}, u32[]{:S(2)}) collective-permute-start(bf16[131,2,512]{2,0,1:T(8,128)(2,1)S(1)} %pad_maximum_fusion.1), channel_id=1, source_target_pairs={{0,8},{8,16},{16,24},{24,32},{32,40},{40,48},{48,56},{56,64},{64,7... | collective-permute-start | bytes 804872 | tf_op jit(solution)/shard_map/ppermute | solution.py:20
  26.0 5.7 %slice-start.1 = ((bf16[512,3,512]{2,0,1:T(8,128)(2,1)}), bf16[512,1,512]{2,0,1:T(8,128)(2,1)S(1)}, s32[]{:S(2)}) async-start(bf16[512,3,512]{2,0,1:T(8,128)(2,1)} %param.4), calls=%async_computation.2 | async-start | bytes 1048576 | tf_op jit(solution)/shard_map/slice | solution.py:138
  26.0 6.7 %copy-start.3 = (f32[3,3,512]{2,1,0:T(4,128)S(1)}, f32[3,3,512]{2,1,0:T(4,128)}, u32[]{:S(2)}) copy-start(f32[3,3,512]{2,1,0:T(4,128)} %param.5) | copy-start | bytes 55300
  26.0 14.1 %slice-start = ((bf16[512,3,512]{2,0,1:T(8,128)(2,1)}), bf16[512,2,512]{2,0,1:T(8,128)(2,1)S(1)}, s32[]{:S(2)}) async-start(bf16[512,3,512]{2,0,1:T(8,128)(2,1)} %param.4), calls=%async_computation.1 | async-start | bytes 2097152 | tf_op jit(solution)/shard_map/slice | solution.py:135
  41.9 1.8 %copy-start = (bf16[32,128,256]{2,1,0:T(8,128)(2,1)S(1)}, bf16[32,128,256]{2,1,0:T(8,128)(2,1)}, u32[]{:S(2)}) copy-start(bf16[32,128,256]{2,1,0:T(8,128)(2,1)} %shard_map.46) | copy-start | bytes 6291460
  45.6 1.0 copy-start.1
  47.9 11.4 %collective-permute-start.1 = (bf16[512,512]{0,1:T(8,128)(2,1)S(1)}, bf16[512,512]{0,1:T(8,128)(2,1)S(1)}, u32[]{:S(2)}, u32[]{:S(2)}) collective-permute-start(bf16[512,512]{0,1:T(8,128)(2,1)S(1)} %fusion.8), channel_id=1, source_target_pairs={{2,0},{4,2},{6,4},{3,1},{5,3},{7,5},{10,8},{12,10},{14,12},{11,9},... | collective-permute-start | bytes 1572872 | tf_op jit(solution)/shard_map/ppermute | solution.py:60
  49.8 16.8 %collective-permute-start.2 = (bf16[512,512]{0,1:T(8,128)(2,1)S(1)}, bf16[512,512]{0,1:T(8,128)(2,1)S(1)}, u32[]{:S(2)}, u32[]{:S(2)}) collective-permute-start(bf16[512,512]{0,1:T(8,128)(2,1)S(1)} %fusion.8), channel_id=1, source_target_pairs={{0,6},{1,7},{8,14},{9,15},{16,22},{17,23},{24,30},{25,31},{32,38},... | collective-permute-start | bytes 1572872 | tf_op jit(solution)/shard_map/ppermute | solution.py:60
  50.5 41.0 %collective-permute-start.3 = (bf16[512,512]{0,1:T(8,128)(2,1)S(1)}, bf16[512,512]{0,1:T(8,128)(2,1)S(1)}, u32[]{:S(2)}, u32[]{:S(2)}) collective-permute-start(bf16[512,512]{0,1:T(8,128)(2,1)S(1)} %fusion.8), channel_id=1, source_target_pairs={{4,0},{6,2},{5,1},{7,3},{12,8},{14,10},{13,9},{15,11},{20,16},{22,... | collective-permute-start | bytes 1572872 | tf_op jit(solution)/shard_map/ppermute | solution.py:60
  57.2 34.2 %collective-permute-start.4 = (bf16[512,512]{0,1:T(8,128)(2,1)S(1)}, bf16[512,512]{0,1:T(8,128)(2,1)S(1)}, u32[]{:S(2)}, u32[]{:S(2)}) collective-permute-start(bf16[512,512]{0,1:T(8,128)(2,1)S(1)} %fusion.8), channel_id=1, source_target_pairs={{0,4},{2,6},{1,5},{3,7},{8,12},{10,14},{9,13},{11,15},{16,20},{18,... | collective-permute-start | bytes 1572872 | tf_op jit(solution)/shard_map/ppermute | solution.py:60
  58.5 33.0 %collective-permute-start.5 = (bf16[512,512]{0,1:T(8,128)(2,1)S(1)}, bf16[512,512]{0,1:T(8,128)(2,1)S(1)}, u32[]{:S(2)}, u32[]{:S(2)}) collective-permute-start(bf16[512,512]{0,1:T(8,128)(2,1)S(1)} %fusion.8), channel_id=1, source_target_pairs={{6,0},{7,1},{14,8},{15,9},{22,16},{23,17},{30,24},{31,25},{38,32},... | collective-permute-start | bytes 1572872 | tf_op jit(solution)/shard_map/ppermute | solution.py:60
  59.3 38.7 %collective-permute-start.6 = (bf16[512,512]{0,1:T(8,128)(2,1)S(1)}, bf16[512,512]{0,1:T(8,128)(2,1)S(1)}, u32[]{:S(2)}, u32[]{:S(2)}) collective-permute-start(bf16[512,512]{0,1:T(8,128)(2,1)S(1)} %fusion.8), channel_id=1, source_target_pairs={{0,2},{2,4},{4,6},{1,3},{3,5},{5,7},{8,10},{10,12},{12,14},{9,11},... | collective-permute-start | bytes 1572872 | tf_op jit(solution)/shard_map/ppermute | solution.py:60
  100.8 9.7 %collective-permute-start.7 = (bf16[512,2048]{1,0:T(8,128)(2,1)}, bf16[512,2048]{1,0:T(8,128)(2,1)S(1)}, u32[]{:S(2)}, u32[]{:S(2)}) collective-permute-start(bf16[512,2048]{1,0:T(8,128)(2,1)} %copy.27.own_ref), channel_id=1, source_target_pairs={{0,1},{1,0},{2,3},{3,2},{4,5},{5,4},{6,7},{7,6},{8,9},{9,8},{10,11... | collective-permute-start | bytes 6291464 | tf_op jit(solution)/shard_map/ppermute | solution.py:150
  110.5 1.4 %copy-start.2 = (bf16[512,2048]{1,0:T(8,128)(2,1)}, bf16[512,2048]{1,0:T(8,128)(2,1)S(1)}, u32[]{:S(2)}) copy-start(bf16[512,2048]{1,0:T(8,128)(2,1)S(1)} %collective-permute-done.7.other_ref) | copy-start | bytes 6291460
Sparse Core Ops, SparseCore 0:
  18.2 86.1 all-gather.2

commit v15 on v13

--- a/solution.py
+++ b/solution.py
@@ -74,24 +74,24 @@
 
     @pl.when(k < half)
     def _():
-        acc_ref[...] += two_blocks(own_ref, weight_a_ref, weight_b_ref)
+        acc_ref[...] += two_blocks(own_ref, 2 * k, weight_a_ref, weight_b_ref)
 
     @pl.when(k >= half)
     def _():
-        acc_ref[...] += two_blocks(other_ref, weight_a_ref, weight_b_ref)
+        acc_ref[...] += two_blocks(other_ref, 2 * (k - half), weight_a_ref, weight_b_ref)
 
     @pl.when(k == pl.num_programs(0) - 1)
     def _():
         out_ref[...] = acc_ref[...].astype(out_ref.dtype)
 
 
-def two_blocks(piece_ref, weight_a_ref, weight_b_ref):
+def two_blocks(piece_ref, first, weight_a_ref, weight_b_ref):
     rows_a = weight_a_ref[0, :, 0]
     rows_b = weight_b_ref[0, :, 0]
     rows_a = rows_a.reshape(-1, rows_a.shape[-1])
     rows_b = rows_b.reshape(-1, rows_b.shape[-1])
-    total = jnp.dot(piece_ref[0], rows_a, preferred_element_type=jnp.float32)
-    return total + jnp.dot(piece_ref[1], rows_b, preferred_element_type=jnp.float32)
+    total = jnp.dot(piece_ref[first], rows_a, preferred_element_type=jnp.float32)
+    return total + jnp.dot(piece_ref[first + 1], rows_b, preferred_element_type=jnp.float32)
 
 
 def block_matmul(table, own, other, weight):
@@ -99,8 +99,8 @@
     _, ys, _, rows, cols = weight.shape
     steps = n // 2
     in_specs = [
-        pl.BlockSpec((2, tok, width), lambda k, t: (jnp.minimum(k, steps - 1), 0, 0)),
-        pl.BlockSpec((2, tok, width), lambda k, t: (jnp.maximum(k - steps, 0), 0, 0)),
+        pl.BlockSpec(memory_space=pltpu.VMEM),
+        pl.BlockSpec(memory_space=pltpu.VMEM),
         pl.BlockSpec((1, ys, 1, rows, cols), lambda k, t: (t[0, 2 * k], 0, t[1, 2 * k], 0, 0)),
         pl.BlockSpec((1, ys, 1, rows, cols), lambda k, t: (t[0, 2 * k + 1], 0, t[1, 2 * k + 1], 0, 0)),
     ]

time: 127 us -> 127 us (level)
  the two profiles are of different devices: /device:TPU:8 before, /device:TPU:385 now
where the time goes in v15:
time: 127 us; the launch traced here: 126 us
  waiting for transfers between devices  51.4 us (40%)
  starting transfers between devices  30.2 us (24%)
  between operations  13.7 us (11%)
  Pallas kernels  13.4 us (11%)
  local copies, waits for them, and re-layouts  9.32 us (7%)
  other arithmetic  6.28 us (5%)
  matrix products  1.87 us (1%)
    ppermute x6, waiting for transfers between devices, line_slots(): received[d] = lax.ppermute(block, axis_name, pairs)  31.3 us
    ppermute x6, starting transfers between devices, line_slots(): received[d] = lax.ppermute(block, axis_name, pairs)  18.7 us
    ppermute x1, waiting for transfers between devices, from_behind(): return lax.ppermute(array, SEQ, pairs)  8.86 us
    ppermute x1, waiting for transfers between devices, on_device(): partner = lax.ppermute(out_weight, 'zh', [(0, 1), (1, 0)])  8.11 us
    pallas_call x1, Pallas kernels, block_matmul(): pl.pallas_call(matmul_kernel, grid_spec=grid_spec, out_shape=jax.ShapeDty...  7.72 us
    ppermute x1, starting transfers between devices, on_device(): other = lax.ppermute(own, 'c', [(0, 1), (1, 0)])  5.71 us
    pallas_call x1, Pallas kernels, toeplitz_blocks(): pl.pallas_call(toeplitz_kernel, out_shape=jax.ShapeDtypeStruct((groups, s...  5.7 us
    slice x7, local copies, waits for them, and re-layouts, on_device(): window = jnp.concatenate([blocks[:-1], blocks[1:]], axis=1)  5.4 us
  transfers between devices with their start and end apart: 10, of which 5 were waited for; matrix products, arithmetic and copies ran while one was open for 13% of the time, Pallas kernels for 5%

profile of v15, /device:TPU:385, one launch (start us, length us, event | category | flops | bytes accessed | tf_op | source)
XLA Modules:
  0.0 126.2 jit_solution(403754061017960041)
XLA Ops:
  6.5 2.0 %collective-permute-start.8 = (bf16[64,512]{1,0:T(8,128)(2,1)}, bf16[64,512]{1,0:T(8,128)(2,1)S(1)}, u32[]{:S(2)}, u32[]{:S(2)}) collective-permute-start(bf16[64,512]{1,0:T(8,128)(2,1)} %param.7), channel_id=1, source_target_pairs={{0,256},{256,0},{1,257},{257,1},{2,258},{258,2},{3,259},{259,3},{4... | collective-permute-start | bytes 196616 | tf_op jit(solution)/shard_map/ppermute | solution.py:126
  8.6 8.1 %collective-permute-done.8 = bf16[64,512]{1,0:T(8,128)(2,1)S(1)} collective-permute-done((bf16[64,512]{1,0:T(8,128)(2,1)}, bf16[64,512]{1,0:T(8,128)(2,1)S(1)}, u32[]{:S(2)}, u32[]{:S(2)}) %collective-permute-start.8) | collective-permute-done | bytes 65568 | tf_op jit(solution)/shard_map/ppermute | solution.py:126
  16.7 1.5 %pad_maximum_fusion.2 = bf16[2,64,512]{2,1,0:T(8,128)(2,1)} fusion(bf16[1,64,512]{2,1,0:T(8,128)(2,1)S(1)} %bitcast.52, bf16[1,64,512]{2,1,0:T(8,128)(2,1)} %bitcast.51), kind=kLoop, calls=%fused_computation.29 | loop fusion | flops 65536 | bytes 262144 | tf_op jit(solution)/shard_map/stack | solution.py:128
  18.2 0.0 all-gather.3.cloned.1.call-update
  18.2 1.0 slice.75
  19.3 0.2 copy.25
  19.5 0.7 slice_bitcast_fusion.5
  20.2 1.1 pad_maximum_fusion.1
  21.2 3.8 %collective-permute-start = (bf16[131,2,512]{2,1,0:T(2,128)(2,1)}, bf16[131,2,512]{2,1,0:T(2,128)(2,1)S(1)}, u32[]{:S(2)}, u32[]{:S(2)}) collective-permute-start(bf16[131,2,512]{2,1,0:T(2,128)(2,1)} %pad_maximum_fusion.1), channel_id=1, source_target_pairs={{0,8},{8,16},{16,24},{24,32},{32,40},{40,48},{48,56},{56,64},{64,7... | collective-permute-start | bytes 804872 | tf_op jit(solution)/shard_map/ppermute | solution.py:20
  25.0 0.8 rev.3
  25.8 0.1 pad.8.clone
  25.9 0.7 maximum_maximum_fusion.row_ref
  26.6 5.7 %shard_map.46 = bf16[32,128,256]{2,1,0:T(8,128)(2,1)} custom-call(f32[32,384]{1,0:T(8,128)} %maximum_maximum_fusion.row_ref), custom_call_target="tpu_custom_call" | custom-call | tf_op jit(solution)/shard_map/pallas_call | solution.py:48
  32.3 8.9 %collective-permute-done = bf16[131,2,512]{2,1,0:T(2,128)(2,1)S(1)} collective-permute-done((bf16[131,2,512]{2,1,0:T(2,128)(2,1)}, bf16[131,2,512]{2,1,0:T(2,128)(2,1)S(1)}, u32[]{:S(2)}, u32[]{:S(2)}) %collective-permute-start) | collective-permute-done | bytes 268320 | tf_op jit(solution)/shard_map/ppermute | solution.py:20
  41.2 0.2 slice.102
  41.4 0.4 maximum_convert_fusion
  41.8 0.8 fusion
  42.6 0.2 fusion.7
  42.8 0.9 fusion.20
  43.7 0.2 copy.18
  43.9 0.1 slice.95
  44.0 0.9 copy.20
  44.9 1.3 copy.19
  46.2 0.9 slice.97
  47.1 1.1 copy.21
  48.2 1.9 %fusion.4 = f32[4,128,32,16]{1,3,0,2:T(8,128)S(1)} fusion(bf16[32,128,256]{2,1,0:T(8,128)(2,1)S(1)} %copy-done, bf16[4,128,32,16]{1,3,0,2:T(8,128)(2,1)S(1)} %copy.21, bf16[4,128,32,16]{1,3,0,2:T(8,128)(2,1)} %copy.20), kind=kOutput, calls=%fused_computation.8 | convolution fusion | flops 136314880 | bytes 4194304 | tf_op jit(solution)/shard_map/gij,bjgc->bigc/dot_general | solution.py:143
  50.1 0.4 copy.22
  50.6 0.1 copy.28
  50.6 0.3 copy.23
  51.0 0.2 maximum_convert_fusion.1
  51.1 0.4 fusion.10
  51.5 1.9 %collective-permute-start.1 = (bf16[512,512]{1,0:T(8,128)(2,1)S(1)}, bf16[512,512]{1,0:T(8,128)(2,1)S(1)}, u32[]{:S(2)}, u32[]{:S(2)}) collective-permute-start(bf16[512,512]{1,0:T(8,128)(2,1)S(1)} %fusion.10), channel_id=1, source_target_pairs={{2,0},{4,2},{6,4},{3,1},{5,3},{7,5},{10,8},{12,10},{14,12},{11,9},... | collective-permute-start | bytes 1572872 | tf_op jit(solution)/shard_map/ppermute | solution.py:60
  53.4 0.7 collective-permute-start.2
  54.1 6.7 %collective-permute-start.3 = (bf16[512,512]{1,0:T(8,128)(2,1)S(1)}, bf16[512,512]{1,0:T(8,128)(2,1)S(1)}, u32[]{:S(2)}, u32[]{:S(2)}) collective-permute-start(bf16[512,512]{1,0:T(8,128)(2,1)S(1)} %fusion.10), channel_id=1, source_target_pairs={{4,0},{6,2},{5,1},{7,3},{12,8},{14,10},{13,9},{15,11},{20,16},{22,... | collective-permute-start | bytes 1572872 | tf_op jit(solution)/shard_map/ppermute | solution.py:60
  60.9 1.3 %collective-permute-start.4 = (bf16[512,512]{1,0:T(8,128)(2,1)S(1)}, bf16[512,512]{1,0:T(8,128)(2,1)S(1)}, u32[]{:S(2)}, u32[]{:S(2)}) collective-permute-start(bf16[512,512]{1,0:T(8,128)(2,1)S(1)} %fusion.10), channel_id=1, source_target_pairs={{0,4},{2,6},{1,5},{3,7},{8,12},{10,14},{9,13},{11,15},{16,20},{18,... | collective-permute-start | bytes 1572872 | tf_op jit(solution)/shard_map/ppermute | solution.py:60
  62.2 0.7 collective-permute-start.5
  62.9 0.0 collective-permute-done.1
  62.9 7.3 %collective-permute-start.6 = (bf16[512,512]{1,0:T(8,128)(2,1)S(1)}, bf16[512,512]{1,0:T(8,128)(2,1)S(1)}, u32[]{:S(2)}, u32[]{:S(2)}) collective-permute-start(bf16[512,512]{1,0:T(8,128)(2,1)S(1)} %fusion.10), channel_id=1, source_target_pairs={{0,2},{2,4},{4,6},{1,3},{3,5},{5,7},{8,10},{10,12},{12,14},{9,11},... | collective-permute-start | bytes 1572872 | tf_op jit(solution)/shard_map/ppermute | solution.py:60
  70.3 0.1 select_bitcast_fusion.2
  70.4 24.8 %collective-permute-done.3 = bf16[512,512]{1,0:T(8,128)(2,1)S(1)} collective-permute-done((bf16[512,512]{1,0:T(8,128)(2,1)S(1)}, bf16[512,512]{1,0:T(8,128)(2,1)S(1)}, u32[]{:S(2)}, u32[]{:S(2)}) %collective-permute-start.3) | collective-permute-done | bytes 524320 | tf_op jit(solution)/shard_map/ppermute | solution.py:60
  95.1 0.1 select_bitcast_fusion.1
  95.2 6.5 %collective-permute-done.6 = bf16[512,512]{1,0:T(8,128)(2,1)S(1)} collective-permute-done((bf16[512,512]{1,0:T(8,128)(2,1)S(1)}, bf16[512,512]{1,0:T(8,128)(2,1)S(1)}, u32[]{:S(2)}, u32[]{:S(2)}) %collective-permute-start.6) | collective-permute-done | bytes 524320 | tf_op jit(solution)/shard_map/ppermute | solution.py:60
  101.7 0.1 select_bitcast_fusion
  101.7 0.3 pad_maximum_fusion.own_ref
  102.0 5.7 %collective-permute-start.7 = (bf16[4,512,512]{2,1,0:T(8,128)(2,1)S(1)}, bf16[4,512,512]{2,1,0:T(8,128)(2,1)}, u32[]{:S(2)}, u32[]{:S(2)}) collective-permute-start(bf16[4,512,512]{2,1,0:T(8,128)(2,1)S(1)} %pad_maximum_fusion.own_ref), channel_id=1, source_target_pairs={{0,1},{1,0},{2,3},{3,2},{4,5},{5,4},{6,7},{7,6},{8,9},{9,8},{10,11... | collective-permute-start | bytes 6291464 | tf_op jit(solution)/shard_map/ppermute | solution.py:149
  107.8 0.7 add_add_fusion.table_ref
  108.5 3.2 %collective-permute-done.7.other_ref = bf16[4,512,512]{2,1,0:T(8,128)(2,1)} collective-permute-done((bf16[4,512,512]{2,1,0:T(8,128)(2,1)S(1)}, bf16[4,512,512]{2,1,0:T(8,128)(2,1)}, u32[]{:S(2)}, u32[]{:S(2)}) %collective-permute-start.7) | collective-permute-done | bytes 2097184 | tf_op jit(solution)/shard_map/ppermute | solution.py:149
  111.6 7.7 %shard_map.47 = bf16[512,512]{1,0:T(8,128)(2,1)} custom-call(s32[2,8]{1,0:T(2,128)} %add_add_fusion.table_ref, bf16[4,512,512]{2,1,0:T(8,128)(2,1)} %copy-done.1, bf16[4,512,512]{2,1,0:T(8,128)(2,1)} %collective-permute-done.7.other_ref, bf16[4,8,2,64,512]{4,3,2,1,0:T(8,128)(2,1)} %bitcast.46, bf16[4,8,2,64,512]{4,3,2,1,0:T(8,128)(2,1)} %bitcast.47), custom_call_target="tpu_custom_call" | custom-call | tf_op jit(solution)/shard_map/pallas_call | solution.py:114
  (25 shorter events, 0.2 us)
Async XLA Ops:
  6.5 19.3 %copy-start.3 = (f32[3,3,512]{2,1,0:T(4,128)S(1)}, f32[3,3,512]{2,1,0:T(4,128)}, u32[]{:S(2)}) copy-start(f32[3,3,512]{2,1,0:T(4,128)} %param.5) | copy-start | bytes 55300
  6.5 105.1 %all-gather.3.cloned.1.call-start = ((), (), s32[]{:S(2)}) async-start(), calls=%async_computation | async-start | bytes 4325376 | tf_op jit(solution)/shard_map/all_gather | solution.py:129
  6.5 10.2 %collective-permute-start.8 = (bf16[64,512]{1,0:T(8,128)(2,1)}, bf16[64,512]{1,0:T(8,128)(2,1)S(1)}, u32[]{:S(2)}, u32[]{:S(2)}) collective-permute-start(bf16[64,512]{1,0:T(8,128)(2,1)} %param.7), channel_id=1, source_target_pairs={{0,256},{256,0},{1,257},{257,1},{2,258},{258,2},{3,259},{259,3},{4... | collective-permute-start | bytes 196616 | tf_op jit(solution)/shard_map/ppermute | solution.py:126
  21.2 20.0 %collective-permute-start = (bf16[131,2,512]{2,1,0:T(2,128)(2,1)}, bf16[131,2,512]{2,1,0:T(2,128)(2,1)S(1)}, u32[]{:S(2)}, u32[]{:S(2)}) collective-permute-start(bf16[131,2,512]{2,1,0:T(2,128)(2,1)} %pad_maximum_fusion.1), channel_id=1, source_target_pairs={{0,8},{8,16},{16,24},{24,32},{32,40},{40,48},{48,56},{56,64},{64,7... | collective-permute-start | bytes 804872 | tf_op jit(solution)/shard_map/ppermute | solution.py:20
  26.6 5.7 %copy-start.2 = (bf16[512,3,512]{2,0,1:T(8,128)(2,1)S(1)}, bf16[512,3,512]{2,0,1:T(8,128)(2,1)}, u32[]{:S(2)}) copy-start(bf16[512,3,512]{2,0,1:T(8,128)(2,1)} %param.4) | copy-start | bytes 4718596
  26.6 14.8 %slice-start = ((bf16[512,3,512]{2,0,1:T(8,128)(2,1)}), bf16[512,2,512]{2,0,1:T(8,128)(2,1)S(1)}, s32[]{:S(2)}) async-start(bf16[512,3,512]{2,0,1:T(8,128)(2,1)} %param.4), calls=%async_computation.1 | async-start | bytes 2097152 | tf_op jit(solution)/shard_map/slice | solution.py:134
  44.0 4.2 %copy-start = (bf16[32,128,256]{2,1,0:T(8,128)(2,1)S(1)}, bf16[32,128,256]{2,1,0:T(8,128)(2,1)}, u32[]{:S(2)}) copy-start(bf16[32,128,256]{2,1,0:T(8,128)(2,1)} %shard_map.46) | copy-start | bytes 6291460
  51.5 11.4 %collective-permute-start.1 = (bf16[512,512]{1,0:T(8,128)(2,1)S(1)}, bf16[512,512]{1,0:T(8,128)(2,1)S(1)}, u32[]{:S(2)}, u32[]{:S(2)}) collective-permute-start(bf16[512,512]{1,0:T(8,128)(2,1)S(1)} %fusion.10), channel_id=1, source_target_pairs={{2,0},{4,2},{6,4},{3,1},{5,3},{7,5},{10,8},{12,10},{14,12},{11,9},... | collective-permute-start | bytes 1572872 | tf_op jit(solution)/shard_map/ppermute | solution.py:60
  53.4 16.8 %collective-permute-start.2 = (bf16[512,512]{1,0:T(8,128)(2,1)S(1)}, bf16[512,512]{1,0:T(8,128)(2,1)S(1)}, u32[]{:S(2)}, u32[]{:S(2)}) collective-permute-start(bf16[512,512]{1,0:T(8,128)(2,1)S(1)} %fusion.10), channel_id=1, source_target_pairs={{0,6},{1,7},{8,14},{9,15},{16,22},{17,23},{24,30},{25,31},{32,38},... | collective-permute-start | bytes 1572872 | tf_op jit(solution)/shard_map/ppermute | solution.py:60
  54.1 41.0 %collective-permute-start.3 = (bf16[512,512]{1,0:T(8,128)(2,1)S(1)}, bf16[512,512]{1,0:T(8,128)(2,1)S(1)}, u32[]{:S(2)}, u32[]{:S(2)}) collective-permute-start(bf16[512,512]{1,0:T(8,128)(2,1)S(1)} %fusion.10), channel_id=1, source_target_pairs={{4,0},{6,2},{5,1},{7,3},{12,8},{14,10},{13,9},{15,11},{20,16},{22,... | collective-permute-start | bytes 1572872 | tf_op jit(solution)/shard_map/ppermute | solution.py:60
  60.9 34.2 %collective-permute-start.4 = (bf16[512,512]{1,0:T(8,128)(2,1)S(1)}, bf16[512,512]{1,0:T(8,128)(2,1)S(1)}, u32[]{:S(2)}, u32[]{:S(2)}) collective-permute-start(bf16[512,512]{1,0:T(8,128)(2,1)S(1)} %fusion.10), channel_id=1, source_target_pairs={{0,4},{2,6},{1,5},{3,7},{8,12},{10,14},{9,13},{11,15},{16,20},{18,... | collective-permute-start | bytes 1572872 | tf_op jit(solution)/shard_map/ppermute | solution.py:60
  62.2 33.0 %collective-permute-start.5 = (bf16[512,512]{1,0:T(8,128)(2,1)S(1)}, bf16[512,512]{1,0:T(8,128)(2,1)S(1)}, u32[]{:S(2)}, u32[]{:S(2)}) collective-permute-start(bf16[512,512]{1,0:T(8,128)(2,1)S(1)} %fusion.10), channel_id=1, source_target_pairs={{6,0},{7,1},{14,8},{15,9},{22,16},{23,17},{30,24},{31,25},{38,32},... | collective-permute-start | bytes 1572872 | tf_op jit(solution)/shard_map/ppermute | solution.py:60
  62.9 38.8 %collective-permute-start.6 = (bf16[512,512]{1,0:T(8,128)(2,1)S(1)}, bf16[512,512]{1,0:T(8,128)(2,1)S(1)}, u32[]{:S(2)}, u32[]{:S(2)}) collective-permute-start(bf16[512,512]{1,0:T(8,128)(2,1)S(1)} %fusion.10), channel_id=1, source_target_pairs={{0,2},{2,4},{4,6},{1,3},{3,5},{5,7},{8,10},{10,12},{12,14},{9,11},... | collective-permute-start | bytes 1572872 | tf_op jit(solution)/shard_map/ppermute | solution.py:60
  102.0 9.6 %copy-start.1 = (bf16[4,512,512]{2,1,0:T(8,128)(2,1)}, bf16[4,512,512]{2,1,0:T(8,128)(2,1)S(1)}, u32[]{:S(2)}) copy-start(bf16[4,512,512]{2,1,0:T(8,128)(2,1)S(1)} %pad_maximum_fusion.own_ref) | copy-start | bytes 6291460
  102.0 9.6 %collective-permute-start.7 = (bf16[4,512,512]{2,1,0:T(8,128)(2,1)S(1)}, bf16[4,512,512]{2,1,0:T(8,128)(2,1)}, u32[]{:S(2)}, u32[]{:S(2)}) collective-permute-start(bf16[4,512,512]{2,1,0:T(8,128)(2,1)S(1)} %pad_maximum_fusion.own_ref), channel_id=1, source_target_pairs={{0,1},{1,0},{2,3},{3,2},{4,5},{5,4},{6,7},{7,6},{8,9},{9,8},{10,11... | collective-permute-start | bytes 6291464 | tf_op jit(solution)/shard_map/ppermute | solution.py:149
Sparse Core Ops, SparseCore 0:
  18.3 86.0 all-gather.2

commit v16 on v13

--- a/solution.py
+++ b/solution.py
@@ -52,15 +52,11 @@
 
 
 def line_slots(block, axis_name, size):
-    index = lax.axis_index(axis_name)
-    received = {}
-    for offset in range(1, size):
-        for d in (offset, -offset):
-            pairs = [(i, i + d) for i in range(size) if 0 <= i + d < size]
-            received[d] = lax.ppermute(block, axis_name, pairs)
     slots = [block]
     for k in range(1, size):
-        slots.append(jnp.where(index + k < size, received[-k], received[size - k]))
+        shift = size - k
+        pairs = [(i, (i + shift) % size) for i in range(size)]
+        slots.append(lax.ppermute(block, axis_name, pairs))
     return jnp.stack(slots)
 
 

time: 127 us -> 127 us (level)
  waiting for transfers between devices: 43.8 us -> 54.9 us
  starting transfers between devices: 37.7 us -> 27 us
    ppermute x6 -> x3, waiting for transfers between devices: 28.6 us -> 39.5 us  [line_slots(): slots.append(lax.ppermute(block, axis_name, pairs))]
    ppermute x6 -> x3, starting transfers between devices: 21.3 us -> 10.5 us  [line_slots(): slots.append(lax.ppermute(block, axis_name, pairs))]
  transfers between devices with their start and end apart: 10 -> 7, of which waited for: 4 -> 5; matrix products, arithmetic and copies ran while one was open for 13% -> 13% of each run, Pallas kernels for 5% -> 5%
where the time goes in v16:
time: 127 us; the launch traced here: 126 us
  waiting for transfers between devices  54.9 us (43%)
  starting transfers between devices  27 us (21%)
  between operations  13.6 us (11%)
  Pallas kernels  13.1 us (10%)
  local copies, waits for them, and re-layouts  9.34 us (7%)
  other arithmetic  6.11 us (5%)
  matrix products  1.88 us (1%)
    ppermute x3, waiting for transfers between devices, line_slots(): slots.append(lax.ppermute(block, axis_name, pairs))  39.5 us
    ppermute x1, starting transfers between devices, on_device(): partner = lax.ppermute(out_weight, 'zh', [(0, 1), (1, 0)])  11 us
    ppermute x3, starting transfers between devices, line_slots(): slots.append(lax.ppermute(block, axis_name, pairs))  10.5 us
    all_gather x1, waiting for transfers between devices, on_device(): weight_xy = lax.all_gather(pair, ('x', 'y'), axis=0, tiled=False)  8.47 us
    pallas_call x1, Pallas kernels, block_matmul(): pl.pallas_call(matmul_kernel, grid_spec=grid_spec, out_shape=jax.ShapeDty...  7.36 us
    pallas_call x1, Pallas kernels, toeplitz_blocks(): pl.pallas_call(toeplitz_kernel, out_shape=jax.ShapeDtypeStruct((groups, s...  5.71 us
    slice x7, local copies, waits for them, and re-layouts, on_device(): window = jnp.concatenate([blocks[:-1], blocks[1:]], axis=1)  5.42 us
    ppermute x1, waiting for transfers between devices, on_device(): other = lax.ppermute(own, 'c', [(0, 1), (1, 0)])  3.54 us
  transfers between devices with their start and end apart: 7, of which 5 were waited for; matrix products, arithmetic and copies ran while one was open for 13% of the time, Pallas kernels for 5%

profile of v16, /device:TPU:8, one launch (start us, length us, event | category | flops | bytes accessed | tf_op | source)
XLA Modules:
  0.0 125.9 jit_solution(15649038184470340068)
XLA Ops:
  6.5 0.0 all-gather.3.cloned.1.call-start
  6.5 11.0 %collective-permute-start.5 = (bf16[64,512]{1,0:T(8,128)(2,1)}, bf16[64,512]{1,0:T(8,128)(2,1)S(1)}, u32[]{:S(2)}, u32[]{:S(2)}) collective-permute-start(bf16[64,512]{1,0:T(8,128)(2,1)} %param.7), channel_id=1, source_target_pairs={{0,256},{256,0},{1,257},{257,1},{2,258},{258,2},{3,259},{259,3},{4... | collective-permute-start | bytes 196616 | tf_op jit(solution)/shard_map/ppermute | solution.py:122
  17.6 3.4 %collective-permute-done.5 = bf16[64,512]{1,0:T(8,128)(2,1)S(1)} collective-permute-done((bf16[64,512]{1,0:T(8,128)(2,1)}, bf16[64,512]{1,0:T(8,128)(2,1)S(1)}, u32[]{:S(2)}, u32[]{:S(2)}) %collective-permute-start.5) | collective-permute-done | bytes 65568 | tf_op jit(solution)/shard_map/ppermute | solution.py:122
  20.9 1.5 %pad_maximum_fusion.2 = bf16[2,64,512]{2,1,0:T(8,128)(2,1)} fusion(bf16[1,64,512]{2,1,0:T(8,128)(2,1)S(1)} %bitcast.52, bf16[1,64,512]{2,1,0:T(8,128)(2,1)} %bitcast.51), kind=kLoop, calls=%fused_computation.26 | loop fusion | flops 65536 | bytes 262144 | tf_op jit(solution)/shard_map/stack | solution.py:124
  22.4 0.0 all-gather.3.cloned.1.call-update
  22.5 1.0 slice.75
  23.5 0.2 copy.25
  23.7 0.7 slice_bitcast_fusion.5
  24.4 1.1 pad_maximum_fusion.1
  25.5 3.5 %collective-permute-start = (bf16[131,2,512]{2,1,0:T(2,128)(2,1)}, bf16[131,2,512]{2,1,0:T(2,128)(2,1)S(1)}, u32[]{:S(2)}, u32[]{:S(2)}) collective-permute-start(bf16[131,2,512]{2,1,0:T(2,128)(2,1)} %pad_maximum_fusion.1), channel_id=1, source_target_pairs={{0,8},{8,16},{16,24},{24,32},{32,40},{40,48},{48,56},{56,64},{64,7... | collective-permute-start | bytes 804872 | tf_op jit(solution)/shard_map/ppermute | solution.py:20
  29.0 0.8 rev.3
  29.7 0.1 pad.8.clone
  29.8 0.0 copy-done.3
  29.8 0.7 maximum_maximum_fusion.row_ref
  30.6 5.7 %shard_map.46 = bf16[32,128,256]{2,1,0:T(8,128)(2,1)} custom-call(f32[32,384]{1,0:T(8,128)} %maximum_maximum_fusion.row_ref), custom_call_target="tpu_custom_call" | custom-call | tf_op jit(solution)/shard_map/pallas_call | solution.py:48
  36.3 0.0 copy-done.2
  36.3 0.0 collective-permute-done
  36.3 0.2 slice.102
  36.5 0.0 slice-done
  36.6 0.4 maximum_convert_fusion
  36.9 0.8 fusion
  37.7 0.2 fusion.7
  37.9 0.9 fusion.20
  38.8 0.2 copy.18
  39.0 0.1 slice.95
  39.1 0.0 copy-start
  39.2 0.9 copy.20
  40.1 1.3 %copy.19 = bf16[512,1,512]{0,2,1:T(8,128)(2,1)S(1)} copy(bf16[512,1,512]{2,0,1:T(8,128)(2,1)} %get-tuple-element.6) | data formatting | bytes 1048576 | tf_op jit(solution)/shard_map/slice | solution.py:137
  41.3 0.9 slice.97
  42.2 1.1 copy.21
  43.4 1.9 %fusion.4 = f32[4,128,32,16]{1,3,0,2:T(8,128)S(1)} fusion(bf16[32,128,256]{2,1,0:T(8,128)(2,1)S(1)} %copy-done, bf16[4,128,32,16]{1,3,0,2:T(8,128)(2,1)S(1)} %copy.21, bf16[4,128,32,16]{1,3,0,2:T(8,128)(2,1)} %copy.20), kind=kOutput, calls=%fused_computation.8 | convolution fusion | flops 136314880 | bytes 4194304 | tf_op jit(solution)/shard_map/gij,bjgc->bigc/dot_general | solution.py:139
  45.3 0.4 copy.22
  45.7 0.1 copy.28
  45.8 0.3 copy.23
  46.1 0.2 maximum_convert_fusion.1
  46.3 0.4 fusion.10
  46.7 4.3 %collective-permute-start.1 = (bf16[512,512]{1,0:T(8,128)(2,1)S(1)}, bf16[512,512]{1,0:T(8,128)(2,1)S(1)}, u32[]{:S(2)}, u32[]{:S(2)}) collective-permute-start(bf16[512,512]{1,0:T(8,128)(2,1)S(1)} %fusion.10), channel_id=1, source_target_pairs={{0,6},{2,0},{4,2},{6,4},{1,7},{3,1},{5,3},{7,5},{8,14},{10,8},{12,... | collective-permute-start | bytes 1572872 | tf_op jit(solution)/shard_map/ppermute | solution.py:59
  50.9 2.3 %collective-permute-start.2 = (bf16[512,512]{1,0:T(8,128)(2,1)S(1)}, bf16[512,512]{1,0:T(8,128)(2,1)S(1)}, u32[]{:S(2)}, u32[]{:S(2)}) collective-permute-start(bf16[512,512]{1,0:T(8,128)(2,1)S(1)} %fusion.10), channel_id=1, source_target_pairs={{0,4},{2,6},{4,0},{6,2},{1,5},{3,7},{5,1},{7,3},{8,12},{10,14},{12... | collective-permute-start | bytes 1572872 | tf_op jit(solution)/shard_map/ppermute | solution.py:59
  53.3 3.9 %collective-permute-start.3 = (bf16[512,512]{1,0:T(8,128)(2,1)S(1)}, bf16[512,512]{1,0:T(8,128)(2,1)S(1)}, u32[]{:S(2)}, u32[]{:S(2)}) collective-permute-start(bf16[512,512]{1,0:T(8,128)(2,1)S(1)} %fusion.10), channel_id=1, source_target_pairs={{0,2},{2,4},{4,6},{6,0},{1,3},{3,5},{5,7},{7,1},{8,10},{10,12},{12... | collective-permute-start | bytes 1572872 | tf_op jit(solution)/shard_map/ppermute | solution.py:59
  57.2 6.2 %collective-permute-done.1 = bf16[512,512]{1,0:T(8,128)(2,1)S(1)} collective-permute-done((bf16[512,512]{1,0:T(8,128)(2,1)S(1)}, bf16[512,512]{1,0:T(8,128)(2,1)S(1)}, u32[]{:S(2)}, u32[]{:S(2)}) %collective-permute-start.1) | collective-permute-done | bytes 524320 | tf_op jit(solution)/shard_map/ppermute | solution.py:59
  63.4 33.3 %collective-permute-done.2 = bf16[512,512]{1,0:T(8,128)(2,1)S(1)} collective-permute-done((bf16[512,512]{1,0:T(8,128)(2,1)S(1)}, bf16[512,512]{1,0:T(8,128)(2,1)S(1)}, u32[]{:S(2)}, u32[]{:S(2)}) %collective-permute-start.2) | collective-permute-done | bytes 524320 | tf_op jit(solution)/shard_map/ppermute | solution.py:59
  96.7 0.0 collective-permute-done.3
  96.7 0.3 pad_maximum_fusion.own_ref
  97.0 1.9 %collective-permute-start.4 = (bf16[4,512,512]{2,1,0:T(8,128)(2,1)S(1)}, bf16[4,512,512]{2,1,0:T(8,128)(2,1)}, u32[]{:S(2)}, u32[]{:S(2)}) collective-permute-start(bf16[4,512,512]{2,1,0:T(8,128)(2,1)S(1)} %pad_maximum_fusion.own_ref), channel_id=1, source_target_pairs={{0,1},{1,0},{2,3},{3,2},{4,5},{5,4},{6,7},{7,6},{8,9},{9,8},{10,11... | collective-permute-start | bytes 6291464 | tf_op jit(solution)/shard_map/ppermute | solution.py:145
  99.0 0.7 add_add_fusion.table_ref
  99.7 3.5 %collective-permute-done.4.other_ref = bf16[4,512,512]{2,1,0:T(8,128)(2,1)} collective-permute-done((bf16[4,512,512]{2,1,0:T(8,128)(2,1)S(1)}, bf16[4,512,512]{2,1,0:T(8,128)(2,1)}, u32[]{:S(2)}, u32[]{:S(2)}) %collective-permute-start.4) | collective-permute-done | bytes 2097184 | tf_op jit(solution)/shard_map/ppermute | solution.py:145
  103.2 8.5 %all-gather.3.cloned.1.call-done = bf16[64,64,512]{2,1,0:T(8,128)(2,1)} async-done(((bf16[2,64,512]{2,1,0:T(8,128)(2,1)}), bf16[64,64,512]{2,1,0:T(8,128)(2,1)}) %all-gather.3.cloned.1.call-update) | async-done | bytes 4194320 | tf_op jit(solution)/shard_map/all_gather | solution.py:125
  111.7 7.4 %shard_map.47 = bf16[512,512]{1,0:T(8,128)(2,1)} custom-call(s32[2,8]{1,0:T(2,128)} %add_add_fusion.table_ref, bf16[4,512,512]{2,1,0:T(8,128)(2,1)} %copy-done.1, bf16[4,512,512]{2,1,0:T(8,128)(2,1)} %collective-permute-done.4.other_ref, bf16[4,8,2,64,512]{4,3,2,1,0:T(8,128)(2,1)} %bitcast.43, bf16[4,8,2,64,512]{4,3,2,1,0:T(8,128)(2,1)} %bitcast.44), custom_call_target="tpu_custom_call" | custom-call | tf_op jit(solution)/shard_map/pallas_call | solution.py:110
  (16 shorter events, 0.2 us)
Async XLA Ops:
  6.5 23.3 %copy-start.3 = (f32[3,3,512]{2,1,0:T(4,128)S(1)}, f32[3,3,512]{2,1,0:T(4,128)}, u32[]{:S(2)}) copy-start(f32[3,3,512]{2,1,0:T(4,128)} %param.5) | copy-start | bytes 55300
  6.5 105.1 %all-gather.3.cloned.1.call-start = ((), (), s32[]{:S(2)}) async-start(), calls=%async_computation | async-start | bytes 4325376 | tf_op jit(solution)/shard_map/all_gather | solution.py:125
  6.5 14.4 %collective-permute-start.5 = (bf16[64,512]{1,0:T(8,128)(2,1)}, bf16[64,512]{1,0:T(8,128)(2,1)S(1)}, u32[]{:S(2)}, u32[]{:S(2)}) collective-permute-start(bf16[64,512]{1,0:T(8,128)(2,1)} %param.7), channel_id=1, source_target_pairs={{0,256},{256,0},{1,257},{257,1},{2,258},{258,2},{3,259},{259,3},{4... | collective-permute-start | bytes 196616 | tf_op jit(solution)/shard_map/ppermute | solution.py:122
  25.5 10.8 %collective-permute-start = (bf16[131,2,512]{2,1,0:T(2,128)(2,1)}, bf16[131,2,512]{2,1,0:T(2,128)(2,1)S(1)}, u32[]{:S(2)}, u32[]{:S(2)}) collective-permute-start(bf16[131,2,512]{2,1,0:T(2,128)(2,1)} %pad_maximum_fusion.1), channel_id=1, source_target_pairs={{0,8},{8,16},{16,24},{24,32},{32,40},{40,48},{48,56},{56,64},{64,7... | collective-permute-start | bytes 804872 | tf_op jit(solution)/shard_map/ppermute | solution.py:20
  30.5 5.7 %copy-start.2 = (bf16[512,3,512]{2,0,1:T(8,128)(2,1)S(1)}, bf16[512,3,512]{2,0,1:T(8,128)(2,1)}, u32[]{:S(2)}) copy-start(bf16[512,3,512]{2,0,1:T(8,128)(2,1)} %param.4) | copy-start | bytes 4718596
  30.5 6.0 %slice-start = ((bf16[512,3,512]{2,0,1:T(8,128)(2,1)}), bf16[512,2,512]{2,0,1:T(8,128)(2,1)S(1)}, s32[]{:S(2)}) async-start(bf16[512,3,512]{2,0,1:T(8,128)(2,1)} %param.4), calls=%async_computation.1 | async-start | bytes 2097152 | tf_op jit(solution)/shard_map/slice | solution.py:130
  39.1 4.2 %copy-start = (bf16[32,128,256]{2,1,0:T(8,128)(2,1)S(1)}, bf16[32,128,256]{2,1,0:T(8,128)(2,1)}, u32[]{:S(2)}) copy-start(bf16[32,128,256]{2,1,0:T(8,128)(2,1)} %shard_map.46) | copy-start | bytes 6291460
  46.7 16.7 %collective-permute-start.1 = (bf16[512,512]{1,0:T(8,128)(2,1)S(1)}, bf16[512,512]{1,0:T(8,128)(2,1)S(1)}, u32[]{:S(2)}, u32[]{:S(2)}) collective-permute-start(bf16[512,512]{1,0:T(8,128)(2,1)S(1)} %fusion.10), channel_id=1, source_target_pairs={{0,6},{2,0},{4,2},{6,4},{1,7},{3,1},{5,3},{7,5},{8,14},{10,8},{12,... | collective-permute-start | bytes 1572872 | tf_op jit(solution)/shard_map/ppermute | solution.py:59
  50.9 45.8 %collective-permute-start.2 = (bf16[512,512]{1,0:T(8,128)(2,1)S(1)}, bf16[512,512]{1,0:T(8,128)(2,1)S(1)}, u32[]{:S(2)}, u32[]{:S(2)}) collective-permute-start(bf16[512,512]{1,0:T(8,128)(2,1)S(1)} %fusion.10), channel_id=1, source_target_pairs={{0,4},{2,6},{4,0},{6,2},{1,5},{3,7},{5,1},{7,3},{8,12},{10,14},{12... | collective-permute-start | bytes 1572872 | tf_op jit(solution)/shard_map/ppermute | solution.py:59
  53.3 43.4 %collective-permute-start.3 = (bf16[512,512]{1,0:T(8,128)(2,1)S(1)}, bf16[512,512]{1,0:T(8,128)(2,1)S(1)}, u32[]{:S(2)}, u32[]{:S(2)}) collective-permute-start(bf16[512,512]{1,0:T(8,128)(2,1)S(1)} %fusion.10), channel_id=1, source_target_pairs={{0,2},{2,4},{4,6},{6,0},{1,3},{3,5},{5,7},{7,1},{8,10},{10,12},{12... | collective-permute-start | bytes 1572872 | tf_op jit(solution)/shard_map/ppermute | solution.py:59
  97.0 14.7 %copy-start.1 = (bf16[4,512,512]{2,1,0:T(8,128)(2,1)}, bf16[4,512,512]{2,1,0:T(8,128)(2,1)S(1)}, u32[]{:S(2)}) copy-start(bf16[4,512,512]{2,1,0:T(8,128)(2,1)S(1)} %pad_maximum_fusion.own_ref) | copy-start | bytes 6291460
  97.0 6.2 %collective-permute-start.4 = (bf16[4,512,512]{2,1,0:T(8,128)(2,1)S(1)}, bf16[4,512,512]{2,1,0:T(8,128)(2,1)}, u32[]{:S(2)}, u32[]{:S(2)}) collective-permute-start(bf16[4,512,512]{2,1,0:T(8,128)(2,1)S(1)} %pad_maximum_fusion.own_ref), channel_id=1, source_target_pairs={{0,1},{1,0},{2,3},{3,2},{4,5},{5,4},{6,7},{7,6},{8,9},{9,8},{10,11... | collective-permute-start | bytes 6291464 | tf_op jit(solution)/shard_map/ppermute | solution.py:145
Sparse Core Ops, SparseCore 0:
  22.6 89.0 all-gather.2

commit v17 on v16

--- a/solution.py
+++ b/solution.py
@@ -119,9 +119,11 @@
     groups, span = long_filter.shape
     channels = projected.shape[2]
 
-    partner = lax.ppermute(out_weight, "zh", [(0, 1), (1, 0)])
+    pair = jnp.stack([out_weight, jnp.zeros_like(out_weight)])
+    pair, sent = lax.optimization_barrier((pair, out_weight))
+    partner = lax.ppermute(sent, "zh", [(0, 1), (1, 0)])
     zh = lax.axis_index("zh")
-    pair = jnp.stack([out_weight, partner])
+    pair = lax.dynamic_update_index_in_dim(pair, partner, 1, 0)
     weight_xy = lax.all_gather(pair, ("x", "y"), axis=0, tiled=False)
 
     kv_tail = projected[tok_rows - span - 2 :, 1:]

time: 127 us -> 126 us (level)
  other arithmetic: 6.11 us -> 4.62 us
    another operation x1 -> x0, other arithmetic: 1.5 us -> none  [on_device(): pair = jnp.stack([out_weight, partner])]
  transfers between devices with their start and end apart: 7 -> 7, of which waited for: 5 -> 5; matrix products, arithmetic and copies ran while one was open for 13% -> 12% of each run, Pallas kernels for 5% -> 5%
where the time goes in v17:
time: 126 us
  waiting for transfers between devices  55.4 us (44%)
  starting transfers between devices  27 us (21%)
  between operations  13.6 us (11%)
  Pallas kernels  13.1 us (10%)
  local copies, waits for them, and re-layouts  10.2 us (8%)
  other arithmetic  4.62 us (4%)
  matrix products  1.88 us (1%)
    ppermute x3, waiting for transfers between devices, line_slots(): slots.append(lax.ppermute(block, axis_name, pairs))  39.4 us
    ppermute x1, starting transfers between devices, on_device(): partner = lax.ppermute(sent, 'zh', [(0, 1), (1, 0)])  10.9 us
    ppermute x3, starting transfers between devices, line_slots(): slots.append(lax.ppermute(block, axis_name, pairs))  10.7 us
    all_gather x1, waiting for transfers between devices, on_device(): weight_xy = lax.all_gather(pair, ('x', 'y'), axis=0, tiled=False)  9.12 us
    pallas_call x1, Pallas kernels, block_matmul(): pl.pallas_call(matmul_kernel, grid_spec=grid_spec, out_shape=jax.ShapeDty...  7.36 us
    pallas_call x1, Pallas kernels, toeplitz_blocks(): pl.pallas_call(toeplitz_kernel, out_shape=jax.ShapeDtypeStruct((groups, s...  5.7 us
    slice x7, local copies, waits for them, and re-layouts, on_device(): window = jnp.concatenate([blocks[:-1], blocks[1:]], axis=1)  5.41 us
    ppermute x1, waiting for transfers between devices, on_device(): other = lax.ppermute(own, 'c', [(0, 1), (1, 0)])  3.52 us
  transfers between devices with their start and end apart: 7, of which 5 were waited for; matrix products, arithmetic and copies ran while one was open for 12% of the time, Pallas kernels for 5%

profile of v17, /device:TPU:8, one launch (start us, length us, event | category | flops | bytes accessed | tf_op | source)
XLA Modules:
  0.0 125.7 jit_solution(3499161028782760149)
XLA Ops:
  6.5 0.0 all-gather.2.cloned.1.call-start
  6.5 0.9 stack.39
  7.4 10.9 %collective-permute-start.5 = (bf16[64,512]{1,0:T(8,128)(2,1)}, bf16[64,512]{1,0:T(8,128)(2,1)S(1)}, u32[]{:S(2)}, u32[]{:S(2)}) collective-permute-start(bf16[64,512]{1,0:T(8,128)(2,1)} %param.7), channel_id=1, source_target_pairs={{0,256},{256,0},{1,257},{257,1},{2,258},{258,2},{3,259},{259,3},{4... | collective-permute-start | bytes 196616 | tf_op jit(solution)/shard_map/ppermute | solution.py:124
  18.3 3.4 %collective-permute-done.5 = bf16[64,512]{1,0:T(8,128)(2,1)S(1)} collective-permute-done((bf16[64,512]{1,0:T(8,128)(2,1)}, bf16[64,512]{1,0:T(8,128)(2,1)S(1)}, u32[]{:S(2)}, u32[]{:S(2)}) %collective-permute-start.5) | collective-permute-done | bytes 65568 | tf_op jit(solution)/shard_map/ppermute | solution.py:124
  21.7 0.7 copy-done.3
  22.4 0.0 all-gather.2.cloned.1.call-update
  22.4 1.0 slice.75
  23.4 0.2 copy.25
  23.6 0.7 slice_bitcast_fusion.5
  24.3 1.1 pad_maximum_fusion.1
  25.4 3.5 %collective-permute-start = (bf16[131,2,512]{2,1,0:T(2,128)(2,1)}, bf16[131,2,512]{2,1,0:T(2,128)(2,1)S(1)}, u32[]{:S(2)}, u32[]{:S(2)}) collective-permute-start(bf16[131,2,512]{2,1,0:T(2,128)(2,1)} %pad_maximum_fusion.1), channel_id=1, source_target_pairs={{0,8},{8,16},{16,24},{24,32},{32,40},{40,48},{48,56},{56,64},{64,7... | collective-permute-start | bytes 804872 | tf_op jit(solution)/shard_map/ppermute | solution.py:20
  28.9 0.0 copy-done.5
  28.9 0.1 rev.3
  29.0 0.1 pad.7.clone
  29.1 0.7 maximum_maximum_fusion.row_ref
  29.8 5.7 %shard_map.46 = bf16[32,128,256]{2,1,0:T(8,128)(2,1)} custom-call(f32[32,384]{1,0:T(8,128)} %maximum_maximum_fusion.row_ref), custom_call_target="tpu_custom_call" | custom-call | tf_op jit(solution)/shard_map/pallas_call | solution.py:48
  35.5 0.0 copy-done.2
  35.5 0.0 collective-permute-done
  35.5 0.2 slice.102
  35.8 0.4 maximum_convert_fusion
  36.2 0.8 fusion
  37.0 0.2 fusion.7
  37.2 0.9 fusion.20
  38.0 0.2 copy.18
  38.3 0.1 slice.95
  38.4 0.9 copy.20
  39.3 1.3 %copy.19 = bf16[512,1,512]{0,2,1:T(8,128)(2,1)S(1)} copy(bf16[512,1,512]{2,0,1:T(8,128)(2,1)} %get-tuple-element.10) | data formatting | bytes 1048576 | tf_op jit(solution)/shard_map/slice | solution.py:139
  40.6 0.9 slice.97
  41.5 1.1 copy.21
  42.6 0.0 copy-done
  42.6 1.9 %fusion.4 = f32[4,128,32,16]{1,3,0,2:T(8,128)S(1)} fusion(bf16[32,128,256]{2,1,0:T(8,128)(2,1)S(1)} %copy-done, bf16[4,128,32,16]{1,3,0,2:T(8,128)(2,1)S(1)} %copy.21, bf16[4,128,32,16]{1,3,0,2:T(8,128)(2,1)} %copy.20), kind=kOutput, calls=%fused_computation.8 | convolution fusion | flops 136314880 | bytes 4194304 | tf_op jit(solution)/shard_map/gij,bjgc->bigc/dot_general | solution.py:141
  44.5 0.4 copy.22
  44.9 0.1 copy.28
  45.0 0.3 copy.23
  45.4 0.2 maximum_convert_fusion.1
  45.5 0.4 fusion.10
  45.9 4.3 %collective-permute-start.1 = (bf16[512,512]{1,0:T(8,128)(2,1)S(1)}, bf16[512,512]{1,0:T(8,128)(2,1)S(1)}, u32[]{:S(2)}, u32[]{:S(2)}) collective-permute-start(bf16[512,512]{1,0:T(8,128)(2,1)S(1)} %fusion.10), channel_id=1, source_target_pairs={{0,6},{2,0},{4,2},{6,4},{1,7},{3,1},{5,3},{7,5},{8,14},{10,8},{12,... | collective-permute-start | bytes 1572872 | tf_op jit(solution)/shard_map/ppermute | solution.py:59
  50.2 2.5 %collective-permute-start.2 = (bf16[512,512]{1,0:T(8,128)(2,1)S(1)}, bf16[512,512]{1,0:T(8,128)(2,1)S(1)}, u32[]{:S(2)}, u32[]{:S(2)}) collective-permute-start(bf16[512,512]{1,0:T(8,128)(2,1)S(1)} %fusion.10), channel_id=1, source_target_pairs={{0,4},{2,6},{4,0},{6,2},{1,5},{3,7},{5,1},{7,3},{8,12},{10,14},{12... | collective-permute-start | bytes 1572872 | tf_op jit(solution)/shard_map/ppermute | solution.py:59
  52.7 3.9 %collective-permute-start.3 = (bf16[512,512]{1,0:T(8,128)(2,1)S(1)}, bf16[512,512]{1,0:T(8,128)(2,1)S(1)}, u32[]{:S(2)}, u32[]{:S(2)}) collective-permute-start(bf16[512,512]{1,0:T(8,128)(2,1)S(1)} %fusion.10), channel_id=1, source_target_pairs={{0,2},{2,4},{4,6},{6,0},{1,3},{3,5},{5,7},{7,1},{8,10},{10,12},{12... | collective-permute-start | bytes 1572872 | tf_op jit(solution)/shard_map/ppermute | solution.py:59
  56.6 6.0 %collective-permute-done.1 = bf16[512,512]{1,0:T(8,128)(2,1)S(1)} collective-permute-done((bf16[512,512]{1,0:T(8,128)(2,1)S(1)}, bf16[512,512]{1,0:T(8,128)(2,1)S(1)}, u32[]{:S(2)}, u32[]{:S(2)}) %collective-permute-start.1) | collective-permute-done | bytes 524320 | tf_op jit(solution)/shard_map/ppermute | solution.py:59
  62.6 33.3 %collective-permute-done.2 = bf16[512,512]{1,0:T(8,128)(2,1)S(1)} collective-permute-done((bf16[512,512]{1,0:T(8,128)(2,1)S(1)}, bf16[512,512]{1,0:T(8,128)(2,1)S(1)}, u32[]{:S(2)}, u32[]{:S(2)}) %collective-permute-start.2) | collective-permute-done | bytes 524320 | tf_op jit(solution)/shard_map/ppermute | solution.py:59
  96.0 0.0 collective-permute-done.3
  96.0 0.3 pad_maximum_fusion.own_ref
  96.2 1.9 %collective-permute-start.4 = (bf16[4,512,512]{2,1,0:T(8,128)(2,1)S(1)}, bf16[4,512,512]{2,1,0:T(8,128)(2,1)}, u32[]{:S(2)}, u32[]{:S(2)}) collective-permute-start(bf16[4,512,512]{2,1,0:T(8,128)(2,1)S(1)} %pad_maximum_fusion.own_ref), channel_id=1, source_target_pairs={{0,1},{1,0},{2,3},{3,2},{4,5},{5,4},{6,7},{7,6},{8,9},{9,8},{10,11... | collective-permute-start | bytes 6291464 | tf_op jit(solution)/shard_map/ppermute | solution.py:147
  98.2 0.7 add_add_fusion.table_ref
  98.9 3.5 %collective-permute-done.4.other_ref = bf16[4,512,512]{2,1,0:T(8,128)(2,1)} collective-permute-done((bf16[4,512,512]{2,1,0:T(8,128)(2,1)S(1)}, bf16[4,512,512]{2,1,0:T(8,128)(2,1)}, u32[]{:S(2)}, u32[]{:S(2)}) %collective-permute-start.4) | collective-permute-done | bytes 2097184 | tf_op jit(solution)/shard_map/ppermute | solution.py:147
  102.4 9.1 %all-gather.2.cloned.1.call-done = bf16[32,2,64,512]{3,2,1,0:T(8,128)(2,1)} async-done(((bf16[1,2,64,512]{3,2,1,0:T(8,128)(2,1)}), bf16[32,2,64,512]{3,2,1,0:T(8,128)(2,1)}) %all-gather.2.cloned.1.call-update) | async-done | bytes 4194320 | tf_op jit(solution)/shard_map/all_gather | solution.py:127
  111.5 7.4 %shard_map.47 = bf16[512,512]{1,0:T(8,128)(2,1)} custom-call(s32[2,8]{1,0:T(2,128)} %add_add_fusion.table_ref, bf16[4,512,512]{2,1,0:T(8,128)(2,1)} %copy-done.1, bf16[4,512,512]{2,1,0:T(8,128)(2,1)} %collective-permute-done.4.other_ref, bf16[4,8,2,64,512]{4,3,2,1,0:T(8,128)(2,1)} %bitcast.45, bf16[4,8,2,64,512]{4,3,2,1,0:T(8,128)(2,1)} %bitcast.46), custom_call_target="tpu_custom_call" | custom-call | tf_op jit(solution)/shard_map/pallas_call | solution.py:110
  (21 shorter events, 0.2 us)
Async XLA Ops:
  6.5 22.3 %copy-start.5 = (bf16[32,128]{1,0:T(8,128)(2,1)S(1)}, bf16[32,128]{1,0:T(8,128)(2,1)}, u32[]{:S(2)}) copy-start(bf16[32,128]{1,0:T(8,128)(2,1)} %param.6) | copy-start | bytes 24580
  6.5 22.5 %copy-start.4 = (f32[3,3,512]{2,1,0:T(4,128)S(1)}, f32[3,3,512]{2,1,0:T(4,128)}, u32[]{:S(2)}) copy-start(f32[3,3,512]{2,1,0:T(4,128)} %param.5) | copy-start | bytes 55300
  6.5 105.0 %all-gather.2.cloned.1.call-start = ((), (), s32[]{:S(2)}) async-start(), calls=%async_computation | async-start | bytes 4325376 | tf_op jit(solution)/shard_map/all_gather | solution.py:127
  7.4 14.3 %collective-permute-start.5 = (bf16[64,512]{1,0:T(8,128)(2,1)}, bf16[64,512]{1,0:T(8,128)(2,1)S(1)}, u32[]{:S(2)}, u32[]{:S(2)}) collective-permute-start(bf16[64,512]{1,0:T(8,128)(2,1)} %param.7), channel_id=1, source_target_pairs={{0,256},{256,0},{1,257},{257,1},{2,258},{258,2},{3,259},{259,3},{4... | collective-permute-start | bytes 196616 | tf_op jit(solution)/shard_map/ppermute | solution.py:124
  21.7 0.7 copy-start.3
  25.4 10.1 %collective-permute-start = (bf16[131,2,512]{2,1,0:T(2,128)(2,1)}, bf16[131,2,512]{2,1,0:T(2,128)(2,1)S(1)}, u32[]{:S(2)}, u32[]{:S(2)}) collective-permute-start(bf16[131,2,512]{2,1,0:T(2,128)(2,1)} %pad_maximum_fusion.1), channel_id=1, source_target_pairs={{0,8},{8,16},{16,24},{24,32},{32,40},{40,48},{48,56},{56,64},{64,7... | collective-permute-start | bytes 804872 | tf_op jit(solution)/shard_map/ppermute | solution.py:20
  29.8 5.7 %copy-start.2 = (bf16[512,3,512]{2,0,1:T(8,128)(2,1)S(1)}, bf16[512,3,512]{2,0,1:T(8,128)(2,1)}, u32[]{:S(2)}) copy-start(bf16[512,3,512]{2,0,1:T(8,128)(2,1)} %param.4) | copy-start | bytes 4718596
  29.8 6.0 %slice-start = ((bf16[512,3,512]{2,0,1:T(8,128)(2,1)}), bf16[512,2,512]{2,0,1:T(8,128)(2,1)S(1)}, s32[]{:S(2)}) async-start(bf16[512,3,512]{2,0,1:T(8,128)(2,1)} %param.4), calls=%async_computation.1 | async-start | bytes 2097152 | tf_op jit(solution)/shard_map/slice | solution.py:132
  38.4 4.2 %copy-start = (bf16[32,128,256]{2,1,0:T(8,128)(2,1)S(1)}, bf16[32,128,256]{2,1,0:T(8,128)(2,1)}, u32[]{:S(2)}) copy-start(bf16[32,128,256]{2,1,0:T(8,128)(2,1)} %shard_map.46) | copy-start | bytes 6291460
  45.9 16.7 %collective-permute-start.1 = (bf16[512,512]{1,0:T(8,128)(2,1)S(1)}, bf16[512,512]{1,0:T(8,128)(2,1)S(1)}, u32[]{:S(2)}, u32[]{:S(2)}) collective-permute-start(bf16[512,512]{1,0:T(8,128)(2,1)S(1)} %fusion.10), channel_id=1, source_target_pairs={{0,6},{2,0},{4,2},{6,4},{1,7},{3,1},{5,3},{7,5},{8,14},{10,8},{12,... | collective-permute-start | bytes 1572872 | tf_op jit(solution)/shard_map/ppermute | solution.py:59
  50.2 45.8 %collective-permute-start.2 = (bf16[512,512]{1,0:T(8,128)(2,1)S(1)}, bf16[512,512]{1,0:T(8,128)(2,1)S(1)}, u32[]{:S(2)}, u32[]{:S(2)}) collective-permute-start(bf16[512,512]{1,0:T(8,128)(2,1)S(1)} %fusion.10), channel_id=1, source_target_pairs={{0,4},{2,6},{4,0},{6,2},{1,5},{3,7},{5,1},{7,3},{8,12},{10,14},{12... | collective-permute-start | bytes 1572872 | tf_op jit(solution)/shard_map/ppermute | solution.py:59
  52.7 43.3 %collective-permute-start.3 = (bf16[512,512]{1,0:T(8,128)(2,1)S(1)}, bf16[512,512]{1,0:T(8,128)(2,1)S(1)}, u32[]{:S(2)}, u32[]{:S(2)}) collective-permute-start(bf16[512,512]{1,0:T(8,128)(2,1)S(1)} %fusion.10), channel_id=1, source_target_pairs={{0,2},{2,4},{4,6},{6,0},{1,3},{3,5},{5,7},{7,1},{8,10},{10,12},{12... | collective-permute-start | bytes 1572872 | tf_op jit(solution)/shard_map/ppermute | solution.py:59
  96.2 15.3 %copy-start.1 = (bf16[4,512,512]{2,1,0:T(8,128)(2,1)}, bf16[4,512,512]{2,1,0:T(8,128)(2,1)S(1)}, u32[]{:S(2)}) copy-start(bf16[4,512,512]{2,1,0:T(8,128)(2,1)S(1)} %pad_maximum_fusion.own_ref) | copy-start | bytes 6291460
  96.2 6.2 %collective-permute-start.4 = (bf16[4,512,512]{2,1,0:T(8,128)(2,1)S(1)}, bf16[4,512,512]{2,1,0:T(8,128)(2,1)}, u32[]{:S(2)}, u32[]{:S(2)}) collective-permute-start(bf16[4,512,512]{2,1,0:T(8,128)(2,1)S(1)} %pad_maximum_fusion.own_ref), channel_id=1, source_target_pairs={{0,1},{1,0},{2,3},{3,2},{4,5},{5,4},{6,7},{7,6},{8,9},{9,8},{10,11... | collective-permute-start | bytes 6291464 | tf_op jit(solution)/shard_map/ppermute | solution.py:147
Sparse Core Ops, SparseCore 0:
  22.5 88.9 all-gather.1

commit v18 on v17

--- a/solution.py
+++ b/solution.py
@@ -63,31 +63,33 @@
 def matmul_kernel(table_ref, own_ref, other_ref, weight_a_ref, weight_b_ref, out_ref, acc_ref):
     k = pl.program_id(0)
     half = pl.num_programs(0) // 2
+    flip = table_ref[2, 0]
 
     @pl.when(k == 0)
     def _():
         acc_ref[...] = jnp.zeros_like(acc_ref)
 
-    @pl.when(k < half)
-    def _():
-        acc_ref[...] += two_blocks(own_ref, weight_a_ref, weight_b_ref)
+    for pieces, first in ((own_ref, True), (other_ref, False)):
+        for turned in (False, True):
 
-    @pl.when(k >= half)
-    def _():
-        acc_ref[...] += two_blocks(other_ref, weight_a_ref, weight_b_ref)
+            @pl.when(((k < half) == first) & ((flip == 1) == turned))
+            def _(pieces=pieces, turned=turned):
+                acc_ref[...] += two_blocks(pieces, weight_a_ref, weight_b_ref, turned)
 
     @pl.when(k == pl.num_programs(0) - 1)
     def _():
         out_ref[...] = acc_ref[...].astype(out_ref.dtype)
 
 
-def two_blocks(piece_ref, weight_a_ref, weight_b_ref):
-    rows_a = weight_a_ref[0, :, 0]
-    rows_b = weight_b_ref[0, :, 0]
-    rows_a = rows_a.reshape(-1, rows_a.shape[-1])
-    rows_b = rows_b.reshape(-1, rows_b.shape[-1])
-    total = jnp.dot(piece_ref[0], rows_a, preferred_element_type=jnp.float32)
-    return total + jnp.dot(piece_ref[1], rows_b, preferred_element_type=jnp.float32)
+def rows_of(weight_ref, turned):
+    ys = weight_ref.shape[1]
+    order = range(ys - 1, -1, -1) if turned else range(ys)
+    return jnp.concatenate([weight_ref[0, y, 0] for y in order], axis=0)
+
+
+def two_blocks(piece_ref, weight_a_ref, weight_b_ref, turned):
+    total = jnp.dot(piece_ref[0], rows_of(weight_a_ref, turned), preferred_element_type=jnp.float32)
+    return total + jnp.dot(piece_ref[1], rows_of(weight_b_ref, turned), preferred_element_type=jnp.float32)
 
 
 def block_matmul(table, own, other, weight):
@@ -124,7 +126,11 @@
     partner = lax.ppermute(sent, "zh", [(0, 1), (1, 0)])
     zh = lax.axis_index("zh")
     pair = lax.dynamic_update_index_in_dim(pair, partner, 1, 0)
-    weight_xy = lax.all_gather(pair, ("x", "y"), axis=0, tiled=False)
+    order = [(x * 8 + y) * 2 for x in range(4) for y in range(8)]
+    turned = [(x * 8 + (7 - y)) * 2 + 1 for x in range(4) for y in range(8)]
+    weight_xy = lax.all_gather(
+        pair, ("x", "y", "c"), axis=0, tiled=False, axis_index_groups=[order, turned]
+    )
 
     kv_tail = projected[tok_rows - span - 2 :, 1:]
     q_tail = projected[tok_rows - 2 :, 0][None]
@@ -155,6 +161,7 @@
 
     weight = weight_xy.reshape(4, 8, *weight_xy.shape[1:])
     table = jnp.concatenate([table_for(core), table_for(1 - core)], axis=1)
+    table = jnp.concatenate([table, jnp.broadcast_to(core, (1, table.shape[1])).astype(jnp.int32)])
     return block_matmul(table, own, other, weight)
 
 

time: 126 us -> 189 us (1.50)
  waiting for transfers between devices: 55.4 us -> 118 us
    all_gather x1, waiting for transfers between devices: 9.12 us -> 71.9 us  [on_device(): lax.all_gather(pair, ('x', 'y', 'c'), axis=0, tiled=False, axis_index_gro...]
  transfers between devices with their start and end apart: 7 -> 7, of which waited for: 5 -> 5; matrix products, arithmetic and copies ran while one was open for 12% -> 8% of each run, Pallas kernels for 5% -> 3%
where the time goes in v18:
time: 189 us
  waiting for transfers between devices  118 us (62%)
  starting transfers between devices  27 us (14%)
  between operations  13.6 us (7%)
  Pallas kernels  13.1 us (7%)
  local copies, waits for them, and re-layouts  10.8 us (6%)
  other arithmetic  4.03 us (2%)
    all_gather x1, waiting for transfers between devices, on_device(): lax.all_gather(pair, ('x', 'y', 'c'), axis=0, tiled=False, axis_index_gro...  71.9 us
    ppermute x3, waiting for transfers between devices, line_slots(): slots.append(lax.ppermute(block, axis_name, pairs))  39.4 us
    ppermute x1, starting transfers between devices, on_device(): partner = lax.ppermute(sent, 'zh', [(0, 1), (1, 0)])  10.9 us
    ppermute x3, starting transfers between devices, line_slots(): slots.append(lax.ppermute(block, axis_name, pairs))  10.7 us
    pallas_call x1, Pallas kernels, block_matmul(): pl.pallas_call(matmul_kernel, grid_spec=grid_spec, out_shape=jax.ShapeDty...  7.39 us
    pallas_call x1, Pallas kernels, toeplitz_blocks(): pl.pallas_call(toeplitz_kernel, out_shape=jax.ShapeDtypeStruct((groups, s...  5.7 us
    slice x7, local copies, waits for them, and re-layouts, on_device(): window = jnp.concatenate([blocks[:-1], blocks[1:]], axis=1)  5.41 us
  transfers between devices with their start and end apart: 7, of which 5 were waited for; matrix products, arithmetic and copies ran while one was open for 8% of the time, Pallas kernels for 3%

profile of v18, /device:TPU:8, one launch (start us, length us, event | category | flops | bytes accessed | tf_op | source)
XLA Modules:
  0.0 188.6 jit_solution(5830682258409402439)
XLA Ops:
  6.5 0.0 all-gather.2.cloned.1.call-start
  6.5 0.9 stack.39
  7.4 10.9 %collective-permute-start.5 = (bf16[64,512]{1,0:T(8,128)(2,1)}, bf16[64,512]{1,0:T(8,128)(2,1)S(1)}, u32[]{:S(2)}, u32[]{:S(2)}) collective-permute-start(bf16[64,512]{1,0:T(8,128)(2,1)} %param.7), channel_id=1, source_target_pairs={{0,256},{256,0},{1,257},{257,1},{2,258},{258,2},{3,259},{259,3},{4... | collective-permute-start | bytes 196616 | tf_op jit(solution)/shard_map/ppermute | solution.py:126
  18.3 3.4 %collective-permute-done.5 = bf16[64,512]{1,0:T(8,128)(2,1)S(1)} collective-permute-done((bf16[64,512]{1,0:T(8,128)(2,1)}, bf16[64,512]{1,0:T(8,128)(2,1)S(1)}, u32[]{:S(2)}, u32[]{:S(2)}) %collective-permute-start.5) | collective-permute-done | bytes 65568 | tf_op jit(solution)/shard_map/ppermute | solution.py:126
  21.7 0.7 copy-done.3
  22.4 0.0 all-gather.2.cloned.1.call-update
  22.4 1.0 slice.75
  23.4 0.2 copy.25
  23.6 0.7 slice_bitcast_fusion.5
  24.3 1.1 pad_maximum_fusion.1
  25.4 3.5 %collective-permute-start = (bf16[131,2,512]{2,1,0:T(2,128)(2,1)}, bf16[131,2,512]{2,1,0:T(2,128)(2,1)S(1)}, u32[]{:S(2)}, u32[]{:S(2)}) collective-permute-start(bf16[131,2,512]{2,1,0:T(2,128)(2,1)} %pad_maximum_fusion.1), channel_id=1, source_target_pairs={{0,8},{8,16},{16,24},{24,32},{32,40},{40,48},{48,56},{56,64},{64,7... | collective-permute-start | bytes 804872 | tf_op jit(solution)/shard_map/ppermute | solution.py:20
  28.9 0.0 copy-done.5
  28.9 0.1 rev.3
  29.0 0.1 pad.8.clone
  29.1 0.7 maximum_maximum_fusion.row_ref
  29.8 5.7 %shard_map.46 = bf16[32,128,256]{2,1,0:T(8,128)(2,1)} custom-call(f32[32,384]{1,0:T(8,128)} %maximum_maximum_fusion.row_ref), custom_call_target="tpu_custom_call" | custom-call | tf_op jit(solution)/shard_map/pallas_call | solution.py:48
  35.5 0.0 collective-permute-done
  35.5 0.2 slice.102
  35.8 0.4 maximum_convert_fusion
  36.2 0.8 fusion
  37.0 0.2 fusion.7
  37.2 0.9 fusion.20
  38.0 0.2 copy.18
  38.3 0.1 slice.95
  38.4 0.9 copy.20
  39.3 1.3 copy.19
  40.5 0.9 slice.97
  41.5 1.1 copy.21
  42.6 0.0 copy-done
  42.6 1.9 fusion.4
  44.5 0.4 copy.22
  44.9 0.1 copy.28
  45.0 0.3 copy.23
  45.4 0.2 maximum_convert_fusion.1
  45.5 0.4 fusion.10
  45.9 4.3 %collective-permute-start.1 = (bf16[512,512]{1,0:T(8,128)(2,1)S(1)}, bf16[512,512]{1,0:T(8,128)(2,1)S(1)}, u32[]{:S(2)}, u32[]{:S(2)}) collective-permute-start(bf16[512,512]{1,0:T(8,128)(2,1)S(1)} %fusion.10), channel_id=1, source_target_pairs={{0,6},{2,0},{4,2},{6,4},{1,7},{3,1},{5,3},{7,5},{8,14},{10,8},{12,... | collective-permute-start | bytes 1572872 | tf_op jit(solution)/shard_map/ppermute | solution.py:59
  50.2 2.5 %collective-permute-start.2 = (bf16[512,512]{1,0:T(8,128)(2,1)S(1)}, bf16[512,512]{1,0:T(8,128)(2,1)S(1)}, u32[]{:S(2)}, u32[]{:S(2)}) collective-permute-start(bf16[512,512]{1,0:T(8,128)(2,1)S(1)} %fusion.10), channel_id=1, source_target_pairs={{0,4},{2,6},{4,0},{6,2},{1,5},{3,7},{5,1},{7,3},{8,12},{10,14},{12... | collective-permute-start | bytes 1572872 | tf_op jit(solution)/shard_map/ppermute | solution.py:59
  52.7 3.9 %collective-permute-start.3 = (bf16[512,512]{1,0:T(8,128)(2,1)S(1)}, bf16[512,512]{1,0:T(8,128)(2,1)S(1)}, u32[]{:S(2)}, u32[]{:S(2)}) collective-permute-start(bf16[512,512]{1,0:T(8,128)(2,1)S(1)} %fusion.10), channel_id=1, source_target_pairs={{0,2},{2,4},{4,6},{6,0},{1,3},{3,5},{5,7},{7,1},{8,10},{10,12},{12... | collective-permute-start | bytes 1572872 | tf_op jit(solution)/shard_map/ppermute | solution.py:59
  56.6 6.0 %collective-permute-done.1 = bf16[512,512]{1,0:T(8,128)(2,1)S(1)} collective-permute-done((bf16[512,512]{1,0:T(8,128)(2,1)S(1)}, bf16[512,512]{1,0:T(8,128)(2,1)S(1)}, u32[]{:S(2)}, u32[]{:S(2)}) %collective-permute-start.1) | collective-permute-done | bytes 524320 | tf_op jit(solution)/shard_map/ppermute | solution.py:59
  62.6 33.3 %collective-permute-done.2 = bf16[512,512]{1,0:T(8,128)(2,1)S(1)} collective-permute-done((bf16[512,512]{1,0:T(8,128)(2,1)S(1)}, bf16[512,512]{1,0:T(8,128)(2,1)S(1)}, u32[]{:S(2)}, u32[]{:S(2)}) %collective-permute-start.2) | collective-permute-done | bytes 524320 | tf_op jit(solution)/shard_map/ppermute | solution.py:59
  96.0 0.0 collective-permute-done.3
  96.0 0.3 pad_maximum_fusion.own_ref
  96.2 1.9 %collective-permute-start.4 = (bf16[4,512,512]{2,1,0:T(8,128)(2,1)S(1)}, bf16[4,512,512]{2,1,0:T(8,128)(2,1)}, u32[]{:S(2)}, u32[]{:S(2)}) collective-permute-start(bf16[4,512,512]{2,1,0:T(8,128)(2,1)S(1)} %pad_maximum_fusion.own_ref), channel_id=1, source_target_pairs={{0,1},{1,0},{2,3},{3,2},{4,5},{5,4},{6,7},{7,6},{8,9},{9,8},{10,11... | collective-permute-start | bytes 6291464 | tf_op jit(solution)/shard_map/ppermute | solution.py:153
  98.2 0.1 add_add_fusion
  98.3 0.6 concatenate.22.table_ref
  98.9 3.5 %collective-permute-done.4.other_ref = bf16[4,512,512]{2,1,0:T(8,128)(2,1)} collective-permute-done((bf16[4,512,512]{2,1,0:T(8,128)(2,1)S(1)}, bf16[4,512,512]{2,1,0:T(8,128)(2,1)}, u32[]{:S(2)}, u32[]{:S(2)}) %collective-permute-start.4) | collective-permute-done | bytes 2097184 | tf_op jit(solution)/shard_map/ppermute | solution.py:153
  102.4 71.9 %all-gather.2.cloned.1.call-done = bf16[32,2,64,512]{3,2,1,0:T(8,128)(2,1)} async-done(((bf16[1,2,64,512]{3,2,1,0:T(8,128)(2,1)}), bf16[32,2,64,512]{3,2,1,0:T(8,128)(2,1)}) %all-gather.2.cloned.1.call-update) | async-done | bytes 4194320 | tf_op jit(solution)/shard_map/all_gather | solution.py:131
  174.3 7.4 %shard_map.47 = bf16[512,512]{1,0:T(8,128)(2,1)} custom-call(s32[3,8]{1,0:T(4,128)} %concatenate.22.table_ref, bf16[4,512,512]{2,1,0:T(8,128)(2,1)} %copy-done.1, bf16[4,512,512]{2,1,0:T(8,128)(2,1)} %collective-permute-done.4.other_ref, bf16[4,8,2,64,512]{4,3,2,1,0:T(8,128)(2,1)} %bitcast.45, bf16[4,8,2,64,512]{4,3,2,1,0:T(8,128)(2,1)} %bitcast.46), custom_call_target="tpu_custom_call" | custom-call | tf_op jit(solution)/shard_map/pallas_call | solution.py:112
  (22 shorter events, 0.2 us)
Async XLA Ops:
  6.5 22.3 %copy-start.5 = (bf16[32,128]{1,0:T(8,128)(2,1)S(1)}, bf16[32,128]{1,0:T(8,128)(2,1)}, u32[]{:S(2)}) copy-start(bf16[32,128]{1,0:T(8,128)(2,1)} %param.6) | copy-start | bytes 24580
  6.5 22.5 %copy-start.4 = (f32[3,3,512]{2,1,0:T(4,128)S(1)}, f32[3,3,512]{2,1,0:T(4,128)}, u32[]{:S(2)}) copy-start(f32[3,3,512]{2,1,0:T(4,128)} %param.5) | copy-start | bytes 55300
  6.5 167.8 %all-gather.2.cloned.1.call-start = ((), (), s32[]{:S(2)}) async-start(), calls=%async_computation | async-start | bytes 4325376 | tf_op jit(solution)/shard_map/all_gather | solution.py:131
  7.4 14.3 %collective-permute-start.5 = (bf16[64,512]{1,0:T(8,128)(2,1)}, bf16[64,512]{1,0:T(8,128)(2,1)S(1)}, u32[]{:S(2)}, u32[]{:S(2)}) collective-permute-start(bf16[64,512]{1,0:T(8,128)(2,1)} %param.7), channel_id=1, source_target_pairs={{0,256},{256,0},{1,257},{257,1},{2,258},{258,2},{3,259},{259,3},{4... | collective-permute-start | bytes 196616 | tf_op jit(solution)/shard_map/ppermute | solution.py:126
  21.7 0.7 copy-start.3
  25.4 10.1 %collective-permute-start = (bf16[131,2,512]{2,1,0:T(2,128)(2,1)}, bf16[131,2,512]{2,1,0:T(2,128)(2,1)S(1)}, u32[]{:S(2)}, u32[]{:S(2)}) collective-permute-start(bf16[131,2,512]{2,1,0:T(2,128)(2,1)} %pad_maximum_fusion.1), channel_id=1, source_target_pairs={{0,8},{8,16},{16,24},{24,32},{32,40},{40,48},{48,56},{56,64},{64,7... | collective-permute-start | bytes 804872 | tf_op jit(solution)/shard_map/ppermute | solution.py:20
  29.8 5.7 %copy-start.2 = (bf16[512,3,512]{2,0,1:T(8,128)(2,1)S(1)}, bf16[512,3,512]{2,0,1:T(8,128)(2,1)}, u32[]{:S(2)}) copy-start(bf16[512,3,512]{2,0,1:T(8,128)(2,1)} %param.4) | copy-start | bytes 4718596
  29.8 6.0 %slice-start = ((bf16[512,3,512]{2,0,1:T(8,128)(2,1)}), bf16[512,2,512]{2,0,1:T(8,128)(2,1)S(1)}, s32[]{:S(2)}) async-start(bf16[512,3,512]{2,0,1:T(8,128)(2,1)} %param.4), calls=%async_computation.1 | async-start | bytes 2097152 | tf_op jit(solution)/shard_map/slice | solution.py:138
  38.4 4.2 %copy-start = (bf16[32,128,256]{2,1,0:T(8,128)(2,1)S(1)}, bf16[32,128,256]{2,1,0:T(8,128)(2,1)}, u32[]{:S(2)}) copy-start(bf16[32,128,256]{2,1,0:T(8,128)(2,1)} %shard_map.46) | copy-start | bytes 6291460
  45.9 16.7 %collective-permute-start.1 = (bf16[512,512]{1,0:T(8,128)(2,1)S(1)}, bf16[512,512]{1,0:T(8,128)(2,1)S(1)}, u32[]{:S(2)}, u32[]{:S(2)}) collective-permute-start(bf16[512,512]{1,0:T(8,128)(2,1)S(1)} %fusion.10), channel_id=1, source_target_pairs={{0,6},{2,0},{4,2},{6,4},{1,7},{3,1},{5,3},{7,5},{8,14},{10,8},{12,... | collective-permute-start | bytes 1572872 | tf_op jit(solution)/shard_map/ppermute | solution.py:59
  50.2 45.8 %collective-permute-start.2 = (bf16[512,512]{1,0:T(8,128)(2,1)S(1)}, bf16[512,512]{1,0:T(8,128)(2,1)S(1)}, u32[]{:S(2)}, u32[]{:S(2)}) collective-permute-start(bf16[512,512]{1,0:T(8,128)(2,1)S(1)} %fusion.10), channel_id=1, source_target_pairs={{0,4},{2,6},{4,0},{6,2},{1,5},{3,7},{5,1},{7,3},{8,12},{10,14},{12... | collective-permute-start | bytes 1572872 | tf_op jit(solution)/shard_map/ppermute | solution.py:59
  52.7 43.3 %collective-permute-start.3 = (bf16[512,512]{1,0:T(8,128)(2,1)S(1)}, bf16[512,512]{1,0:T(8,128)(2,1)S(1)}, u32[]{:S(2)}, u32[]{:S(2)}) collective-permute-start(bf16[512,512]{1,0:T(8,128)(2,1)S(1)} %fusion.10), channel_id=1, source_target_pairs={{0,2},{2,4},{4,6},{6,0},{1,3},{3,5},{5,7},{7,1},{8,10},{10,12},{12... | collective-permute-start | bytes 1572872 | tf_op jit(solution)/shard_map/ppermute | solution.py:59
  96.2 78.1 %copy-start.1 = (bf16[4,512,512]{2,1,0:T(8,128)(2,1)}, bf16[4,512,512]{2,1,0:T(8,128)(2,1)S(1)}, u32[]{:S(2)}) copy-start(bf16[4,512,512]{2,1,0:T(8,128)(2,1)S(1)} %pad_maximum_fusion.own_ref) | copy-start | bytes 6291460
  96.2 6.2 %collective-permute-start.4 = (bf16[4,512,512]{2,1,0:T(8,128)(2,1)S(1)}, bf16[4,512,512]{2,1,0:T(8,128)(2,1)}, u32[]{:S(2)}, u32[]{:S(2)}) collective-permute-start(bf16[4,512,512]{2,1,0:T(8,128)(2,1)S(1)} %pad_maximum_fusion.own_ref), channel_id=1, source_target_pairs={{0,1},{1,0},{2,3},{3,2},{4,5},{5,4},{6,7},{7,6},{8,9},{9,8},{10,11... | collective-permute-start | bytes 6291464 | tf_op jit(solution)/shard_map/ppermute | solution.py:153
Sparse Core Ops, SparseCore 0:
  22.5 151.7 all-gather.1

commit v19 on v17

--- a/solution.py
+++ b/solution.py
@@ -82,8 +82,8 @@
 
 
 def two_blocks(piece_ref, weight_a_ref, weight_b_ref):
-    rows_a = weight_a_ref[0, :, 0]
-    rows_b = weight_b_ref[0, :, 0]
+    rows_a = weight_a_ref[:, 0, 0]
+    rows_b = weight_b_ref[:, 0, 0]
     rows_a = rows_a.reshape(-1, rows_a.shape[-1])
     rows_b = rows_b.reshape(-1, rows_b.shape[-1])
     total = jnp.dot(piece_ref[0], rows_a, preferred_element_type=jnp.float32)
@@ -92,13 +92,13 @@
 
 def block_matmul(table, own, other, weight):
     n, tok, width = own.shape
-    _, ys, _, rows, cols = weight.shape
+    ys, _, _, rows, cols = weight.shape
     steps = n // 2
     in_specs = [
         pl.BlockSpec((2, tok, width), lambda k, t: (jnp.minimum(k, steps - 1), 0, 0)),
         pl.BlockSpec((2, tok, width), lambda k, t: (jnp.maximum(k - steps, 0), 0, 0)),
-        pl.BlockSpec((1, ys, 1, rows, cols), lambda k, t: (t[0, 2 * k], 0, t[1, 2 * k], 0, 0)),
-        pl.BlockSpec((1, ys, 1, rows, cols), lambda k, t: (t[0, 2 * k + 1], 0, t[1, 2 * k + 1], 0, 0)),
+        pl.BlockSpec((ys, 1, 1, rows, cols), lambda k, t: (0, t[0, 2 * k], t[1, 2 * k], 0, 0)),
+        pl.BlockSpec((ys, 1, 1, rows, cols), lambda k, t: (0, t[0, 2 * k + 1], t[1, 2 * k + 1], 0, 0)),
     ]
     grid_spec = pltpu.PrefetchScalarGridSpec(
         num_scalar_prefetch=1,
@@ -124,7 +124,7 @@
     partner = lax.ppermute(sent, "zh", [(0, 1), (1, 0)])
     zh = lax.axis_index("zh")
     pair = lax.dynamic_update_index_in_dim(pair, partner, 1, 0)
-    weight_xy = lax.all_gather(pair, ("x", "y"), axis=0, tiled=False)
+    weight_yx = lax.all_gather(pair, ("y", "x"), axis=0, tiled=False)
 
     kv_tail = projected[tok_rows - span - 2 :, 1:]
     q_tail = projected[tok_rows - 2 :, 0][None]
@@ -153,7 +153,7 @@
         w = 2 * sources + c
         return jnp.stack([w % 4, (w // 4 + zh) % 2]).astype(jnp.int32)
 
-    weight = weight_xy.reshape(4, 8, *weight_xy.shape[1:])
+    weight = weight_yx.reshape(8, 4, *weight_yx.shape[1:])
     table = jnp.concatenate([table_for(core), table_for(1 - core)], axis=1)
     return block_matmul(table, own, other, weight)
 

time: 126 us -> 126 us (level)
  no operation moved by 1% of the time
where the time goes in v19:
time: 126 us
  waiting for transfers between devices  55.5 us (44%)
  starting transfers between devices  27 us (21%)
  between operations  13.6 us (11%)
  Pallas kernels  13.1 us (10%)
  local copies, waits for them, and re-layouts  10.2 us (8%)
  other arithmetic  4.62 us (4%)
  matrix products  1.88 us (1%)
    ppermute x3, waiting for transfers between devices, line_slots(): slots.append(lax.ppermute(block, axis_name, pairs))  39.4 us
    ppermute x1, starting transfers between devices, on_device(): partner = lax.ppermute(sent, 'zh', [(0, 1), (1, 0)])  10.9 us
    ppermute x3, starting transfers between devices, line_slots(): slots.append(lax.ppermute(block, axis_name, pairs))  10.7 us
    all_gather x1, waiting for transfers between devices, on_device(): weight_yx = lax.all_gather(pair, ('y', 'x'), axis=0, tiled=False)  9.21 us
    pallas_call x1, Pallas kernels, block_matmul(): pl.pallas_call(matmul_kernel, grid_spec=grid_spec, out_shape=jax.ShapeDty...  7.36 us
    pallas_call x1, Pallas kernels, toeplitz_blocks(): pl.pallas_call(toeplitz_kernel, out_shape=jax.ShapeDtypeStruct((groups, s...  5.7 us
    slice x7, local copies, waits for them, and re-layouts, on_device(): window = jnp.concatenate([blocks[:-1], blocks[1:]], axis=1)  5.41 us
    ppermute x1, waiting for transfers between devices, on_device(): other = lax.ppermute(own, 'c', [(0, 1), (1, 0)])  3.52 us
  transfers between devices with their start and end apart: 7, of which 5 were waited for; matrix products, arithmetic and copies ran while one was open for 12% of the time, Pallas kernels for 5%

profile of v19, /device:TPU:8, one launch (start us, length us, event | category | flops | bytes accessed | tf_op | source)
XLA Modules:
  0.0 125.8 jit_solution(54043419509107007)
XLA Ops:
  6.5 0.0 all-gather.2.cloned.1.call-start
  6.5 0.9 stack.39
  7.4 10.9 %collective-permute-start.5 = (bf16[64,512]{1,0:T(8,128)(2,1)}, bf16[64,512]{1,0:T(8,128)(2,1)S(1)}, u32[]{:S(2)}, u32[]{:S(2)}) collective-permute-start(bf16[64,512]{1,0:T(8,128)(2,1)} %param.7), channel_id=1, source_target_pairs={{0,256},{256,0},{1,257},{257,1},{2,258},{258,2},{3,259},{259,3},{4... | collective-permute-start | bytes 196616 | tf_op jit(solution)/shard_map/ppermute | solution.py:124
  18.3 3.4 %collective-permute-done.5 = bf16[64,512]{1,0:T(8,128)(2,1)S(1)} collective-permute-done((bf16[64,512]{1,0:T(8,128)(2,1)}, bf16[64,512]{1,0:T(8,128)(2,1)S(1)}, u32[]{:S(2)}, u32[]{:S(2)}) %collective-permute-start.5) | collective-permute-done | bytes 65568 | tf_op jit(solution)/shard_map/ppermute | solution.py:124
  21.7 0.7 copy-done.3
  22.4 0.0 all-gather.2.cloned.1.call-update
  22.4 1.0 slice.75
  23.4 0.2 copy.25
  23.6 0.7 slice_bitcast_fusion.5
  24.3 1.1 pad_maximum_fusion.1
  25.4 3.5 %collective-permute-start = (bf16[131,2,512]{2,1,0:T(2,128)(2,1)}, bf16[131,2,512]{2,1,0:T(2,128)(2,1)S(1)}, u32[]{:S(2)}, u32[]{:S(2)}) collective-permute-start(bf16[131,2,512]{2,1,0:T(2,128)(2,1)} %pad_maximum_fusion.1), channel_id=1, source_target_pairs={{0,8},{8,16},{16,24},{24,32},{32,40},{40,48},{48,56},{56,64},{64,7... | collective-permute-start | bytes 804872 | tf_op jit(solution)/shard_map/ppermute | solution.py:20
  28.9 0.0 copy-done.5
  28.9 0.1 rev.3
  29.0 0.1 pad.7.clone
  29.1 0.0 copy-done.4
  29.1 0.7 maximum_maximum_fusion.row_ref
  29.8 5.7 %shard_map.46 = bf16[32,128,256]{2,1,0:T(8,128)(2,1)} custom-call(f32[32,384]{1,0:T(8,128)} %maximum_maximum_fusion.row_ref), custom_call_target="tpu_custom_call" | custom-call | tf_op jit(solution)/shard_map/pallas_call | solution.py:48
  35.5 0.0 collective-permute-done
  35.5 0.2 slice.102
  35.8 0.4 maximum_convert_fusion
  36.2 0.8 fusion
  37.0 0.2 fusion.7
  37.2 0.9 fusion.20
  38.0 0.2 copy.18
  38.3 0.1 slice.95
  38.4 0.9 copy.20
  39.3 1.3 %copy.19 = bf16[512,1,512]{0,2,1:T(8,128)(2,1)S(1)} copy(bf16[512,1,512]{2,0,1:T(8,128)(2,1)} %get-tuple-element.10) | data formatting | bytes 1048576 | tf_op jit(solution)/shard_map/slice | solution.py:139
  40.6 0.9 slice.97
  41.5 1.1 copy.21
  42.6 1.9 %fusion.4 = f32[4,128,32,16]{1,3,0,2:T(8,128)S(1)} fusion(bf16[32,128,256]{2,1,0:T(8,128)(2,1)S(1)} %copy-done, bf16[4,128,32,16]{1,3,0,2:T(8,128)(2,1)S(1)} %copy.21, bf16[4,128,32,16]{1,3,0,2:T(8,128)(2,1)} %copy.20), kind=kOutput, calls=%fused_computation.8 | convolution fusion | flops 136314880 | bytes 4194304 | tf_op jit(solution)/shard_map/gij,bjgc->bigc/dot_general | solution.py:141
  44.5 0.4 copy.22
  44.9 0.1 copy.28
  45.0 0.3 copy.23
  45.4 0.2 maximum_convert_fusion.1
  45.5 0.4 fusion.10
  45.9 4.3 %collective-permute-start.1 = (bf16[512,512]{1,0:T(8,128)(2,1)S(1)}, bf16[512,512]{1,0:T(8,128)(2,1)S(1)}, u32[]{:S(2)}, u32[]{:S(2)}) collective-permute-start(bf16[512,512]{1,0:T(8,128)(2,1)S(1)} %fusion.10), channel_id=1, source_target_pairs={{0,6},{2,0},{4,2},{6,4},{1,7},{3,1},{5,3},{7,5},{8,14},{10,8},{12,... | collective-permute-start | bytes 1572872 | tf_op jit(solution)/shard_map/ppermute | solution.py:59
  50.2 2.5 %collective-permute-start.2 = (bf16[512,512]{1,0:T(8,128)(2,1)S(1)}, bf16[512,512]{1,0:T(8,128)(2,1)S(1)}, u32[]{:S(2)}, u32[]{:S(2)}) collective-permute-start(bf16[512,512]{1,0:T(8,128)(2,1)S(1)} %fusion.10), channel_id=1, source_target_pairs={{0,4},{2,6},{4,0},{6,2},{1,5},{3,7},{5,1},{7,3},{8,12},{10,14},{12... | collective-permute-start | bytes 1572872 | tf_op jit(solution)/shard_map/ppermute | solution.py:59
  52.7 3.9 %collective-permute-start.3 = (bf16[512,512]{1,0:T(8,128)(2,1)S(1)}, bf16[512,512]{1,0:T(8,128)(2,1)S(1)}, u32[]{:S(2)}, u32[]{:S(2)}) collective-permute-start(bf16[512,512]{1,0:T(8,128)(2,1)S(1)} %fusion.10), channel_id=1, source_target_pairs={{0,2},{2,4},{4,6},{6,0},{1,3},{3,5},{5,7},{7,1},{8,10},{10,12},{12... | collective-permute-start | bytes 1572872 | tf_op jit(solution)/shard_map/ppermute | solution.py:59
  56.6 6.0 %collective-permute-done.1 = bf16[512,512]{1,0:T(8,128)(2,1)S(1)} collective-permute-done((bf16[512,512]{1,0:T(8,128)(2,1)S(1)}, bf16[512,512]{1,0:T(8,128)(2,1)S(1)}, u32[]{:S(2)}, u32[]{:S(2)}) %collective-permute-start.1) | collective-permute-done | bytes 524320 | tf_op jit(solution)/shard_map/ppermute | solution.py:59
  62.6 33.3 %collective-permute-done.2 = bf16[512,512]{1,0:T(8,128)(2,1)S(1)} collective-permute-done((bf16[512,512]{1,0:T(8,128)(2,1)S(1)}, bf16[512,512]{1,0:T(8,128)(2,1)S(1)}, u32[]{:S(2)}, u32[]{:S(2)}) %collective-permute-start.2) | collective-permute-done | bytes 524320 | tf_op jit(solution)/shard_map/ppermute | solution.py:59
  96.0 0.0 collective-permute-done.3
  96.0 0.3 pad_maximum_fusion.own_ref
  96.2 0.0 copy-start.1
  96.2 1.9 %collective-permute-start.4 = (bf16[4,512,512]{2,1,0:T(8,128)(2,1)S(1)}, bf16[4,512,512]{2,1,0:T(8,128)(2,1)}, u32[]{:S(2)}, u32[]{:S(2)}) collective-permute-start(bf16[4,512,512]{2,1,0:T(8,128)(2,1)S(1)} %pad_maximum_fusion.own_ref), channel_id=1, source_target_pairs={{0,1},{1,0},{2,3},{3,2},{4,5},{5,4},{6,7},{7,6},{8,9},{9,8},{10,11... | collective-permute-start | bytes 6291464 | tf_op jit(solution)/shard_map/ppermute | solution.py:147
  98.2 0.7 add_add_fusion.table_ref
  98.9 3.5 %collective-permute-done.4.other_ref = bf16[4,512,512]{2,1,0:T(8,128)(2,1)} collective-permute-done((bf16[4,512,512]{2,1,0:T(8,128)(2,1)S(1)}, bf16[4,512,512]{2,1,0:T(8,128)(2,1)}, u32[]{:S(2)}, u32[]{:S(2)}) %collective-permute-start.4) | collective-permute-done | bytes 2097184 | tf_op jit(solution)/shard_map/ppermute | solution.py:147
  102.4 9.2 %all-gather.2.cloned.1.call-done = bf16[32,2,64,512]{3,2,1,0:T(8,128)(2,1)} async-done(((bf16[1,2,64,512]{3,2,1,0:T(8,128)(2,1)}), bf16[32,2,64,512]{3,2,1,0:T(8,128)(2,1)}) %all-gather.2.cloned.1.call-update) | async-done | bytes 4194320 | tf_op jit(solution)/shard_map/all_gather | solution.py:127
  111.6 7.4 %shard_map.47 = bf16[512,512]{1,0:T(8,128)(2,1)} custom-call(s32[2,8]{1,0:T(2,128)} %add_add_fusion.table_ref, bf16[4,512,512]{2,1,0:T(8,128)(2,1)} %copy-done.1, bf16[4,512,512]{2,1,0:T(8,128)(2,1)} %collective-permute-done.4.other_ref, bf16[8,4,2,64,512]{4,3,2,1,0:T(8,128)(2,1)} %bitcast.45, bf16[8,4,2,64,512]{4,3,2,1,0:T(8,128)(2,1)} %bitcast.46), custom_call_target="tpu_custom_call" | custom-call | tf_op jit(solution)/shard_map/pallas_call | solution.py:110
  (21 shorter events, 0.2 us)
Async XLA Ops:
  6.5 22.3 %copy-start.5 = (bf16[32,128]{1,0:T(8,128)(2,1)S(1)}, bf16[32,128]{1,0:T(8,128)(2,1)}, u32[]{:S(2)}) copy-start(bf16[32,128]{1,0:T(8,128)(2,1)} %param.6) | copy-start | bytes 24580
  6.5 22.5 %copy-start.4 = (f32[3,3,512]{2,1,0:T(4,128)S(1)}, f32[3,3,512]{2,1,0:T(4,128)}, u32[]{:S(2)}) copy-start(f32[3,3,512]{2,1,0:T(4,128)} %param.5) | copy-start | bytes 55300
  6.5 105.1 %all-gather.2.cloned.1.call-start = ((), (), s32[]{:S(2)}) async-start(), calls=%async_computation | async-start | bytes 4325376 | tf_op jit(solution)/shard_map/all_gather | solution.py:127
  7.4 14.3 %collective-permute-start.5 = (bf16[64,512]{1,0:T(8,128)(2,1)}, bf16[64,512]{1,0:T(8,128)(2,1)S(1)}, u32[]{:S(2)}, u32[]{:S(2)}) collective-permute-start(bf16[64,512]{1,0:T(8,128)(2,1)} %param.7), channel_id=1, source_target_pairs={{0,256},{256,0},{1,257},{257,1},{2,258},{258,2},{3,259},{259,3},{4... | collective-permute-start | bytes 196616 | tf_op jit(solution)/shard_map/ppermute | solution.py:124
  21.7 0.7 copy-start.3
  25.4 10.1 %collective-permute-start = (bf16[131,2,512]{2,1,0:T(2,128)(2,1)}, bf16[131,2,512]{2,1,0:T(2,128)(2,1)S(1)}, u32[]{:S(2)}, u32[]{:S(2)}) collective-permute-start(bf16[131,2,512]{2,1,0:T(2,128)(2,1)} %pad_maximum_fusion.1), channel_id=1, source_target_pairs={{0,8},{8,16},{16,24},{24,32},{32,40},{40,48},{48,56},{56,64},{64,7... | collective-permute-start | bytes 804872 | tf_op jit(solution)/shard_map/ppermute | solution.py:20
  29.8 5.7 %copy-start.2 = (bf16[512,3,512]{2,0,1:T(8,128)(2,1)S(1)}, bf16[512,3,512]{2,0,1:T(8,128)(2,1)}, u32[]{:S(2)}) copy-start(bf16[512,3,512]{2,0,1:T(8,128)(2,1)} %param.4) | copy-start | bytes 4718596
  29.8 6.0 %slice-start = ((bf16[512,3,512]{2,0,1:T(8,128)(2,1)}), bf16[512,2,512]{2,0,1:T(8,128)(2,1)S(1)}, s32[]{:S(2)}) async-start(bf16[512,3,512]{2,0,1:T(8,128)(2,1)} %param.4), calls=%async_computation.1 | async-start | bytes 2097152 | tf_op jit(solution)/shard_map/slice | solution.py:132
  38.4 4.2 %copy-start = (bf16[32,128,256]{2,1,0:T(8,128)(2,1)S(1)}, bf16[32,128,256]{2,1,0:T(8,128)(2,1)}, u32[]{:S(2)}) copy-start(bf16[32,128,256]{2,1,0:T(8,128)(2,1)} %shard_map.46) | copy-start | bytes 6291460
  45.9 16.7 %collective-permute-start.1 = (bf16[512,512]{1,0:T(8,128)(2,1)S(1)}, bf16[512,512]{1,0:T(8,128)(2,1)S(1)}, u32[]{:S(2)}, u32[]{:S(2)}) collective-permute-start(bf16[512,512]{1,0:T(8,128)(2,1)S(1)} %fusion.10), channel_id=1, source_target_pairs={{0,6},{2,0},{4,2},{6,4},{1,7},{3,1},{5,3},{7,5},{8,14},{10,8},{12,... | collective-permute-start | bytes 1572872 | tf_op jit(solution)/shard_map/ppermute | solution.py:59
  50.2 45.8 %collective-permute-start.2 = (bf16[512,512]{1,0:T(8,128)(2,1)S(1)}, bf16[512,512]{1,0:T(8,128)(2,1)S(1)}, u32[]{:S(2)}, u32[]{:S(2)}) collective-permute-start(bf16[512,512]{1,0:T(8,128)(2,1)S(1)} %fusion.10), channel_id=1, source_target_pairs={{0,4},{2,6},{4,0},{6,2},{1,5},{3,7},{5,1},{7,3},{8,12},{10,14},{12... | collective-permute-start | bytes 1572872 | tf_op jit(solution)/shard_map/ppermute | solution.py:59
  52.7 43.3 %collective-permute-start.3 = (bf16[512,512]{1,0:T(8,128)(2,1)S(1)}, bf16[512,512]{1,0:T(8,128)(2,1)S(1)}, u32[]{:S(2)}, u32[]{:S(2)}) collective-permute-start(bf16[512,512]{1,0:T(8,128)(2,1)S(1)} %fusion.10), channel_id=1, source_target_pairs={{0,2},{2,4},{4,6},{6,0},{1,3},{3,5},{5,7},{7,1},{8,10},{10,12},{12... | collective-permute-start | bytes 1572872 | tf_op jit(solution)/shard_map/ppermute | solution.py:59
  96.2 15.4 %copy-start.1 = (bf16[4,512,512]{2,1,0:T(8,128)(2,1)}, bf16[4,512,512]{2,1,0:T(8,128)(2,1)S(1)}, u32[]{:S(2)}) copy-start(bf16[4,512,512]{2,1,0:T(8,128)(2,1)S(1)} %pad_maximum_fusion.own_ref) | copy-start | bytes 6291460
  96.2 6.2 %collective-permute-start.4 = (bf16[4,512,512]{2,1,0:T(8,128)(2,1)S(1)}, bf16[4,512,512]{2,1,0:T(8,128)(2,1)}, u32[]{:S(2)}, u32[]{:S(2)}) collective-permute-start(bf16[4,512,512]{2,1,0:T(8,128)(2,1)S(1)} %pad_maximum_fusion.own_ref), channel_id=1, source_target_pairs={{0,1},{1,0},{2,3},{3,2},{4,5},{5,4},{6,7},{7,6},{8,9},{9,8},{10,11... | collective-permute-start | bytes 6291464 | tf_op jit(solution)/shard_map/ppermute | solution.py:147
Sparse Core Ops, SparseCore 0:
  22.5 89.0 all-gather.1
